TPU v7x, 32 devices: a whole 2x2x4 slice. The times are simulated.
32 devices in a mesh: tm: 8 (over z, y), patch: 4 (over x, core).
Axes of the slice: x: 2, y: 2, z: 4, core: 2. Of those that a mesh axis runs over, the one named last changes fastest.
Arguments:
- tokens: bfloat16 [64, 64, 1408], P(('tm', 'patch')), may hold values from -6 to 6
- ln_gain: float32 [1408], replicated, may hold values from 0.1 to 1.9
- ln_bias: float32 [1408], replicated, may hold values from -3 to 3
- w_qkv: bfloat16 [1408, 4224], replicated, may hold values from -0.15625 to 0.15625
- w_out: bfloat16 [1408, 1408], replicated, may hold values from -0.15625 to 0.15625
- q_time: bfloat16 [64, 64, 1408], P(None, 'tm', 'patch'), may hold values from -24 to 24
- k_time: bfloat16 [64, 64, 1408], P(None, 'tm', 'patch'), may hold values from -24 to 24
- v_time: bfloat16 [64, 64, 1408], P(None, 'tm', 'patch'), may hold values from -4 to 4
- grad_out: bfloat16 [64, 64, 1408], P(('tm', 'patch')), may hold values from -6 to 6
Outputs:
- grad_x: bfloat16 [64, 64, 1408], P(('tm', 'patch'))
- grad_w_qkv: float32 [1408, 4224], P(('tm', 'patch'))
All inputs are finite; a program needn't handle non-finite values.
Results may differ from a plain program's by a relative error of at most 0.0061.
Values may be sent and summed in bfloat16 or wider, within the bound.
No kernel may reach another device: no remote copies, remote signals or barrier semaphores. Data moves between devices by JAX's collectives and lax.ppermute only.
A program may use at most 128 MiB of HBM per device.

v0:
```python
import math

import jax
import jax.numpy as jnp
from jax import lax
from jax.sharding import PartitionSpec as P

DH = 88


def attend_head(items):
    query_one, key_one, value_one, grad_one = items
    factor = 1.0 / math.sqrt(DH)
    scores = (
        jnp.einsum("td,sd->ts", query_one, key_one, preferred_element_type=jnp.float32) * factor
    )
    row_max = jnp.max(scores, axis=-1, keepdims=True)
    exponent = jnp.exp(scores - row_max)
    probability = exponent / jnp.sum(exponent, axis=-1, keepdims=True)
    prob_grad = jnp.einsum("td,sd->ts", grad_one, value_one, preferred_element_type=jnp.float32)
    row_dot = jnp.sum(probability * prob_grad, axis=-1, keepdims=True)
    score_grad = (probability * (prob_grad - row_dot) * factor).astype(jnp.bfloat16)
    prob_low = probability.astype(jnp.bfloat16)
    grad_query = jnp.einsum("ts,sd->td", score_grad, key_one, preferred_element_type=jnp.float32)
    grad_key = jnp.einsum("ts,td->sd", score_grad, query_one, preferred_element_type=jnp.float32)
    grad_value = jnp.einsum("ts,td->sd", prob_low, grad_one, preferred_element_type=jnp.float32)
    return (
        grad_query.astype(jnp.bfloat16),
        grad_key.astype(jnp.bfloat16),
        grad_value.astype(jnp.bfloat16),
    )


def attend(query_rows, key_rows, value_rows, grad_rows, heads_part):
    frames = query_rows.shape[0]

    def split_heads(values):
        return values.reshape(frames, heads_part, DH).transpose(1, 0, 2)

    results = lax.map(
        attend_head,
        (
            split_heads(query_rows),
            split_heads(key_rows),
            split_heads(value_rows),
            split_heads(grad_rows),
        ),
    )
    width_part = heads_part * DH

    def join_heads(values):
        return values.transpose(1, 0, 2).reshape(frames, width_part)

    return (join_heads(results[0]), join_heads(results[1]), join_heads(results[2]))


def per_device(tokens, ln_gain, ln_bias, w_qkv, w_out, q_time, k_time, v_time, grad_out):
    t_dev, patches, model_width = tokens.shape
    frames, patch_part, width_part = q_time.shape
    n_time = lax.axis_size("tm")
    n_patch = lax.axis_size("patch")
    devices = n_time * n_patch
    heads_part = width_part // DH
    factor = 1.0 / math.sqrt(frames * patches)
    contract_rows = (((0,), (0,)), ((), ()))
    contract_cols = (((1,), (1,)), ((), ()))
    grad_rows = grad_out.reshape(-1, model_width)
    d_attn = lax.dot_general(grad_rows, w_out, contract_cols, preferred_element_type=jnp.float32)
    d_attn = d_attn.astype(jnp.bfloat16).reshape(t_dev, patches, model_width)
    d_time = lax.all_to_all(
        lax.all_to_all(d_attn, "patch", split_axis=2, concat_axis=0, tiled=True),
        "tm",
        split_axis=1,
        concat_axis=0,
        tiled=True,
    )
    query_list = []
    key_list = []
    value_list = []
    for column in range(patch_part):
        grad_query, grad_key, grad_value = attend(
            q_time[:, column], k_time[:, column], v_time[:, column], d_time[:, column], heads_part
        )
        query_list.append(grad_query)
        key_list.append(grad_key)
        value_list.append(grad_value)
    query_time = jnp.stack(query_list, axis=1)
    key_time = jnp.stack(key_list, axis=1)
    value_time = jnp.stack(value_list, axis=1)
    query_space, key_space, value_space = (
        lax.all_to_all(
            lax.all_to_all(query_time, "tm", split_axis=0, concat_axis=1, tiled=True),
            "patch",
            split_axis=0,
            concat_axis=2,
            tiled=True,
        ),
        lax.all_to_all(
            lax.all_to_all(key_time, "tm", split_axis=0, concat_axis=1, tiled=True),
            "patch",
            split_axis=0,
            concat_axis=2,
            tiled=True,
        ),
        lax.all_to_all(
            lax.all_to_all(value_time, "tm", split_axis=0, concat_axis=1, tiled=True),
            "patch",
            split_axis=0,
            concat_axis=2,
            tiled=True,
        ),
    )
    grad_qkv = jnp.concatenate([query_space, key_space, value_space], axis=-1).reshape(
        -1, 3 * model_width
    )
    as_float = tokens.reshape(-1, model_width).astype(jnp.float32)
    centered = as_float - jnp.mean(as_float, axis=-1, keepdims=True)
    variance = jnp.mean(centered * centered, axis=-1, keepdims=True)
    inverse = lax.rsqrt(variance + 1e-06)
    normed = centered * inverse
    norm_out = (normed * ln_gain + ln_bias).astype(jnp.bfloat16)
    grouped = lax.all_gather(
        norm_out.reshape(t_dev, patches, model_width), "patch", axis=0, tiled=True
    )
    norm_time = lax.all_to_all(grouped, "tm", split_axis=1, concat_axis=0, tiled=True)
    time_rows = norm_time.reshape(-1, model_width)
    pieces_in = (
        query_time.reshape(-1, width_part),
        key_time.reshape(-1, width_part),
        value_time.reshape(-1, width_part),
    )
    pieces = [
        lax.dot_general(time_rows, other, contract_rows, preferred_element_type=jnp.float32)
        for other in pieces_in
    ]
    partial_sum = lax.psum_scatter(
        jnp.stack(pieces, axis=1) * factor, "tm", scatter_dimension=0, tiled=True
    )
    grad_w_qkv = lax.all_to_all(partial_sum, "patch", split_axis=0, concat_axis=2, tiled=True)
    grad_w_qkv = grad_w_qkv.reshape(model_width // devices, 3 * model_width)
    d_norm = lax.dot_general(grad_qkv, w_qkv, contract_cols, preferred_element_type=jnp.float32)
    scaled = d_norm * ln_gain
    branch = inverse * (
        scaled
        - jnp.mean(scaled, axis=-1, keepdims=True)
        - normed * jnp.mean(scaled * normed, axis=-1, keepdims=True)
    )
    grad_x = (
        (grad_rows.astype(jnp.float32) + branch)
        .astype(jnp.bfloat16)
        .reshape(t_dev, patches, model_width)
    )
    return (grad_x, grad_w_qkv)


def solution(mesh):
    return jax.shard_map(
        per_device,
        mesh=mesh,
        in_specs=(
            P(("tm", "patch"), None, None),
            P(),
            P(),
            P(),
            P(),
            P(None, "tm", "patch"),
            P(None, "tm", "patch"),
            P(None, "tm", "patch"),
            P(("tm", "patch"), None, None),
        ),
        out_specs=(P(("tm", "patch"), None, None), P(("tm", "patch"), None)),
        check_vma=False,
    )
```

profile of v0, /device:TPU:0, one launch (start us, length us, event | category | flops | bytes accessed | tf_op | source)
XLA Modules:
  0.0 314.8 jit_solution(4595179374015032559)
XLA Ops:
  7.2 1.2 convert_reduce_fusion
  8.4 1.2 multiply_reduce_fusion.9
  10.2 2.0 add_convert_fusion
  12.2 3.4 %convolution_convert_fusion.24 = bf16[128,1408]{1,0:T(8,128)(2,1)S(1)} fusion(bf16[128,1408]{1,0:T(8,128)(2,1)S(1)} %bitcast.671, bf16[1408,1408]{1,0:T(8,128)(2,1)} %param.29), kind=kOutput, calls=%fused_computation.293 | convolution fusion | flops 507691008 | bytes 4685824 | tf_op jit(solution)/shard_map/dot_general | solution.py:68
  15.6 1.0 copy.221
  16.6 1.3 reshape.169
  17.9 4.2 %all-to-all-start = ((bf16[4,2,22528]{2,1,0:T(2,128)(2,1)}), bf16[4,2,22528]{2,1,0:T(2,128)(2,1)S(1)}, u32[]{:S(2)}, u32[]{:S(2)}) async-start(bf16[4,2,22528]{2,1,0:T(2,128)(2,1)} %reshape.169), calls=%async_computation | async-start | bytes 720896 | tf_op jit(solution)/shard_map/all_to_all | solution.py:71
  22.1 2.1 slice_reduce_fusion.10
  25.1 8.0 %all-to-all-done = bf16[4,2,22528]{2,1,0:T(2,128)(2,1)S(1)} async-done(((bf16[4,2,22528]{2,1,0:T(2,128)(2,1)}), bf16[4,2,22528]{2,1,0:T(2,128)(2,1)S(1)}, u32[]{:S(2)}, u32[]{:S(2)}) %all-to-all-start) | async-done | bytes 360480 | tf_op jit(solution)/shard_map/all_to_all | solution.py:71
  35.5 6.8 %all-to-all-start.1 = ((bf16[8,64,352]{2,0,1:T(8,128)(2,1)}), bf16[8,64,352]{2,0,1:T(8,128)(2,1)S(1)}, u32[]{:S(2)}, u32[]{:S(2)}) async-start(bf16[8,64,352]{2,0,1:T(8,128)(2,1)} %copy.224), calls=%async_computation.1 | async-start | bytes 786432 | tf_op jit(solution)/shard_map/all_to_all | solution.py:70
  42.3 2.1 slice_reduce_fusion.9
  45.3 2.1 slice_reduce_fusion.8
  48.4 5.3 %all-to-all-done.1 = bf16[8,64,352]{2,0,1:T(8,128)(2,1)S(1)} async-done(((bf16[8,64,352]{2,0,1:T(8,128)(2,1)}), bf16[8,64,352]{2,0,1:T(8,128)(2,1)S(1)}, u32[]{:S(2)}, u32[]{:S(2)}) %all-to-all-start.1) | async-done | bytes 360480 | tf_op jit(solution)/shard_map/all_to_all | solution.py:70
  53.8 2.1 slice_reduce_fusion
  56.9 3.4 %while.119 = (s32[]{:T(128)}, bf16[4,64,88]{2,1,0:T(8,128)(2,1)S(1)}, bf16[4,64,88]{2,1,0:T(8,128)(2,1)S(1)}, bf16[4,64,88]{2,1,0:T(8,128)(2,1)S(1)}, bf16[4,64,...) while((s32[]{:T(128)}, ...), condition=%wide.region_41.42_spmd, body=%wide.region_37.41_spmd.sunk | while | flops 3690818 | bytes 361317 | solution.py:40
  60.4 3.4 %while.117 = (s32[]{:T(128)}, bf16[4,64,88]{2,1,0:T(8,128)(2,1)S(1)}, bf16[4,64,88]{2,1,0:T(8,128)(2,1)S(1)}, bf16[4,64,88]{2,1,0:T(8,128)(2,1)S(1)}, bf16[4,64,...) while((s32[]{:T(128)}, ...), condition=%wide.region_31.32_spmd, body=%wide.region_27.31_spmd.sunk | while | flops 3690818 | bytes 361317 | solution.py:40
  63.8 3.4 %while.116 = (s32[]{:T(128)}, bf16[4,64,88]{2,1,0:T(8,128)(2,1)S(1)}, bf16[4,64,88]{2,1,0:T(8,128)(2,1)S(1)}, bf16[4,64,88]{2,1,0:T(8,128)(2,1)S(1)}, bf16[4,64,...) while((s32[]{:T(128)}, ...), condition=%wide.region_26.27_spmd, body=%wide.region_22.26_spmd.sunk | while | flops 3690818 | bytes 361317 | solution.py:40
  67.3 3.4 %while.115 = (s32[]{:T(128)}, bf16[4,64,88]{2,1,0:T(8,128)(2,1)S(1)}, bf16[4,64,88]{2,1,0:T(8,128)(2,1)S(1)}, bf16[4,64,88]{2,1,0:T(8,128)(2,1)S(1)}, bf16[4,64,...) while((s32[]{:T(128)}, ...), condition=%wide.region_21.22_spmd, body=%wide.region_17.21_spmd.sunk | while | flops 3690818 | bytes 361317 | solution.py:40
  70.8 3.4 %while.114 = (s32[]{:T(128)}, bf16[4,64,88]{2,1,0:T(8,128)(2,1)S(1)}, bf16[4,64,88]{2,1,0:T(8,128)(2,1)S(1)}, bf16[4,64,88]{2,1,0:T(8,128)(2,1)S(1)}, bf16[4,64,...) while((s32[]{:T(128)}, ...), condition=%wide.region_16.17_spmd, body=%wide.region_12.16_spmd.sunk | while | flops 3690818 | bytes 361317 | solution.py:40
  74.3 3.4 %while.113 = (s32[]{:T(128)}, bf16[4,64,88]{2,1,0:T(8,128)(2,1)S(1)}, bf16[4,64,88]{2,1,0:T(8,128)(2,1)S(1)}, bf16[4,64,88]{2,1,0:T(8,128)(2,1)S(1)}, bf16[4,64,...) while((s32[]{:T(128)}, ...), condition=%wide.region_11.12_spmd, body=%wide.region_7.11_spmd.sunk | while | flops 3690818 | bytes 361317 | solution.py:40
  77.8 3.4 %while.112 = (s32[]{:T(128)}, bf16[4,64,88]{2,1,0:T(8,128)(2,1)S(1)}, bf16[4,64,88]{2,1,0:T(8,128)(2,1)S(1)}, bf16[4,64,88]{2,1,0:T(8,128)(2,1)S(1)}, bf16[4,64,...) while((s32[]{:T(128)}, ...), condition=%wide.region_6.7_spmd, body=%wide.region_2.6_spmd.sunk | while | flops 3690818 | bytes 361317 | solution.py:40
  81.3 3.4 %while.118 = (s32[]{:T(128)}, bf16[4,64,88]{2,1,0:T(8,128)(2,1)S(1)}, bf16[4,64,88]{2,1,0:T(8,128)(2,1)S(1)}, bf16[4,64,88]{2,1,0:T(8,128)(2,1)S(1)}, bf16[4,64,...) while((s32[]{:T(128)}, ...), condition=%wide.region_36.37_spmd, body=%wide.region_32.36_spmd.sunk | while | flops 3690818 | bytes 361317 | solution.py:40
  85.1 3.3 %copy.292 = bf16[8,64,1408]{2,0,1:T(8,128)(2,1)} copy(bf16[8,64,1408]{2,1,0:T(8,128)(2,1)} %all-gather.2.cloned.1.call-done) | data formatting | bytes 2883584 | tf_op jit(solution)/shard_map/all_gather | solution.py:122
  88.4 3.6 %all-to-all-start.8 = ((bf16[8,64,1408]{2,0,1:T(8,128)(2,1)}), bf16[8,64,1408]{2,0,1:T(8,128)(2,1)S(1)}, u32[]{:S(2)}, u32[]{:S(2)}) async-start(bf16[8,64,1408]{2,0,1:T(8,128)(2,1)} %copy.292), calls=%async_computation.8 | async-start | bytes 2883584 | tf_op jit(solution)/shard_map/all_to_all | solution.py:125
  120.3 5.3 %all-to-all-done.8 = bf16[8,64,1408]{2,0,1:T(8,128)(2,1)S(1)} async-done(((bf16[8,64,1408]{2,0,1:T(8,128)(2,1)}), bf16[8,64,1408]{2,0,1:T(8,128)(2,1)S(1)}, u32[]{:S(2)}, u32[]{:S(2)}) %all-to-all-start.8) | async-done | bytes 1441824 | tf_op jit(solution)/shard_map/all_to_all | solution.py:125
  128.4 2.9 maximum_multiply_fusion
  131.3 7.2 %copy.307 = f32[1408,1056]{1,0:T(8,128)} copy(f32[1408,1056]{0,1:T(8,128)} %bitcast.649) | data formatting | bytes 11894784
  139.5 3.6 %all-to-all-start.6 = ((bf16[64,8,352]{2,1,0:T(8,128)(2,1)}), bf16[64,8,352]{2,1,0:T(8,128)(2,1)S(1)}, u32[]{:S(2)}, u32[]{:S(2)}) async-start(bf16[64,8,352]{2,1,0:T(8,128)(2,1)} %copy.289), calls=%async_computation.6 | async-start | bytes 786432 | tf_op jit(solution)/shard_map/all_to_all | solution.py:106
  144.1 20.6 %all-to-all-done.6 = bf16[64,8,352]{2,1,0:T(8,128)(2,1)S(1)} async-done(((bf16[64,8,352]{2,1,0:T(8,128)(2,1)}), bf16[64,8,352]{2,1,0:T(8,128)(2,1)S(1)}, u32[]{:S(2)}, u32[]{:S(2)}) %all-to-all-start.6) | async-done | bytes 360480 | tf_op jit(solution)/shard_map/all_to_all | solution.py:106
  164.7 4.8 %all-to-all-start.2 = ((bf16[64,8,352]{2,1,0:T(8,128)(2,1)}), bf16[64,8,352]{2,1,0:T(8,128)(2,1)S(1)}, u32[]{:S(2)}, u32[]{:S(2)}) async-start(bf16[64,8,352]{2,1,0:T(8,128)(2,1)} %copy.267), calls=%async_computation.2 | async-start | bytes 786432 | tf_op jit(solution)/shard_map/all_to_all | solution.py:92
  169.5 1.0 copy.278
  170.5 21.0 %all-to-all-done.2 = bf16[64,8,352]{2,1,0:T(8,128)(2,1)S(1)} async-done(((bf16[64,8,352]{2,1,0:T(8,128)(2,1)}), bf16[64,8,352]{2,1,0:T(8,128)(2,1)S(1)}, u32[]{:S(2)}, u32[]{:S(2)}) %all-to-all-start.2) | async-done | bytes 360480 | tf_op jit(solution)/shard_map/all_to_all | solution.py:92
  191.5 3.7 %all-to-all-start.4 = ((bf16[64,8,352]{2,1,0:T(8,128)(2,1)}), bf16[64,8,352]{2,1,0:T(8,128)(2,1)S(1)}, u32[]{:S(2)}, u32[]{:S(2)}) async-start(bf16[64,8,352]{2,1,0:T(8,128)(2,1)} %copy.278), calls=%async_computation.4 | async-start | bytes 786432 | tf_op jit(solution)/shard_map/all_to_all | solution.py:99
  196.0 22.3 %all-to-all-done.4 = bf16[64,8,352]{2,1,0:T(8,128)(2,1)S(1)} async-done(((bf16[64,8,352]{2,1,0:T(8,128)(2,1)}), bf16[64,8,352]{2,1,0:T(8,128)(2,1)S(1)}, u32[]{:S(2)}, u32[]{:S(2)}) %all-to-all-start.4) | async-done | bytes 360480 | tf_op jit(solution)/shard_map/all_to_all | solution.py:99
  218.3 3.5 %all-to-all-start.7 = ((bf16[8,64,352]{2,1,0:T(8,128)(2,1)}), bf16[8,64,352]{2,1,0:T(8,128)(2,1)S(1)}, u32[]{:S(2)}, u32[]{:S(2)}) async-start(bf16[8,64,352]{2,1,0:T(8,128)(2,1)} %bitcast.453), calls=%async_computation.7 | async-start | bytes 786432 | tf_op jit(solution)/shard_map/all_to_all | solution.py:105
  222.5 6.6 %all-to-all-done.7 = bf16[8,64,352]{2,1,0:T(8,128)(2,1)S(1)} async-done(((bf16[8,64,352]{2,1,0:T(8,128)(2,1)}), bf16[8,64,352]{2,1,0:T(8,128)(2,1)S(1)}, u32[]{:S(2)}, u32[]{:S(2)}) %all-to-all-start.7) | async-done | bytes 360480 | tf_op jit(solution)/shard_map/all_to_all | solution.py:105
  229.1 3.5 %all-to-all-start.3 = ((bf16[8,64,352]{2,1,0:T(8,128)(2,1)}), bf16[8,64,352]{2,1,0:T(8,128)(2,1)S(1)}, u32[]{:S(2)}, u32[]{:S(2)}) async-start(bf16[8,64,352]{2,1,0:T(8,128)(2,1)} %bitcast.456), calls=%async_computation.3 | async-start | bytes 786432 | tf_op jit(solution)/shard_map/all_to_all | solution.py:91
  233.4 6.6 %all-to-all-done.3 = bf16[8,64,352]{2,1,0:T(8,128)(2,1)S(1)} async-done(((bf16[8,64,352]{2,1,0:T(8,128)(2,1)}), bf16[8,64,352]{2,1,0:T(8,128)(2,1)S(1)}, u32[]{:S(2)}, u32[]{:S(2)}) %all-to-all-start.3) | async-done | bytes 360480 | tf_op jit(solution)/shard_map/all_to_all | solution.py:91
  240.0 3.7 %all-to-all-start.5 = ((bf16[8,64,352]{2,1,0:T(8,128)(2,1)}), bf16[8,64,352]{2,1,0:T(8,128)(2,1)S(1)}, u32[]{:S(2)}, u32[]{:S(2)}) async-start(bf16[8,64,352]{2,1,0:T(8,128)(2,1)} %bitcast.454), calls=%async_computation.5 | async-start | bytes 786432 | tf_op jit(solution)/shard_map/all_to_all | solution.py:98
  245.2 5.7 %all-to-all-done.5 = bf16[8,64,352]{2,1,0:T(8,128)(2,1)S(1)} async-done(((bf16[8,64,352]{2,1,0:T(8,128)(2,1)}), bf16[8,64,352]{2,1,0:T(8,128)(2,1)S(1)}, u32[]{:S(2)}, u32[]{:S(2)}) %all-to-all-start.5) | async-done | bytes 360480 | tf_op jit(solution)/shard_map/all_to_all | solution.py:98
  251.5 8.6 %fusion.253 = (f32[128]{0:T(128)S(1)}, f32[128]{0:T(128)S(1)}, f32[128,1408]{1,0:T(8,128)S(1)}) fusion(f32[128]{0:T(128)S(1)} %rsqrt.13, f32[128]{0:T(128)S(1)} %div.81, bf16[2,64,1408]{2,1,0:T(8,128)(2,1)S(1)} %copy-done, f32[1408]{0:T(1024)S(1)} %copy-done.22, bf16[1408,4224]{1,0:T(8,128)(2,1)} %param.28, bf16[128,1408]{1,0:T(8,128)(2,1)S(1)} %concatenate.12, ...), kind=kOutput, calls=%fused_computation.378 | convolution fusion | flops 1527037696 | bytes 14065152 | tf_op jit(solution)/shard_map/dot_general | solution.py:141
  260.1 24.7 %reduce-scatter.4.cloned.1.call-done = f32[176,1056]{1,0:T(8,128)} async-done(((f32[1408,1056]{1,0:T(8,128)}), f32[176,1056]{1,0:T(8,128)}) %reduce-scatter.4.cloned.1.call-update) | async-done | bytes 743440
  284.8 1.5 copy.308
  286.3 1.6 copy.298
  287.9 3.5 %all-to-all-start.9 = ((f32[176,3,352]{2,1,0:T(4,128)}), f32[176,3,352]{2,1,0:T(4,128)S(1)}, u32[]{:S(2)}, u32[]{:S(2)}) async-start(f32[176,3,352]{2,1,0:T(4,128)} %copy.298), calls=%async_computation.9 | async-start | bytes 2162688 | tf_op jit(solution)/shard_map/all_to_all | solution.py:139
  291.5 1.1 add_convert_fusion.1
  292.5 13.7 %all-to-all-done.9 = f32[176,3,352]{2,1,0:T(4,128)S(1)} async-done(((f32[176,3,352]{2,1,0:T(4,128)}), f32[176,3,352]{2,1,0:T(4,128)S(1)}, u32[]{:S(2)}, u32[]{:S(2)}) %all-to-all-start.9) | async-done | bytes 743456 | tf_op jit(solution)/shard_map/all_to_all | solution.py:139
  306.6 1.3 reshape.133
  (466 shorter events, 71.1 us)
Async XLA Ops:
  7.2 5.1 %copy-start.4 = (bf16[2,64,1408]{2,1,0:T(8,128)(2,1)S(1)}, bf16[2,64,1408]{2,1,0:T(8,128)(2,1)}, u32[]{:S(2)}) copy-start(bf16[2,64,1408]{2,1,0:T(8,128)(2,1)} %param.33) | copy-start | bytes 1081348
  7.2 77.9 %all-gather.2.cloned.1.call-start = ((), (), s32[]{:S(2)}) async-start(), calls=%async_computation.11 | async-start | bytes 1802240 | tf_op jit(solution)/shard_map/all_gather | solution.py:122
  8.4 1.2 copy-start.20
  9.6 0.5 copy-start.23
  15.6 6.5 %copy-start.1 = (bf16[64,8,352]{2,1,0:T(8,128)(2,1)S(1)}, bf16[64,8,352]{2,1,0:T(8,128)(2,1)}, u32[]{:S(2)}) copy-start(bf16[64,8,352]{2,1,0:T(8,128)(2,1)} %param.30) | copy-start | bytes 1081348
  17.9 15.3 %all-to-all-start = ((bf16[4,2,22528]{2,1,0:T(2,128)(2,1)}), bf16[4,2,22528]{2,1,0:T(2,128)(2,1)S(1)}, u32[]{:S(2)}, u32[]{:S(2)}) async-start(bf16[4,2,22528]{2,1,0:T(2,128)(2,1)} %reshape.169), calls=%async_computation | async-start | bytes 720896 | tf_op jit(solution)/shard_map/all_to_all | solution.py:71
  33.6 8.7 %copy-start.2 = (bf16[64,8,352]{2,1,0:T(8,128)(2,1)S(1)}, bf16[64,8,352]{2,1,0:T(8,128)(2,1)}, u32[]{:S(2)}) copy-start(bf16[64,8,352]{2,1,0:T(8,128)(2,1)} %param.31) | copy-start | bytes 1081348
  35.5 9.9 %copy-start.3 = (bf16[64,8,352]{2,1,0:T(8,128)(2,1)S(1)}, bf16[64,8,352]{2,1,0:T(8,128)(2,1)}, u32[]{:S(2)}) copy-start(bf16[64,8,352]{2,1,0:T(8,128)(2,1)} %param.32) | copy-start | bytes 1081348
  35.5 18.3 %all-to-all-start.1 = ((bf16[8,64,352]{2,0,1:T(8,128)(2,1)}), bf16[8,64,352]{2,0,1:T(8,128)(2,1)S(1)}, u32[]{:S(2)}, u32[]{:S(2)}) async-start(bf16[8,64,352]{2,0,1:T(8,128)(2,1)} %copy.224), calls=%async_computation.1 | async-start | bytes 786432 | tf_op jit(solution)/shard_map/all_to_all | solution.py:70
  70.7 3.6 %copy-start.5 = (bf16[4,64,88]{2,1,0:T(8,128)(2,1)}, bf16[4,64,88]{2,1,0:T(8,128)(2,1)S(1)}, u32[]{:S(2)}) copy-start(bf16[4,64,88]{2,1,0:T(8,128)(2,1)S(1)} %get-tuple-element.365) | copy-start | bytes 135172
  70.7 3.6 %copy-start.6 = (bf16[4,64,88]{2,1,0:T(8,128)(2,1)}, bf16[4,64,88]{2,1,0:T(8,128)(2,1)S(1)}, u32[]{:S(2)}) copy-start(bf16[4,64,88]{2,1,0:T(8,128)(2,1)S(1)} %get-tuple-element.357) | copy-start | bytes 135172
  74.2 3.6 %copy-start.7 = (bf16[4,64,88]{2,1,0:T(8,128)(2,1)}, bf16[4,64,88]{2,1,0:T(8,128)(2,1)S(1)}, u32[]{:S(2)}) copy-start(bf16[4,64,88]{2,1,0:T(8,128)(2,1)S(1)} %get-tuple-element.372) | copy-start | bytes 135172
  74.2 3.6 %copy-start.8 = (bf16[4,64,88]{2,1,0:T(8,128)(2,1)}, bf16[4,64,88]{2,1,0:T(8,128)(2,1)S(1)}, u32[]{:S(2)}) copy-start(bf16[4,64,88]{2,1,0:T(8,128)(2,1)S(1)} %get-tuple-element.364) | copy-start | bytes 135172
  74.2 3.6 %copy-start.9 = (bf16[4,64,88]{2,1,0:T(8,128)(2,1)}, bf16[4,64,88]{2,1,0:T(8,128)(2,1)S(1)}, u32[]{:S(2)}) copy-start(bf16[4,64,88]{2,1,0:T(8,128)(2,1)S(1)} %get-tuple-element.356) | copy-start | bytes 135172
  77.7 3.6 %copy-start.10 = (bf16[4,64,88]{2,1,0:T(8,128)(2,1)}, bf16[4,64,88]{2,1,0:T(8,128)(2,1)S(1)}, u32[]{:S(2)}) copy-start(bf16[4,64,88]{2,1,0:T(8,128)(2,1)S(1)} %get-tuple-element.371) | copy-start | bytes 135172
  77.7 3.6 %copy-start.11 = (bf16[4,64,88]{2,1,0:T(8,128)(2,1)}, bf16[4,64,88]{2,1,0:T(8,128)(2,1)S(1)}, u32[]{:S(2)}) copy-start(bf16[4,64,88]{2,1,0:T(8,128)(2,1)S(1)} %get-tuple-element.363) | copy-start | bytes 135172
  77.7 3.6 %copy-start.13 = (bf16[4,64,88]{2,1,0:T(8,128)(2,1)}, bf16[4,64,88]{2,1,0:T(8,128)(2,1)S(1)}, u32[]{:S(2)}) copy-start(bf16[4,64,88]{2,1,0:T(8,128)(2,1)S(1)} %get-tuple-element.355) | copy-start | bytes 135172
  81.2 7.2 %copy-start.14 = (bf16[4,64,88]{2,1,0:T(8,128)(2,1)}, bf16[4,64,88]{2,1,0:T(8,128)(2,1)S(1)}, u32[]{:S(2)}) copy-start(bf16[4,64,88]{2,1,0:T(8,128)(2,1)S(1)} %get-tuple-element.370) | copy-start | bytes 135172
  88.4 37.3 %all-to-all-start.8 = ((bf16[8,64,1408]{2,0,1:T(8,128)(2,1)}), bf16[8,64,1408]{2,0,1:T(8,128)(2,1)S(1)}, u32[]{:S(2)}, u32[]{:S(2)}) async-start(bf16[8,64,1408]{2,0,1:T(8,128)(2,1)} %copy.292), calls=%async_computation.8 | async-start | bytes 2883584 | tf_op jit(solution)/shard_map/all_to_all | solution.py:125
  92.0 192.8 %reduce-scatter.4.cloned.1.call-start = ((), (), s32[]{:S(2)}) async-start(), calls=%async_computation.12 | async-start | bytes 7299072
  92.5 14.8 %copy-start.12 = (bf16[4,64,88]{2,1,0:T(8,128)(2,1)S(1)}, bf16[4,64,88]{2,1,0:T(8,128)(2,1)}, u32[]{:S(2)}) copy-start(bf16[4,64,88]{2,1,0:T(8,128)(2,1)} %copy-done.11) | copy-start | bytes 135172
  93.3 14.8 %copy-start.15 = (bf16[4,64,88]{2,1,0:T(8,128)(2,1)S(1)}, bf16[4,64,88]{2,1,0:T(8,128)(2,1)}, u32[]{:S(2)}) copy-start(bf16[4,64,88]{2,1,0:T(8,128)(2,1)} %copy-done.14) | copy-start | bytes 135172
  96.3 20.6 %copy-start.17 = (bf16[64,1,352]{2,0,1:T(8,128)(2,1)S(1)}, bf16[64,1,352]{2,0,1:T(8,128)(2,1)}, u32[]{:S(2)}) copy-start(bf16[64,1,352]{2,0,1:T(8,128)(2,1)} %stack_reshape.87) | copy-start | bytes 135172
  99.0 20.4 %copy-start.16 = (bf16[64,1,352]{2,0,1:T(8,128)(2,1)S(1)}, bf16[64,1,352]{2,0,1:T(8,128)(2,1)}, u32[]{:S(2)}) copy-start(bf16[64,1,352]{2,0,1:T(8,128)(2,1)} %stack_reshape.79) | copy-start | bytes 135172
  107.3 11.2 %copy-start.18 = (bf16[64,1,352]{2,0,1:T(8,128)(2,1)S(1)}, bf16[64,1,352]{2,0,1:T(8,128)(2,1)}, u32[]{:S(2)}) copy-start(bf16[64,1,352]{2,0,1:T(8,128)(2,1)} %stack_reshape.75) | copy-start | bytes 135172
  111.2 9.1 %copy-start.19 = (bf16[64,1,352]{2,0,1:T(8,128)(2,1)S(1)}, bf16[64,1,352]{2,0,1:T(8,128)(2,1)}, u32[]{:S(2)}) copy-start(bf16[64,1,352]{2,0,1:T(8,128)(2,1)} %stack_reshape.94) | copy-start | bytes 135172
  139.5 25.2 %all-to-all-start.6 = ((bf16[64,8,352]{2,1,0:T(8,128)(2,1)}), bf16[64,8,352]{2,1,0:T(8,128)(2,1)S(1)}, u32[]{:S(2)}, u32[]{:S(2)}) async-start(bf16[64,8,352]{2,1,0:T(8,128)(2,1)} %copy.289), calls=%async_computation.6 | async-start | bytes 786432 | tf_op jit(solution)/shard_map/all_to_all | solution.py:106
  164.7 26.8 %all-to-all-start.2 = ((bf16[64,8,352]{2,1,0:T(8,128)(2,1)}), bf16[64,8,352]{2,1,0:T(8,128)(2,1)S(1)}, u32[]{:S(2)}, u32[]{:S(2)}) async-start(bf16[64,8,352]{2,1,0:T(8,128)(2,1)} %copy.267), calls=%async_computation.2 | async-start | bytes 786432 | tf_op jit(solution)/shard_map/all_to_all | solution.py:92
  191.5 26.7 %all-to-all-start.4 = ((bf16[64,8,352]{2,1,0:T(8,128)(2,1)}), bf16[64,8,352]{2,1,0:T(8,128)(2,1)S(1)}, u32[]{:S(2)}, u32[]{:S(2)}) async-start(bf16[64,8,352]{2,1,0:T(8,128)(2,1)} %copy.278), calls=%async_computation.4 | async-start | bytes 786432 | tf_op jit(solution)/shard_map/all_to_all | solution.py:99
  196.0 47.8 %copy-start.21 = (f32[2,64]{1,0:T(2,128)S(1)}, f32[2,64]{1,0:T(2,128)}, u32[]{:S(2)}) copy-start(f32[2,64]{1,0:T(2,128)} %copy-done.20) | copy-start | bytes 1540
  196.0 47.9 %copy-start.24 = (f32[2,64]{1,0:T(2,128)S(1)}, f32[2,64]{1,0:T(2,128)}, u32[]{:S(2)}) copy-start(f32[2,64]{1,0:T(2,128)} %copy-done.23) | copy-start | bytes 1540
  218.3 10.9 %all-to-all-start.7 = ((bf16[8,64,352]{2,1,0:T(8,128)(2,1)}), bf16[8,64,352]{2,1,0:T(8,128)(2,1)S(1)}, u32[]{:S(2)}, u32[]{:S(2)}) async-start(bf16[8,64,352]{2,1,0:T(8,128)(2,1)} %bitcast.453), calls=%async_computation.7 | async-start | bytes 786432 | tf_op jit(solution)/shard_map/all_to_all | solution.py:105
  229.1 10.9 %all-to-all-start.3 = ((bf16[8,64,352]{2,1,0:T(8,128)(2,1)}), bf16[8,64,352]{2,1,0:T(8,128)(2,1)S(1)}, u32[]{:S(2)}, u32[]{:S(2)}) async-start(bf16[8,64,352]{2,1,0:T(8,128)(2,1)} %bitcast.456), calls=%async_computation.3 | async-start | bytes 786432 | tf_op jit(solution)/shard_map/all_to_all | solution.py:91
  240.0 10.9 %all-to-all-start.5 = ((bf16[8,64,352]{2,1,0:T(8,128)(2,1)}), bf16[8,64,352]{2,1,0:T(8,128)(2,1)S(1)}, u32[]{:S(2)}, u32[]{:S(2)}) async-start(bf16[8,64,352]{2,1,0:T(8,128)(2,1)} %bitcast.454), calls=%async_computation.5 | async-start | bytes 786432 | tf_op jit(solution)/shard_map/all_to_all | solution.py:98
  244.2 7.3 %copy-start = (bf16[2,64,1408]{2,1,0:T(8,128)(2,1)S(1)}, bf16[2,64,1408]{2,1,0:T(8,128)(2,1)}, u32[]{:S(2)}) copy-start(bf16[2,64,1408]{2,1,0:T(8,128)(2,1)} %param.25) | copy-start | bytes 1081348
  244.2 7.3 %copy-start.22 = (f32[1408]{0:T(1024)S(1)}, f32[1408]{0:T(1024)}, u32[]{:S(2)}) copy-start(f32[1408]{0:T(1024)} %param.26) | copy-start | bytes 16900
  287.9 18.3 %all-to-all-start.9 = ((f32[176,3,352]{2,1,0:T(4,128)}), f32[176,3,352]{2,1,0:T(4,128)S(1)}, u32[]{:S(2)}, u32[]{:S(2)}) async-start(f32[176,3,352]{2,1,0:T(4,128)} %copy.298), calls=%async_computation.9 | async-start | bytes 2162688 | tf_op jit(solution)/shard_map/all_to_all | solution.py:139
Sparse Core Ops, SparseCore 0:
  12.3 25.4 all-gather.1
  138.7 146.0 reduce-scatter.3
where the time goes:
time: 317 us; the launch traced here: 315 us
  waiting for transfers between devices  140 us (44%)
  local copies, waits for them, and re-layouts  68 us (21%)
  starting transfers between devices  41.1 us (13%)
  matrix products  39.1 us (12%)
  between operations  15.4 us (5%)
  other arithmetic  10.5 us (3%)
    unnamed x3, waiting for transfers between devices  24.7 us
    all_to_all x1, waiting for transfers between devices, per_device(): lax.all_to_all(key_time, 'tm', split_axis=0, concat_axis=1, tiled=True)  22.3 us
    all_to_all x1, waiting for transfers between devices, per_device(): lax.all_to_all(query_time, 'tm', split_axis=0, concat_axis=1, tiled=True)  21 us
    all_to_all x1, waiting for transfers between devices, per_device(): lax.all_to_all(value_time, 'tm', split_axis=0, concat_axis=1, tiled=True)  20.6 us
    unnamed x75, local copies, waits for them, and re-layouts  20.1 us
    all_to_all x1, waiting for transfers between devices, per_device(): lax.all_to_all(partial_sum, 'patch', split_axis=0, concat_axis=2, tiled=T...  13.7 us
    dot_general x1, matrix products, per_device(): lax.dot_general(grad_qkv, w_qkv, contract_cols, preferred_element_type=jn...  8.62 us
    all_to_all x1, waiting for transfers between devices, per_device(): lax.all_to_all(d_attn, 'patch', split_axis=2, concat_axis=0, tiled=True)  8.02 us
  transfers between devices with their start and end apart: 12, of which 11 were waited for; matrix products, arithmetic and copies ran while one was open for 29% of the time, Pallas kernels for 0%

commit v1 on v0

v1 whole, which is shorter than its diff:
```python
import functools
import math

import jax
import jax.numpy as jnp
from jax import lax
from jax.experimental import pallas as pl
from jax.experimental.pallas import tpu as pltpu
from jax.sharding import PartitionSpec as P

DH = 88
BF = jnp.bfloat16
F32 = jnp.float32
ROWS = (((0,), (0,)), ((), ()))
COLS = (((1,), (1,)), ((), ()))


def attend_kernel(q_ref, k_ref, v_ref, d_ref, out_ref, acc_ref, *, columns, block):
    head = pl.program_id(0)
    n_tok, width = q_ref.shape
    factor = 1.0 / math.sqrt(DH)
    lane = lax.broadcasted_iota(jnp.int32, (1, width), 1)
    keep = jnp.where((lane >= head * DH) & (lane < (head + 1) * DH), 1.0, 0.0).astype(BF)

    @pl.when(head == 0)
    def _():
        acc_ref[...] = jnp.zeros_like(acc_ref)

    k_head = k_ref[...] * keep
    v_head = v_ref[...] * keep
    source = lax.broadcasted_iota(jnp.int32, (n_tok, block), 0) % columns
    target = lax.broadcasted_iota(jnp.int32, (n_tok, block), 1) % columns
    same = source == target
    for start in range(0, n_tok, block):
        rows = pl.ds(start, block)
        q_rows = q_ref[rows, :]
        d_rows = d_ref[rows, :]
        scores = lax.dot_general(k_head, q_rows, COLS, preferred_element_type=F32) * factor
        scores = jnp.where(same, scores, -jnp.inf)
        exponent = jnp.exp(scores - jnp.max(scores, axis=0, keepdims=True))
        probability = exponent * (1.0 / jnp.sum(exponent, axis=0, keepdims=True))
        prob_grad = lax.dot_general(v_head, d_rows, COLS, preferred_element_type=F32)
        row_dot = jnp.sum(probability * prob_grad, axis=0, keepdims=True)
        score_grad = (probability * (prob_grad - row_dot) * factor).astype(BF)
        prob_low = probability.astype(BF)
        acc_ref[0, rows, :] += lax.dot_general(score_grad, k_head, ROWS, preferred_element_type=F32)
        acc_ref[1] += jnp.dot(score_grad, q_rows * keep, preferred_element_type=F32)
        acc_ref[2] += jnp.dot(prob_low, d_rows * keep, preferred_element_type=F32)

    @pl.when(head == pl.num_programs(0) - 1)
    def _():
        out_ref[...] = acc_ref[...].astype(BF)


def attend(query, key, value, grad, columns):
    n_tok, width = query.shape
    whole = pl.BlockSpec((n_tok, width), lambda h: (0, 0))
    block = min(256, n_tok)
    return pl.pallas_call(
        functools.partial(attend_kernel, columns=columns, block=block),
        grid=(width // DH,),
        in_specs=[whole] * 4,
        out_specs=pl.BlockSpec((3, n_tok, width), lambda h: (0, 0, 0)),
        out_shape=jax.ShapeDtypeStruct((3, n_tok, width), BF),
        scratch_shapes=[pltpu.VMEM((3, n_tok, width), F32)],
        compiler_params=pltpu.CompilerParams(vmem_limit_bytes=48 * 1024 * 1024),
    )(query, key, value, grad)


def per_device(tokens, ln_gain, ln_bias, w_qkv, w_out, q_time, k_time, v_time, grad_out):
    t_dev, patches, width = tokens.shape
    frames, columns, part = q_time.shape
    n_tm = lax.axis_size("tm")
    n_patch = lax.axis_size("patch")
    n_pair = n_tm // 2
    devices = n_tm * n_patch
    n_tok = frames * columns
    own_rows = width // devices
    tm = lax.axis_index("tm")
    patch = lax.axis_index("patch")
    side = tm % 2
    both = ("tm", "patch")

    def swap(values, axis, size, bit):
        return lax.ppermute(values, axis, [(i, i ^ bit) for i in range(size)])

    grad_rows = grad_out.reshape(-1, width)
    d_attn = jnp.einsum(
        "to,jfo->jtf", grad_rows, w_out.reshape(n_patch, part, width), preferred_element_type=F32
    ).astype(BF)
    d_attn = d_attn.reshape(n_patch, t_dev, n_tm, columns, part).transpose(2, 0, 1, 3, 4)
    d_time = lax.all_to_all(
        d_attn.reshape(devices, t_dev, columns, part), both, 0, 0, tiled=True
    ).reshape(n_tok, part)

    as_float = tokens.reshape(-1, width).astype(F32)
    centered = as_float - jnp.mean(as_float, axis=-1, keepdims=True)
    variance = jnp.mean(centered * centered, axis=-1, keepdims=True)
    inverse = lax.rsqrt(variance + 1e-06)
    normed = centered * inverse
    norm_out = (normed * ln_gain + ln_bias).astype(BF)

    half = width // 2
    sent = norm_out.reshape(t_dev, n_pair, 2 * columns, n_pair, 2, n_patch * own_rows)
    sent = sent.transpose(1, 4, 0, 2, 3, 5).reshape(n_tm, t_dev, 2 * columns, half)
    got = lax.all_to_all(sent, "tm", 0, 0, tiled=True)
    bits = [1 << n for n in reversed(range(n_patch.bit_length() - 1))]
    for bit in bits:
        other = swap(got, "patch", n_patch, bit)
        high = (patch & bit) != 0
        got = jnp.stack([jnp.where(high, other, got), jnp.where(high, got, other)])
    order = tuple(reversed(range(len(bits))))
    at = len(bits)
    got = got.transpose((at,) + order + tuple(range(at + 1, got.ndim)))
    got = got.reshape(n_tm, n_patch, t_dev, 2, columns, half)
    norm_own, norm_other = [
        lax.dynamic_index_in_dim(got, index, 3, keepdims=False).reshape(n_tok, half)
        for index in (side, 1 - side)
    ]

    grads = attend(
        q_time.reshape(n_tok, part),
        k_time.reshape(n_tok, part),
        v_time.reshape(n_tok, part),
        d_time,
        columns,
    )
    grads_other = swap(grads, "tm", n_tm, 1)

    factor = 1.0 / math.sqrt(frames * patches)
    partial = jnp.einsum("na,cnf->caf", norm_own, grads, preferred_element_type=F32) + jnp.einsum(
        "na,cnf->caf", norm_other, grads_other, preferred_element_type=F32
    )
    partial = (partial * factor).astype(BF).reshape(3, n_pair * n_patch, own_rows, part)
    groups = [
        [(2 * z + y) * n_patch + p for z in range(n_pair) for p in range(n_patch)] for y in range(2)
    ]
    pieces = lax.all_to_all(
        partial.transpose(1, 0, 2, 3), both, 0, 0, axis_index_groups=groups, tiled=True
    )
    pieces = pieces.reshape(n_pair, n_patch, 3, own_rows, part).astype(F32)
    grad_w_qkv = jnp.sum(pieces, axis=0).transpose(2, 1, 0, 3).reshape(own_rows, 3 * width)

    weights = jnp.stack(
        [lax.dynamic_slice_in_dim(w_qkv, c * width + patch * part, part, 1) for c in range(3)]
    )
    share = jnp.einsum("cnf,caf->na", grads, weights, preferred_element_type=F32)
    share = share.reshape((n_tm,) + (2,) * len(bits) + (t_dev * columns, width))
    for bit in reversed(bits):
        high = (patch & bit) != 0
        axis = share.ndim - 3
        low_part = lax.index_in_dim(share, 0, axis, keepdims=False)
        high_part = lax.index_in_dim(share, 1, axis, keepdims=False)
        leave = jnp.where(high, low_part, high_part).astype(BF)
        stay = jnp.where(high, high_part, low_part)
        share = stay + swap(leave, "patch", n_patch, bit).astype(F32)
    d_norm = lax.all_to_all(share.astype(BF), "tm", 0, 0, tiled=True)
    d_norm = d_norm.reshape(n_tm, t_dev, columns, width).transpose(1, 0, 2, 3)
    d_norm = d_norm.reshape(-1, width).astype(F32)
    scaled = d_norm * ln_gain
    branch = inverse * (
        scaled
        - jnp.mean(scaled, axis=-1, keepdims=True)
        - normed * jnp.mean(scaled * normed, axis=-1, keepdims=True)
    )
    grad_x = (grad_rows.astype(F32) + branch).astype(BF).reshape(t_dev, patches, width)
    return (grad_x, grad_w_qkv)


def solution(mesh):
    return jax.shard_map(
        per_device,
        mesh=mesh,
        in_specs=(
            P(("tm", "patch"), None, None),
            P(),
            P(),
            P(),
            P(),
            P(None, "tm", "patch"),
            P(None, "tm", "patch"),
            P(None, "tm", "patch"),
            P(("tm", "patch"), None, None),
        ),
        out_specs=(P(("tm", "patch"), None, None), P(("tm", "patch"), None)),
        check_vma=False,
    )
```

time: 317 us -> 142 us (0.45)
  the two profiles are of different devices: /device:TPU:0 before, /device:TPU:11 now
where the time goes in v1:
time: 142 us; the launch traced here: 141 us
  waiting for transfers between devices  57.6 us (41%)
  starting transfers between devices  30.3 us (21%)
  local copies, waits for them, and re-layouts  24.7 us (17%)
  matrix products  10 us (7%)
  Pallas kernels  9.66 us (7%)
  other arithmetic  8.19 us (6%)
    all_to_all x1, waiting for transfers between devices, per_device(): lax.all_to_all(partial.transpose(1, 0, 2, 3), both, 0, 0, axis_index_grou...  36.7 us
    ppermute x5, waiting for transfers between devices, swap(): return lax.ppermute(values, axis, [(i, i ^ bit) for i in range(size)])  16.8 us
    dynamic_slice x4, local copies, waits for them, and re-layouts, per_device(): lax.dynamic_slice_in_dim(w_qkv, c * width + patch * part, part, 1)  11.3 us
    pallas_call x1, Pallas kernels, attend(): pl.pallas_call(functools.partial(attend_kernel, columns=columns, block=bl...  9.66 us
    all_to_all x1, starting transfers between devices, per_device(): lax.all_to_all(partial.transpose(1, 0, 2, 3), both, 0, 0, axis_index_grou...  7.59 us
    all_to_all x1, starting transfers between devices, per_device(): lax.all_to_all(d_attn.reshape(devices, t_dev, columns, part), both, 0, 0,...  7.51 us
    all_to_all x1, starting transfers between devices, per_device(): got = lax.all_to_all(sent, 'tm', 0, 0, tiled=True)  5.72 us
    all_to_all x1, starting transfers between devices, per_device(): d_norm = lax.all_to_all(share.astype(BF), 'tm', 0, 0, tiled=True)  5.53 us
  transfers between devices with their start and end apart: 9, of which 5 were waited for; matrix products, arithmetic and copies ran while one was open for 23% of the time, Pallas kernels for 7%

profile of v1, /device:TPU:11, one launch (start us, length us, event | category | flops | bytes accessed | tf_op | source)
XLA Modules:
  0.0 141.4 jit_solution(9482454739161950021)
XLA Ops:
  0.6 1.1 convert_reduce_fusion.1
  1.8 1.2 multiply_reduce_fusion
  3.1 2.7 %reshape.229 = f32[2,4,16,4,2,176]{5,4,3,2,1,0:T(2,128)S(1)} reshape(bf16[2,64,1408]{2,1,0:T(8,128)(2,1)} %param.9) | data formatting | bytes 1081344 | tf_op jit(solution)/shard_map/convert_element_type | solution.py:96
  5.8 0.1 add.73
  6.1 0.4 fusion.26
  6.6 1.1 reshape.221
  7.7 5.7 %all-to-all-start.2 = ((bf16[8,2,16,704]{3,2,1,0:T(8,128)(2,1)}), bf16[8,2,16,704]{3,2,1,0:T(8,128)(2,1)S(1)}, u32[]{:S(2)}, u32[]{:S(2)}) async-start(bf16[8,2,16,704]{3,2,1,0:T(8,128)(2,1)} %reshape.221), calls=%async_computation.2 | async-start | bytes 786432 | tf_op jit(solution)/shard_map/all_to_all | solution.py:106
  13.4 3.3 %fusion.9 = bf16[4,128,352]{1,2,0:T(8,128)(2,1)S(1)} fusion(bf16[4,352,1408]{2,1,0:T(8,128)(2,1)} %bitcast.144, bf16[128,1408,1]{1,0,2:T(8,128)(2,1)S(1)} %bitcast.143), kind=kOutput, calls=%fused_computation.15 | convolution fusion | flops 507691008 | bytes 4685824 | tf_op jit(solution)/shard_map/to,jfo->jtf/dot_general | solution.py:88
  16.7 0.2 copy.108
  17.0 0.8 copy.109
  17.8 4.1 %all-to-all-done.2 = bf16[8,2,16,704]{3,2,1,0:T(8,128)(2,1)S(1)} async-done(((bf16[8,2,16,704]{3,2,1,0:T(8,128)(2,1)}), bf16[8,2,16,704]{3,2,1,0:T(8,128)(2,1)S(1)}, u32[]{:S(2)}, u32[]{:S(2)}) %all-to-all-start.2) | async-done | bytes 360480 | tf_op jit(solution)/shard_map/all_to_all | solution.py:106
  21.8 7.5 %all-to-all-start = ((bf16[32,2,8,352]{3,2,1,0:T(8,128)(2,1)}), bf16[32,2,8,352]{3,2,1,0:T(8,128)(2,1)S(1)}, u32[]{:S(2)}, u32[]{:S(2)}) async-start(bf16[32,2,8,352]{3,2,1,0:T(8,128)(2,1)} %bitcast.9), calls=%async_computation | async-start | bytes 786432 | tf_op jit(solution)/shard_map/all_to_all | solution.py:92
  29.4 5.0 %constant_dynamic-slice_fusion.4 = (bf16[1408,352]{1,0:T(8,128)(2,1)S(1)}, bf16[1408,352]{1,0:T(8,128)(2,1)S(1)}, bf16[1408,352]{1,0:T(8,128)(2,1)}) fusion(bf16[1408,4224]{1,0:T(8,128)(2,1)} %param.12, s32[]{:T(128)S(6)} %select_n.81, s32[]{:T(128)S(6)} %select_n.83, s32[]{:T(128)S(6)} %select_n.82), kind=kLoop, calls=%fused_computation.55 | loop fusion | bytes 5947404 | tf_op jit(solution)/shard_map/dynamic_slice | solution.py:145
  34.4 1.9 %copy.112 = bf16[1408,352]{0,1:T(8,128)(2,1)} copy(bf16[1408,352]{1,0:T(8,128)(2,1)S(1)} %get-tuple-element.5) | data formatting | bytes 1982464 | tf_op jit(solution)/shard_map/dynamic_slice | solution.py:145
  36.3 2.5 %copy.111 = bf16[1408,352]{0,1:T(8,128)(2,1)} copy(bf16[1408,352]{1,0:T(8,128)(2,1)} %get-tuple-element.6) | data formatting | bytes 1982464 | tf_op jit(solution)/shard_map/dynamic_slice | solution.py:145
  38.7 1.9 %copy.110 = bf16[1408,352]{0,1:T(8,128)(2,1)} copy(bf16[1408,352]{1,0:T(8,128)(2,1)S(1)} %get-tuple-element.4) | data formatting | bytes 1982464 | tf_op jit(solution)/shard_map/dynamic_slice | solution.py:145
  40.7 0.4 collective-permute-start.2
  41.1 9.7 %shard_map.104 = bf16[3,512,352]{2,1,0:T(8,128)(2,1)S(1)} custom-call(bf16[512,352]{1,0:T(8,128)(2,1)S(1)} %bitcast.128, bf16[512,352]{1,0:T(8,128)(2,1)S(1)} %bitcast.129, bf16[512,352]{1,0:T(8,128)(2,1)S(1)} %bitcast.130, bf16[512,352]{1,0:T(8,128)(2,1)S(1)} %bitcast.127), custom_call_target="tpu_custom_call" | custom-call | tf_op jit(solution)/shard_map/pallas_call | solution.py:59
  50.8 3.4 %fusion = f32[512,1408,1]{1,0,2:T(8,128)S(1)} fusion(bf16[3,512,352]{2,1,0:T(8,128)(2,1)S(1)} %shard_map.104, bf16[1,1408,352]{1,2,0:T(8,128)(2,1)S(1)} %bitcast.140, bf16[1,1408,352]{1,2,0:T(8,128)(2,1)S(1)} %bitcast.141, bf16[1,1408,352]{1,2,0:T(8,128)(2,1)} %bitcast.142), kind=kOutput, calls=%fused_computation.2 | convolution fusion | flops 1525506048 | bytes 6938624 | tf_op jit(solution)/shard_map/cnf,caf->na/dot_general | solution.py:147
  54.3 1.6 %copy-done.4 = f32[512,1408,1]{1,0,2:T(8,128)} copy-done((f32[512,1408,1]{1,0,2:T(8,128)}, f32[512,1408,1]{1,0,2:T(8,128)S(1)}, u32[]{:S(2)}) %copy-start.4) | copy-done | bytes 2883608
  55.8 0.1 fusion.14
  56.0 0.7 collective-permute-start
  56.7 1.5 %copy.132 = bf16[3,512,352]{1,2,0:T(8,128)(2,1)} copy(bf16[3,512,352]{2,1,0:T(8,128)(2,1)S(1)} %shard_map.104) | data formatting | bytes 2162688 | tf_op jit(solution)/shard_map/pallas_call | solution.py:59
  58.1 1.2 collective-permute-start.4
  59.5 0.4 collective-permute-start.3
  59.9 0.2 fusion.8
  60.3 1.3 collective-permute-start.1
  61.5 0.3 collective-permute-done.3
  61.8 0.1 select_bitcast_fusion.1
  62.0 0.2 maximum_bitcast_fusion
  62.1 0.1 copy.129
  62.2 0.1 constant_dynamic-slice_fusion
  62.3 8.1 %collective-permute-done.1 = bf16[8,16,1408]{2,1,0:T(8,128)(2,1)S(1)} collective-permute-done((bf16[8,16,1408]{2,1,0:T(8,128)(2,1)S(1)}, bf16[8,16,1408]{2,1,0:T(8,128)(2,1)S(1)}, u32[]{:S(2)}, u32[]{:S(2)}) %collective-permute-start.1) | collective-permute-done | bytes 360480 | tf_op jit(solution)/shard_map/ppermute | solution.py:85
  70.4 0.8 fusion.17
  71.3 5.5 %all-to-all-start.1 = ((bf16[8,16,1408]{2,1,0:T(8,128)(2,1)}), bf16[8,16,1408]{2,1,0:T(8,128)(2,1)}, u32[]{:S(2)}, u32[]{:S(2)}) async-start(bf16[8,16,1408]{2,1,0:T(8,128)(2,1)} %fusion.17), calls=%async_computation.1 | async-start | bytes 720896 | tf_op jit(solution)/shard_map/all_to_all | solution.py:157
  76.8 1.0 fusion.29
  77.8 8.5 %collective-permute-done.4 = bf16[3,512,352]{1,2,0:T(8,128)(2,1)} collective-permute-done((bf16[3,512,352]{1,2,0:T(8,128)(2,1)}, bf16[3,512,352]{1,2,0:T(8,128)(2,1)}, u32[]{:S(2)}, u32[]{:S(2)}) %collective-permute-start.4) | collective-permute-done | bytes 1081376 | tf_op jit(solution)/shard_map/ppermute | solution.py:85
  86.3 2.2 %fusion.6 = bf16[3,704,352]{1,2,0:T(8,128)(2,1)S(1)} fusion(f32[3,352,704]{2,1,0:T(8,128)S(1)} %fusion.29, bf16[3,512,352]{1,2,0:T(8,128)(2,1)} %collective-permute-done.4, bf16[512,704,1]{1,0,2:T(8,128)(2,1)S(1)} %bitcast.137), kind=kOutput, calls=%fused_computation.9 | convolution fusion | flops 763496448 | bytes 6262784 | tf_op jit(solution)/shard_map/na,cnf->caf/dot_general | solution.py:131
  88.6 1.0 copy.134
  89.6 0.4 reshape.225
  90.0 1.4 copy.135
  91.5 7.6 %all-to-all-start.3 = ((bf16[16,3,44,352]{3,2,1,0:T(8,128)(2,1)}), bf16[16,3,44,352]{3,2,1,0:T(8,128)(2,1)S(1)}, u32[]{:S(2)}, u32[]{:S(2)}) async-start(bf16[16,3,44,352]{3,2,1,0:T(8,128)(2,1)} %copy.135), calls=%async_computation.3 | async-start | bytes 3538944 | tf_op jit(solution)/shard_map/all_to_all | solution.py:138
  99.2 1.3 bitcast_reduce_fusion
  100.7 2.1 %fusion.22 = bf16[2,64,1408]{2,1,0:T(8,128)(2,1)} fusion(bf16[2,64,1408]{2,1,0:T(8,128)(2,1)S(1)} %copy-done.9, bf16[2,64,1408]{2,1,0:T(8,128)(2,1)S(1)} %copy-done.3, f32[2,64]{1,0:T(2,128)S(1)} %div.26, f32[2,64]{1,0:T(2,128)S(1)} %div.23, f32[1408]{0:T(1024)S(1)} %copy-done.10, f32[2,64]{1,0:T(2,128)S(1)} %add_rsqrt_fusion, ...), kind=kLoop, calls=%fused_computation.34 | loop fusion | flops 2162688 | bytes 1449472 | tf_op jit(solution)/shard_map/convert_element_type | solution.py:166
  102.7 36.7 %all-to-all-done.3 = bf16[16,3,44,352]{3,2,1,0:T(8,128)(2,1)S(1)} async-done(((bf16[16,3,44,352]{3,2,1,0:T(8,128)(2,1)}), bf16[16,3,44,352]{3,2,1,0:T(8,128)(2,1)S(1)}, u32[]{:S(2)}, u32[]{:S(2)}) %all-to-all-start.3) | async-done | bytes 1486880 | tf_op jit(solution)/shard_map/all_to_all | solution.py:138
  139.5 0.3 convert_reduce_fusion
  139.8 0.3 copy.137
  140.1 1.3 reshape.226
  (44 shorter events, 0.9 us)
Async XLA Ops:
  0.6 5.2 %copy-start.11 = (f32[1408]{0:T(1024)S(1)}, f32[1408]{0:T(1024)}, u32[]{:S(2)}) copy-start(f32[1408]{0:T(1024)} %param.11) | copy-start | bytes 16900
  0.6 5.3 %copy-start.10 = (f32[1408]{0:T(1024)S(1)}, f32[1408]{0:T(1024)}, u32[]{:S(2)}) copy-start(f32[1408]{0:T(1024)} %param.10) | copy-start | bytes 16900
  6.1 7.3 %copy-start.8 = (bf16[2,64,1408]{2,1,0:T(8,128)(2,1)S(1)}, bf16[2,64,1408]{2,1,0:T(8,128)(2,1)}, u32[]{:S(2)}) copy-start(bf16[2,64,1408]{2,1,0:T(8,128)(2,1)} %param.17) | copy-start | bytes 1081348
  7.7 14.1 %all-to-all-start.2 = ((bf16[8,2,16,704]{3,2,1,0:T(8,128)(2,1)}), bf16[8,2,16,704]{3,2,1,0:T(8,128)(2,1)S(1)}, u32[]{:S(2)}, u32[]{:S(2)}) async-start(bf16[8,2,16,704]{3,2,1,0:T(8,128)(2,1)} %reshape.221), calls=%async_computation.2 | async-start | bytes 786432 | tf_op jit(solution)/shard_map/all_to_all | solution.py:106
  21.8 19.2 %all-to-all-start = ((bf16[32,2,8,352]{3,2,1,0:T(8,128)(2,1)}), bf16[32,2,8,352]{3,2,1,0:T(8,128)(2,1)S(1)}, u32[]{:S(2)}, u32[]{:S(2)}) async-start(bf16[32,2,8,352]{3,2,1,0:T(8,128)(2,1)} %bitcast.9), calls=%async_computation | async-start | bytes 786432 | tf_op jit(solution)/shard_map/all_to_all | solution.py:92
  36.3 4.8 %copy-start = (bf16[64,8,352]{2,1,0:T(8,128)(2,1)S(1)}, bf16[64,8,352]{2,1,0:T(8,128)(2,1)}, u32[]{:S(2)}) copy-start(bf16[64,8,352]{2,1,0:T(8,128)(2,1)} %param.14) | copy-start | bytes 1081348
  36.3 4.8 %copy-start.1 = (bf16[64,8,352]{2,1,0:T(8,128)(2,1)S(1)}, bf16[64,8,352]{2,1,0:T(8,128)(2,1)}, u32[]{:S(2)}) copy-start(bf16[64,8,352]{2,1,0:T(8,128)(2,1)} %param.15) | copy-start | bytes 1081348
  36.3 4.8 %copy-start.2 = (bf16[64,8,352]{2,1,0:T(8,128)(2,1)S(1)}, bf16[64,8,352]{2,1,0:T(8,128)(2,1)}, u32[]{:S(2)}) copy-start(bf16[64,8,352]{2,1,0:T(8,128)(2,1)} %param.16) | copy-start | bytes 1081348
  40.7 18.7 %collective-permute-start.2 = (bf16[8,2,16,704]{3,2,1,0:T(8,128)(2,1)S(1)}, bf16[8,2,16,704]{3,2,1,0:T(8,128)(2,1)S(1)}, u32[]{:S(2)}, u32[]{:S(2)}) collective-permute-start(bf16[8,2,16,704]{3,2,1,0:T(8,128)(2,1)S(1)} %all-to-all-done.2), channel_id=1, source_target_pairs={{0,2},{1,3},{2,0},{3,1},{4,6},{5,7},{6,4},{7,5},{8,10},{9,11},{10,... | collective-permute-start | bytes 1081352 | tf_op jit(solution)/shard_map/ppermute | solution.py:85
  41.1 9.7 %copy-start.6 = (bf16[1408,352]{0,1:T(8,128)(2,1)S(1)}, bf16[1408,352]{0,1:T(8,128)(2,1)}, u32[]{:S(2)}) copy-start(bf16[1408,352]{0,1:T(8,128)(2,1)} %copy.112) | copy-start | bytes 2973700
  41.1 9.7 %copy-start.7 = (bf16[1408,352]{0,1:T(8,128)(2,1)S(1)}, bf16[1408,352]{0,1:T(8,128)(2,1)}, u32[]{:S(2)}) copy-start(bf16[1408,352]{0,1:T(8,128)(2,1)} %copy.111) | copy-start | bytes 2973700
  54.2 1.6 %copy-start.4 = (f32[512,1408,1]{1,0,2:T(8,128)}, f32[512,1408,1]{1,0,2:T(8,128)S(1)}, u32[]{:S(2)}) copy-start(f32[512,1408,1]{1,0,2:T(8,128)S(1)} %fusion) | copy-start | bytes 8650756
  56.0 3.9 %collective-permute-start = (bf16[8,2,16,1408]{3,2,1,0:T(8,128)(2,1)S(1)}, bf16[8,2,16,1408]{3,2,1,0:T(8,128)(2,1)S(1)}, u32[]{:S(2)}, u32[]{:S(2)}) collective-permute-start(bf16[8,2,16,1408]{3,2,1,0:T(8,128)(2,1)S(1)} %fusion.14), channel_id=1, source_target_pairs={{0,1},{1,0},{2,3},{3,2},{4,5},{5,4},{6,7},{7,6},{8,9},{9,8},{10,11... | collective-permute-start | bytes 2162696 | tf_op jit(solution)/shard_map/ppermute | solution.py:85
  58.1 1.8 %copy-start.5 = (f32[512,1408,1]{1,0,2:T(8,128)S(1)}, f32[512,1408,1]{1,0,2:T(8,128)}, u32[]{:S(2)}) copy-start(f32[512,1408,1]{1,0,2:T(8,128)} %copy-done.4) | copy-start | bytes 8650756
  58.1 28.2 %collective-permute-start.4 = (bf16[3,512,352]{1,2,0:T(8,128)(2,1)}, bf16[3,512,352]{1,2,0:T(8,128)(2,1)}, u32[]{:S(2)}, u32[]{:S(2)}) collective-permute-start(bf16[3,512,352]{1,2,0:T(8,128)(2,1)} %copy.132), channel_id=1, source_target_pairs={{0,4},{4,0},{8,12},{12,8},{16,20},{20,16},{24,28},{28,24},{1,5},{5... | collective-permute-start | bytes 3244040 | tf_op jit(solution)/shard_map/ppermute | solution.py:85
  59.5 2.4 %collective-permute-start.3 = (bf16[2,8,2,16,704]{4,3,2,1,0:T(8,128)(2,1)S(1)}, bf16[2,8,2,16,704]{4,3,2,1,0:T(8,128)(2,1)S(1)}, u32[]{:S(2)}, u32[]{:S(2)}) collective-permute-start(bf16[2,8,2,16,704]{4,3,2,1,0:T(8,128)(2,1)S(1)} %pad_maximum_fusion), channel_id=1, source_target_pairs={{0,1},{1,0},{2,3},{3,2},{4,5},{5,4},{6,7},{7,6},{8,9},{9,8},{10,11... | collective-permute-start | bytes 2162696 | tf_op jit(solution)/shard_map/ppermute | solution.py:85
  60.3 10.2 %collective-permute-start.1 = (bf16[8,16,1408]{2,1,0:T(8,128)(2,1)S(1)}, bf16[8,16,1408]{2,1,0:T(8,128)(2,1)S(1)}, u32[]{:S(2)}, u32[]{:S(2)}) collective-permute-start(bf16[8,16,1408]{2,1,0:T(8,128)(2,1)S(1)} %fusion.27), channel_id=1, source_target_pairs={{0,2},{1,3},{2,0},{3,1},{4,6},{5,7},{6,4},{7,5},{8,10},{9,11},{10,... | collective-permute-start | bytes 1081352 | tf_op jit(solution)/shard_map/ppermute | solution.py:85
  71.3 20.2 %all-to-all-start.1 = ((bf16[8,16,1408]{2,1,0:T(8,128)(2,1)}), bf16[8,16,1408]{2,1,0:T(8,128)(2,1)}, u32[]{:S(2)}, u32[]{:S(2)}) async-start(bf16[8,16,1408]{2,1,0:T(8,128)(2,1)} %fusion.17), calls=%async_computation.1 | async-start | bytes 720896 | tf_op jit(solution)/shard_map/all_to_all | solution.py:157
  91.5 7.8 %copy-start.3 = (bf16[2,64,1408]{2,1,0:T(8,128)(2,1)S(1)}, bf16[2,64,1408]{2,1,0:T(8,128)(2,1)}, u32[]{:S(2)}) copy-start(bf16[2,64,1408]{2,1,0:T(8,128)(2,1)} %param.9) | copy-start | bytes 1081348
  91.5 9.2 %copy-start.9 = (bf16[2,64,1408]{2,1,0:T(8,128)(2,1)S(1)}, bf16[2,64,1408]{2,1,0:T(8,128)(2,1)}, u32[]{:S(2)}) copy-start(bf16[2,64,1408]{2,1,0:T(8,128)(2,1)} %param.17) | copy-start | bytes 1081348
  91.5 48.0 %all-to-all-start.3 = ((bf16[16,3,44,352]{3,2,1,0:T(8,128)(2,1)}), bf16[16,3,44,352]{3,2,1,0:T(8,128)(2,1)S(1)}, u32[]{:S(2)}, u32[]{:S(2)}) async-start(bf16[16,3,44,352]{3,2,1,0:T(8,128)(2,1)} %copy.135), calls=%async_computation.3 | async-start | bytes 3538944 | tf_op jit(solution)/shard_map/all_to_all | solution.py:138

commit v2 on v1

--- a/solution.py
+++ b/solution.py
@@ -64,6 +64,11 @@
         out_shape=jax.ShapeDtypeStruct((3, n_tok, width), BF),
         scratch_shapes=[pltpu.VMEM((3, n_tok, width), F32)],
         compiler_params=pltpu.CompilerParams(vmem_limit_bytes=48 * 1024 * 1024),
+        cost_estimate=pl.CostEstimate(
+            flops=10 * n_tok * n_tok * width * (width // DH),
+            transcendentals=n_tok * n_tok * (width // DH),
+            bytes_accessed=14 * n_tok * width,
+        ),
     )(query, key, value, grad)
 
 
@@ -73,12 +78,14 @@
     n_tm = lax.axis_size("tm")
     n_patch = lax.axis_size("patch")
     n_pair = n_tm // 2
+    n_chip = n_patch // 2
     devices = n_tm * n_patch
     n_tok = frames * columns
     own_rows = width // devices
     tm = lax.axis_index("tm")
     patch = lax.axis_index("patch")
     side = tm % 2
+    core = patch % 2
     both = ("tm", "patch")
 
     def swap(values, axis, size, bit):
@@ -89,9 +96,13 @@
         "to,jfo->jtf", grad_rows, w_out.reshape(n_patch, part, width), preferred_element_type=F32
     ).astype(BF)
     d_attn = d_attn.reshape(n_patch, t_dev, n_tm, columns, part).transpose(2, 0, 1, 3, 4)
+    d_attn, tokens = lax.optimization_barrier((d_attn, tokens))
     d_time = lax.all_to_all(
         d_attn.reshape(devices, t_dev, columns, part), both, 0, 0, tiled=True
     ).reshape(n_tok, part)
+
+    saved = [values.reshape(n_tok, part) for values in (q_time, k_time, v_time)]
+    saved_other = [swap(values, "tm", n_tm, 1) for values in saved]
 
     as_float = tokens.reshape(-1, width).astype(F32)
     centered = as_float - jnp.mean(as_float, axis=-1, keepdims=True)
@@ -100,62 +111,82 @@
     normed = centered * inverse
     norm_out = (normed * ln_gain + ln_bias).astype(BF)
 
-    half = width // 2
-    sent = norm_out.reshape(t_dev, n_pair, 2 * columns, n_pair, 2, n_patch * own_rows)
-    sent = sent.transpose(1, 4, 0, 2, 3, 5).reshape(n_tm, t_dev, 2 * columns, half)
-    got = lax.all_to_all(sent, "tm", 0, 0, tiled=True)
-    bits = [1 << n for n in reversed(range(n_patch.bit_length() - 1))]
-    for bit in bits:
-        other = swap(got, "patch", n_patch, bit)
-        high = (patch & bit) != 0
-        got = jnp.stack([jnp.where(high, other, got), jnp.where(high, got, other)])
-    order = tuple(reversed(range(len(bits))))
-    at = len(bits)
-    got = got.transpose((at,) + order + tuple(range(at + 1, got.ndim)))
-    got = got.reshape(n_tm, n_patch, t_dev, 2, columns, half)
+    quarter = width // 4
+    sent = norm_out.reshape(t_dev, n_pair, 2 * columns, n_pair, 2, n_chip, 2, own_rows)
+    sent = sent.transpose(1, 4, 6, 0, 2, 3, 5, 7).reshape(
+        n_pair, 2, 1, 2, t_dev, 2 * columns, quarter
+    )
+    sent = jnp.broadcast_to(sent, (n_pair, 2, n_chip, 2, t_dev, 2 * columns, quarter))
+    weights = [
+        lax.dynamic_slice_in_dim(w_qkv, c * width + patch * part, part, 1)
+        for c in range(3)
+    ]
+    d_time, sent, saved_other, weights = lax.optimization_barrier(
+        (d_time, sent, saved_other, weights)
+    )
+    d_other = swap(d_time, "tm", n_tm, 1)
+    got = lax.all_to_all(
+        sent.reshape(devices, t_dev, 2 * columns, quarter), both, 0, 0, tiled=True
+    )
+    got = got.reshape(frames, 2, columns, quarter)
     norm_own, norm_other = [
-        lax.dynamic_index_in_dim(got, index, 3, keepdims=False).reshape(n_tok, half)
+        lax.dynamic_index_in_dim(got, index, 1, keepdims=False).reshape(n_tok, quarter)
         for index in (side, 1 - side)
     ]
 
-    grads = attend(
-        q_time.reshape(n_tok, part),
-        k_time.reshape(n_tok, part),
-        v_time.reshape(n_tok, part),
-        d_time,
-        columns,
-    )
-    grads_other = swap(grads, "tm", n_tm, 1)
+    grads = attend(*saved, d_time, columns)
+    grads_other = attend(*saved_other, d_other, columns)
+    grads_core = swap(grads, "patch", n_patch, 1)
+    grads_other_core = swap(grads_other, "patch", n_patch, 1)
+    grads, grads_other, grads_core, grads_other_core, norm_own, norm_other = (
+        lax.optimization_barrier(
+            (grads, grads_other, grads_core, grads_other_core, norm_own, norm_other)
+        )
+    )
 
     factor = 1.0 / math.sqrt(frames * patches)
-    partial = jnp.einsum("na,cnf->caf", norm_own, grads, preferred_element_type=F32) + jnp.einsum(
-        "na,cnf->caf", norm_other, grads_other, preferred_element_type=F32
-    )
-    partial = (partial * factor).astype(BF).reshape(3, n_pair * n_patch, own_rows, part)
+
+    def product(one, other):
+        total = jnp.einsum("na,cnf->caf", norm_own, one, preferred_element_type=F32)
+        total += jnp.einsum("na,cnf->caf", norm_other, other, preferred_element_type=F32)
+        return (total * factor).astype(BF).reshape(3, n_pair * n_chip, own_rows, part)
+
+    partial = jnp.stack([product(grads, grads_other), product(grads_core, grads_other_core)])
     groups = [
-        [(2 * z + y) * n_patch + p for z in range(n_pair) for p in range(n_patch)] for y in range(2)
+        [(2 * z + y) * n_patch + 2 * x + c for z in range(n_pair) for x in range(n_chip)]
+        for y in range(2)
+        for c in range(2)
     ]
     pieces = lax.all_to_all(
-        partial.transpose(1, 0, 2, 3), both, 0, 0, axis_index_groups=groups, tiled=True
-    )
-    pieces = pieces.reshape(n_pair, n_patch, 3, own_rows, part).astype(F32)
-    grad_w_qkv = jnp.sum(pieces, axis=0).transpose(2, 1, 0, 3).reshape(own_rows, 3 * width)
-
-    weights = jnp.stack(
-        [lax.dynamic_slice_in_dim(w_qkv, c * width + patch * part, part, 1) for c in range(3)]
-    )
-    share = jnp.einsum("cnf,caf->na", grads, weights, preferred_element_type=F32)
-    share = share.reshape((n_tm,) + (2,) * len(bits) + (t_dev * columns, width))
-    for bit in reversed(bits):
-        high = (patch & bit) != 0
-        axis = share.ndim - 3
-        low_part = lax.index_in_dim(share, 0, axis, keepdims=False)
-        high_part = lax.index_in_dim(share, 1, axis, keepdims=False)
-        leave = jnp.where(high, low_part, high_part).astype(BF)
-        stay = jnp.where(high, high_part, low_part)
-        share = stay + swap(leave, "patch", n_patch, bit).astype(F32)
-    d_norm = lax.all_to_all(share.astype(BF), "tm", 0, 0, tiled=True)
-    d_norm = d_norm.reshape(n_tm, t_dev, columns, width).transpose(1, 0, 2, 3)
+        partial.transpose(2, 0, 1, 3, 4), both, 0, 0, axis_index_groups=groups, tiled=True
+    )
+    pieces = pieces.reshape(n_pair, n_chip, 2, 3, own_rows, part).astype(F32)
+    summed = jnp.sum(pieces, axis=0)
+    summed = jnp.where(core == 0, summed, summed[:, ::-1])
+    grad_w_qkv = summed.transpose(3, 2, 0, 1, 4).reshape(own_rows, 3 * width)
+
+    share = sum(
+        lax.dot_general(grads[c], weights[c], COLS, preferred_element_type=F32) for c in range(3)
+    )
+
+    def split(values, axis, high):
+        low_part = lax.index_in_dim(values, 0, axis, keepdims=False)
+        high_part = lax.index_in_dim(values, 1, axis, keepdims=False)
+        return jnp.where(high, high_part, low_part), jnp.where(high, low_part, high_part)
+
+    bits = n_patch.bit_length() - 1
+    share = share.reshape((n_tm,) + (2,) * bits + (t_dev * columns, width))
+    for n in range(bits):
+        stay, leave = split(share, bits - n, (patch & (1 << n)) != 0)
+        share = stay + swap(leave.astype(BF), "patch", n_patch, 1 << n).astype(F32)
+    bits = n_tm.bit_length() - 1
+    share = share.astype(BF).reshape((2,) * bits + (1, t_dev * columns, width))
+    for n in range(bits):
+        high = (tm & (1 << n)) != 0
+        stay, leave = split(share, bits - 1 - n, high)
+        come = swap(leave, "tm", n_tm, 1 << n)
+        share = jnp.concatenate([jnp.where(high, come, stay), jnp.where(high, stay, come)], bits - 1 - n)
+    d_norm = share.reshape(n_tm, t_dev, columns, width).transpose(1, 0, 2, 3)
     d_norm = d_norm.reshape(-1, width).astype(F32)
     scaled = d_norm * ln_gain
     branch = inverse * (

time: 142 us -> 164 us (1.15)
  the two profiles are of different devices: /device:TPU:11 before, /device:TPU:0 now
where the time goes in v2:
time: 164 us
  waiting for transfers between devices  54.2 us (33%)
  starting transfers between devices  33.8 us (21%)
  local copies, waits for them, and re-layouts  31 us (19%)
  Pallas kernels  20.3 us (12%)
  matrix products  12.5 us (8%)
  other arithmetic  11 us (7%)
    ppermute x11, waiting for transfers between devices, swap(): return lax.ppermute(values, axis, [(i, i ^ bit) for i in range(size)])  54.2 us
    pallas_call x2, Pallas kernels, attend(): pl.pallas_call(functools.partial(attend_kernel, columns=columns, block=bl...  20.3 us
    ppermute x11, starting transfers between devices, swap(): return lax.ppermute(values, axis, [(i, i ^ bit) for i in range(size)])  15.7 us
    all_to_all x1, starting transfers between devices, per_device(): lax.all_to_all(d_attn.reshape(devices, t_dev, columns, part), both, 0, 0,...  7.3 us
    dynamic_slice x1, local copies, waits for them, and re-layouts, per_device(): lax.dynamic_slice_in_dim(w_qkv, c * width + patch * part, part, 1)  5.82 us
    all_to_all x1, starting transfers between devices, per_device(): lax.all_to_all(partial.transpose(2, 0, 1, 3, 4), both, 0, 0, axis_index_g...  5.54 us
    transpose x1, other arithmetic, per_device(): sent.transpose(1, 4, 6, 0, 2, 3, 5, 7)  5.36 us
    all_to_all x1, starting transfers between devices, per_device(): lax.all_to_all(sent.reshape(devices, t_dev, 2 * columns, quarter), both,...  5.24 us
  transfers between devices with their start and end apart: 14, of which 6 were waited for; matrix products, arithmetic and copies ran while one was open for 24% of the time, Pallas kernels for 12%

profile of v2, /device:TPU:0, one launch (start us, length us, event | category | flops | bytes accessed | tf_op | source)
XLA Modules:
  0.0 163.8 jit_solution(3001836201847190276)
XLA Ops:
  0.6 3.4 %fusion.7 = bf16[4,128,352]{1,2,0:T(8,128)(2,1)S(1)} fusion(bf16[4,352,1408]{2,1,0:T(8,128)(2,1)} %bitcast.196, bf16[128,1408,1]{1,0,2:T(8,128)(2,1)} %bitcast.195), kind=kOutput, calls=%fused_computation.17 | convolution fusion | flops 507691008 | bytes 4685824 | tf_op jit(solution)/shard_map/to,jfo->jtf/dot_general | solution.py:95
  4.3 0.8 copy.168
  5.1 7.3 %all-to-all-start = ((bf16[32,2,8,352]{3,2,1,0:T(8,128)(2,1)}), bf16[32,2,8,352]{3,2,1,0:T(8,128)(2,1)S(1)}, u32[]{:S(2)}, u32[]{:S(2)}) async-start(bf16[32,2,8,352]{3,2,1,0:T(8,128)(2,1)} %bitcast.9), calls=%async_computation | async-start | bytes 786432 | tf_op jit(solution)/shard_map/all_to_all | solution.py:100
  12.4 1.8 %collective-permute-start = (bf16[512,352]{1,0:T(8,128)(2,1)S(1)}, bf16[512,352]{1,0:T(8,128)(2,1)S(1)}, u32[]{:S(2)}, u32[]{:S(2)}) collective-permute-start(bf16[512,352]{1,0:T(8,128)(2,1)S(1)} %bitcast.184), channel_id=1, source_target_pairs={{0,4},{4,0},{8,12},{12,8},{16,20},{20,16},{24,28},{28,24},{1,5},{5... | collective-permute-start | bytes 1081352 | tf_op jit(solution)/shard_map/ppermute | solution.py:92
  14.5 1.8 %collective-permute-start.2 = (bf16[512,352]{1,0:T(8,128)(2,1)S(1)}, bf16[512,352]{1,0:T(8,128)(2,1)S(1)}, u32[]{:S(2)}, u32[]{:S(2)}) collective-permute-start(bf16[512,352]{1,0:T(8,128)(2,1)S(1)} %bitcast.188), channel_id=1, source_target_pairs={{0,4},{4,0},{8,12},{12,8},{16,20},{20,16},{24,28},{28,24},{1,5},{5... | collective-permute-start | bytes 1081352 | tf_op jit(solution)/shard_map/ppermute | solution.py:92
  16.7 4.9 %reshape.281 = f32[2,4,16,4,2,2,2,44]{7,6,5,4,3,2,1,0:T(2,128)} reshape(bf16[2,64,1408]{2,1,0:T(8,128)(2,1)S(1)} %copy-done.9) | data formatting | bytes 1081344 | tf_op jit(solution)/shard_map/convert_element_type | solution.py:107
  22.0 5.4 %fusion.8 = bf16[4,2,2,2,16,4,2,44]{7,6,5,4,3,2,1,0:T(2,128)(2,1)} fusion(f32[4,2,2,2,44]{4,2,0,3,1:T(2,128)S(1)} %copy.173, f32[4,2,2,2,44]{4,2,0,3,1:T(2,128)S(1)} %copy.172, f32[2,4,16]{2,0,1:T(2,128)S(1)} %copy.171, f32[2,4,16]{2,0,1:T(2,128)S(1)} %copy.169, f32[2,4,16,4,2,2,2,44]{7,6,5,4,3,2,1,0:T(2,128)} %reshape.281), kind=kLoop, calls=%fused_computation.18 | loop fusion | flops 901120 | bytes 1093632 | tf_op jit(solution)/shard_map/transpose | solution.py:116
  27.4 3.9 %broadcast_in_dim.4 = bf16[4,2,2,2,16,352]{5,4,3,2,1,0:T(8,128)(2,1)S(1)} reshape(bf16[4,2,2,2,16,4,2,44]{7,6,5,4,3,2,1,0:T(2,128)(2,1)} %fusion.8) | data formatting | bytes 720896 | tf_op jit(solution)/shard_map/broadcast_in_dim | solution.py:119
  31.3 5.8 %constant_dynamic-slice_fusion = (bf16[1408,352]{1,0:T(8,128)(2,1)}, bf16[1408,352]{1,0:T(8,128)(2,1)}, bf16[1408,352]{1,0:T(8,128)(2,1)}) fusion(bf16[1408,4224]{1,0:T(8,128)(2,1)} %param.12, s32[]{:T(128)S(6)} %select_n.177, s32[]{:T(128)S(6)} %select_n.175, s32[]{:T(128)S(6)} %select_n.176), kind=kLoop, calls=%fused_computation.87 | loop fusion | bytes 5947404 | tf_op jit(solution)/shard_map/dynamic_slice | solution.py:121
  37.1 7.6 %collective-permute-done.2.v_ref = bf16[512,352]{1,0:T(8,128)(2,1)S(1)} collective-permute-done((bf16[512,352]{1,0:T(8,128)(2,1)S(1)}, bf16[512,352]{1,0:T(8,128)(2,1)S(1)}, u32[]{:S(2)}, u32[]{:S(2)}) %collective-permute-start.2) | collective-permute-done | bytes 360480 | tf_op jit(solution)/shard_map/ppermute | solution.py:92
  44.7 1.0 broadcast_in_dim.5
  45.7 1.1 collective-permute-start.3
  46.8 5.2 %all-to-all-start.1 = ((bf16[32,2,16,352]{3,2,1,0:T(8,128)(2,1)}), bf16[32,2,16,352]{3,2,1,0:T(8,128)(2,1)}, u32[]{:S(2)}, u32[]{:S(2)}) async-start(bf16[32,2,16,352]{3,2,1,0:T(8,128)(2,1)} %bitcast.12), calls=%async_computation.1 | async-start | bytes 1572864 | tf_op jit(solution)/shard_map/all_to_all | solution.py:128
  52.1 9.7 %shard_map.104 = bf16[3,512,352]{2,1,0:T(8,128)(2,1)S(1)} custom-call(bf16[512,352]{1,0:T(8,128)(2,1)S(1)} %bitcast.185, bf16[512,352]{1,0:T(8,128)(2,1)S(1)} %bitcast.187, bf16[512,352]{1,0:T(8,128)(2,1)S(1)} %bitcast.189, bf16[512,352]{1,0:T(8,128)(2,1)S(1)} %bitcast.183), custom_call_target="tpu_custom_call" | custom-call | flops 3690987520 | bytes 2523136 | tf_op jit(solution)/shard_map/pallas_call | solution.py:59
  61.7 1.4 copy.174
  63.2 10.7 %shard_map.105 = bf16[3,512,352]{2,1,0:T(8,128)(2,1)S(1)} custom-call(bf16[512,352]{1,0:T(8,128)(2,1)S(1)} %collective-permute-done.q_ref, bf16[512,352]{1,0:T(8,128)(2,1)S(1)} %collective-permute-done.1.k_ref, bf16[512,352]{1,0:T(8,128)(2,1)S(1)} %copy-done.4, bf16[512,352]{1,0:T(8,128)(2,1)} %collective-permute-done.3.d_ref), custom_call_target="tpu_custom_call" | custom-call | flops 3690987520 | bytes 2523136 | tf_op jit(solution)/shard_map/pallas_call | solution.py:59
  73.9 1.5 copy.175
  75.4 0.5 collective-permute-start.5
  75.9 2.1 %dynamic-slice_bitcast_fusion = (bf16[512,352]{1,0:T(8,128)(2,1)}, bf16[512,352]{1,0:T(8,128)(2,1)}) fusion(bf16[64,2,8,352]{3,2,1,0:T(8,128)(2,1)} %bitcast.13, s32[]{:T(128)S(6)} %select_n.180, s32[]{:T(128)S(6)} %select_n.179), kind=kLoop, calls=%fused_computation.55 | loop fusion | bytes 1441800 | tf_op jit(solution)/shard_map/reshape | solution.py:133
  78.0 0.6 collective-permute-done.5
  78.5 0.9 fusion.30
  79.8 1.0 fusion.28
  81.0 1.1 fusion
  82.1 0.3 fusion.45
  82.5 1.0 fusion.14
  83.5 0.3 copy-done.5
  83.8 0.5 copy-done.7
  84.3 0.4 collective-permute-start.6
  84.7 0.7 fusion.24
  85.3 1.3 collective-permute-done.6
  87.0 1.6 collective-permute-start.7
  88.7 1.9 %fusion.22 = f32[3,352,352]{1,2,0:T(8,128)S(1)} fusion(bf16[3,512,352]{1,2,0:T(8,128)(2,1)} %collective-permute-done.5, bf16[512,352]{1,0:T(8,128)(2,1)S(1)} %copy-done.14), kind=kOutput, calls=%fused_computation.41 | convolution fusion | flops 380633088 | bytes 2928640 | tf_op jit(solution)/shard_map/na,cnf->caf/dot_general | solution.py:151
  90.6 0.7 fusion.5
  91.3 6.5 %collective-permute-done.7 = bf16[8,16,1408]{2,1,0:T(8,128)(2,1)S(1)} collective-permute-done((bf16[8,16,1408]{2,1,0:T(8,128)(2,1)S(1)}, bf16[8,16,1408]{2,1,0:T(8,128)(2,1)S(1)}, u32[]{:S(2)}, u32[]{:S(2)}) %collective-permute-start.7) | collective-permute-done | bytes 360480 | tf_op jit(solution)/shard_map/ppermute | solution.py:92
  97.9 1.6 collective-permute-start.8
  99.5 2.8 %fusion.6 = bf16[3,352,352]{2,1,0:T(8,128)(2,1)} fusion(f32[3,352,352]{1,2,0:T(8,128)S(1)} %fusion.22, bf16[3,512,352]{1,2,0:T(8,128)(2,1)} %collective-permute-done.4, bf16[512,352]{1,0:T(8,128)(2,1)S(1)} %copy-done.15), kind=kOutput, calls=%fused_computation.15 | convolution fusion | flops 381748224 | bytes 3672064 | tf_op jit(solution)/shard_map/na,cnf->caf/dot_general | solution.py:150
  102.6 1.5 stack_reshape.7
  104.0 0.4 maximum_bitcast_fusion
  104.4 2.9 %copy.202 = bf16[8,2,3,44,352]{4,1,3,2,0:T(2,128)(2,1)} copy(bf16[8,2,3,44,352]{4,3,0,2,1:T(8,128)(2,1)S(1)} %maximum_bitcast_fusion) | data formatting | bytes 2973696 | tf_op jit(solution)/shard_map/transpose | solution.py:161
  107.3 5.5 %all-to-all-start.2 = ((bf16[8,2,3,44,352]{4,1,3,2,0:T(2,128)(2,1)}), bf16[8,2,3,44,352]{4,1,3,2,0:T(2,128)(2,1)S(1)}, u32[]{:S(2)}, u32[]{:S(2)}) async-start(bf16[8,2,3,44,352]{4,1,3,2,0:T(2,128)(2,1)} %copy.202), calls=%async_computation.2 | async-start | bytes 3244032 | tf_op jit(solution)/shard_map/all_to_all | solution.py:160
  113.0 2.1 %collective-permute-start.9 = (bf16[2,2,16,1408]{3,2,0,1:T(8,128)(2,1)S(1)}, bf16[2,2,16,1408]{3,2,0,1:T(8,128)(2,1)S(1)}, u32[]{:S(2)}, u32[]{:S(2)}) collective-permute-start(bf16[2,2,16,1408]{3,2,0,1:T(8,128)(2,1)S(1)} %fusion.43), channel_id=1, source_target_pairs={{0,8},{4,12},{8,0},{12,4},{16,24},{20,28},{24,16},{28,20},{1,9},{5... | collective-permute-start | bytes 540680 | tf_op jit(solution)/shard_map/ppermute | solution.py:92
  115.0 27.4 %collective-permute-done.9 = bf16[2,2,16,1408]{3,2,0,1:T(8,128)(2,1)S(1)} collective-permute-done((bf16[2,2,16,1408]{3,2,0,1:T(8,128)(2,1)S(1)}, bf16[2,2,16,1408]{3,2,0,1:T(8,128)(2,1)S(1)}, u32[]{:S(2)}, u32[]{:S(2)}) %collective-permute-start.9) | collective-permute-done | bytes 180256 | tf_op jit(solution)/shard_map/ppermute | solution.py:92
  142.5 4.6 %collective-permute-start.10 = (bf16[4,16,1408]{2,1,0:T(8,128)(2,1)S(1)}, bf16[4,16,1408]{2,1,0:T(8,128)(2,1)S(1)}, u32[]{:S(2)}, u32[]{:S(2)}) collective-permute-start(bf16[4,16,1408]{2,1,0:T(8,128)(2,1)S(1)} %fusion.42), channel_id=1, source_target_pairs={{0,16},{4,20},{8,24},{12,28},{16,0},{20,4},{24,8},{28,12},{1,17},{... | collective-permute-start | bytes 540680 | tf_op jit(solution)/shard_map/ppermute | solution.py:92
  147.3 10.7 %collective-permute-done.10 = bf16[4,16,1408]{2,1,0:T(8,128)(2,1)S(1)} collective-permute-done((bf16[4,16,1408]{2,1,0:T(8,128)(2,1)S(1)}, bf16[4,16,1408]{2,1,0:T(8,128)(2,1)S(1)}, u32[]{:S(2)}, u32[]{:S(2)}) %collective-permute-start.10) | collective-permute-done | bytes 180256 | tf_op jit(solution)/shard_map/ppermute | solution.py:92
  158.6 1.1 fusion.19
  159.7 1.7 %convert_reduce_fusion = f32[2,2,3,44,352]{4,1,3,2,0:T(2,128)S(1)} fusion(bf16[4,2,2,3,44,352]{5,2,4,3,1,0:T(2,128)(2,1)S(1)} %bitcast.191), kind=kLoop, calls=%fused_computation.2 | loop fusion | flops 1300992 | bytes 2230272 | tf_op jit(solution)/shard_map/reduce_sum | solution.py:164
  161.5 0.6 copy.204
  162.2 1.6 reshape.280
  (79 shorter events, 3.6 us)
Async XLA Ops:
  4.0 8.4 %copy-start = (bf16[64,8,352]{2,1,0:T(8,128)(2,1)S(1)}, bf16[64,8,352]{2,1,0:T(8,128)(2,1)}, u32[]{:S(2)}) copy-start(bf16[64,8,352]{2,1,0:T(8,128)(2,1)} %param.14) | copy-start | bytes 1081348
  4.0 10.2 %copy-start.1 = (bf16[64,8,352]{2,1,0:T(8,128)(2,1)S(1)}, bf16[64,8,352]{2,1,0:T(8,128)(2,1)}, u32[]{:S(2)}) copy-start(bf16[64,8,352]{2,1,0:T(8,128)(2,1)} %param.15) | copy-start | bytes 1081348
  4.0 10.5 %copy-start.2 = (bf16[64,8,352]{2,1,0:T(8,128)(2,1)S(1)}, bf16[64,8,352]{2,1,0:T(8,128)(2,1)}, u32[]{:S(2)}) copy-start(bf16[64,8,352]{2,1,0:T(8,128)(2,1)} %param.16) | copy-start | bytes 1081348
  4.0 12.2 %copy-start.9 = (bf16[2,64,1408]{2,1,0:T(8,128)(2,1)S(1)}, bf16[2,64,1408]{2,1,0:T(8,128)(2,1)}, u32[]{:S(2)}) copy-start(bf16[2,64,1408]{2,1,0:T(8,128)(2,1)} %param.9) | copy-start | bytes 1081348
  5.1 39.7 %all-to-all-start = ((bf16[32,2,8,352]{3,2,1,0:T(8,128)(2,1)}), bf16[32,2,8,352]{3,2,1,0:T(8,128)(2,1)S(1)}, u32[]{:S(2)}, u32[]{:S(2)}) async-start(bf16[32,2,8,352]{3,2,1,0:T(8,128)(2,1)} %bitcast.9), calls=%async_computation | async-start | bytes 786432 | tf_op jit(solution)/shard_map/all_to_all | solution.py:100
  12.4 24.7 %collective-permute-start = (bf16[512,352]{1,0:T(8,128)(2,1)S(1)}, bf16[512,352]{1,0:T(8,128)(2,1)S(1)}, u32[]{:S(2)}, u32[]{:S(2)}) collective-permute-start(bf16[512,352]{1,0:T(8,128)(2,1)S(1)} %bitcast.184), channel_id=1, source_target_pairs={{0,4},{4,0},{8,12},{12,8},{16,20},{20,16},{24,28},{28,24},{1,5},{5... | collective-permute-start | bytes 1081352 | tf_op jit(solution)/shard_map/ppermute | solution.py:92
  14.2 22.9 %collective-permute-start.1 = (bf16[512,352]{1,0:T(8,128)(2,1)S(1)}, bf16[512,352]{1,0:T(8,128)(2,1)S(1)}, u32[]{:S(2)}, u32[]{:S(2)}) collective-permute-start(bf16[512,352]{1,0:T(8,128)(2,1)S(1)} %bitcast.186), channel_id=1, source_target_pairs={{0,4},{4,0},{8,12},{12,8},{16,20},{20,16},{24,28},{28,24},{1,5},{5... | collective-permute-start | bytes 1081352 | tf_op jit(solution)/shard_map/ppermute | solution.py:92
  14.5 30.2 %collective-permute-start.2 = (bf16[512,352]{1,0:T(8,128)(2,1)S(1)}, bf16[512,352]{1,0:T(8,128)(2,1)S(1)}, u32[]{:S(2)}, u32[]{:S(2)}) collective-permute-start(bf16[512,352]{1,0:T(8,128)(2,1)S(1)} %bitcast.188), channel_id=1, source_target_pairs={{0,4},{4,0},{8,12},{12,8},{16,20},{20,16},{24,28},{28,24},{1,5},{5... | collective-permute-start | bytes 1081352 | tf_op jit(solution)/shard_map/ppermute | solution.py:92
  16.4 5.4 %copy-start.17 = (f32[1408]{0:T(1024)S(1)}, f32[1408]{0:T(1024)}, u32[]{:S(2)}) copy-start(f32[1408]{0:T(1024)} %param.10) | copy-start | bytes 16900
  16.4 5.5 %copy-start.18 = (f32[1408]{0:T(1024)S(1)}, f32[1408]{0:T(1024)}, u32[]{:S(2)}) copy-start(f32[1408]{0:T(1024)} %param.11) | copy-start | bytes 16900
  44.7 2.1 %copy-start.3 = (bf16[512,352]{1,0:T(8,128)(2,1)}, bf16[512,352]{1,0:T(8,128)(2,1)S(1)}, u32[]{:S(2)}) copy-start(bf16[512,352]{1,0:T(8,128)(2,1)S(1)} %collective-permute-done.2.v_ref) | copy-start | bytes 1081348
  45.7 17.5 %collective-permute-start.3 = (bf16[512,352]{1,0:T(8,128)(2,1)S(1)}, bf16[512,352]{1,0:T(8,128)(2,1)}, u32[]{:S(2)}, u32[]{:S(2)}) collective-permute-start(bf16[512,352]{1,0:T(8,128)(2,1)S(1)} %bitcast.182), channel_id=1, source_target_pairs={{0,4},{4,0},{8,12},{12,8},{16,20},{20,16},{24,28},{28,24},{1,5},{5... | collective-permute-start | bytes 1081352 | tf_op jit(solution)/shard_map/ppermute | solution.py:92
  46.8 29.1 %all-to-all-start.1 = ((bf16[32,2,16,352]{3,2,1,0:T(8,128)(2,1)}), bf16[32,2,16,352]{3,2,1,0:T(8,128)(2,1)}, u32[]{:S(2)}, u32[]{:S(2)}) async-start(bf16[32,2,16,352]{3,2,1,0:T(8,128)(2,1)} %bitcast.12), calls=%async_computation.1 | async-start | bytes 1572864 | tf_op jit(solution)/shard_map/all_to_all | solution.py:128
  61.7 1.5 copy-start.4
  63.2 14.8 %collective-permute-start.4 = (bf16[3,512,352]{1,2,0:T(8,128)(2,1)}, bf16[3,512,352]{1,2,0:T(8,128)(2,1)}, u32[]{:S(2)}, u32[]{:S(2)}) collective-permute-start(bf16[3,512,352]{1,2,0:T(8,128)(2,1)} %copy.174), channel_id=1, source_target_pairs={{0,1},{1,0},{2,3},{3,2},{4,5},{5,4},{6,7},{7,6},{8,9},{9,8},{10,11... | collective-permute-start | bytes 3244040 | tf_op jit(solution)/shard_map/ppermute | solution.py:92
  73.9 4.6 %copy-start.13 = (bf16[1408,352]{1,0:T(8,128)(2,1)S(1)}, bf16[1408,352]{1,0:T(8,128)(2,1)}, u32[]{:S(2)}) copy-start(bf16[1408,352]{1,0:T(8,128)(2,1)} %get-tuple-element.27) | copy-start | bytes 2973700
  75.4 3.2 %collective-permute-start.5 = (bf16[3,512,352]{1,2,0:T(8,128)(2,1)}, bf16[3,512,352]{1,2,0:T(8,128)(2,1)}, u32[]{:S(2)}, u32[]{:S(2)}) collective-permute-start(bf16[3,512,352]{1,2,0:T(8,128)(2,1)} %copy.175), channel_id=1, source_target_pairs={{0,1},{1,0},{2,3},{3,2},{4,5},{5,4},{6,7},{7,6},{8,9},{9,8},{10,11... | collective-permute-start | bytes 3244040 | tf_op jit(solution)/shard_map/ppermute | solution.py:92
  78.5 1.2 copy-start.12
  79.8 1.2 copy-start.11
  82.4 1.3 copy-start.5
  82.5 1.8 %copy-start.7 = (f32[8,2,1,16,1408]{4,3,2,1,0:T(8,128)}, f32[8,2,1,16,1408]{4,3,2,1,0:T(8,128)S(1)}, u32[]{:S(2)}) copy-start(f32[8,2,1,16,1408]{4,3,2,1,0:T(8,128)S(1)} %get-tuple-element.40) | copy-start | bytes 4325380
  82.5 2.2 %copy-start.14 = (bf16[512,352]{1,0:T(8,128)(2,1)S(1)}, bf16[512,352]{1,0:T(8,128)(2,1)}, u32[]{:S(2)}) copy-start(bf16[512,352]{1,0:T(8,128)(2,1)} %get-tuple-element.31) | copy-start | bytes 1081348
  84.3 2.4 %collective-permute-start.6 = (bf16[8,2,16,1408]{3,2,0,1:T(8,128)(2,1)}, bf16[8,2,16,1408]{3,2,0,1:T(8,128)(2,1)S(1)}, u32[]{:S(2)}, u32[]{:S(2)}) collective-permute-start(bf16[8,2,16,1408]{3,2,0,1:T(8,128)(2,1)} %fusion.14), channel_id=1, source_target_pairs={{0,1},{1,0},{2,3},{3,2},{4,5},{5,4},{6,7},{7,6},{8,9},{9,8},{10,11... | collective-permute-start | bytes 2162696 | tf_op jit(solution)/shard_map/ppermute | solution.py:92
  84.7 2.0 %copy-start.6 = (f32[8,2,1,16,1408]{4,3,2,1,0:T(8,128)S(1)}, f32[8,2,1,16,1408]{4,3,2,1,0:T(8,128)}, u32[]{:S(2)}) copy-start(f32[8,2,1,16,1408]{4,3,2,1,0:T(8,128)} %copy-done.5) | copy-start | bytes 4325380
  84.7 2.0 %copy-start.8 = (f32[8,2,1,16,1408]{4,3,2,1,0:T(8,128)S(1)}, f32[8,2,1,16,1408]{4,3,2,1,0:T(8,128)}, u32[]{:S(2)}) copy-start(f32[8,2,1,16,1408]{4,3,2,1,0:T(8,128)} %copy-done.7) | copy-start | bytes 4325380
  87.0 3.6 %copy-start.15 = (bf16[512,352]{1,0:T(8,128)(2,1)S(1)}, bf16[512,352]{1,0:T(8,128)(2,1)}, u32[]{:S(2)}) copy-start(bf16[512,352]{1,0:T(8,128)(2,1)} %get-tuple-element.29) | copy-start | bytes 1081348
  87.0 10.8 %collective-permute-start.7 = (bf16[8,16,1408]{2,1,0:T(8,128)(2,1)S(1)}, bf16[8,16,1408]{2,1,0:T(8,128)(2,1)S(1)}, u32[]{:S(2)}, u32[]{:S(2)}) collective-permute-start(bf16[8,16,1408]{2,1,0:T(8,128)(2,1)S(1)} %fusion.36), channel_id=1, source_target_pairs={{0,2},{1,3},{2,0},{3,1},{4,6},{5,7},{6,4},{7,5},{8,10},{9,11},{10,... | collective-permute-start | bytes 1081352 | tf_op jit(solution)/shard_map/ppermute | solution.py:92
  97.9 14.9 %collective-permute-start.8 = (bf16[2,2,1,16,1408]{4,3,1,0,2:T(8,128)(2,1)S(1)}, bf16[2,2,1,16,1408]{4,3,1,0,2:T(8,128)(2,1)S(1)}, u32[]{:S(2)}, u32[]{:S(2)}) collective-permute-start(bf16[2,2,1,16,1408]{4,3,1,0,2:T(8,128)(2,1)S(1)} %fusion.44), channel_id=1, source_target_pairs={{0,4},{4,0},{8,12},{12,8},{16,20},{20,16},{24,28},{28,24},{1,5},{5... | collective-permute-start | bytes 540680 | tf_op jit(solution)/shard_map/ppermute | solution.py:92
  107.3 52.4 %all-to-all-start.2 = ((bf16[8,2,3,44,352]{4,1,3,2,0:T(2,128)(2,1)}), bf16[8,2,3,44,352]{4,1,3,2,0:T(2,128)(2,1)S(1)}, u32[]{:S(2)}, u32[]{:S(2)}) async-start(bf16[8,2,3,44,352]{4,1,3,2,0:T(2,128)(2,1)} %copy.202), calls=%async_computation.2 | async-start | bytes 3244032 | tf_op jit(solution)/shard_map/all_to_all | solution.py:160
  112.9 45.2 %copy-start.10 = (bf16[2,64,1408]{2,1,0:T(8,128)(2,1)S(1)}, bf16[2,64,1408]{2,1,0:T(8,128)(2,1)}, u32[]{:S(2)}) copy-start(bf16[2,64,1408]{2,1,0:T(8,128)(2,1)} %param.9) | copy-start | bytes 1081348
  113.0 29.5 %collective-permute-start.9 = (bf16[2,2,16,1408]{3,2,0,1:T(8,128)(2,1)S(1)}, bf16[2,2,16,1408]{3,2,0,1:T(8,128)(2,1)S(1)}, u32[]{:S(2)}, u32[]{:S(2)}) collective-permute-start(bf16[2,2,16,1408]{3,2,0,1:T(8,128)(2,1)S(1)} %fusion.43), channel_id=1, source_target_pairs={{0,8},{4,12},{8,0},{12,4},{16,24},{20,28},{24,16},{28,20},{1,9},{5... | collective-permute-start | bytes 540680 | tf_op jit(solution)/shard_map/ppermute | solution.py:92
  115.0 43.5 %copy-start.16 = (bf16[2,64,1408]{2,1,0:T(8,128)(2,1)S(1)}, bf16[2,64,1408]{2,1,0:T(8,128)(2,1)}, u32[]{:S(2)}) copy-start(bf16[2,64,1408]{2,1,0:T(8,128)(2,1)} %param.17) | copy-start | bytes 1081348
  142.5 15.5 %collective-permute-start.10 = (bf16[4,16,1408]{2,1,0:T(8,128)(2,1)S(1)}, bf16[4,16,1408]{2,1,0:T(8,128)(2,1)S(1)}, u32[]{:S(2)}, u32[]{:S(2)}) collective-permute-start(bf16[4,16,1408]{2,1,0:T(8,128)(2,1)S(1)} %fusion.42), channel_id=1, source_target_pairs={{0,16},{4,20},{8,24},{12,28},{16,0},{20,4},{24,8},{28,12},{1,17},{... | collective-permute-start | bytes 540680 | tf_op jit(solution)/shard_map/ppermute | solution.py:92

commit v3 on v2

v3 whole, which is shorter than its diff:
```python
import functools
import math

import jax
import jax.numpy as jnp
from jax import lax
from jax.experimental import pallas as pl
from jax.experimental.pallas import tpu as pltpu
from jax.sharding import PartitionSpec as P

DH = 88
BF = jnp.bfloat16
F32 = jnp.float32
ROWS = (((0,), (0,)), ((), ()))
COLS = (((1,), (1,)), ((), ()))
ROOM = pltpu.CompilerParams(vmem_limit_bytes=48 * 1024 * 1024)


def attend_kernel(q_ref, k_ref, v_ref, d_ref, out_ref, *, columns, block):
    n_tok, width = q_ref.shape
    factor = 1.0 / math.sqrt(DH)
    source = lax.broadcasted_iota(jnp.int32, (n_tok, block), 0)
    target = lax.broadcasted_iota(jnp.int32, (n_tok, block), 1)
    same = ((source ^ target) & (columns - 1)) == 0
    for head in range(width // DH):
        lanes = slice(head * DH, (head + 1) * DH)
        k_head = k_ref[:, lanes]
        v_head = v_ref[:, lanes]
        key_sum = value_sum = None
        for start in range(0, n_tok, block):
            rows = slice(start, start + block)
            q_rows = q_ref[rows, lanes]
            d_rows = d_ref[rows, lanes]
            scores = lax.dot_general(k_head, q_rows, COLS, preferred_element_type=F32) * factor
            scores = jnp.where(same, scores, -jnp.inf)
            exponent = jnp.exp(scores - jnp.max(scores, axis=0, keepdims=True))
            probability = exponent * (1.0 / jnp.sum(exponent, axis=0, keepdims=True))
            prob_grad = lax.dot_general(v_head, d_rows, COLS, preferred_element_type=F32)
            row_dot = jnp.sum(probability * prob_grad, axis=0, keepdims=True)
            score_grad = (probability * (prob_grad - row_dot) * factor).astype(BF)
            prob_low = probability.astype(BF)
            query = lax.dot_general(score_grad, k_head, ROWS, preferred_element_type=F32)
            out_ref[0, rows, lanes] = query.astype(BF)
            key = jnp.dot(score_grad, q_rows, preferred_element_type=F32)
            value = jnp.dot(prob_low, d_rows, preferred_element_type=F32)
            key_sum = key if key_sum is None else key_sum + key
            value_sum = value if value_sum is None else value_sum + value
        out_ref[1, :, lanes] = key_sum.astype(BF)
        out_ref[2, :, lanes] = value_sum.astype(BF)
def attend(query,key,value,grad,columns,block=512):
    n_tok,width=query.shape
    return pl.pallas_call(functools.partial(attend_kernel,columns=columns,block=min(block,n_tok)),
        out_shape=jax.ShapeDtypeStruct((3,n_tok,width),BF),
        compiler_params=ROOM)(query,key,value,grad)

def first_kernel(
    x_ref, gain_ref, bias_ref, grad_ref, w_ref, out_ref, norm_ref, *, n_pair, columns, own_rows, t_dev
):
    step = pl.program_id(0)
    n_rows, width = x_ref.shape
    part = w_ref.shape[0]
    patches = n_rows // t_dev

    @pl.when(step == 0)
    def _():
        rows = x_ref[...].astype(F32)
        centered = rows - jnp.mean(rows, axis=-1, keepdims=True)
        variance = jnp.mean(centered * centered, axis=-1, keepdims=True)
        norm_ref[...] = centered * lax.rsqrt(variance + 1e-06) * gain_ref[...] + bias_ref[...]

    def pick(values, at):
        pieces = [values[t * patches + at : t * patches + at + columns] for t in range(t_dev)]
        return jnp.concatenate(pieces, axis=0).astype(BF)

    d_attn = lax.dot_general(grad_ref[...], w_ref[...], COLS, preferred_element_type=F32)
    for tm in range(2 * n_pair):
        out_ref[tm * 4 + step, 0] = pick(d_attn, tm * columns)
    for y in range(2):
        for c in range(2):

            @pl.when(step == 2 * y + c)
            def _(y=y, c=c):
                starts = [
                    (((2 * z + y) * 2 + x) * 2 + c) * own_rows for z in range(n_pair) for x in range(2)
                ]
                quarter = jnp.concatenate(
                    [norm_ref[:, start : start + own_rows] for start in starts], axis=1
                )
                for z in range(n_pair):
                    for x in range(2):
                        out_ref[((2 * z + y) * 2 + x) * 2 + c, 1] = pick(
                            quarter, (2 * z + (y ^ x)) * columns
                        )


def first_product(tokens, gain, bias, grads, w_out, n_pair, columns, own_rows, t_dev):
    n_rows, width = tokens.shape
    part = width // 4
    rows = pl.BlockSpec((n_rows, width), lambda j: (0, 0))
    line = pl.BlockSpec((1, width), lambda j: (0, 0))
    shape = (8 * n_pair, 2, t_dev * columns, part)
    return pl.pallas_call(
        functools.partial(
            first_kernel, n_pair=n_pair, columns=columns, own_rows=own_rows, t_dev=t_dev
        ),
        grid=(4,),
        in_specs=[rows, line, line, rows, pl.BlockSpec((part, width), lambda j: (j, 0))],
        out_specs=pl.BlockSpec(shape, lambda j: (0, 0, 0, 0)),
        out_shape=jax.ShapeDtypeStruct(shape, BF),
        scratch_shapes=[pltpu.VMEM((n_rows, width), F32)],
        compiler_params=ROOM,
    )(tokens, gain[None], bias[None], grads, w_out)


def share_kernel(where_ref, g_ref, w_ref, leave_ref, stay_ref, win_ref, pad_ref, sem, *, n_patch):
    kinds, n_tok, part = g_ref.shape
    window = win_ref.shape[2]
    width = win_ref.shape[1]
    patch = where_ref[0]
    core = patch % 2
    starts=[min(part * j // 128 * 128, width - window) for j in range(n_patch)]
    start = sum(jnp.where(patch == j, s, 0) for j, s in enumerate(starts))
    copies = [pltpu.make_async_copy(w_ref.at[:, pl.ds(pl.multiple_of(c * width + start, 128), window)], win_ref.at[c], sem.at[c]) for c in range(kinds)]
    for copy in copies:
        copy.start()
    for j in range(n_patch):
        @pl.when(patch == j)
        def _(j=j):
            before = part * j - starts[j]
            for c in range(kinds):
                pieces = [g_ref[c]]
                if before: pieces = [jnp.zeros((n_tok, before), BF)] + pieces
                after = window - before - part
                if after: pieces = pieces + [jnp.zeros((n_tok, after), BF)]
                pad_ref[c] = jnp.concatenate(pieces, axis=1).reshape(pad_ref.shape[1:])
    for copy in copies:
        copy.wait()
    shape = leave_ref.shape
    def product(which):
        total = None
        for c in range(kinds):
            one = lax.dot_general(pad_ref[c, :, which].reshape(n_tok // 2, window), win_ref[c], COLS, preferred_element_type=F32)
            total = one if total is None else total + one
        return total.reshape(shape)
    leave_ref[...] = product(1 - core).astype(BF)
    stay_ref[...] = product(core)
def share_send(grads, w_qkv, patch, n_patch, group):
    kinds,n_tok,part=grads.shape
    width=w_qkv.shape[0]
    window=-(-(part+96)//128)*128
    n=n_tok//(2*group)
    return pl.pallas_call(functools.partial(share_kernel,n_patch=n_patch),
        grid_spec=pltpu.PrefetchScalarGridSpec(num_scalar_prefetch=1,grid=(1,),
            in_specs=[pl.BlockSpec((kinds,n_tok,part),lambda i,s:(0,0,0)),pl.BlockSpec(memory_space=pl.ANY)],
            out_specs=[pl.BlockSpec((n,group,width),lambda i,s:(0,0,0))]*2,
            scratch_shapes=[pltpu.VMEM((kinds,width,window),BF),pltpu.VMEM((kinds,n,2,group,window),BF),pltpu.SemaphoreType.DMA((kinds,))]),
        out_shape=[jax.ShapeDtypeStruct((n,group,width),BF),jax.ShapeDtypeStruct((n,group,width),F32)],
        compiler_params=ROOM)(patch[None],grads,w_qkv)

def product_kernel(
    chip_ref, mine_ref, theirs_ref, own_ref, other_ref, own_core_ref, other_core_ref, out_ref, *, factor
):
    kinds, n_tok, part = own_ref.shape
    own_rows = out_ref.shape[1]
    mine = mine_ref[...].astype(F32).T.astype(BF)
    theirs = theirs_ref[...].astype(F32).T.astype(BF)
    first = chip_ref[0] == 0
    left = [jnp.where(first, mine, theirs), jnp.where(first, theirs, mine)]
    for r, pair in enumerate(((own_ref, other_ref), (own_core_ref, other_core_ref))):
        for c in range(kinds):
            total = jnp.dot(left[0], pair[0][c], preferred_element_type=F32)
            total += jnp.dot(left[1], pair[1][c], preferred_element_type=F32)
            total = total * factor
            at = (r * kinds + c) * part
            for k in range(out_ref.shape[0]):
                out_ref[k, :, at : at + part] = total[k * own_rows : (k + 1) * own_rows].astype(BF)


def product(chip, mine, theirs, grads, other, core, other_core, own_rows, factor):
    kinds, n_tok, part = grads.shape
    norm = pl.BlockSpec(mine.shape, lambda i, s: (0, 0))
    whole = pl.BlockSpec(grads.shape, lambda i, s: (0, 0, 0))
    shape = (part // own_rows, own_rows, 2 * kinds * part)
    return pl.pallas_call(
        functools.partial(product_kernel, factor=factor),
        grid_spec=pltpu.PrefetchScalarGridSpec(
            num_scalar_prefetch=1,
            grid=(1,),
            in_specs=[norm, norm, whole, whole, whole, whole],
            out_specs=pl.BlockSpec(shape, lambda i, s: (0, 0, 0)),
        ),
        out_shape=jax.ShapeDtypeStruct(shape, BF),
        compiler_params=ROOM,
    )(chip[None], mine, theirs, grads, other, core, other_core)


def final_kernel(core_ref, in_ref, out_ref, *, part, kinds):
    n_pair, n_chip, own_rows, _ = in_ref.shape
    for core in range(2):
        @pl.when(core_ref[0] == core)
        def _(core=core):
            for x in range(n_chip):
                total = in_ref[0, x].astype(F32)
                for z in range(1, n_pair):
                    total = total + in_ref[z, x].astype(F32)
                for r in range(2):
                    for c in range(kinds):
                        at = (c * n_chip * 2 + 2 * x + (r ^ core)) * part
                        src = (r * kinds + c) * part
                        out_ref[:, at : at + part] = total[:, src : src + part]
def final_sum(pieces, core, part, kinds):
    n_pair,n_chip,own_rows,_=pieces.shape
    return pl.pallas_call(functools.partial(final_kernel,part=part,kinds=kinds),
        grid_spec=pltpu.PrefetchScalarGridSpec(num_scalar_prefetch=1,grid=(1,),
            in_specs=[pl.BlockSpec(pieces.shape,lambda i,s:(0,0,0,0))],
            out_specs=pl.BlockSpec((own_rows,2*n_chip*kinds*part),lambda i,s:(0,0))),
        out_shape=jax.ShapeDtypeStruct((own_rows,2*n_chip*kinds*part),F32),compiler_params=ROOM)(core[None],pieces)


def per_device(tokens, ln_gain, ln_bias, w_qkv, w_out, q_time, k_time, v_time, grad_out):
    t_dev, patches, width = tokens.shape
    frames, columns, part = q_time.shape
    n_tm = lax.axis_size("tm")
    n_patch = lax.axis_size("patch")
    n_pair = n_tm // 2
    n_chip = n_patch // 2
    devices = n_tm * n_patch
    n_tok = frames * columns
    own_rows = width // devices
    tm = lax.axis_index("tm")
    patch = lax.axis_index("patch")
    side = tm % 2
    core = patch % 2
    both = ("tm", "patch")

    def swap(values, axis, size, bit):
        return lax.ppermute(values, axis, [(i, i ^ bit) for i in range(size)])

    grad_rows = grad_out.reshape(-1, width)
    token_rows = tokens.reshape(-1, width)
    sent = first_product(
        token_rows, ln_gain, ln_bias, grad_rows, w_out, n_pair, columns, own_rows, t_dev
    )
    got = lax.all_to_all(sent, both, 0, 0, tiled=True)

    saved = [values.reshape(n_tok, part) for values in (q_time, k_time, v_time)]
    saved_other = [swap(values, "tm", n_tm, 1) for values in saved]
    got, saved_other = lax.optimization_barrier((got, saved_other))
    d_time = got[:, 0].reshape(n_tok, part)
    mine = got[:, 1].reshape(n_tok, part)
    d_other = swap(d_time, "tm", n_tm, 1)
    theirs = swap(mine, "patch", n_patch, 2)
    d_other, theirs = lax.optimization_barrier((d_other, theirs))

    as_float = token_rows.astype(F32)
    centered = as_float - jnp.mean(as_float, axis=-1, keepdims=True)
    variance = jnp.mean(centered * centered, axis=-1, keepdims=True)
    inverse = lax.rsqrt(variance + 1e-06)
    normed = centered * inverse

    grads = attend(*saved, d_time, columns)
    grads_core = swap(grads, "patch", n_patch, 1)
    grads_other = attend(*saved_other, d_other, columns)
    leave, stay = share_send(grads, w_qkv, patch, n_patch, t_dev * columns)
    leave, stay, grads_other = lax.optimization_barrier((leave, stay, grads_other))
    grads_other_core = swap(grads_other, "patch", n_patch, 1)

    factor = 1.0 / math.sqrt(frames * patches)
    groups = [
        [(2 * z + y) * n_patch + 2 * x + c for z in range(n_pair) for x in range(n_chip)]
        for y in range(2)
        for c in range(2)
    ]
    pieces = lax.all_to_all(
        product(
            patch // 2, mine, theirs, grads, grads_other, grads_core, grads_other_core, own_rows, factor
        ),
        both,
        0,
        0,
        axis_index_groups=groups,
        tiled=True,
    )
    grad_w_qkv = final_sum(pieces.reshape(n_pair, n_chip, own_rows, 6 * part), core, part, 3)

    def split(values, axis, high):
        low_part = lax.index_in_dim(values, 0, axis, keepdims=False)
        high_part = lax.index_in_dim(values, 1, axis, keepdims=False)
        return jnp.where(high, high_part, low_part), jnp.where(high, low_part, high_part)

    share = stay + swap(leave, "patch", n_patch, 1).astype(F32)
    bits = n_patch.bit_length() - 1
    share = share.reshape((n_tm,) + (2,) * (bits - 1) + (t_dev * columns, width))
    for n in range(1, bits):
        stay, leave = split(share, bits - n, (patch & (1 << n)) != 0)
        share = stay + swap(leave.astype(BF), "patch", n_patch, 1 << n).astype(F32)
    bits = n_tm.bit_length() - 1
    share = share.astype(BF).reshape((2,) * bits + (1, t_dev * columns, width))
    for n in range(bits):
        high = (tm & (1 << n)) != 0
        stay, leave = split(share, bits - 1 - n, high)
        come = swap(leave, "tm", n_tm, 1 << n)
        share = jnp.concatenate([jnp.where(high, come, stay), jnp.where(high, stay, come)], bits - 1 - n)
    d_norm = share.reshape(n_tm, t_dev, columns, width).transpose(1, 0, 2, 3)
    d_norm = d_norm.reshape(-1, width).astype(F32)
    scaled = d_norm * ln_gain
    branch = inverse * (
        scaled
        - jnp.mean(scaled, axis=-1, keepdims=True)
        - normed * jnp.mean(scaled * normed, axis=-1, keepdims=True)
    )
    grad_x = (grad_rows.astype(F32) + branch).astype(BF).reshape(t_dev, patches, width)
    return (grad_x, grad_w_qkv)


def solution(mesh):
    return jax.shard_map(
        per_device,
        mesh=mesh,
        in_specs=(
            P(("tm", "patch"), None, None),
            P(),
            P(),
            P(),
            P(),
            P(None, "tm", "patch"),
            P(None, "tm", "patch"),
            P(None, "tm", "patch"),
            P(("tm", "patch"), None, None),
        ),
        out_specs=(P(("tm", "patch"), None, None), P(("tm", "patch"), None)),
        check_vma=False,
    )
```

time: 164 us -> 164 us (level)
  waiting for transfers between devices: 54.2 us -> 79.2 us
  matrix products: 12.5 us -> 0 us
  local copies, waits for them, and re-layouts: 31 us -> 20.8 us
  starting transfers between devices: 33.8 us -> 27.9 us
  Pallas kernels: 20.3 us -> 24.3 us
    ppermute x11 -> x12, waiting for transfers between devices: 54.2 us -> 79.2 us  [swap(): return lax.ppermute(values, axis, [(i, i ^ bit) for i in range(size)])]
    dot_general x8 -> x0, matrix products: 12.5 us -> none  [the longest x2 3.53 us: product(): total = jnp.einsum('na,cnf->caf', norm_own, one, preferred_element_type=F32)]
    unnamed x39 -> x44, local copies, waits for them, and re-layouts: 1.5 us -> 10.3 us
    all_to_all x3 -> x2, starting transfers between devices: 18.1 us -> 12.2 us  [the longest x1 7.42 us: per_device(): got = lax.all_to_all(sent, both, 0, 0, tiled=True)]
    dynamic_slice x1 -> x0, local copies, waits for them, and re-layouts: 5.82 us -> none  [per_device(): lax.dynamic_slice_in_dim(w_qkv, c * width + patch * part, part, 1)]
    transpose x3 -> x0, other arithmetic: 5.79 us -> none  [the longest x1 5.36 us: per_device(): sent.transpose(1, 4, 6, 0, 2, 3, 5, 7)]
    convert_element_type x2 -> x0, local copies, waits for them, and re-layouts: 5.12 us -> none  [the longest x1 4.9 us: per_device(): as_float = tokens.reshape(-1, width).astype(F32)]
    ppermute x0 -> x2, local copies, waits for them, and re-layouts: none -> 4.73 us  [swap(): return lax.ppermute(values, axis, [(i, i ^ bit) for i in range(size)])]
  transfers between devices with their start and end apart: 14 -> 14, of which waited for: 6 -> 7; matrix products, arithmetic and copies ran while one was open for 24% -> 8% of each run, Pallas kernels for 12% -> 8%
where the time goes in v3:
time: 164 us; the launch traced here: 163 us
  waiting for transfers between devices  79.2 us (48%)
  starting transfers between devices  27.9 us (17%)
  Pallas kernels  24.3 us (15%)
  local copies, waits for them, and re-layouts  20.8 us (13%)
  other arithmetic  10.1 us (6%)
    ppermute x12, waiting for transfers between devices, swap(): return lax.ppermute(values, axis, [(i, i ^ bit) for i in range(size)])  79.2 us
    ppermute x12, starting transfers between devices, swap(): return lax.ppermute(values, axis, [(i, i ^ bit) for i in range(size)])  15.7 us
    pallas_call x2, Pallas kernels, attend(): pl.pallas_call(functools.partial(attend_kernel, columns=columns, block=mi...  10.7 us
    unnamed x44, local copies, waits for them, and re-layouts  10.3 us
    all_to_all x1, starting transfers between devices, per_device(): got = lax.all_to_all(sent, both, 0, 0, tiled=True)  7.42 us
    pallas_call x1, Pallas kernels, share_send(): pl.pallas_call(functools.partial(share_kernel, n_patch=n_patch), grid_spe...  5.01 us
    all_to_all x1, starting transfers between devices, per_device(): lax.all_to_all(product(patch // 2, mine, theirs, grads, grads_other, grad...  4.76 us
    ppermute x2, local copies, waits for them, and re-layouts, swap(): return lax.ppermute(values, axis, [(i, i ^ bit) for i in range(size)])  4.73 us
  transfers between devices with their start and end apart: 14, of which 7 were waited for; matrix products, arithmetic and copies ran while one was open for 8% of the time, Pallas kernels for 8%

profile of v3, /device:TPU:0, one launch (start us, length us, event | category | flops | bytes accessed | tf_op | source)
XLA Modules:
  0.0 163.1 jit_solution(8915564027564088609)
XLA Ops:
  0.6 0.7 broadcast_in_dim.21.gain_ref
  1.3 0.7 broadcast_in_dim.22.bias_ref
  2.0 1.0 copy-done
  3.0 2.1 %copy-done.4 = bf16[1408,1408]{1,0:T(8,128)(2,1)S(1)} copy-done((bf16[1408,1408]{1,0:T(8,128)(2,1)S(1)}, bf16[1408,1408]{1,0:T(8,128)(2,1)}, u32[]{:S(2)}) %copy-start.4) | copy-done | bytes 3964952
  5.1 1.0 copy-done.6
  6.1 3.7 %shard_map.104 = bf16[32,2,16,352]{3,2,1,0:T(8,128)(2,1)} custom-call(bf16[128,1408]{1,0:T(8,128)(2,1)S(1)} %bitcast.137, f32[1,1408]{1,0:T(1,128)S(1)} %broadcast_in_dim.21.gain_ref, f32[1,1408]{1,0:T(1,128)S(1)} %broadcast_in_dim.22.bias_ref, bf16[128,1408]{1,0:T(8,128)(2,1)S(1)} %bitcast.143, bf16[1408,1408]{1,0:T(8,128)(2,1)S(1)} %copy-done.4), custom_call_target="tpu_custom_call" | custom-call | tf_op jit(solution)/shard_map/pallas_call | solution.py:102
  9.8 7.4 %all-to-all-start = ((bf16[32,2,16,352]{3,2,1,0:T(8,128)(2,1)}), bf16[32,2,16,352]{3,2,1,0:T(8,128)(2,1)}, u32[]{:S(2)}, u32[]{:S(2)}) async-start(bf16[32,2,16,352]{3,2,1,0:T(8,128)(2,1)} %shard_map.104), calls=%async_computation | async-start | bytes 1572864 | tf_op jit(solution)/shard_map/all_to_all | solution.py:244
  17.3 1.8 %collective-permute-start = (bf16[512,352]{1,0:T(8,128)(2,1)S(1)}, bf16[512,352]{1,0:T(8,128)(2,1)S(1)}, u32[]{:S(2)}, u32[]{:S(2)}) collective-permute-start(bf16[512,352]{1,0:T(8,128)(2,1)S(1)} %bitcast.144), channel_id=1, source_target_pairs={{0,4},{4,0},{8,12},{12,8},{16,20},{20,16},{24,28},{28,24},{1,5},{5... | collective-permute-start | bytes 1081352 | tf_op jit(solution)/shard_map/ppermute | solution.py:237
  19.0 0.3 collective-permute-start.1
  19.4 1.7 %collective-permute-start.2 = (bf16[512,352]{1,0:T(8,128)(2,1)S(1)}, bf16[512,352]{1,0:T(8,128)(2,1)S(1)}, u32[]{:S(2)}, u32[]{:S(2)}) collective-permute-start(bf16[512,352]{1,0:T(8,128)(2,1)S(1)} %bitcast.148), channel_id=1, source_target_pairs={{0,4},{4,0},{8,12},{12,8},{16,20},{20,16},{24,28},{28,24},{1,5},{5... | collective-permute-start | bytes 1081352 | tf_op jit(solution)/shard_map/ppermute | solution.py:237
  21.1 15.7 %collective-permute-done.q_ref = bf16[512,352]{1,0:T(8,128)(2,1)S(1)} collective-permute-done((bf16[512,352]{1,0:T(8,128)(2,1)S(1)}, bf16[512,352]{1,0:T(8,128)(2,1)S(1)}, u32[]{:S(2)}, u32[]{:S(2)}) %collective-permute-start) | collective-permute-done | bytes 360480 | tf_op jit(solution)/shard_map/ppermute | solution.py:237
  36.8 9.0 %collective-permute-done.1.k_ref = bf16[512,352]{1,0:T(8,128)(2,1)S(1)} collective-permute-done((bf16[512,352]{1,0:T(8,128)(2,1)S(1)}, bf16[512,352]{1,0:T(8,128)(2,1)S(1)}, u32[]{:S(2)}, u32[]{:S(2)}) %collective-permute-start.1) | collective-permute-done | bytes 360480 | tf_op jit(solution)/shard_map/ppermute | solution.py:237
  45.7 8.0 %collective-permute-done.2.v_ref = bf16[512,352]{1,0:T(8,128)(2,1)S(1)} collective-permute-done((bf16[512,352]{1,0:T(8,128)(2,1)S(1)}, bf16[512,352]{1,0:T(8,128)(2,1)S(1)}, u32[]{:S(2)}, u32[]{:S(2)}) %collective-permute-start.2) | collective-permute-done | bytes 360480 | tf_op jit(solution)/shard_map/ppermute | solution.py:237
  53.7 0.8 copy-done.17
  54.5 1.2 fusion.24
  55.7 0.7 collective-permute-start.3
  56.4 1.2 collective-permute-start.4
  57.6 1.0 copy-done.12
  58.6 4.8 %shard_map.105.g_ref.own_ref = bf16[3,512,352]{2,1,0:T(8,128)(2,1)S(1)} custom-call(bf16[512,352]{1,0:T(8,128)(2,1)S(1)} %bitcast.145, bf16[512,352]{1,0:T(8,128)(2,1)S(1)} %bitcast.147, bf16[512,352]{1,0:T(8,128)(2,1)S(1)} %bitcast.149, bf16[512,352]{1,0:T(8,128)(2,1)S(1)} %bitcast.142), custom_call_target="tpu_custom_call" | custom-call | tf_op jit(solution)/shard_map/pallas_call | solution.py:52
  63.4 5.0 %shard_map.106 = (bf16[16,16,1408]{2,1,0:T(8,128)(2,1)}, f32[16,16,1408]{2,1,0:T(8,128)S(1)}) custom-call(s32[1]{0:T(128)} %bitcast.where_ref, bf16[3,512,352]{2,1,0:T(8,128)(2,1)S(1)} %shard_map.105.g_ref.own_ref, bf16[1408,4224]{1,0:T(8,128)(2,1)} %w_ref.3), custom_call_target="tpu_custom_call" | custom-call | tf_op jit(solution)/shard_map/pallas_call | solution.py:152
  68.4 1.1 copy-done.5
  69.6 5.8 %shard_map.107.other_ref = bf16[3,512,352]{2,1,0:T(8,128)(2,1)S(1)} custom-call(bf16[512,352]{1,0:T(8,128)(2,1)S(1)} %copy-done.14, bf16[512,352]{1,0:T(8,128)(2,1)S(1)} %copy-done.16, bf16[512,352]{1,0:T(8,128)(2,1)S(1)} %copy-done.18, bf16[512,352]{1,0:T(8,128)(2,1)} %collective-permute-done.3.d_ref), custom_call_target="tpu_custom_call" | custom-call | tf_op jit(solution)/shard_map/pallas_call | solution.py:52
  75.5 2.5 %collective-permute-done.5 = bf16[16,16,1408]{2,1,0:T(8,128)(2,1)} collective-permute-done((bf16[16,16,1408]{2,1,0:T(8,128)(2,1)}, bf16[16,16,1408]{2,1,0:T(8,128)(2,1)}, u32[]{:S(2)}, u32[]{:S(2)}) %collective-permute-start.5) | collective-permute-done | bytes 720928 | tf_op jit(solution)/shard_map/ppermute | solution.py:237
  78.0 2.8 %convert_add_fusion = f32[16,16,1408]{2,1,0:T(8,128)} fusion(f32[16,16,1408]{2,1,0:T(8,128)} %copy-done.5, bf16[16,16,1408]{2,1,0:T(8,128)(2,1)} %collective-permute-done.5), kind=kLoop, calls=%fused_computation | loop fusion | flops 720896 | bytes 3604480 | tf_op jit(solution)/shard_map/add | solution.py:291
  80.8 2.1 %fusion.15 = bf16[8,16,1408]{2,1,0:T(8,128)(2,1)} fusion(f32[8,2,16,1408]{3,2,1,0:T(8,128)} %bitcast.8, pred[]{:T(512)S(6)} %ne.27), kind=kLoop, calls=%fused_computation.27 | loop fusion | flops 180224 | bytes 1081345 | tf_op jit(solution)/shard_map/convert_element_type | solution.py:296
  83.0 0.9 collective-permute-start.6
  83.9 1.5 copy.96
  85.3 1.4 copy.97
  86.7 0.5 collective-permute-start.11
  87.2 6.5 %collective-permute-done.6 = bf16[8,16,1408]{2,1,0:T(8,128)(2,1)} collective-permute-done((bf16[8,16,1408]{2,1,0:T(8,128)(2,1)}, bf16[8,16,1408]{2,1,0:T(8,128)(2,1)}, u32[]{:S(2)}, u32[]{:S(2)}) %collective-permute-start.6) | collective-permute-done | bytes 360480 | tf_op jit(solution)/shard_map/ppermute | solution.py:237
  93.8 1.5 fusion.13
  95.3 0.7 copy-done.19
  96.0 0.7 fusion.23
  96.7 1.7 %collective-permute-start.7 = (bf16[2,2,1,16,1408]{4,3,1,0,2:T(8,128)(2,1)}, bf16[2,2,1,16,1408]{4,3,1,0,2:T(8,128)(2,1)}, u32[]{:S(2)}, u32[]{:S(2)}) collective-permute-start(bf16[2,2,1,16,1408]{4,3,1,0,2:T(8,128)(2,1)} %fusion.23), channel_id=1, source_target_pairs={{0,4},{4,0},{8,12},{12,8},{16,20},{20,16},{24,28},{28,24},{1,5},{5... | collective-permute-start | bytes 540680 | tf_op jit(solution)/shard_map/ppermute | solution.py:237
  98.5 2.4 %copy.98.own_core_ref = bf16[3,512,352]{2,1,0:T(8,128)(2,1)} copy(bf16[3,512,352]{1,2,0:T(8,128)(2,1)} %collective-permute-done.10) | data formatting | bytes 2162688 | tf_op jit(solution)/shard_map/ppermute | solution.py:237
  100.9 2.3 %copy.99.other_core_ref = bf16[3,512,352]{2,1,0:T(8,128)(2,1)} copy(bf16[3,512,352]{1,2,0:T(8,128)(2,1)} %collective-permute-done.11) | data formatting | bytes 2162688 | tf_op jit(solution)/shard_map/ppermute | solution.py:237
  103.3 1.3 copy-done.2
  104.5 1.3 copy-done.3
  105.8 3.8 %shard_map.108 = bf16[8,44,2112]{2,1,0:T(8,128)(2,1)} custom-call(s32[1]{0:T(128)} %bitcast.34.chip_ref, bf16[512,352]{1,0:T(8,128)(2,1)S(1)} %bitcast.140, bf16[512,352]{1,0:T(8,128)(2,1)S(1)} %collective-permute-done.4.theirs_ref, bf16[3,512,352]{2,1,0:T(8,128)(2,1)S(1)} %shard_map.105.g_ref.own_ref, bf16[3,512,352]{2,1,0:T(8,128)(2,1)S(1)} %shard_map.107.other_ref, ...), custom_call_target="tpu_custom_call" | custom-call | tf_op jit(solution)/shard_map/pallas_call | solution.py:184
  109.6 4.8 %all-to-all-start.1 = ((bf16[8,44,2112]{2,1,0:T(8,128)(2,1)}), bf16[8,44,2112]{2,1,0:T(8,128)(2,1)S(1)}, u32[]{:S(2)}, u32[]{:S(2)}) async-start(bf16[8,44,2112]{2,1,0:T(8,128)(2,1)} %shard_map.108), calls=%async_computation.1 | async-start | bytes 3342336 | tf_op jit(solution)/shard_map/all_to_all | solution.py:274
  114.4 1.0 broadcast_select_fusion.1
  115.4 2.1 %collective-permute-start.8 = (bf16[2,2,16,1408]{3,2,0,1:T(8,128)(2,1)S(1)}, bf16[2,2,16,1408]{3,2,0,1:T(8,128)(2,1)S(1)}, u32[]{:S(2)}, u32[]{:S(2)}) collective-permute-start(bf16[2,2,16,1408]{3,2,0,1:T(8,128)(2,1)S(1)} %fusion.22), channel_id=1, source_target_pairs={{0,8},{4,12},{8,0},{12,4},{16,24},{20,28},{24,16},{28,20},{1,9},{5... | collective-permute-start | bytes 540680 | tf_op jit(solution)/shard_map/ppermute | solution.py:237
  117.8 26.7 %collective-permute-done.8 = bf16[2,2,16,1408]{3,2,0,1:T(8,128)(2,1)S(1)} collective-permute-done((bf16[2,2,16,1408]{3,2,0,1:T(8,128)(2,1)S(1)}, bf16[2,2,16,1408]{3,2,0,1:T(8,128)(2,1)S(1)}, u32[]{:S(2)}, u32[]{:S(2)}) %collective-permute-start.8) | collective-permute-done | bytes 180256 | tf_op jit(solution)/shard_map/ppermute | solution.py:237
  144.6 4.8 %collective-permute-start.9 = (bf16[4,16,1408]{2,1,0:T(8,128)(2,1)S(1)}, bf16[4,16,1408]{2,1,0:T(8,128)(2,1)S(1)}, u32[]{:S(2)}, u32[]{:S(2)}) collective-permute-start(bf16[4,16,1408]{2,1,0:T(8,128)(2,1)S(1)} %fusion.21), channel_id=1, source_target_pairs={{0,16},{4,20},{8,24},{12,28},{16,0},{20,4},{24,8},{28,12},{1,17},{... | collective-permute-start | bytes 540680 | tf_op jit(solution)/shard_map/ppermute | solution.py:237
  149.5 10.9 %collective-permute-done.9 = bf16[4,16,1408]{2,1,0:T(8,128)(2,1)S(1)} collective-permute-done((bf16[4,16,1408]{2,1,0:T(8,128)(2,1)S(1)}, bf16[4,16,1408]{2,1,0:T(8,128)(2,1)S(1)}, u32[]{:S(2)}, u32[]{:S(2)}) %collective-permute-start.9) | collective-permute-done | bytes 180256 | tf_op jit(solution)/shard_map/ppermute | solution.py:237
  160.4 0.3 fusion.10
  160.9 1.1 fusion.7
  162.0 1.1 shard_map.109
  (59 shorter events, 1.1 us)
Async XLA Ops:
  2.0 1.0 copy-start
  3.0 2.1 %copy-start.4 = (bf16[1408,1408]{1,0:T(8,128)(2,1)S(1)}, bf16[1408,1408]{1,0:T(8,128)(2,1)}, u32[]{:S(2)}) copy-start(bf16[1408,1408]{1,0:T(8,128)(2,1)} %w_ref.2) | copy-start | bytes 11894788
  5.1 1.0 copy-start.6
  9.8 7.4 %copy-start.8 = (bf16[64,8,352]{2,1,0:T(8,128)(2,1)S(1)}, bf16[64,8,352]{2,1,0:T(8,128)(2,1)}, u32[]{:S(2)}) copy-start(bf16[64,8,352]{2,1,0:T(8,128)(2,1)} %param.14) | copy-start | bytes 1081348
  9.8 9.2 %copy-start.10 = (bf16[64,8,352]{2,1,0:T(8,128)(2,1)S(1)}, bf16[64,8,352]{2,1,0:T(8,128)(2,1)}, u32[]{:S(2)}) copy-start(bf16[64,8,352]{2,1,0:T(8,128)(2,1)} %param.15) | copy-start | bytes 1081348
  9.8 9.5 %copy-start.11 = (bf16[64,8,352]{2,1,0:T(8,128)(2,1)S(1)}, bf16[64,8,352]{2,1,0:T(8,128)(2,1)}, u32[]{:S(2)}) copy-start(bf16[64,8,352]{2,1,0:T(8,128)(2,1)} %param.16) | copy-start | bytes 1081348
  9.8 47.7 %copy-start.9 = (bf16[64,8,352]{2,1,0:T(8,128)(2,1)S(1)}, bf16[64,8,352]{2,1,0:T(8,128)(2,1)}, u32[]{:S(2)}) copy-start(bf16[64,8,352]{2,1,0:T(8,128)(2,1)} %param.14) | copy-start | bytes 1081348
  9.8 44.6 %all-to-all-start = ((bf16[32,2,16,352]{3,2,1,0:T(8,128)(2,1)}), bf16[32,2,16,352]{3,2,1,0:T(8,128)(2,1)}, u32[]{:S(2)}, u32[]{:S(2)}) async-start(bf16[32,2,16,352]{3,2,1,0:T(8,128)(2,1)} %shard_map.104), calls=%async_computation | async-start | bytes 1572864 | tf_op jit(solution)/shard_map/all_to_all | solution.py:244
  17.3 19.5 %collective-permute-start = (bf16[512,352]{1,0:T(8,128)(2,1)S(1)}, bf16[512,352]{1,0:T(8,128)(2,1)S(1)}, u32[]{:S(2)}, u32[]{:S(2)}) collective-permute-start(bf16[512,352]{1,0:T(8,128)(2,1)S(1)} %bitcast.144), channel_id=1, source_target_pairs={{0,4},{4,0},{8,12},{12,8},{16,20},{20,16},{24,28},{28,24},{1,5},{5... | collective-permute-start | bytes 1081352 | tf_op jit(solution)/shard_map/ppermute | solution.py:237
  19.0 26.7 %collective-permute-start.1 = (bf16[512,352]{1,0:T(8,128)(2,1)S(1)}, bf16[512,352]{1,0:T(8,128)(2,1)S(1)}, u32[]{:S(2)}, u32[]{:S(2)}) collective-permute-start(bf16[512,352]{1,0:T(8,128)(2,1)S(1)} %bitcast.146), channel_id=1, source_target_pairs={{0,4},{4,0},{8,12},{12,8},{16,20},{20,16},{24,28},{28,24},{1,5},{5... | collective-permute-start | bytes 1081352 | tf_op jit(solution)/shard_map/ppermute | solution.py:237
  19.4 34.3 %collective-permute-start.2 = (bf16[512,352]{1,0:T(8,128)(2,1)S(1)}, bf16[512,352]{1,0:T(8,128)(2,1)S(1)}, u32[]{:S(2)}, u32[]{:S(2)}) collective-permute-start(bf16[512,352]{1,0:T(8,128)(2,1)S(1)} %bitcast.148), channel_id=1, source_target_pairs={{0,4},{4,0},{8,12},{12,8},{16,20},{20,16},{24,28},{28,24},{1,5},{5... | collective-permute-start | bytes 1081352 | tf_op jit(solution)/shard_map/ppermute | solution.py:237
  36.8 20.8 %copy-start.13 = (bf16[512,352]{1,0:T(8,128)(2,1)}, bf16[512,352]{1,0:T(8,128)(2,1)S(1)}, u32[]{:S(2)}) copy-start(bf16[512,352]{1,0:T(8,128)(2,1)S(1)} %collective-permute-done.q_ref) | copy-start | bytes 1081348
  45.7 11.8 %copy-start.15 = (bf16[512,352]{1,0:T(8,128)(2,1)}, bf16[512,352]{1,0:T(8,128)(2,1)S(1)}, u32[]{:S(2)}) copy-start(bf16[512,352]{1,0:T(8,128)(2,1)S(1)} %collective-permute-done.1.k_ref) | copy-start | bytes 1081348
  53.7 0.8 copy-start.17
  55.7 13.9 %collective-permute-start.3 = (bf16[512,352]{1,0:T(8,128)(2,1)S(1)}, bf16[512,352]{1,0:T(8,128)(2,1)}, u32[]{:S(2)}, u32[]{:S(2)}) collective-permute-start(bf16[512,352]{1,0:T(8,128)(2,1)S(1)} %bitcast.141), channel_id=1, source_target_pairs={{0,4},{4,0},{8,12},{12,8},{16,20},{20,16},{24,28},{28,24},{1,5},{5... | collective-permute-start | bytes 1081352 | tf_op jit(solution)/shard_map/ppermute | solution.py:237
  56.4 13.2 %collective-permute-start.4 = (bf16[512,352]{1,0:T(8,128)(2,1)S(1)}, bf16[512,352]{1,0:T(8,128)(2,1)S(1)}, u32[]{:S(2)}, u32[]{:S(2)}) collective-permute-start(bf16[512,352]{1,0:T(8,128)(2,1)S(1)} %bitcast.139), channel_id=1, source_target_pairs={{0,2},{1,3},{2,0},{3,1},{4,6},{5,7},{6,4},{7,5},{8,10},{9,11},{10,... | collective-permute-start | bytes 1081352 | tf_op jit(solution)/shard_map/ppermute | solution.py:237
  57.6 1.0 copy-start.12
  63.4 6.2 %copy-start.14 = (bf16[512,352]{1,0:T(8,128)(2,1)S(1)}, bf16[512,352]{1,0:T(8,128)(2,1)}, u32[]{:S(2)}) copy-start(bf16[512,352]{1,0:T(8,128)(2,1)} %copy-done.13) | copy-start | bytes 1081348
  63.4 6.2 %copy-start.16 = (bf16[512,352]{1,0:T(8,128)(2,1)S(1)}, bf16[512,352]{1,0:T(8,128)(2,1)}, u32[]{:S(2)}) copy-start(bf16[512,352]{1,0:T(8,128)(2,1)} %copy-done.15) | copy-start | bytes 1081348
  63.4 6.2 %copy-start.18 = (bf16[512,352]{1,0:T(8,128)(2,1)S(1)}, bf16[512,352]{1,0:T(8,128)(2,1)}, u32[]{:S(2)}) copy-start(bf16[512,352]{1,0:T(8,128)(2,1)} %copy-done.17) | copy-start | bytes 1081348
  68.4 1.1 copy-start.5
  75.4 2.6 %collective-permute-start.5 = (bf16[16,16,1408]{2,1,0:T(8,128)(2,1)}, bf16[16,16,1408]{2,1,0:T(8,128)(2,1)}, u32[]{:S(2)}, u32[]{:S(2)}) collective-permute-start(bf16[16,16,1408]{2,1,0:T(8,128)(2,1)} %get-tuple-element.21), channel_id=1, source_target_pairs={{0,1},{1,0},{2,3},{3,2},{4,5},{5,4},{6,7},{7,6},{8,9},{9,8},{10,11... | collective-permute-start | bytes 2162696 | tf_op jit(solution)/shard_map/ppermute | solution.py:237
  83.0 10.8 %collective-permute-start.6 = (bf16[8,16,1408]{2,1,0:T(8,128)(2,1)}, bf16[8,16,1408]{2,1,0:T(8,128)(2,1)}, u32[]{:S(2)}, u32[]{:S(2)}) collective-permute-start(bf16[8,16,1408]{2,1,0:T(8,128)(2,1)} %fusion.15), channel_id=1, source_target_pairs={{0,2},{1,3},{2,0},{3,1},{4,6},{5,7},{6,4},{7,5},{8,10},{9,11},{10,... | collective-permute-start | bytes 1081352 | tf_op jit(solution)/shard_map/ppermute | solution.py:237
  85.3 13.2 %collective-permute-start.10 = (bf16[3,512,352]{1,2,0:T(8,128)(2,1)}, bf16[3,512,352]{1,2,0:T(8,128)(2,1)}, u32[]{:S(2)}, u32[]{:S(2)}) collective-permute-start(bf16[3,512,352]{1,2,0:T(8,128)(2,1)} %copy.96), channel_id=1, source_target_pairs={{0,1},{1,0},{2,3},{3,2},{4,5},{5,4},{6,7},{7,6},{8,9},{9,8},{10,11... | collective-permute-start | bytes 3244040 | tf_op jit(solution)/shard_map/ppermute | solution.py:237
  86.7 11.7 %copy-start.1 = (bf16[2,64,1408]{2,1,0:T(8,128)(2,1)S(1)}, bf16[2,64,1408]{2,1,0:T(8,128)(2,1)}, u32[]{:S(2)}) copy-start(bf16[2,64,1408]{2,1,0:T(8,128)(2,1)} %param.9) | copy-start | bytes 1081348
  86.7 14.2 %collective-permute-start.11 = (bf16[3,512,352]{1,2,0:T(8,128)(2,1)}, bf16[3,512,352]{1,2,0:T(8,128)(2,1)}, u32[]{:S(2)}, u32[]{:S(2)}) collective-permute-start(bf16[3,512,352]{1,2,0:T(8,128)(2,1)} %copy.97), channel_id=1, source_target_pairs={{0,1},{1,0},{2,3},{3,2},{4,5},{5,4},{6,7},{7,6},{8,9},{9,8},{10,11... | collective-permute-start | bytes 3244040 | tf_op jit(solution)/shard_map/ppermute | solution.py:237
  95.3 0.7 copy-start.19
  96.7 17.6 %collective-permute-start.7 = (bf16[2,2,1,16,1408]{4,3,1,0,2:T(8,128)(2,1)}, bf16[2,2,1,16,1408]{4,3,1,0,2:T(8,128)(2,1)}, u32[]{:S(2)}, u32[]{:S(2)}) collective-permute-start(bf16[2,2,1,16,1408]{4,3,1,0,2:T(8,128)(2,1)} %fusion.23), channel_id=1, source_target_pairs={{0,4},{4,0},{8,12},{12,8},{16,20},{20,16},{24,28},{28,24},{1,5},{5... | collective-permute-start | bytes 540680 | tf_op jit(solution)/shard_map/ppermute | solution.py:237
  103.3 1.3 copy-start.2
  104.5 1.3 copy-start.3
  109.6 4.8 %copy-start.20 = (bf16[8,16,1408]{2,1,0:T(8,128)(2,1)S(1)}, bf16[8,16,1408]{2,1,0:T(8,128)(2,1)}, u32[]{:S(2)}) copy-start(bf16[8,16,1408]{2,1,0:T(8,128)(2,1)} %copy-done.19) | copy-start | bytes 1081348
  109.6 52.4 %all-to-all-start.1 = ((bf16[8,44,2112]{2,1,0:T(8,128)(2,1)}), bf16[8,44,2112]{2,1,0:T(8,128)(2,1)S(1)}, u32[]{:S(2)}, u32[]{:S(2)}) async-start(bf16[8,44,2112]{2,1,0:T(8,128)(2,1)} %shard_map.108), calls=%async_computation.1 | async-start | bytes 3342336 | tf_op jit(solution)/shard_map/all_to_all | solution.py:274
  115.4 45.1 %copy-start.21 = (f32[1408]{0:T(1024)S(1)}, f32[1408]{0:T(1024)}, u32[]{:S(2)}) copy-start(f32[1408]{0:T(1024)} %param.10) | copy-start | bytes 16900
  115.4 29.1 %collective-permute-start.8 = (bf16[2,2,16,1408]{3,2,0,1:T(8,128)(2,1)S(1)}, bf16[2,2,16,1408]{3,2,0,1:T(8,128)(2,1)S(1)}, u32[]{:S(2)}, u32[]{:S(2)}) collective-permute-start(bf16[2,2,16,1408]{3,2,0,1:T(8,128)(2,1)S(1)} %fusion.22), channel_id=1, source_target_pairs={{0,8},{4,12},{8,0},{12,4},{16,24},{20,28},{24,16},{28,20},{1,9},{5... | collective-permute-start | bytes 540680 | tf_op jit(solution)/shard_map/ppermute | solution.py:237
  117.8 43.1 %copy-start.7 = (bf16[2,64,1408]{2,1,0:T(8,128)(2,1)S(1)}, bf16[2,64,1408]{2,1,0:T(8,128)(2,1)}, u32[]{:S(2)}) copy-start(bf16[2,64,1408]{2,1,0:T(8,128)(2,1)} %param.17) | copy-start | bytes 1081348
  144.6 15.8 %collective-permute-start.9 = (bf16[4,16,1408]{2,1,0:T(8,128)(2,1)S(1)}, bf16[4,16,1408]{2,1,0:T(8,128)(2,1)S(1)}, u32[]{:S(2)}, u32[]{:S(2)}) collective-permute-start(bf16[4,16,1408]{2,1,0:T(8,128)(2,1)S(1)} %fusion.21), channel_id=1, source_target_pairs={{0,16},{4,20},{8,24},{12,28},{16,0},{20,4},{24,8},{28,12},{1,17},{... | collective-permute-start | bytes 540680 | tf_op jit(solution)/shard_map/ppermute | solution.py:237

commit v4 on v1

v4 whole, which is shorter than its diff:
```python
import functools
import math

import jax
import jax.numpy as jnp
from jax import lax
from jax.experimental import pallas as pl
from jax.experimental.pallas import tpu as pltpu
from jax.sharding import PartitionSpec as P

DH = 88
BF = jnp.bfloat16
F32 = jnp.float32
ROWS = (((0,), (0,)), ((), ()))
COLS = (((1,), (1,)), ((), ()))
CROSS = (((0,), (1,)), ((), ()))
ROOM = pltpu.CompilerParams(vmem_limit_bytes=48 * 1024 * 1024)


def attend_kernel(q_ref, k_ref, v_ref, d_ref, out_ref, *, columns):
    n_tok, width = q_ref.shape
    factor = 1.0 / math.sqrt(DH)
    source = lax.broadcasted_iota(jnp.int32, (n_tok, n_tok), 0)
    target = lax.broadcasted_iota(jnp.int32, (n_tok, n_tok), 1)
    same = ((source ^ target) & (columns - 1)) == 0
    for start in range(0, width, DH):
        lanes = slice(start, start + DH)
        query, key, value, grad = [ref[:, lanes] for ref in (q_ref, k_ref, v_ref, d_ref)]
        scores = lax.dot_general(key, query, COLS, preferred_element_type=F32) * factor
        scores = jnp.where(same, scores, -jnp.inf)
        exponent = jnp.exp(scores - jnp.max(scores, axis=0, keepdims=True))
        probability = exponent * (1.0 / jnp.sum(exponent, axis=0, keepdims=True))
        prob_grad = lax.dot_general(value, grad, COLS, preferred_element_type=F32)
        row_dot = jnp.sum(probability * prob_grad, axis=0, keepdims=True)
        score_grad = (probability * (prob_grad - row_dot) * factor).astype(BF)
        prob_low = probability.astype(BF)
        for kind, (left, right, dims) in enumerate(
            ((key, score_grad, ROWS), (query, score_grad, CROSS), (grad, prob_low, CROSS))
        ):
            total = lax.dot_general(left, right, dims, preferred_element_type=F32)
            out_ref[kind, lanes, :] = total.astype(BF)


def attend(query, key, value, grad, columns):
    n_tok, width = query.shape
    return pl.pallas_call(
        functools.partial(attend_kernel, columns=columns),
        out_shape=jax.ShapeDtypeStruct((3, width, n_tok), BF),
        compiler_params=ROOM,
    )(query, key, value, grad)


def norm_kernel(x_ref, gain_ref, bias_ref, out_ref, *, n_pair, n_chip, columns, own_rows, t_dev):
    width = x_ref.shape[1]
    rows = x_ref[...].astype(F32)
    centered = rows - jnp.mean(rows, axis=-1, keepdims=True)
    variance = jnp.mean(centered * centered, axis=-1, keepdims=True)
    norm = centered * lax.rsqrt(variance + 1e-06) * gain_ref[...] + bias_ref[...]
    patches = x_ref.shape[0] // t_dev
    for y in range(2):
        for c in range(2):
            starts = [((2 * z + y) * n_chip + x) * 2 * own_rows + c * own_rows for z in range(n_pair) for x in range(n_chip)]
            part = jnp.concatenate([norm[:, s : s + own_rows] for s in starts], axis=1)
            for z in range(n_pair):
                for slot in range(2):
                    at = (2 * z + (y ^ slot)) * columns
                    piece = jnp.concatenate([part[t * patches + at : t * patches + at + columns] for t in range(t_dev)], axis=0).astype(BF)
                    for x in range(n_chip):
                        out_ref[((2 * z + y) * n_chip + x) * 2 + c, slot] = piece
def norm_send(tokens, gain, bias, n_pair, n_chip, columns, own_rows, t_dev):
    devices = 4 * n_pair * n_chip
    return pl.pallas_call(functools.partial(norm_kernel,n_pair=n_pair,n_chip=n_chip,columns=columns,own_rows=own_rows,t_dev=t_dev),
        out_shape=jax.ShapeDtypeStruct((devices,2,t_dev*columns,tokens.shape[1]//4),BF),compiler_params=ROOM)(tokens,gain[None],bias[None])

def share_kernel(where_ref, g_ref, w_ref, leave_ref, stay_ref, win_ref, pad_ref, acc_ref, sem, *, n_patch):
    kinds, part, n_tok = g_ref.shape
    _, width, window = win_ref.shape
    patch = where_ref[0]
    starts = [min(part * j // 128 * 128, width - window) for j in range(n_patch)]
    start = sum(jnp.where(patch == j, at, 0) for j, at in enumerate(starts))
    copies = [
        pltpu.make_async_copy(
            w_ref.at[:, pl.ds(pl.multiple_of(c * width + start, 128), window)], win_ref.at[c], sem.at[c]
        )
        for c in range(kinds)
    ]
    for copy in copies:
        copy.start()
    pad_ref[...] = jnp.zeros_like(pad_ref)
    for j in range(n_patch):

        @pl.when(patch == j)
        def _(j=j):
            before = part * j - starts[j]
            for c in range(kinds):
                pad_ref[c, before : before + part, :] = g_ref[c]

    total = None
    for c, copy in enumerate(copies):
        copy.wait()
        one = lax.dot_general(pad_ref[c], win_ref[c], CROSS, preferred_element_type=F32)
        total = one if total is None else total + one
    acc_ref[...] = total.reshape(acc_ref.shape)
    leave_ref[...] = acc_ref[:, 1 - patch % 2].astype(BF)
    stay_ref[...] = acc_ref[:, patch % 2]


def share_send(grads, w_qkv, patch, n_patch, group):
    kinds, part, n_tok = grads.shape
    width = w_qkv.shape[0]
    window = -(-(part + 96) // 128) * 128
    n = n_tok // (2 * group)
    return pl.pallas_call(
        functools.partial(share_kernel, n_patch=n_patch),
        grid_spec=pltpu.PrefetchScalarGridSpec(
            num_scalar_prefetch=1,
            grid=(1,),
            in_specs=[
                pl.BlockSpec((kinds, part, n_tok), lambda i, s: (0, 0, 0)),
                pl.BlockSpec(memory_space=pl.ANY),
            ],
            out_specs=[pl.BlockSpec((n, group, width), lambda i, s: (0, 0, 0))] * 2,
            scratch_shapes=[
                pltpu.VMEM((kinds, width, window), BF),
                pltpu.VMEM((kinds, window, n_tok), BF),
                pltpu.VMEM((n, 2, group, width), F32),
                pltpu.SemaphoreType.DMA((kinds,)),
            ],
        ),
        out_shape=[
            jax.ShapeDtypeStruct((n, group, width), BF),
            jax.ShapeDtypeStruct((n, group, width), F32),
        ],
        compiler_params=ROOM,
    )(patch[None], grads, w_qkv)


def merge_kernel(chip_ref, stay_ref, come_ref, leave_ref, keep_ref):
    chip = chip_ref[0]
    leave_ref[...] = (stay_ref[:, 1 - chip] + come_ref[:, 1 - chip].astype(F32)).astype(BF)
    keep_ref[...] = stay_ref[:, chip] + come_ref[:, chip].astype(F32)


def merge(stay, come, chip):
    n, group, width = stay.shape
    both = pl.BlockSpec((n // 2, 2, group, width), lambda i, s: (0, 0, 0, 0))
    half = pl.BlockSpec((n // 2, group, width), lambda i, s: (0, 0, 0))
    return pl.pallas_call(
        merge_kernel,
        grid_spec=pltpu.PrefetchScalarGridSpec(
            num_scalar_prefetch=1, grid=(1,), in_specs=[both, both], out_specs=[half, half]
        ),
        out_shape=[
            jax.ShapeDtypeStruct((n // 2, group, width), BF),
            jax.ShapeDtypeStruct((n // 2, group, width), F32),
        ],
        compiler_params=ROOM,
    )(chip[None], stay.reshape(n // 2, 2, group, width), come.reshape(n // 2, 2, group, width))


def add_kernel(stay_ref, come_ref, out_ref):
    out_ref[...] = (stay_ref[...] + come_ref[...].astype(F32)).astype(BF)


def product_kernel(a_ref, own_ref, other_ref, own_core_ref, other_core_ref, out_ref, *, factor):
    n, _, group, quarter = a_ref.shape
    kinds, part, n_tok = own_ref.shape
    own_rows = out_ref.shape[1]
    left = [a_ref[:, slot].reshape(n_tok, quarter).astype(F32).T.astype(BF) for slot in range(2)]
    for r, pair in enumerate(((own_ref, other_ref), (own_core_ref, other_core_ref))):
        for c in range(kinds):
            total = lax.dot_general(left[0], pair[0][c], COLS, preferred_element_type=F32)
            total += lax.dot_general(left[1], pair[1][c], COLS, preferred_element_type=F32)
            total = total * factor
            at = (r * kinds + c) * part
            for k in range(out_ref.shape[0]):
                out_ref[k, :, at : at + part] = total[k * own_rows : (k + 1) * own_rows].astype(BF)
def product(got, grads, other, core, other_core, own_rows, factor):
    kinds, part, n_tok = grads.shape
    quarter = got.shape[-1]
    return pl.pallas_call(functools.partial(product_kernel,factor=factor),
        out_shape=jax.ShapeDtypeStruct((quarter//own_rows,own_rows,2*kinds*part),BF),compiler_params=ROOM)(got,grads,other,core,other_core)

def final_kernel(core_ref, in_ref, out_ref, *, part, kinds):
    n_pair, n_chip, own_rows, _ = in_ref.shape
    for core in range(2):
        @pl.when(core_ref[0] == core)
        def _(core=core):
            for x in range(n_chip):
                total = in_ref[0, x].astype(F32)
                for z in range(1, n_pair):
                    total = total + in_ref[z, x].astype(F32)
                for r in range(2):
                    for c in range(kinds):
                        at = (c * n_chip * 2 + 2 * x + (r ^ core)) * part
                        src = (r * kinds + c) * part
                        out_ref[:, at : at + part] = total[:, src : src + part]
def final_sum(pieces, core, part, kinds):
    n_pair,n_chip,own_rows,_=pieces.shape
    return pl.pallas_call(functools.partial(final_kernel,part=part,kinds=kinds),
        grid_spec=pltpu.PrefetchScalarGridSpec(num_scalar_prefetch=1,grid=(1,),
            in_specs=[pl.BlockSpec(pieces.shape,lambda i,s:(0,0,0,0))],
            out_specs=pl.BlockSpec((own_rows,2*n_chip*kinds*part),lambda i,s:(0,0))),
        out_shape=jax.ShapeDtypeStruct((own_rows,2*n_chip*kinds*part),F32),compiler_params=ROOM)(core[None],pieces)


def per_device(tokens, ln_gain, ln_bias, w_qkv, w_out, q_time, k_time, v_time, grad_out):
    t_dev, patches, width = tokens.shape
    frames, columns, part = q_time.shape
    n_tm = lax.axis_size("tm")
    n_patch = lax.axis_size("patch")
    n_pair = n_tm // 2
    n_chip = n_patch // 2
    devices = n_tm * n_patch
    n_tok = frames * columns
    own_rows = width // devices
    tm = lax.axis_index("tm")
    patch = lax.axis_index("patch")
    core = patch % 2
    both = ("tm", "patch")

    def swap(values, axis, size, bit):
        return lax.ppermute(values, axis, [(i, i ^ bit) for i in range(size)])

    grad_rows = grad_out.reshape(-1, width)
    d_attn = jnp.einsum(
        "to,jfo->jtf", grad_rows, w_out.reshape(n_patch, part, width), preferred_element_type=F32
    ).astype(BF)
    d_attn = d_attn.reshape(n_patch, t_dev, n_tm, columns, part).transpose(2, 0, 1, 3, 4)
    d_attn, tokens = lax.optimization_barrier((d_attn, tokens))
    d_time = lax.all_to_all(
        d_attn.reshape(devices, t_dev, columns, part), both, 0, 0, tiled=True
    ).reshape(n_tok, part)

    as_float = tokens.reshape(-1, width).astype(F32)
    centered = as_float - jnp.mean(as_float, axis=-1, keepdims=True)
    variance = jnp.mean(centered * centered, axis=-1, keepdims=True)
    inverse = lax.rsqrt(variance + 1e-06)
    normed = centered * inverse

    quarter = width // 4
    sent = norm_send(tokens.reshape(-1, width), ln_gain, ln_bias, n_pair, n_chip, columns, own_rows, t_dev)
    d_time, sent = lax.optimization_barrier((d_time, sent))
    got = lax.all_to_all(sent, both, 0, 0, tiled=True)

    saved = [values.reshape(n_tok, part) for values in (q_time, k_time, v_time)]
    grads = attend(*saved, d_time, columns)
    grads_other = swap(grads, "tm", n_tm, 1)
    leave, stay = share_send(grads, w_qkv, patch, n_patch, t_dev * columns)
    leave, stay = merge(stay, swap(leave, "patch", n_patch, 1), patch // 2)
    share = pl.pallas_call(
        add_kernel, out_shape=jax.ShapeDtypeStruct(leave.shape, BF), compiler_params=ROOM
    )(stay, swap(leave, "patch", n_patch, 2))
    grads_other, share = lax.optimization_barrier((grads_other, share))
    grads_core = swap(grads, "patch", n_patch, 1)
    grads_other_core = swap(grads_other, "patch", n_patch, 1)

    factor = 1.0 / math.sqrt(frames * patches)
    groups = [
        [(2 * z + y) * n_patch + 2 * x + c for z in range(n_pair) for x in range(n_chip)]
        for y in range(2)
        for c in range(2)
    ]
    pieces = lax.all_to_all(
        product(got, grads, grads_other, grads_core, grads_other_core, own_rows, factor),
        both,
        0,
        0,
        axis_index_groups=groups,
        tiled=True,
    )
    grad_w_qkv = final_sum(pieces.reshape(n_pair, n_chip, own_rows, 6 * part), core, part, 3)

    bits = n_tm.bit_length() - 1
    share = share.reshape((2,) * bits + (1, t_dev * columns, width))
    for n in range(bits):
        high = (tm & (1 << n)) != 0
        at = bits - 1 - n
        low_part, high_part = [lax.index_in_dim(share, i, at, keepdims=False) for i in range(2)]
        stay = jnp.where(high, high_part, low_part)
        come = swap(jnp.where(high, low_part, high_part), "tm", n_tm, 1 << n)
        share = jnp.concatenate([jnp.where(high, come, stay), jnp.where(high, stay, come)], at)
    d_norm = share
    d_norm = d_norm.reshape(n_tm, t_dev, columns, width).transpose(1, 0, 2, 3)
    d_norm = d_norm.reshape(-1, width).astype(F32)
    scaled = d_norm * ln_gain
    branch = inverse * (
        scaled
        - jnp.mean(scaled, axis=-1, keepdims=True)
        - normed * jnp.mean(scaled * normed, axis=-1, keepdims=True)
    )
    grad_x = (grad_rows.astype(F32) + branch).astype(BF).reshape(t_dev, patches, width)
    return (grad_x, grad_w_qkv)


def solution(mesh):
    return jax.shard_map(
        per_device,
        mesh=mesh,
        in_specs=(
            P(("tm", "patch"), None, None),
            P(),
            P(),
            P(),
            P(),
            P(None, "tm", "patch"),
            P(None, "tm", "patch"),
            P(None, "tm", "patch"),
            P(("tm", "patch"), None, None),
        ),
        out_specs=(P(("tm", "patch"), None, None), P(("tm", "patch"), None)),
        check_vma=False,
    )
```

time: 142 us -> 138 us (0.972)
  the two profiles are of different devices: /device:TPU:11 before, /device:TPU:0 now
where the time goes in v4:
time: 138 us
  waiting for transfers between devices  85.6 us (62%)
  Pallas kernels  21.5 us (16%)
  starting transfers between devices  20.6 us (15%)
  local copies, waits for them, and re-layouts  4 us (3%)
  matrix products  3.37 us (2%)
  other arithmetic  2.02 us (1%)
    ppermute x8, waiting for transfers between devices, swap(): return lax.ppermute(values, axis, [(i, i ^ bit) for i in range(size)])  73.9 us
    all_to_all x1, waiting for transfers between devices, per_device(): lax.all_to_all(d_attn.reshape(devices, t_dev, columns, part), both, 0, 0,...  11.6 us
    all_to_all x1, starting transfers between devices, per_device(): lax.all_to_all(d_attn.reshape(devices, t_dev, columns, part), both, 0, 0,...  7.3 us
    ppermute x8, starting transfers between devices, swap(): return lax.ppermute(values, axis, [(i, i ^ bit) for i in range(size)])  6.88 us
    pallas_call x1, Pallas kernels, share_send(): pl.pallas_call(functools.partial(share_kernel, n_patch=n_patch), grid_spe...  6 us
    pallas_call x1, Pallas kernels, product(): pl.pallas_call(functools.partial(product_kernel, factor=factor), out_shap...  5.66 us
    pallas_call x1, Pallas kernels, attend(): pl.pallas_call(functools.partial(attend_kernel, columns=columns), out_sha...  5.14 us
    all_to_all x1, starting transfers between devices, per_device(): lax.all_to_all(product(got, grads, grads_other, grads_core, grads_other_c...  3.58 us
  transfers between devices with their start and end apart: 11, of which 6 were waited for; matrix products, arithmetic and copies ran while one was open for 2% of the time, Pallas kernels for 7%

profile of v4, /device:TPU:0, one launch (start us, length us, event | category | flops | bytes accessed | tf_op | source)
XLA Modules:
  0.0 137.9 jit_solution(1455893720211377026)
XLA Ops:
  0.6 3.4 %fusion = bf16[4,128,352]{1,2,0:T(8,128)(2,1)S(1)} fusion(bf16[4,352,1408]{2,1,0:T(8,128)(2,1)} %bitcast.135, bf16[128,1408,1]{1,0,2:T(8,128)(2,1)} %bitcast.134), kind=kOutput, calls=%fused_computation.1 | convolution fusion | flops 507691008 | bytes 4685824 | tf_op jit(solution)/shard_map/to,jfo->jtf/dot_general | solution.py:226
  4.0 0.0 copy-start.9
  4.0 0.0 copy-start.10
  4.0 0.0 copy-start
  4.0 0.0 copy-start.3
  4.1 0.0 copy-start.4
  4.1 0.0 copy-start.5
  4.1 0.2 copy.41
  4.3 0.8 copy.42
  5.1 7.3 %all-to-all-start = ((bf16[32,2,8,352]{3,2,1,0:T(8,128)(2,1)}), bf16[32,2,8,352]{3,2,1,0:T(8,128)(2,1)S(1)}, u32[]{:S(2)}, u32[]{:S(2)}) async-start(bf16[32,2,8,352]{3,2,1,0:T(8,128)(2,1)} %bitcast.9), calls=%async_computation | async-start | bytes 786432 | tf_op jit(solution)/shard_map/all_to_all | solution.py:231
  12.5 1.5 %shard_map.104 = bf16[32,2,16,352]{3,2,1,0:T(8,128)(2,1)} custom-call(bf16[128,1408]{1,0:T(8,128)(2,1)S(1)} %bitcast.124, f32[1,1408]{1,0:T(1,128)S(1)} %broadcast_in_dim.20.gain_ref, f32[1,1408]{1,0:T(1,128)S(1)} %broadcast_in_dim.21.bias_ref), custom_call_target="tpu_custom_call" | custom-call | tf_op jit(solution)/shard_map/pallas_call | solution.py:72
  14.0 11.6 %all-to-all-done = bf16[32,2,8,352]{3,2,1,0:T(8,128)(2,1)S(1)} async-done(((bf16[32,2,8,352]{3,2,1,0:T(8,128)(2,1)}), bf16[32,2,8,352]{3,2,1,0:T(8,128)(2,1)S(1)}, u32[]{:S(2)}, u32[]{:S(2)}) %all-to-all-start) | async-done | bytes 360480 | tf_op jit(solution)/shard_map/all_to_all | solution.py:231
  25.6 5.1 %shard_map.105.g_ref.own_ref = bf16[3,352,512]{2,1,0:T(8,128)(2,1)S(1)} custom-call(bf16[512,352]{1,0:T(8,128)(2,1)S(1)} %bitcast.130, bf16[512,352]{1,0:T(8,128)(2,1)S(1)} %bitcast.131, bf16[512,352]{1,0:T(8,128)(2,1)S(1)} %bitcast.132, bf16[512,352]{1,0:T(8,128)(2,1)S(1)} %bitcast.128), custom_call_target="tpu_custom_call" | custom-call | tf_op jit(solution)/shard_map/pallas_call | solution.py:46
  30.8 6.0 %shard_map.106 = (bf16[16,16,1408]{2,1,0:T(8,128)(2,1)}, f32[16,16,1408]{2,1,0:T(8,128)S(1)}) custom-call(s32[1]{0:T(128)} %bitcast.13.where_ref, bf16[3,352,512]{2,1,0:T(8,128)(2,1)S(1)} %shard_map.105.g_ref.own_ref, bf16[1408,4224]{1,0:T(8,128)(2,1)} %w_ref.1), custom_call_target="tpu_custom_call" | custom-call | tf_op jit(solution)/shard_map/pallas_call | solution.py:113
  36.8 0.1 collective-permute-start.1
  36.8 1.0 collective-permute-start
  37.9 1.5 %collective-permute-done.1 = bf16[16,16,1408]{2,1,0:T(8,128)(2,1)} collective-permute-done((bf16[16,16,1408]{2,1,0:T(8,128)(2,1)}, bf16[16,16,1408]{2,1,0:T(8,128)(2,1)}, u32[]{:S(2)}, u32[]{:S(2)}) %collective-permute-start.1) | collective-permute-done | bytes 720928 | tf_op jit(solution)/shard_map/ppermute | solution.py:223
  39.4 2.0 %shard_map.107 = (bf16[8,16,1408]{2,1,0:T(8,128)(2,1)}, f32[8,16,1408]{2,1,0:T(8,128)S(1)}) custom-call(s32[1]{0:T(128)} %bitcast.12.chip_ref, f32[8,2,16,1408]{3,2,1,0:T(8,128)S(1)} %bitcast.129, bf16[8,2,16,1408]{3,2,1,0:T(8,128)(2,1)} %bitcast.15.come_ref), custom_call_target="tpu_custom_call" | custom-call | tf_op jit(solution)/shard_map/pallas_call | solution.py:148
  41.3 0.9 copy-done.1
  42.2 0.6 collective-permute-start.2
  42.8 2.9 %all-to-all-start.1 = ((bf16[32,2,16,352]{3,2,1,0:T(8,128)(2,1)}), bf16[32,2,16,352]{3,2,1,0:T(8,128)(2,1)S(1)}, u32[]{:S(2)}, u32[]{:S(2)}) async-start(bf16[32,2,16,352]{3,2,1,0:T(8,128)(2,1)} %shard_map.104), calls=%async_computation.1 | async-start | bytes 1572864 | tf_op jit(solution)/shard_map/all_to_all | solution.py:244
  45.7 0.1 collective-permute-start.6
  45.8 12.0 %collective-permute-done.2.come_ref = bf16[8,16,1408]{2,1,0:T(8,128)(2,1)S(1)} collective-permute-done((bf16[8,16,1408]{2,1,0:T(8,128)(2,1)}, bf16[8,16,1408]{2,1,0:T(8,128)(2,1)S(1)}, u32[]{:S(2)}, u32[]{:S(2)}) %collective-permute-start.2) | collective-permute-done | bytes 360480 | tf_op jit(solution)/shard_map/ppermute | solution.py:223
  57.9 0.7 copy-done.6
  58.6 1.0 copy-done.7
  59.6 0.1 shard_map.108
  59.7 11.4 %collective-permute-done.other_ref = bf16[3,352,512]{2,1,0:T(8,128)(2,1)} collective-permute-done((bf16[3,352,512]{2,1,0:T(8,128)(2,1)S(1)}, bf16[3,352,512]{2,1,0:T(8,128)(2,1)}, u32[]{:S(2)}, u32[]{:S(2)}) %collective-permute-start) | collective-permute-done | bytes 1081376 | tf_op jit(solution)/shard_map/ppermute | solution.py:223
  71.0 0.0 collective-permute-start.7
  71.1 1.0 collective-permute-start.3
  72.1 0.1 convert_reduce_fusion
  72.2 5.9 %collective-permute-done.3 = bf16[2,2,1,16,1408]{4,3,1,0,2:T(8,128)(2,1)S(1)} collective-permute-done((bf16[2,2,1,16,1408]{4,3,1,0,2:T(8,128)(2,1)S(1)}, bf16[2,2,1,16,1408]{4,3,1,0,2:T(8,128)(2,1)S(1)}, u32[]{:S(2)}, u32[]{:S(2)}) %collective-permute-start.3) | collective-permute-done | bytes 180256 | tf_op jit(solution)/shard_map/ppermute | solution.py:223
  78.2 1.1 collective-permute-start.4
  79.3 0.0 collective-permute-done.6.own_core_ref
  79.3 0.0 all-to-all-done.1.a_ref
  79.3 5.7 %shard_map.109 = bf16[8,44,2112]{2,1,0:T(8,128)(2,1)} custom-call(bf16[32,2,16,352]{3,2,1,0:T(8,128)(2,1)S(1)} %all-to-all-done.1.a_ref, bf16[3,352,512]{2,1,0:T(8,128)(2,1)S(1)} %shard_map.105.g_ref.own_ref, bf16[3,352,512]{2,1,0:T(8,128)(2,1)} %collective-permute-done.other_ref, bf16[3,352,512]{2,1,0:T(8,128)(2,1)} %collective-permute-done.6.own_core_ref, ...), custom_call_target="tpu_custom_call" | custom-call | tf_op jit(solution)/shard_map/pallas_call | solution.py:181
  84.9 3.6 %all-to-all-start.2 = ((bf16[8,44,2112]{2,1,0:T(8,128)(2,1)}), bf16[8,44,2112]{2,1,0:T(8,128)(2,1)S(1)}, u32[]{:S(2)}, u32[]{:S(2)}) async-start(bf16[8,44,2112]{2,1,0:T(8,128)(2,1)} %shard_map.109), calls=%async_computation.2 | async-start | bytes 3342336 | tf_op jit(solution)/shard_map/all_to_all | solution.py:264
  88.6 0.1 div.33
  88.6 0.2 fusion.3
  88.9 0.1 broadcast_select_fusion.3
  89.0 2.9 %collective-permute-start.5 = (bf16[4,16,1408]{2,1,0:T(8,128)(2,1)S(1)}, bf16[4,16,1408]{2,1,0:T(8,128)(2,1)S(1)}, u32[]{:S(2)}, u32[]{:S(2)}) collective-permute-start(bf16[4,16,1408]{2,1,0:T(8,128)(2,1)S(1)} %fusion.20), channel_id=1, source_target_pairs={{0,16},{4,20},{8,24},{12,28},{16,0},{20,4},{24,8},{28,12},{1,17},{... | collective-permute-start | bytes 540680 | tf_op jit(solution)/shard_map/ppermute | solution.py:223
  91.9 0.1 rsqrt.13
  92.0 43.2 %collective-permute-done.5 = bf16[4,16,1408]{2,1,0:T(8,128)(2,1)S(1)} collective-permute-done((bf16[4,16,1408]{2,1,0:T(8,128)(2,1)S(1)}, bf16[4,16,1408]{2,1,0:T(8,128)(2,1)S(1)}, u32[]{:S(2)}, u32[]{:S(2)}) %collective-permute-start.5) | collective-permute-done | bytes 180256 | tf_op jit(solution)/shard_map/ppermute | solution.py:223
  135.2 0.1 broadcast_select_fusion.5
  135.2 0.3 bitcast_reduce_fusion
  135.5 0.1 div.35
  135.6 0.1 div.32
  135.7 1.1 fusion.8
  136.8 1.1 shard_map.110
  (25 shorter events, 0.2 us)
Async XLA Ops:
  4.0 8.4 %copy-start.9 = (f32[1408]{0:T(1024)S(1)}, f32[1408]{0:T(1024)}, u32[]{:S(2)}) copy-start(f32[1408]{0:T(1024)} %param.10) | copy-start | bytes 16900
  4.0 8.4 %copy-start.10 = (f32[1408]{0:T(1024)S(1)}, f32[1408]{0:T(1024)}, u32[]{:S(2)}) copy-start(f32[1408]{0:T(1024)} %param.11) | copy-start | bytes 16900
  4.0 8.4 %copy-start = (bf16[2,64,1408]{2,1,0:T(8,128)(2,1)S(1)}, bf16[2,64,1408]{2,1,0:T(8,128)(2,1)}, u32[]{:S(2)}) copy-start(bf16[2,64,1408]{2,1,0:T(8,128)(2,1)} %param.9) | copy-start | bytes 1081348
  4.0 21.5 %copy-start.3 = (bf16[64,8,352]{2,1,0:T(8,128)(2,1)S(1)}, bf16[64,8,352]{2,1,0:T(8,128)(2,1)}, u32[]{:S(2)}) copy-start(bf16[64,8,352]{2,1,0:T(8,128)(2,1)} %param.14) | copy-start | bytes 1081348
  4.1 21.5 %copy-start.4 = (bf16[64,8,352]{2,1,0:T(8,128)(2,1)S(1)}, bf16[64,8,352]{2,1,0:T(8,128)(2,1)}, u32[]{:S(2)}) copy-start(bf16[64,8,352]{2,1,0:T(8,128)(2,1)} %param.15) | copy-start | bytes 1081348
  4.1 21.5 %copy-start.5 = (bf16[64,8,352]{2,1,0:T(8,128)(2,1)S(1)}, bf16[64,8,352]{2,1,0:T(8,128)(2,1)}, u32[]{:S(2)}) copy-start(bf16[64,8,352]{2,1,0:T(8,128)(2,1)} %param.16) | copy-start | bytes 1081348
  5.1 20.5 %all-to-all-start = ((bf16[32,2,8,352]{3,2,1,0:T(8,128)(2,1)}), bf16[32,2,8,352]{3,2,1,0:T(8,128)(2,1)S(1)}, u32[]{:S(2)}, u32[]{:S(2)}) async-start(bf16[32,2,8,352]{3,2,1,0:T(8,128)(2,1)} %bitcast.9), calls=%async_computation | async-start | bytes 786432 | tf_op jit(solution)/shard_map/all_to_all | solution.py:231
  36.8 2.6 %collective-permute-start.1 = (bf16[16,16,1408]{2,1,0:T(8,128)(2,1)}, bf16[16,16,1408]{2,1,0:T(8,128)(2,1)}, u32[]{:S(2)}, u32[]{:S(2)}) collective-permute-start(bf16[16,16,1408]{2,1,0:T(8,128)(2,1)} %get-tuple-element.16), channel_id=1, source_target_pairs={{0,1},{1,0},{2,3},{3,2},{4,5},{5,4},{6,7},{7,6},{8,9},{9,8},{10,11... | collective-permute-start | bytes 2162696 | tf_op jit(solution)/shard_map/ppermute | solution.py:223
  36.8 34.2 %collective-permute-start = (bf16[3,352,512]{2,1,0:T(8,128)(2,1)S(1)}, bf16[3,352,512]{2,1,0:T(8,128)(2,1)}, u32[]{:S(2)}, u32[]{:S(2)}) collective-permute-start(bf16[3,352,512]{2,1,0:T(8,128)(2,1)S(1)} %shard_map.105.g_ref.own_ref), channel_id=1, source_target_pairs={{0,4},{4,0},{8,12},{12,8},{16,20},{20,16},{24,28},{28,24},{1,5},{5... | collective-permute-start | bytes 3244040 | tf_op jit(solution)/shard_map/ppermute | solution.py:223
  41.3 0.9 copy-start.1
  42.2 16.4 %copy-start.2 = (f32[8,16,1408]{2,1,0:T(8,128)S(1)}, f32[8,16,1408]{2,1,0:T(8,128)}, u32[]{:S(2)}) copy-start(f32[8,16,1408]{2,1,0:T(8,128)} %copy-done.1) | copy-start | bytes 2162692
  42.2 15.7 %collective-permute-start.2 = (bf16[8,16,1408]{2,1,0:T(8,128)(2,1)}, bf16[8,16,1408]{2,1,0:T(8,128)(2,1)S(1)}, u32[]{:S(2)}, u32[]{:S(2)}) collective-permute-start(bf16[8,16,1408]{2,1,0:T(8,128)(2,1)} %get-tuple-element.18), channel_id=1, source_target_pairs={{0,2},{1,3},{2,0},{3,1},{4,6},{5,7},{6,4},{7,5},{8,10},{9,11},{10,... | collective-permute-start | bytes 1081352 | tf_op jit(solution)/shard_map/ppermute | solution.py:223
  42.8 36.5 %all-to-all-start.1 = ((bf16[32,2,16,352]{3,2,1,0:T(8,128)(2,1)}), bf16[32,2,16,352]{3,2,1,0:T(8,128)(2,1)S(1)}, u32[]{:S(2)}, u32[]{:S(2)}) async-start(bf16[32,2,16,352]{3,2,1,0:T(8,128)(2,1)} %shard_map.104), calls=%async_computation.1 | async-start | bytes 1572864 | tf_op jit(solution)/shard_map/all_to_all | solution.py:244
  45.7 33.6 %collective-permute-start.6 = (bf16[3,352,512]{2,1,0:T(8,128)(2,1)S(1)}, bf16[3,352,512]{2,1,0:T(8,128)(2,1)}, u32[]{:S(2)}, u32[]{:S(2)}) collective-permute-start(bf16[3,352,512]{2,1,0:T(8,128)(2,1)S(1)} %shard_map.105.g_ref.own_ref), channel_id=1, source_target_pairs={{0,1},{1,0},{2,3},{3,2},{4,5},{5,4},{6,7},{7,6},{8,9},{9,8},{10,11... | collective-permute-start | bytes 3244040 | tf_op jit(solution)/shard_map/ppermute | solution.py:223
  57.9 0.7 copy-start.6
  58.6 1.0 copy-start.7
  71.0 8.2 %collective-permute-start.7 = (bf16[3,352,512]{2,1,0:T(8,128)(2,1)}, bf16[3,352,512]{2,1,0:T(8,128)(2,1)}, u32[]{:S(2)}, u32[]{:S(2)}) collective-permute-start(bf16[3,352,512]{2,1,0:T(8,128)(2,1)} %collective-permute-done.other_ref), channel_id=1, source_target_pairs={{0,1},{1,0},{2,3},{3,2},{4,5},{5,4},{6,7},{7,6},{8,9},{9,8},{10,11... | collective-permute-start | bytes 3244040 | tf_op jit(solution)/shard_map/ppermute | solution.py:223
  71.1 7.0 %collective-permute-start.3 = (bf16[2,2,1,16,1408]{4,3,1,0,2:T(8,128)(2,1)S(1)}, bf16[2,2,1,16,1408]{4,3,1,0,2:T(8,128)(2,1)S(1)}, u32[]{:S(2)}, u32[]{:S(2)}) collective-permute-start(bf16[2,2,1,16,1408]{4,3,1,0,2:T(8,128)(2,1)S(1)} %fusion.22), channel_id=1, source_target_pairs={{0,4},{4,0},{8,12},{12,8},{16,20},{20,16},{24,28},{28,24},{1,5},{5... | collective-permute-start | bytes 540680 | tf_op jit(solution)/shard_map/ppermute | solution.py:223
  78.2 10.7 %collective-permute-start.4 = (bf16[2,2,16,1408]{3,2,0,1:T(8,128)(2,1)S(1)}, bf16[2,2,16,1408]{3,2,0,1:T(8,128)(2,1)S(1)}, u32[]{:S(2)}, u32[]{:S(2)}) collective-permute-start(bf16[2,2,16,1408]{3,2,0,1:T(8,128)(2,1)S(1)} %fusion.21), channel_id=1, source_target_pairs={{0,8},{4,12},{8,0},{12,4},{16,24},{20,28},{24,16},{28,20},{1,9},{5... | collective-permute-start | bytes 540680 | tf_op jit(solution)/shard_map/ppermute | solution.py:223
  84.9 51.8 %all-to-all-start.2 = ((bf16[8,44,2112]{2,1,0:T(8,128)(2,1)}), bf16[8,44,2112]{2,1,0:T(8,128)(2,1)S(1)}, u32[]{:S(2)}, u32[]{:S(2)}) async-start(bf16[8,44,2112]{2,1,0:T(8,128)(2,1)} %shard_map.109), calls=%async_computation.2 | async-start | bytes 3342336 | tf_op jit(solution)/shard_map/all_to_all | solution.py:264
  88.9 46.8 %copy-start.8 = (bf16[2,64,1408]{2,1,0:T(8,128)(2,1)S(1)}, bf16[2,64,1408]{2,1,0:T(8,128)(2,1)}, u32[]{:S(2)}) copy-start(bf16[2,64,1408]{2,1,0:T(8,128)(2,1)} %param.17) | copy-start | bytes 1081348
  89.0 46.2 %collective-permute-start.5 = (bf16[4,16,1408]{2,1,0:T(8,128)(2,1)S(1)}, bf16[4,16,1408]{2,1,0:T(8,128)(2,1)S(1)}, u32[]{:S(2)}, u32[]{:S(2)}) collective-permute-start(bf16[4,16,1408]{2,1,0:T(8,128)(2,1)S(1)} %fusion.20), channel_id=1, source_target_pairs={{0,16},{4,20},{8,24},{12,28},{16,0},{20,4},{24,8},{28,12},{1,17},{... | collective-permute-start | bytes 540680 | tf_op jit(solution)/shard_map/ppermute | solution.py:223

commit v5 on v4

--- a/solution.py
+++ b/solution.py
@@ -65,16 +65,15 @@
                 for slot in range(2):
                     at = (2 * z + (y ^ slot)) * columns
                     piece = jnp.concatenate([part[t * patches + at : t * patches + at + columns] for t in range(t_dev)], axis=0).astype(BF)
-                    for x in range(n_chip):
-                        out_ref[((2 * z + y) * n_chip + x) * 2 + c, slot] = piece
+                    out_ref[((2 * z + y) * 2 + slot) * 2 + c] = piece
 def norm_send(tokens, gain, bias, n_pair, n_chip, columns, own_rows, t_dev):
     devices = 4 * n_pair * n_chip
     return pl.pallas_call(functools.partial(norm_kernel,n_pair=n_pair,n_chip=n_chip,columns=columns,own_rows=own_rows,t_dev=t_dev),
-        out_shape=jax.ShapeDtypeStruct((devices,2,t_dev*columns,tokens.shape[1]//4),BF),compiler_params=ROOM)(tokens,gain[None],bias[None])
-
-def share_kernel(where_ref, g_ref, w_ref, leave_ref, stay_ref, win_ref, pad_ref, acc_ref, sem, *, n_patch):
-    kinds, part, n_tok = g_ref.shape
-    _, width, window = win_ref.shape
+        out_shape=jax.ShapeDtypeStruct((devices,t_dev*columns,tokens.shape[1]//4),BF),compiler_params=ROOM)(tokens,gain[None],bias[None])
+
+def weights_kernel(where_ref, w_ref, out_ref, win_ref, sem, *, n_patch):
+    kinds, width, part = out_ref.shape
+    window = win_ref.shape[2]
     patch = where_ref[0]
     starts = [min(part * j // 128 * 128, width - window) for j in range(n_patch)]
     start = sum(jnp.where(patch == j, at, 0) for j, at in enumerate(starts))
@@ -86,53 +85,71 @@
     ]
     for copy in copies:
         copy.start()
-    pad_ref[...] = jnp.zeros_like(pad_ref)
+    for copy in copies:
+        copy.wait()
     for j in range(n_patch):
 
         @pl.when(patch == j)
         def _(j=j):
             before = part * j - starts[j]
             for c in range(kinds):
-                pad_ref[c, before : before + part, :] = g_ref[c]
-
+                out_ref[c] = win_ref[c, :, before : before + part]
+
+
+def own_weights(w_qkv, patch, n_patch):
+    width = w_qkv.shape[0]
+    kinds, part = w_qkv.shape[1] // width, width // n_patch
+    window = -(-(part + 96) // 128) * 128
+    return pl.pallas_call(
+        functools.partial(weights_kernel, n_patch=n_patch),
+        grid_spec=pltpu.PrefetchScalarGridSpec(
+            num_scalar_prefetch=1,
+            grid=(1,),
+            in_specs=[pl.BlockSpec(memory_space=pl.ANY)],
+            out_specs=pl.BlockSpec((kinds, width, part), lambda i, s: (0, 0, 0)),
+            scratch_shapes=[
+                pltpu.VMEM((kinds, width, window), BF),
+                pltpu.SemaphoreType.DMA((kinds,)),
+            ],
+        ),
+        out_shape=jax.ShapeDtypeStruct((kinds, width, part), BF),
+        compiler_params=ROOM,
+    )(patch[None], w_qkv)
+
+
+def share_kernel(where_ref, g_ref, w_ref, leave_ref, stay_ref, acc_ref):
+    core = where_ref[0] % 2
     total = None
-    for c, copy in enumerate(copies):
-        copy.wait()
-        one = lax.dot_general(pad_ref[c], win_ref[c], CROSS, preferred_element_type=F32)
+    for c in range(g_ref.shape[0]):
+        one = lax.dot_general(g_ref[c], w_ref[c], CROSS, preferred_element_type=F32)
         total = one if total is None else total + one
     acc_ref[...] = total.reshape(acc_ref.shape)
-    leave_ref[...] = acc_ref[:, 1 - patch % 2].astype(BF)
-    stay_ref[...] = acc_ref[:, patch % 2]
-
-
-def share_send(grads, w_qkv, patch, n_patch, group):
+    leave_ref[...] = acc_ref[:, 1 - core].astype(BF)
+    stay_ref[...] = acc_ref[:, core]
+
+
+def share_send(grads, weights, patch, group):
     kinds, part, n_tok = grads.shape
-    width = w_qkv.shape[0]
-    window = -(-(part + 96) // 128) * 128
+    width = weights.shape[1]
     n = n_tok // (2 * group)
     return pl.pallas_call(
-        functools.partial(share_kernel, n_patch=n_patch),
+        share_kernel,
         grid_spec=pltpu.PrefetchScalarGridSpec(
             num_scalar_prefetch=1,
             grid=(1,),
             in_specs=[
                 pl.BlockSpec((kinds, part, n_tok), lambda i, s: (0, 0, 0)),
-                pl.BlockSpec(memory_space=pl.ANY),
+                pl.BlockSpec((kinds, width, part), lambda i, s: (0, 0, 0)),
             ],
             out_specs=[pl.BlockSpec((n, group, width), lambda i, s: (0, 0, 0))] * 2,
-            scratch_shapes=[
-                pltpu.VMEM((kinds, width, window), BF),
-                pltpu.VMEM((kinds, window, n_tok), BF),
-                pltpu.VMEM((n, 2, group, width), F32),
-                pltpu.SemaphoreType.DMA((kinds,)),
-            ],
+            scratch_shapes=[pltpu.VMEM((n, 2, group, width), F32)],
         ),
         out_shape=[
             jax.ShapeDtypeStruct((n, group, width), BF),
             jax.ShapeDtypeStruct((n, group, width), F32),
         ],
         compiler_params=ROOM,
-    )(patch[None], grads, w_qkv)
+    )(patch[None], grads, weights)
 
 
 def merge_kernel(chip_ref, stay_ref, come_ref, leave_ref, keep_ref):
@@ -162,24 +179,93 @@
     out_ref[...] = (stay_ref[...] + come_ref[...].astype(F32)).astype(BF)
 
 
-def product_kernel(a_ref, own_ref, other_ref, own_core_ref, other_core_ref, out_ref, *, factor):
-    n, _, group, quarter = a_ref.shape
+def product_kernel(
+    chip_ref, mine_ref, theirs_ref, own_ref, other_ref, own_core_ref, other_core_ref, out_ref, *, factor
+):
     kinds, part, n_tok = own_ref.shape
     own_rows = out_ref.shape[1]
-    left = [a_ref[:, slot].reshape(n_tok, quarter).astype(F32).T.astype(BF) for slot in range(2)]
-    for r, pair in enumerate(((own_ref, other_ref), (own_core_ref, other_core_ref))):
-        for c in range(kinds):
-            total = lax.dot_general(left[0], pair[0][c], COLS, preferred_element_type=F32)
-            total += lax.dot_general(left[1], pair[1][c], COLS, preferred_element_type=F32)
-            total = total * factor
-            at = (r * kinds + c) * part
-            for k in range(out_ref.shape[0]):
-                out_ref[k, :, at : at + part] = total[k * own_rows : (k + 1) * own_rows].astype(BF)
-def product(got, grads, other, core, other_core, own_rows, factor):
+
+    def write(norm_own, norm_other):
+        for r, (own, other) in enumerate(((own_ref, other_ref), (own_core_ref, other_core_ref))):
+            for c in range(kinds):
+                total = jnp.dot(own[c], norm_own[...], preferred_element_type=F32)
+                total += jnp.dot(other[c], norm_other[...], preferred_element_type=F32)
+                total = (total * factor).T
+                at = (r * kinds + c) * part
+                for k in range(out_ref.shape[0]):
+                    rows = total[k * own_rows : (k + 1) * own_rows]
+                    out_ref[k, :, at : at + part] = rows.astype(BF)
+
+    @pl.when(chip_ref[0] == 0)
+    def _():
+        write(mine_ref, theirs_ref)
+
+    @pl.when(chip_ref[0] == 1)
+    def _():
+        write(theirs_ref, mine_ref)
+
+
+def product(chip, mine, theirs, grads, other, core, other_core, own_rows, factor):
     kinds, part, n_tok = grads.shape
-    quarter = got.shape[-1]
-    return pl.pallas_call(functools.partial(product_kernel,factor=factor),
-        out_shape=jax.ShapeDtypeStruct((quarter//own_rows,own_rows,2*kinds*part),BF),compiler_params=ROOM)(got,grads,other,core,other_core)
+    norm = pl.BlockSpec(mine.shape, lambda i, s: (0, 0))
+    whole = pl.BlockSpec(grads.shape, lambda i, s: (0, 0, 0))
+    shape = (part // own_rows, own_rows, 2 * kinds * part)
+    return pl.pallas_call(
+        functools.partial(product_kernel, factor=factor),
+        grid_spec=pltpu.PrefetchScalarGridSpec(
+            num_scalar_prefetch=1,
+            grid=(1,),
+            in_specs=[norm, norm, whole, whole, whole, whole],
+            out_specs=pl.BlockSpec(shape, lambda i, s: (0, 0, 0)),
+        ),
+        out_shape=jax.ShapeDtypeStruct(shape, BF),
+        compiler_params=ROOM,
+    )(chip[None], mine, theirs, grads, other, core, other_core)
+
+
+def last_kernel(tm_ref, stay_ref, come_ref, x_ref, grad_ref, gain_ref, out_ref, *, columns, t_dev):
+    n_pair, group, width = stay_ref.shape
+    patches = x_ref.shape[0] // t_dev
+    tm = tm_ref[0]
+    first = tm % 2 == 0
+    for z in range(n_pair):
+        slot = (tm // 2) ^ z
+        stay, come = stay_ref[slot].astype(F32), come_ref[slot].astype(F32)
+        for y in range(2):
+            d_norm = jnp.where(first == (y == 0), stay, come)
+            for t in range(t_dev):
+                at = t * patches + (2 * z + y) * columns
+                rows = slice(at, at + columns)
+                tokens = x_ref[rows, :].astype(F32)
+                centered = tokens - jnp.mean(tokens, axis=-1, keepdims=True)
+                variance = jnp.mean(centered * centered, axis=-1, keepdims=True)
+                inverse = lax.rsqrt(variance + 1e-06)
+                normed = centered * inverse
+                scaled = d_norm[t * columns : (t + 1) * columns] * gain_ref[...]
+                branch = inverse * (
+                    scaled
+                    - jnp.mean(scaled, axis=-1, keepdims=True)
+                    - normed * jnp.mean(scaled * normed, axis=-1, keepdims=True)
+                )
+                out_ref[rows, :] = (grad_ref[rows, :].astype(F32) + branch).astype(BF)
+
+
+def last(stay, come, tokens, grads, gain, tm, columns, t_dev):
+    n_rows, width = tokens.shape
+    part = pl.BlockSpec(stay.shape, lambda i, s: (0, 0, 0))
+    rows = pl.BlockSpec((n_rows, width), lambda i, s: (0, 0))
+    return pl.pallas_call(
+        functools.partial(last_kernel, columns=columns, t_dev=t_dev),
+        grid_spec=pltpu.PrefetchScalarGridSpec(
+            num_scalar_prefetch=1,
+            grid=(1,),
+            in_specs=[part, part, rows, rows, pl.BlockSpec((1, width), lambda i, s: (0, 0))],
+            out_specs=rows,
+        ),
+        out_shape=jax.ShapeDtypeStruct((n_rows, width), BF),
+        compiler_params=ROOM,
+    )(tm[None], stay, come, tokens, grads, gain[None])
+
 
 def final_kernel(core_ref, in_ref, out_ref, *, part, kinds):
     n_pair, n_chip, own_rows, _ = in_ref.shape
@@ -216,6 +302,7 @@
     own_rows = width // devices
     tm = lax.axis_index("tm")
     patch = lax.axis_index("patch")
+    side = tm % 2
     core = patch % 2
     both = ("tm", "patch")
 
@@ -232,26 +319,29 @@
         d_attn.reshape(devices, t_dev, columns, part), both, 0, 0, tiled=True
     ).reshape(n_tok, part)
 
-    as_float = tokens.reshape(-1, width).astype(F32)
-    centered = as_float - jnp.mean(as_float, axis=-1, keepdims=True)
-    variance = jnp.mean(centered * centered, axis=-1, keepdims=True)
-    inverse = lax.rsqrt(variance + 1e-06)
-    normed = centered * inverse
-
     quarter = width // 4
     sent = norm_send(tokens.reshape(-1, width), ln_gain, ln_bias, n_pair, n_chip, columns, own_rows, t_dev)
-    d_time, sent = lax.optimization_barrier((d_time, sent))
-    got = lax.all_to_all(sent, both, 0, 0, tiled=True)
+    weights = own_weights(w_qkv, patch, n_patch)
+    d_time, sent, weights = lax.optimization_barrier((d_time, sent, weights))
+    mine = lax.all_to_all(sent, both, 0, 0, tiled=True).reshape(n_tok, quarter)
+    theirs = swap(mine, "patch", n_patch, 2)
 
     saved = [values.reshape(n_tok, part) for values in (q_time, k_time, v_time)]
     grads = attend(*saved, d_time, columns)
     grads_other = swap(grads, "tm", n_tm, 1)
-    leave, stay = share_send(grads, w_qkv, patch, n_patch, t_dev * columns)
+    leave, stay = share_send(grads, weights, patch, t_dev * columns)
     leave, stay = merge(stay, swap(leave, "patch", n_patch, 1), patch // 2)
     share = pl.pallas_call(
         add_kernel, out_shape=jax.ShapeDtypeStruct(leave.shape, BF), compiler_params=ROOM
     )(stay, swap(leave, "patch", n_patch, 2))
-    grads_other, share = lax.optimization_barrier((grads_other, share))
+    share = share.reshape((n_pair, 2) + share.shape[1:])
+    spread = [
+        swap(lax.dynamic_index_in_dim(share, (tm // 2) ^ n, 0, keepdims=False), "tm", n_tm, 2 * n)
+        if n
+        else lax.dynamic_index_in_dim(share, tm // 2, 0, keepdims=False)
+        for n in range(n_pair)
+    ]
+    grads_other, spread, theirs = lax.optimization_barrier((grads_other, spread, theirs))
     grads_core = swap(grads, "patch", n_patch, 1)
     grads_other_core = swap(grads_other, "patch", n_patch, 1)
 
@@ -262,7 +352,9 @@
         for c in range(2)
     ]
     pieces = lax.all_to_all(
-        product(got, grads, grads_other, grads_core, grads_other_core, own_rows, factor),
+        product(
+            patch // 2, mine, theirs, grads, grads_other, grads_core, grads_other_core, own_rows, factor
+        ),
         both,
         0,
         0,
@@ -271,25 +363,11 @@
     )
     grad_w_qkv = final_sum(pieces.reshape(n_pair, n_chip, own_rows, 6 * part), core, part, 3)
 
-    bits = n_tm.bit_length() - 1
-    share = share.reshape((2,) * bits + (1, t_dev * columns, width))
-    for n in range(bits):
-        high = (tm & (1 << n)) != 0
-        at = bits - 1 - n
-        low_part, high_part = [lax.index_in_dim(share, i, at, keepdims=False) for i in range(2)]
-        stay = jnp.where(high, high_part, low_part)
-        come = swap(jnp.where(high, low_part, high_part), "tm", n_tm, 1 << n)
-        share = jnp.concatenate([jnp.where(high, come, stay), jnp.where(high, stay, come)], at)
-    d_norm = share
-    d_norm = d_norm.reshape(n_tm, t_dev, columns, width).transpose(1, 0, 2, 3)
-    d_norm = d_norm.reshape(-1, width).astype(F32)
-    scaled = d_norm * ln_gain
-    branch = inverse * (
-        scaled
-        - jnp.mean(scaled, axis=-1, keepdims=True)
-        - normed * jnp.mean(scaled * normed, axis=-1, keepdims=True)
-    )
-    grad_x = (grad_rows.astype(F32) + branch).astype(BF).reshape(t_dev, patches, width)
+    spread = jnp.stack(spread)
+    stay = lax.dynamic_index_in_dim(spread, side, 1, keepdims=False)
+    come = swap(lax.dynamic_index_in_dim(spread, 1 - side, 1, keepdims=False), "tm", n_tm, 1)
+    grad_x = last(stay, come, tokens.reshape(-1, width), grad_rows, ln_gain, tm, columns, t_dev)
+    grad_x = grad_x.reshape(t_dev, patches, width)
     return (grad_x, grad_w_qkv)
 
 

time: 138 us -> 133 us (0.964)
  waiting for transfers between devices: 85.6 us -> 75.9 us
  Pallas kernels: 21.5 us -> 25.3 us
  other arithmetic: 2.02 us -> 0.06 us
  starting transfers between devices: 20.6 us -> 22.3 us
    ppermute x8 -> x10, waiting for transfers between devices: 73.9 us -> 14.8 us  [swap(): return lax.ppermute(values, axis, [(i, i ^ bit) for i in range(size)])]
    all_to_all x2, waiting for transfers between devices: 0.01 us -> 53.9 us  [the longest x1 31.5 us: per_device(): lax.all_to_all(product(patch // 2, mine, theirs, grads, grads_other, grad...]
    all_to_all x1, waiting for transfers between devices: 11.6 us -> 7.18 us  [per_device(): lax.all_to_all(d_attn.reshape(devices, t_dev, columns, part), both, 0, 0,...]
    pallas_call x2 -> x4, Pallas kernels: 11.7 us -> 15.5 us  [the longest x1 6.03 us: share_send(): pl.pallas_call(share_kernel, grid_spec=pltpu.PrefetchScalarGridSpec(num_s...]
    ppermute x8 -> x10, starting transfers between devices: 6.88 us -> 8.65 us  [swap(): return lax.ppermute(values, axis, [(i, i ^ bit) for i in range(size)])]
    unnamed x22 -> x20, local copies, waits for them, and re-layouts: 2.65 us -> 3.66 us
  transfers between devices with their start and end apart: 11 -> 13, of which waited for: 6 -> 8; matrix products, arithmetic and copies ran while one was open for 2% -> 0% of each run, Pallas kernels for 7% -> 6%
where the time goes in v5:
time: 133 us; the launch traced here: 132 us
  waiting for transfers between devices  75.9 us (57%)
  Pallas kernels  25.3 us (19%)
  starting transfers between devices  22.3 us (17%)
  local copies, waits for them, and re-layouts  4.76 us (4%)
  matrix products  3.37 us (3%)
    all_to_all x1, waiting for transfers between devices, per_device(): lax.all_to_all(product(patch // 2, mine, theirs, grads, grads_other, grad...  31.5 us
    all_to_all x1, waiting for transfers between devices, per_device(): mine = lax.all_to_all(sent, both, 0, 0, tiled=True).reshape(n_tok, quarter)  22.4 us
    ppermute x10, waiting for transfers between devices, swap(): return lax.ppermute(values, axis, [(i, i ^ bit) for i in range(size)])  14.8 us
    ppermute x10, starting transfers between devices, swap(): return lax.ppermute(values, axis, [(i, i ^ bit) for i in range(size)])  8.65 us
    all_to_all x1, starting transfers between devices, per_device(): lax.all_to_all(d_attn.reshape(devices, t_dev, columns, part), both, 0, 0,...  7.3 us
    all_to_all x1, waiting for transfers between devices, per_device(): lax.all_to_all(d_attn.reshape(devices, t_dev, columns, part), both, 0, 0,...  7.18 us
    pallas_call x1, Pallas kernels, share_send(): pl.pallas_call(share_kernel, grid_spec=pltpu.PrefetchScalarGridSpec(num_s...  6.03 us
    pallas_call x1, Pallas kernels, product(): pl.pallas_call(functools.partial(product_kernel, factor=factor), grid_spe...  5.3 us
  transfers between devices with their start and end apart: 13, of which 8 were waited for; matrix products, arithmetic and copies ran while one was open for 0% of the time, Pallas kernels for 6%

profile of v5, /device:TPU:0, one launch (start us, length us, event | category | flops | bytes accessed | tf_op | source)
XLA Modules:
  0.0 132.5 jit_solution(14161272336031930673)
XLA Ops:
  0.6 3.4 %fusion = bf16[4,128,352]{1,2,0:T(8,128)(2,1)S(1)} fusion(bf16[4,352,1408]{2,1,0:T(8,128)(2,1)} %bitcast.62, bf16[128,1408,1]{1,0,2:T(8,128)(2,1)} %bitcast.54), kind=kOutput, calls=%fused_computation.1 | convolution fusion | flops 507691008 | bytes 4685824 | tf_op jit(solution)/shard_map/to,jfo->jtf/dot_general | solution.py:313
  4.0 0.0 copy-start.8
  4.0 0.0 copy-start.9
  4.0 0.2 copy.13
  4.3 0.8 copy.14
  5.1 7.3 %all-to-all-start = ((bf16[32,2,8,352]{3,2,1,0:T(8,128)(2,1)}), bf16[32,2,8,352]{3,2,1,0:T(8,128)(2,1)S(1)}, u32[]{:S(2)}, u32[]{:S(2)}) async-start(bf16[32,2,8,352]{3,2,1,0:T(8,128)(2,1)} %bitcast.10), calls=%async_computation | async-start | bytes 786432 | tf_op jit(solution)/shard_map/all_to_all | solution.py:318
  12.4 0.0 copy-start.1
  12.4 0.0 copy-start.4
  12.4 0.0 copy-start.5
  12.4 0.0 copy-start.6
  12.5 2.9 %shard_map.105.w_ref = bf16[3,1408,352]{2,1,0:T(8,128)(2,1)S(1)} custom-call(s32[1]{0:T(128)} %bitcast.13.where_ref, bf16[1408,4224]{1,0:T(8,128)(2,1)} %w_ref.1), custom_call_target="tpu_custom_call" | custom-call | tf_op jit(solution)/shard_map/pallas_call | solution.py:103
  15.3 1.6 %copy-done = bf16[3,1408,352]{2,1,0:T(8,128)(2,1)} copy-done((bf16[3,1408,352]{2,1,0:T(8,128)(2,1)}, bf16[3,1408,352]{2,1,0:T(8,128)(2,1)S(1)}, u32[]{:S(2)}) %copy-start) | copy-done | bytes 2973720
  17.0 1.4 %shard_map.104 = bf16[32,16,352]{2,1,0:T(8,128)(2,1)} custom-call(bf16[128,1408]{1,0:T(8,128)(2,1)S(1)} %bitcast.48, f32[1,1408]{1,0:T(1,128)S(1)} %broadcast_in_dim.22.gain_ref, f32[1,1408]{1,0:T(1,128)S(1)} %broadcast_in_dim.23.bias_ref), custom_call_target="tpu_custom_call" | custom-call | tf_op jit(solution)/shard_map/pallas_call | solution.py:71
  18.4 7.2 %all-to-all-done = bf16[32,2,8,352]{3,2,1,0:T(8,128)(2,1)S(1)} async-done(((bf16[32,2,8,352]{3,2,1,0:T(8,128)(2,1)}), bf16[32,2,8,352]{3,2,1,0:T(8,128)(2,1)S(1)}, u32[]{:S(2)}, u32[]{:S(2)}) %all-to-all-start) | async-done | bytes 360480 | tf_op jit(solution)/shard_map/all_to_all | solution.py:318
  25.5 5.2 %shard_map.106.g_ref.own_ref = bf16[3,352,512]{2,1,0:T(8,128)(2,1)S(1)} custom-call(bf16[512,352]{1,0:T(8,128)(2,1)S(1)} %bitcast.51, bf16[512,352]{1,0:T(8,128)(2,1)S(1)} %bitcast.52, bf16[512,352]{1,0:T(8,128)(2,1)S(1)} %bitcast.53, bf16[512,352]{1,0:T(8,128)(2,1)S(1)} %bitcast.44), custom_call_target="tpu_custom_call" | custom-call | tf_op jit(solution)/shard_map/pallas_call | solution.py:46
  30.8 6.0 %shard_map.107 = (bf16[16,16,1408]{2,1,0:T(8,128)(2,1)}, f32[16,16,1408]{2,1,0:T(8,128)S(1)}) custom-call(s32[1]{0:T(128)} %bitcast.13.where_ref, bf16[3,352,512]{2,1,0:T(8,128)(2,1)S(1)} %shard_map.106.g_ref.own_ref, bf16[3,1408,352]{2,1,0:T(8,128)(2,1)} %copy-done), custom_call_target="tpu_custom_call" | custom-call | tf_op jit(solution)/shard_map/pallas_call | solution.py:135
  36.8 0.0 collective-permute-start.1
  36.8 1.0 collective-permute-start
  37.8 2.6 %all-to-all-start.1 = ((bf16[32,16,352]{2,1,0:T(8,128)(2,1)}), bf16[32,16,352]{2,1,0:T(8,128)(2,1)S(1)}, u32[]{:S(2)}, u32[]{:S(2)}) async-start(bf16[32,16,352]{2,1,0:T(8,128)(2,1)} %shard_map.104), calls=%async_computation.1 | async-start | bytes 786432 | tf_op jit(solution)/shard_map/all_to_all | solution.py:326
  40.4 0.0 collective-permute-done.1
  40.4 2.0 %shard_map.108 = (bf16[8,16,1408]{2,1,0:T(8,128)(2,1)}, f32[8,16,1408]{2,1,0:T(8,128)S(1)}) custom-call(s32[1]{0:T(128)} %bitcast.14.chip_ref, f32[8,2,16,1408]{3,2,1,0:T(8,128)S(1)} %bitcast.47, bf16[8,2,16,1408]{3,2,1,0:T(8,128)(2,1)} %bitcast.16.come_ref), custom_call_target="tpu_custom_call" | custom-call | tf_op jit(solution)/shard_map/pallas_call | solution.py:165
  42.4 0.9 copy-done.2
  43.2 1.6 %collective-permute-start.2 = (bf16[8,16,1408]{2,1,0:T(8,128)(2,1)}, bf16[8,16,1408]{2,1,0:T(8,128)(2,1)S(1)}, u32[]{:S(2)}, u32[]{:S(2)}) collective-permute-start(bf16[8,16,1408]{2,1,0:T(8,128)(2,1)} %get-tuple-element.24), channel_id=1, source_target_pairs={{0,2},{1,3},{2,0},{3,1},{4,6},{5,7},{6,4},{7,5},{8,10},{9,11},{10,... | collective-permute-start | bytes 1081352 | tf_op jit(solution)/shard_map/ppermute | solution.py:310
  44.9 22.4 %all-to-all-done.1 = bf16[32,16,352]{2,1,0:T(8,128)(2,1)S(1)} async-done(((bf16[32,16,352]{2,1,0:T(8,128)(2,1)}), bf16[32,16,352]{2,1,0:T(8,128)(2,1)S(1)}, u32[]{:S(2)}, u32[]{:S(2)}) %all-to-all-start.1) | async-done | bytes 360480 | tf_op jit(solution)/shard_map/all_to_all | solution.py:326
  67.3 0.5 collective-permute-start.6
  67.8 0.0 collective-permute-done.2.come_ref
  67.8 1.1 copy-done.3
  68.9 0.1 shard_map.109
  69.0 0.8 collective-permute-start.3
  69.8 1.3 collective-permute-start.4
  71.1 2.4 %collective-permute-start.5 = (bf16[2,16,1408]{2,1,0:T(8,128)(2,1)S(1)}, bf16[2,16,1408]{2,1,0:T(8,128)(2,1)S(1)}, u32[]{:S(2)}, u32[]{:S(2)}) collective-permute-start(bf16[2,16,1408]{2,1,0:T(8,128)(2,1)S(1)} %get-tuple-element.34), channel_id=1, source_target_pairs={{0,24},{4,28},{8,16},{12,20},{16,8},{20,12},{24,0},{28,4},{1,25},{... | collective-permute-start | bytes 270344 | tf_op jit(solution)/shard_map/ppermute | solution.py:310
  73.4 4.8 %collective-permute-done.6.theirs_ref = bf16[512,352]{1,0:T(8,128)(2,1)S(1)} collective-permute-done((bf16[512,352]{1,0:T(8,128)(2,1)S(1)}, bf16[512,352]{1,0:T(8,128)(2,1)S(1)}, u32[]{:S(2)}, u32[]{:S(2)}) %collective-permute-start.6) | collective-permute-done | bytes 360480 | tf_op jit(solution)/shard_map/ppermute | solution.py:310
  78.3 0.0 collective-permute-start.8
  78.3 0.0 collective-permute-done.other_ref
  78.3 0.0 collective-permute-done.3
  78.3 1.2 collective-permute-done.4
  79.5 0.0 collective-permute-done.5
  79.5 0.0 collective-permute-start.9
  79.5 1.4 %collective-permute-done.8.own_core_ref = bf16[3,352,512]{2,1,0:T(8,128)(2,1)S(1)} collective-permute-done((bf16[3,352,512]{2,1,0:T(8,128)(2,1)S(1)}, bf16[3,352,512]{2,1,0:T(8,128)(2,1)S(1)}, u32[]{:S(2)}, u32[]{:S(2)}) %collective-permute-start.8) | collective-permute-done | bytes 1081376 | tf_op jit(solution)/shard_map/ppermute | solution.py:310
  81.0 1.8 %collective-permute-done.9.other_core_ref = bf16[3,352,512]{2,1,0:T(8,128)(2,1)S(1)} collective-permute-done((bf16[3,352,512]{2,1,0:T(8,128)(2,1)}, bf16[3,352,512]{2,1,0:T(8,128)(2,1)S(1)}, u32[]{:S(2)}, u32[]{:S(2)}) %collective-permute-start.9) | collective-permute-done | bytes 1081376 | tf_op jit(solution)/shard_map/ppermute | solution.py:310
  82.7 5.3 %shard_map.111 = bf16[8,44,2112]{2,1,0:T(8,128)(2,1)} custom-call(s32[1]{0:T(128)} %bitcast.14.chip_ref, bf16[512,352]{1,0:T(8,128)(2,1)S(1)} %bitcast.46, bf16[512,352]{1,0:T(8,128)(2,1)S(1)} %collective-permute-done.6.theirs_ref, bf16[3,352,512]{2,1,0:T(8,128)(2,1)S(1)} %shard_map.106.g_ref.own_ref, bf16[3,352,512]{2,1,0:T(8,128)(2,1)} %collective-permute-done.other_ref, ...), custom_call_target="tpu_custom_call" | custom-call | tf_op jit(solution)/shard_map/pallas_call | solution.py:213
  88.0 3.7 %all-to-all-start.2 = ((bf16[8,44,2112]{2,1,0:T(8,128)(2,1)}), bf16[8,44,2112]{2,1,0:T(8,128)(2,1)S(1)}, u32[]{:S(2)}, u32[]{:S(2)}) async-start(bf16[8,44,2112]{2,1,0:T(8,128)(2,1)} %shard_map.111), calls=%async_computation.2 | async-start | bytes 3342336 | tf_op jit(solution)/shard_map/all_to_all | solution.py:354
  91.8 0.1 pad_maximum_fusion
  91.9 1.1 collective-permute-start.7
  93.0 5.6 %collective-permute-done.7.come_ref = bf16[4,16,1408]{2,1,0:T(8,128)(2,1)S(1)} collective-permute-done((bf16[4,16,1408]{2,1,0:T(8,128)(2,1)S(1)}, bf16[4,16,1408]{2,1,0:T(8,128)(2,1)S(1)}, u32[]{:S(2)}, u32[]{:S(2)}) %collective-permute-start.7) | collective-permute-done | bytes 180256 | tf_op jit(solution)/shard_map/ppermute | solution.py:310
  98.5 1.3 %shard_map.110 = bf16[128,1408]{1,0:T(8,128)(2,1)} custom-call(s32[1]{0:T(128)} %bitcast.tm_ref, bf16[4,16,1408]{2,1,0:T(8,128)(2,1)S(1)} %get-tuple-element.33.stay_ref, bf16[4,16,1408]{2,1,0:T(8,128)(2,1)S(1)} %collective-permute-done.7.come_ref, bf16[128,1408]{1,0:T(8,128)(2,1)S(1)} %bitcast.49, bf16[128,1408]{1,0:T(8,128)(2,1)S(1)} %bitcast.55, ...), custom_call_target="tpu_custom_call" | custom-call | tf_op jit(solution)/shard_map/pallas_call | solution.py:257
  99.9 31.5 %all-to-all-done.2 = bf16[8,44,2112]{2,1,0:T(8,128)(2,1)S(1)} async-done(((bf16[8,44,2112]{2,1,0:T(8,128)(2,1)}), bf16[8,44,2112]{2,1,0:T(8,128)(2,1)S(1)}, u32[]{:S(2)}, u32[]{:S(2)}) %all-to-all-start.2) | async-done | bytes 1486880 | tf_op jit(solution)/shard_map/all_to_all | solution.py:354
  131.4 1.1 shard_map.112
  (15 shorter events, 0.1 us)
Async XLA Ops:
  4.0 8.4 %copy-start.8 = (f32[1408]{0:T(1024)S(1)}, f32[1408]{0:T(1024)}, u32[]{:S(2)}) copy-start(f32[1408]{0:T(1024)} %param.10) | copy-start | bytes 16900
  4.0 8.4 %copy-start.9 = (f32[1408]{0:T(1024)S(1)}, f32[1408]{0:T(1024)}, u32[]{:S(2)}) copy-start(f32[1408]{0:T(1024)} %param.11) | copy-start | bytes 16900
  5.1 20.5 %all-to-all-start = ((bf16[32,2,8,352]{3,2,1,0:T(8,128)(2,1)}), bf16[32,2,8,352]{3,2,1,0:T(8,128)(2,1)S(1)}, u32[]{:S(2)}, u32[]{:S(2)}) async-start(bf16[32,2,8,352]{3,2,1,0:T(8,128)(2,1)} %bitcast.10), calls=%async_computation | async-start | bytes 786432 | tf_op jit(solution)/shard_map/all_to_all | solution.py:318
  12.4 4.6 %copy-start.1 = (bf16[2,64,1408]{2,1,0:T(8,128)(2,1)S(1)}, bf16[2,64,1408]{2,1,0:T(8,128)(2,1)}, u32[]{:S(2)}) copy-start(bf16[2,64,1408]{2,1,0:T(8,128)(2,1)} %param.9) | copy-start | bytes 1081348
  12.4 13.1 %copy-start.4 = (bf16[64,8,352]{2,1,0:T(8,128)(2,1)S(1)}, bf16[64,8,352]{2,1,0:T(8,128)(2,1)}, u32[]{:S(2)}) copy-start(bf16[64,8,352]{2,1,0:T(8,128)(2,1)} %param.14) | copy-start | bytes 1081348
  12.4 13.1 %copy-start.5 = (bf16[64,8,352]{2,1,0:T(8,128)(2,1)S(1)}, bf16[64,8,352]{2,1,0:T(8,128)(2,1)}, u32[]{:S(2)}) copy-start(bf16[64,8,352]{2,1,0:T(8,128)(2,1)} %param.15) | copy-start | bytes 1081348
  12.4 13.1 %copy-start.6 = (bf16[64,8,352]{2,1,0:T(8,128)(2,1)S(1)}, bf16[64,8,352]{2,1,0:T(8,128)(2,1)}, u32[]{:S(2)}) copy-start(bf16[64,8,352]{2,1,0:T(8,128)(2,1)} %param.16) | copy-start | bytes 1081348
  15.3 1.7 %copy-start = (bf16[3,1408,352]{2,1,0:T(8,128)(2,1)}, bf16[3,1408,352]{2,1,0:T(8,128)(2,1)S(1)}, u32[]{:S(2)}) copy-start(bf16[3,1408,352]{2,1,0:T(8,128)(2,1)S(1)} %shard_map.105.w_ref) | copy-start | bytes 8921092
  36.8 3.6 %collective-permute-start.1 = (bf16[16,16,1408]{2,1,0:T(8,128)(2,1)}, bf16[16,16,1408]{2,1,0:T(8,128)(2,1)}, u32[]{:S(2)}, u32[]{:S(2)}) collective-permute-start(bf16[16,16,1408]{2,1,0:T(8,128)(2,1)} %get-tuple-element.22), channel_id=1, source_target_pairs={{0,1},{1,0},{2,3},{3,2},{4,5},{5,4},{6,7},{7,6},{8,9},{9,8},{10,11... | collective-permute-start | bytes 2162696 | tf_op jit(solution)/shard_map/ppermute | solution.py:310
  36.8 41.5 %collective-permute-start = (bf16[3,352,512]{2,1,0:T(8,128)(2,1)S(1)}, bf16[3,352,512]{2,1,0:T(8,128)(2,1)}, u32[]{:S(2)}, u32[]{:S(2)}) collective-permute-start(bf16[3,352,512]{2,1,0:T(8,128)(2,1)S(1)} %shard_map.106.g_ref.own_ref), channel_id=1, source_target_pairs={{0,4},{4,0},{8,12},{12,8},{16,20},{20,16},{24,28},{28,24},{1,5},{5... | collective-permute-start | bytes 3244040 | tf_op jit(solution)/shard_map/ppermute | solution.py:310
  37.8 29.5 %all-to-all-start.1 = ((bf16[32,16,352]{2,1,0:T(8,128)(2,1)}), bf16[32,16,352]{2,1,0:T(8,128)(2,1)S(1)}, u32[]{:S(2)}, u32[]{:S(2)}) async-start(bf16[32,16,352]{2,1,0:T(8,128)(2,1)} %shard_map.104), calls=%async_computation.1 | async-start | bytes 786432 | tf_op jit(solution)/shard_map/all_to_all | solution.py:326
  42.4 0.9 copy-start.2
  43.2 24.5 %collective-permute-start.2 = (bf16[8,16,1408]{2,1,0:T(8,128)(2,1)}, bf16[8,16,1408]{2,1,0:T(8,128)(2,1)S(1)}, u32[]{:S(2)}, u32[]{:S(2)}) collective-permute-start(bf16[8,16,1408]{2,1,0:T(8,128)(2,1)} %get-tuple-element.24), channel_id=1, source_target_pairs={{0,2},{1,3},{2,0},{3,1},{4,6},{5,7},{6,4},{7,5},{8,10},{9,11},{10,... | collective-permute-start | bytes 1081352 | tf_op jit(solution)/shard_map/ppermute | solution.py:310
  67.3 11.0 %collective-permute-start.6 = (bf16[512,352]{1,0:T(8,128)(2,1)S(1)}, bf16[512,352]{1,0:T(8,128)(2,1)S(1)}, u32[]{:S(2)}, u32[]{:S(2)}) collective-permute-start(bf16[512,352]{1,0:T(8,128)(2,1)S(1)} %bitcast.45), channel_id=1, source_target_pairs={{0,2},{1,3},{2,0},{3,1},{4,6},{5,7},{6,4},{7,5},{8,10},{9,11},{10,... | collective-permute-start | bytes 1081352 | tf_op jit(solution)/shard_map/ppermute | solution.py:310
  67.8 1.1 copy-start.3
  69.0 9.3 %collective-permute-start.3 = (bf16[2,16,1408]{2,1,0:T(8,128)(2,1)S(1)}, bf16[2,16,1408]{2,1,0:T(8,128)(2,1)S(1)}, u32[]{:S(2)}, u32[]{:S(2)}) collective-permute-start(bf16[2,16,1408]{2,1,0:T(8,128)(2,1)S(1)} %get-tuple-element.36), channel_id=1, source_target_pairs={{0,8},{4,12},{8,0},{12,4},{16,24},{20,28},{24,16},{28,20},{1,9},{5... | collective-permute-start | bytes 270344 | tf_op jit(solution)/shard_map/ppermute | solution.py:310
  69.8 9.7 %collective-permute-start.4 = (bf16[2,16,1408]{2,1,0:T(8,128)(2,1)S(1)}, bf16[2,16,1408]{2,1,0:T(8,128)(2,1)S(1)}, u32[]{:S(2)}, u32[]{:S(2)}) collective-permute-start(bf16[2,16,1408]{2,1,0:T(8,128)(2,1)S(1)} %get-tuple-element.35), channel_id=1, source_target_pairs={{0,16},{4,20},{8,24},{12,28},{16,0},{20,4},{24,8},{28,12},{1,17},{... | collective-permute-start | bytes 270344 | tf_op jit(solution)/shard_map/ppermute | solution.py:310
  71.1 8.4 %collective-permute-start.5 = (bf16[2,16,1408]{2,1,0:T(8,128)(2,1)S(1)}, bf16[2,16,1408]{2,1,0:T(8,128)(2,1)S(1)}, u32[]{:S(2)}, u32[]{:S(2)}) collective-permute-start(bf16[2,16,1408]{2,1,0:T(8,128)(2,1)S(1)} %get-tuple-element.34), channel_id=1, source_target_pairs={{0,24},{4,28},{8,16},{12,20},{16,8},{20,12},{24,0},{28,4},{1,25},{... | collective-permute-start | bytes 270344 | tf_op jit(solution)/shard_map/ppermute | solution.py:310
  78.3 2.7 %collective-permute-start.8 = (bf16[3,352,512]{2,1,0:T(8,128)(2,1)S(1)}, bf16[3,352,512]{2,1,0:T(8,128)(2,1)S(1)}, u32[]{:S(2)}, u32[]{:S(2)}) collective-permute-start(bf16[3,352,512]{2,1,0:T(8,128)(2,1)S(1)} %shard_map.106.g_ref.own_ref), channel_id=1, source_target_pairs={{0,1},{1,0},{2,3},{3,2},{4,5},{5,4},{6,7},{7,6},{8,9},{9,8},{10,11... | collective-permute-start | bytes 3244040 | tf_op jit(solution)/shard_map/ppermute | solution.py:310
  79.5 3.2 %collective-permute-start.9 = (bf16[3,352,512]{2,1,0:T(8,128)(2,1)}, bf16[3,352,512]{2,1,0:T(8,128)(2,1)S(1)}, u32[]{:S(2)}, u32[]{:S(2)}) collective-permute-start(bf16[3,352,512]{2,1,0:T(8,128)(2,1)} %collective-permute-done.other_ref), channel_id=1, source_target_pairs={{0,1},{1,0},{2,3},{3,2},{4,5},{5,4},{6,7},{7,6},{8,9},{9,8},{10,11... | collective-permute-start | bytes 3244040 | tf_op jit(solution)/shard_map/ppermute | solution.py:310
  88.0 10.5 %copy-start.7 = (bf16[2,64,1408]{2,1,0:T(8,128)(2,1)S(1)}, bf16[2,64,1408]{2,1,0:T(8,128)(2,1)}, u32[]{:S(2)}) copy-start(bf16[2,64,1408]{2,1,0:T(8,128)(2,1)} %param.17) | copy-start | bytes 1081348
  88.0 43.3 %all-to-all-start.2 = ((bf16[8,44,2112]{2,1,0:T(8,128)(2,1)}), bf16[8,44,2112]{2,1,0:T(8,128)(2,1)S(1)}, u32[]{:S(2)}, u32[]{:S(2)}) async-start(bf16[8,44,2112]{2,1,0:T(8,128)(2,1)} %shard_map.111), calls=%async_computation.2 | async-start | bytes 3342336 | tf_op jit(solution)/shard_map/all_to_all | solution.py:354
  91.9 6.7 %collective-permute-start.7 = (bf16[4,16,1408]{2,1,0:T(8,128)(2,1)S(1)}, bf16[4,16,1408]{2,1,0:T(8,128)(2,1)S(1)}, u32[]{:S(2)}, u32[]{:S(2)}) collective-permute-start(bf16[4,16,1408]{2,1,0:T(8,128)(2,1)S(1)} %get-tuple-element.32), channel_id=1, source_target_pairs={{0,4},{4,0},{8,12},{12,8},{16,20},{20,16},{24,28},{28,24},{1,5},{5... | collective-permute-start | bytes 540680 | tf_op jit(solution)/shard_map/ppermute | solution.py:310

commit v6 on v5

--- a/solution.py
+++ b/solution.py
@@ -50,33 +50,80 @@
     )(query, key, value, grad)
 
 
-def norm_kernel(x_ref, gain_ref, bias_ref, out_ref, *, n_pair, n_chip, columns, own_rows, t_dev):
-    width = x_ref.shape[1]
-    rows = x_ref[...].astype(F32)
+def first_kernel(
+    gain_ref, bias_ref, x_ref, grad_ref, w_ref, out_ref, x_buf, grad_buf, w_buf, sem, *, n_pair, columns, own_rows, t_dev
+):
+    n_rows, width = x_buf.shape
+    heads, part, _ = w_buf.shape
+    patches = n_rows // t_dev
+    copies = [
+        pltpu.make_async_copy(x_ref, x_buf, sem.at[0]),
+        pltpu.make_async_copy(grad_ref, grad_buf, sem.at[1]),
+    ] + [
+        pltpu.make_async_copy(w_ref.at[pl.ds(j * part, part), :], w_buf.at[j], sem.at[2 + j])
+        for j in range(heads)
+    ]
+    for copy in copies:
+        copy.start()
+
+    def pick(values, at):
+        pieces = [values[t * patches + at : t * patches + at + columns] for t in range(t_dev)]
+        return jnp.concatenate(pieces, axis=0).astype(BF)
+
+    copies[0].wait()
+    rows = x_buf[...].astype(F32)
     centered = rows - jnp.mean(rows, axis=-1, keepdims=True)
     variance = jnp.mean(centered * centered, axis=-1, keepdims=True)
     norm = centered * lax.rsqrt(variance + 1e-06) * gain_ref[...] + bias_ref[...]
-    patches = x_ref.shape[0] // t_dev
     for y in range(2):
         for c in range(2):
-            starts = [((2 * z + y) * n_chip + x) * 2 * own_rows + c * own_rows for z in range(n_pair) for x in range(n_chip)]
-            part = jnp.concatenate([norm[:, s : s + own_rows] for s in starts], axis=1)
+            starts = [
+                (((2 * z + y) * 2 + x) * 2 + c) * own_rows for z in range(n_pair) for x in range(2)
+            ]
+            quarter = jnp.concatenate([norm[:, at : at + own_rows] for at in starts], axis=1)
             for z in range(n_pair):
-                for slot in range(2):
-                    at = (2 * z + (y ^ slot)) * columns
-                    piece = jnp.concatenate([part[t * patches + at : t * patches + at + columns] for t in range(t_dev)], axis=0).astype(BF)
-                    out_ref[((2 * z + y) * 2 + slot) * 2 + c] = piece
-def norm_send(tokens, gain, bias, n_pair, n_chip, columns, own_rows, t_dev):
-    devices = 4 * n_pair * n_chip
-    return pl.pallas_call(functools.partial(norm_kernel,n_pair=n_pair,n_chip=n_chip,columns=columns,own_rows=own_rows,t_dev=t_dev),
-        out_shape=jax.ShapeDtypeStruct((devices,t_dev*columns,tokens.shape[1]//4),BF),compiler_params=ROOM)(tokens,gain[None],bias[None])
-
-def weights_kernel(where_ref, w_ref, out_ref, win_ref, sem, *, n_patch):
+                for x in range(2):
+                    out_ref[((2 * z + y) * 2 + x) * 2 + c, 1] = pick(
+                        quarter, (2 * z + (y ^ x)) * columns
+                    )
+    copies[1].wait()
+    for j in range(heads):
+        copies[2 + j].wait()
+        d_attn = lax.dot_general(grad_buf[...], w_buf[j], COLS, preferred_element_type=F32)
+        for tm in range(2 * n_pair):
+            out_ref[tm * heads + j, 0] = pick(d_attn, tm * columns)
+
+
+def first_product(tokens, gain, bias, grads, w_out, n_pair, columns, own_rows, t_dev):
+    n_rows, width = tokens.shape
+    heads = 4
+    part = width // heads
+    line = pl.BlockSpec((1, width), lambda i: (0, 0))
+    shape = (2 * heads * n_pair, 2, t_dev * columns, part)
+    return pl.pallas_call(
+        functools.partial(
+            first_kernel, n_pair=n_pair, columns=columns, own_rows=own_rows, t_dev=t_dev
+        ),
+        grid=(1,),
+        in_specs=[line, line] + [pl.BlockSpec(memory_space=pl.ANY)] * 3,
+        out_specs=pl.BlockSpec(shape, lambda i: (0, 0, 0, 0)),
+        out_shape=jax.ShapeDtypeStruct(shape, BF),
+        scratch_shapes=[
+            pltpu.VMEM((n_rows, width), BF),
+            pltpu.VMEM((n_rows, width), BF),
+            pltpu.VMEM((heads, part, width), BF),
+            pltpu.SemaphoreType.DMA((2 + heads,)),
+        ],
+        compiler_params=ROOM,
+    )(gain[None], bias[None], tokens, grads, w_out)
+
+
+def weights_kernel(chip_ref, w_ref, out_ref, win_ref, sem, *, n_chip):
     kinds, width, part = out_ref.shape
     window = win_ref.shape[2]
-    patch = where_ref[0]
-    starts = [min(part * j // 128 * 128, width - window) for j in range(n_patch)]
-    start = sum(jnp.where(patch == j, at, 0) for j, at in enumerate(starts))
+    chip = chip_ref[0]
+    starts = [min(part * j // 128 * 128, width - window) for j in range(n_chip)]
+    start = sum(jnp.where(chip == j, at, 0) for j, at in enumerate(starts))
     copies = [
         pltpu.make_async_copy(
             w_ref.at[:, pl.ds(pl.multiple_of(c * width + start, 128), window)], win_ref.at[c], sem.at[c]
@@ -87,21 +134,21 @@
         copy.start()
     for copy in copies:
         copy.wait()
-    for j in range(n_patch):
-
-        @pl.when(patch == j)
+    for j in range(n_chip):
+
+        @pl.when(chip == j)
         def _(j=j):
             before = part * j - starts[j]
             for c in range(kinds):
                 out_ref[c] = win_ref[c, :, before : before + part]
 
 
-def own_weights(w_qkv, patch, n_patch):
+def own_weights(w_qkv, chip, n_chip):
     width = w_qkv.shape[0]
-    kinds, part = w_qkv.shape[1] // width, width // n_patch
-    window = -(-(part + 96) // 128) * 128
-    return pl.pallas_call(
-        functools.partial(weights_kernel, n_patch=n_patch),
+    kinds, part = w_qkv.shape[1] // width, width // n_chip
+    window = -(-(part + 64) // 128) * 128
+    return pl.pallas_call(
+        functools.partial(weights_kernel, n_chip=n_chip),
         grid_spec=pltpu.PrefetchScalarGridSpec(
             num_scalar_prefetch=1,
             grid=(1,),
@@ -114,65 +161,55 @@
         ),
         out_shape=jax.ShapeDtypeStruct((kinds, width, part), BF),
         compiler_params=ROOM,
-    )(patch[None], w_qkv)
-
-
-def share_kernel(where_ref, g_ref, w_ref, leave_ref, stay_ref, acc_ref):
-    core = where_ref[0] % 2
+    )(chip[None], w_qkv)
+
+
+def share_kernel(where_ref, own_ref, core_ref, w_ref, leave_ref, stay_ref, turn_ref):
+    patch = where_ref[0]
+    chip, core = patch // 2, patch % 2
+    kinds, part, _ = own_ref.shape
+    n, group, _ = leave_ref.shape
+    for side in range(2):
+
+        @pl.when(core == side)
+        def _(side=side):
+            for c in range(kinds):
+                for grads_ref, at in ((own_ref, side * part), (core_ref, (1 - side) * part)):
+                    rows = grads_ref[c].astype(F32).T.astype(BF)
+                    turn_ref[c, :, :, :, :, at : at + part] = rows.reshape(n, 2, 2, group, part)
+
     total = None
-    for c in range(g_ref.shape[0]):
-        one = lax.dot_general(g_ref[c], w_ref[c], CROSS, preferred_element_type=F32)
+    for c in range(kinds):
+        rows = jnp.concatenate(
+            [turn_ref[c, :, which, core].reshape(n * group, 2 * part) for which in (1 - chip, chip)],
+            axis=0,
+        )
+        one = lax.dot_general(rows, w_ref[c], COLS, preferred_element_type=F32)
         total = one if total is None else total + one
-    acc_ref[...] = total.reshape(acc_ref.shape)
-    leave_ref[...] = acc_ref[:, 1 - core].astype(BF)
-    stay_ref[...] = acc_ref[:, core]
-
-
-def share_send(grads, weights, patch, group):
+    leave_ref[...] = total[: n * group].reshape(leave_ref.shape).astype(BF)
+    stay_ref[...] = total[n * group :].reshape(stay_ref.shape)
+
+
+def share_send(grads, grads_core, weights, patch, group):
     kinds, part, n_tok = grads.shape
     width = weights.shape[1]
-    n = n_tok // (2 * group)
+    n = n_tok // (4 * group)
+    whole = pl.BlockSpec((kinds, part, n_tok), lambda i, s: (0, 0, 0))
     return pl.pallas_call(
         share_kernel,
         grid_spec=pltpu.PrefetchScalarGridSpec(
             num_scalar_prefetch=1,
             grid=(1,),
-            in_specs=[
-                pl.BlockSpec((kinds, part, n_tok), lambda i, s: (0, 0, 0)),
-                pl.BlockSpec((kinds, width, part), lambda i, s: (0, 0, 0)),
-            ],
+            in_specs=[whole, whole, pl.BlockSpec((kinds, width, 2 * part), lambda i, s: (0, 0, 0))],
             out_specs=[pl.BlockSpec((n, group, width), lambda i, s: (0, 0, 0))] * 2,
-            scratch_shapes=[pltpu.VMEM((n, 2, group, width), F32)],
+            scratch_shapes=[pltpu.VMEM((kinds, n, 2, 2, group, 2 * part), BF)],
         ),
         out_shape=[
             jax.ShapeDtypeStruct((n, group, width), BF),
             jax.ShapeDtypeStruct((n, group, width), F32),
         ],
         compiler_params=ROOM,
-    )(patch[None], grads, weights)
-
-
-def merge_kernel(chip_ref, stay_ref, come_ref, leave_ref, keep_ref):
-    chip = chip_ref[0]
-    leave_ref[...] = (stay_ref[:, 1 - chip] + come_ref[:, 1 - chip].astype(F32)).astype(BF)
-    keep_ref[...] = stay_ref[:, chip] + come_ref[:, chip].astype(F32)
-
-
-def merge(stay, come, chip):
-    n, group, width = stay.shape
-    both = pl.BlockSpec((n // 2, 2, group, width), lambda i, s: (0, 0, 0, 0))
-    half = pl.BlockSpec((n // 2, group, width), lambda i, s: (0, 0, 0))
-    return pl.pallas_call(
-        merge_kernel,
-        grid_spec=pltpu.PrefetchScalarGridSpec(
-            num_scalar_prefetch=1, grid=(1,), in_specs=[both, both], out_specs=[half, half]
-        ),
-        out_shape=[
-            jax.ShapeDtypeStruct((n // 2, group, width), BF),
-            jax.ShapeDtypeStruct((n // 2, group, width), F32),
-        ],
-        compiler_params=ROOM,
-    )(chip[None], stay.reshape(n // 2, 2, group, width), come.reshape(n // 2, 2, group, width))
+    )(patch[None], grads, grads_core, weights)
 
 
 def add_kernel(stay_ref, come_ref, out_ref):
@@ -310,39 +347,30 @@
         return lax.ppermute(values, axis, [(i, i ^ bit) for i in range(size)])
 
     grad_rows = grad_out.reshape(-1, width)
-    d_attn = jnp.einsum(
-        "to,jfo->jtf", grad_rows, w_out.reshape(n_patch, part, width), preferred_element_type=F32
-    ).astype(BF)
-    d_attn = d_attn.reshape(n_patch, t_dev, n_tm, columns, part).transpose(2, 0, 1, 3, 4)
-    d_attn, tokens = lax.optimization_barrier((d_attn, tokens))
-    d_time = lax.all_to_all(
-        d_attn.reshape(devices, t_dev, columns, part), both, 0, 0, tiled=True
-    ).reshape(n_tok, part)
-
-    quarter = width // 4
-    sent = norm_send(tokens.reshape(-1, width), ln_gain, ln_bias, n_pair, n_chip, columns, own_rows, t_dev)
-    weights = own_weights(w_qkv, patch, n_patch)
-    d_time, sent, weights = lax.optimization_barrier((d_time, sent, weights))
-    mine = lax.all_to_all(sent, both, 0, 0, tiled=True).reshape(n_tok, quarter)
+    sent = first_product(
+        tokens.reshape(-1, width), ln_gain, ln_bias, grad_rows, w_out, n_pair, columns, own_rows, t_dev
+    )
+    got = lax.all_to_all(sent, both, 0, 0, tiled=True)
+    sent, w_late = lax.optimization_barrier((sent, w_qkv))
+    weights = own_weights(w_late, patch // 2, n_chip)
+    got, weights = lax.optimization_barrier((got, weights))
+    d_time = got[:, 0].reshape(n_tok, part)
+    mine = got[:, 1].reshape(n_tok, part)
     theirs = swap(mine, "patch", n_patch, 2)
 
     saved = [values.reshape(n_tok, part) for values in (q_time, k_time, v_time)]
     grads = attend(*saved, d_time, columns)
     grads_other = swap(grads, "tm", n_tm, 1)
-    leave, stay = share_send(grads, weights, patch, t_dev * columns)
-    leave, stay = merge(stay, swap(leave, "patch", n_patch, 1), patch // 2)
+    grads_core = swap(grads, "patch", n_patch, 1)
+
+    leave, stay = share_send(grads, grads_core, weights, patch, t_dev * columns)
     share = pl.pallas_call(
         add_kernel, out_shape=jax.ShapeDtypeStruct(leave.shape, BF), compiler_params=ROOM
     )(stay, swap(leave, "patch", n_patch, 2))
     share = share.reshape((n_pair, 2) + share.shape[1:])
-    spread = [
-        swap(lax.dynamic_index_in_dim(share, (tm // 2) ^ n, 0, keepdims=False), "tm", n_tm, 2 * n)
-        if n
-        else lax.dynamic_index_in_dim(share, tm // 2, 0, keepdims=False)
-        for n in range(n_pair)
-    ]
-    grads_other, spread, theirs = lax.optimization_barrier((grads_other, spread, theirs))
-    grads_core = swap(grads, "patch", n_patch, 1)
+    spread = [lax.dynamic_index_in_dim(share, (tm // 2) ^ n, 0, keepdims=False) for n in range(n_pair)]
+    spread = spread[:1] + [swap(spread[n], "tm", n_tm, 2 * n) for n in range(1, n_pair)]
+    grads_other, theirs, spread = lax.optimization_barrier((grads_other, theirs, spread))
     grads_other_core = swap(grads_other, "patch", n_patch, 1)
 
     factor = 1.0 / math.sqrt(frames * patches)
@@ -351,16 +379,11 @@
         for y in range(2)
         for c in range(2)
     ]
-    pieces = lax.all_to_all(
-        product(
-            patch // 2, mine, theirs, grads, grads_other, grads_core, grads_other_core, own_rows, factor
-        ),
-        both,
-        0,
-        0,
-        axis_index_groups=groups,
-        tiled=True,
+    partial = product(
+        patch // 2, mine, theirs, grads, grads_other, grads_core, grads_other_core, own_rows, factor
     )
+    partial, spread = lax.optimization_barrier((partial, spread))
+    pieces = lax.all_to_all(partial, both, 0, 0, axis_index_groups=groups, tiled=True)
     grad_w_qkv = final_sum(pieces.reshape(n_pair, n_chip, own_rows, 6 * part), core, part, 3)
 
     spread = jnp.stack(spread)

time: 133 us -> 130 us (0.977)
  Pallas kernels: 25.3 us -> 32.1 us
  waiting for transfers between devices: 75.9 us -> 70.6 us
  matrix products: 3.37 us -> 0 us
  starting transfers between devices: 22.3 us -> 20.2 us
    all_to_all x3 -> x2, waiting for transfers between devices: 61.1 us -> 45.9 us  [the longest x1 31.5 us: per_device(): lax.all_to_all(partial, both, 0, 0, axis_index_groups=groups, tiled=True)]
    ppermute x10 -> x9, waiting for transfers between devices: 14.8 us -> 24.7 us  [swap(): return lax.ppermute(values, axis, [(i, i ^ bit) for i in range(size)])]
    pallas_call x3 -> x2, Pallas kernels: 6.19 us -> 11.3 us  [the longest x1 6.08 us: own_weights(): pl.pallas_call(functools.partial(weights_kernel, n_chip=n_chip), grid_spe...]
    dot_general x1 -> x0, matrix products: 3.37 us -> none  [per_device(): jnp.einsum('to,jfo->jtf', grad_rows, w_out.reshape(n_patch, part, width),...]
    all_to_all x3 -> x2, starting transfers between devices: 13.6 us -> 11 us  [the longest x1 7.3 us: per_device(): got = lax.all_to_all(sent, both, 0, 0, tiled=True)]
    broadcast_in_dim x2, local copies, waits for them, and re-layouts: 0.01 us -> 1.4 us  [the longest x1 0.7 us: first_product(): gain[None]]
    ppermute x10 -> x9, starting transfers between devices: 8.65 us -> 9.18 us  [swap(): return lax.ppermute(values, axis, [(i, i ^ bit) for i in range(size)])]
    unnamed x20 -> x16, local copies, waits for them, and re-layouts: 3.66 us -> 4.12 us
  transfers between devices with their start and end apart: 13 -> 11, of which waited for: 8 -> 8; matrix products, arithmetic and copies ran while one was open for 0% -> 0% of each run, Pallas kernels for 6% -> 12%
where the time goes in v6:
time: 130 us
  waiting for transfers between devices  70.6 us (54%)
  Pallas kernels  32.1 us (25%)
  starting transfers between devices  20.2 us (16%)
  local copies, waits for them, and re-layouts  5.68 us (4%)
    all_to_all x1, waiting for transfers between devices, per_device(): lax.all_to_all(partial, both, 0, 0, axis_index_groups=groups, tiled=True)  31.5 us
    ppermute x9, waiting for transfers between devices, swap(): return lax.ppermute(values, axis, [(i, i ^ bit) for i in range(size)])  24.7 us
    all_to_all x1, waiting for transfers between devices, per_device(): got = lax.all_to_all(sent, both, 0, 0, tiled=True)  14.5 us
    ppermute x9, starting transfers between devices, swap(): return lax.ppermute(values, axis, [(i, i ^ bit) for i in range(size)])  9.18 us
    all_to_all x1, starting transfers between devices, per_device(): got = lax.all_to_all(sent, both, 0, 0, tiled=True)  7.3 us
    pallas_call x1, Pallas kernels, share_send(): pl.pallas_call(share_kernel, grid_spec=pltpu.PrefetchScalarGridSpec(num_s...  6.87 us
    pallas_call x1, Pallas kernels, own_weights(): pl.pallas_call(functools.partial(weights_kernel, n_chip=n_chip), grid_spe...  6.08 us
    pallas_call x1, Pallas kernels, product(): pl.pallas_call(functools.partial(product_kernel, factor=factor), grid_spe...  5.23 us
  transfers between devices with their start and end apart: 11, of which 8 were waited for; matrix products, arithmetic and copies ran while one was open for 0% of the time, Pallas kernels for 12%

profile of v6, /device:TPU:0, one launch (start us, length us, event | category | flops | bytes accessed | tf_op | source)
XLA Modules:
  0.0 129.5 jit_solution(4438907534703886879)
XLA Ops:
  0.6 0.7 broadcast_in_dim.22.gain_ref
  1.3 0.7 broadcast_in_dim.23.bias_ref
  2.0 0.0 copy-start
  2.0 2.1 %copy-done = bf16[1408,1408]{1,0:T(8,128)(2,1)S(1)} copy-done((bf16[1408,1408]{1,0:T(8,128)(2,1)S(1)}, bf16[1408,1408]{1,0:T(8,128)(2,1)}, u32[]{:S(2)}) %copy-start) | copy-done | bytes 3964952
  4.2 0.0 copy-start.1
  4.2 1.0 copy-done.1
  5.1 0.0 copy-start.3
  5.1 1.0 copy-done.3
  6.1 5.2 %shard_map.104 = bf16[32,2,16,352]{3,2,1,0:T(8,128)(2,1)} custom-call(f32[1,1408]{1,0:T(1,128)S(1)} %broadcast_in_dim.22.gain_ref, f32[1,1408]{1,0:T(1,128)S(1)} %broadcast_in_dim.23.bias_ref, bf16[128,1408]{1,0:T(8,128)(2,1)S(1)} %bitcast.35, bf16[128,1408]{1,0:T(8,128)(2,1)S(1)} %bitcast.37, bf16[1408,1408]{1,0:T(8,128)(2,1)S(1)} %copy-done), custom_call_target="tpu_custom_call" | custom-call | tf_op jit(solution)/shard_map/pallas_call | solution.py:103
  11.3 7.3 %all-to-all-start = ((bf16[32,2,16,352]{3,2,1,0:T(8,128)(2,1)}), bf16[32,2,16,352]{3,2,1,0:T(8,128)(2,1)S(1)}, u32[]{:S(2)}, u32[]{:S(2)}) async-start(bf16[32,2,16,352]{3,2,1,0:T(8,128)(2,1)} %shard_map.104), calls=%async_computation | async-start | bytes 1572864 | tf_op jit(solution)/shard_map/all_to_all | solution.py:353
  18.7 6.1 %shard_map.105.w_ref = bf16[3,1408,704]{2,1,0:T(8,128)(2,1)} custom-call(s32[1]{0:T(128)} %bitcast.1.chip_ref, bf16[1408,4224]{1,0:T(8,128)(2,1)} %w_ref.2), custom_call_target="tpu_custom_call" | custom-call | tf_op jit(solution)/shard_map/pallas_call | solution.py:150
  24.8 0.0 copy-start.5
  24.8 0.0 copy-start.6
  24.8 0.0 copy-start.7
  24.8 14.5 %all-to-all-done = bf16[32,2,16,352]{3,2,1,0:T(8,128)(2,1)S(1)} async-done(((bf16[32,2,16,352]{3,2,1,0:T(8,128)(2,1)}), bf16[32,2,16,352]{3,2,1,0:T(8,128)(2,1)S(1)}, u32[]{:S(2)}, u32[]{:S(2)}) %all-to-all-start) | async-done | bytes 720928 | tf_op jit(solution)/shard_map/all_to_all | solution.py:353
  39.3 0.1 fusion
  39.4 0.0 copy-done.5
  39.4 0.0 copy-done.6
  39.4 0.0 copy-done.7
  39.4 5.2 %shard_map.106.own_ref = bf16[3,352,512]{2,1,0:T(8,128)(2,1)S(1)} custom-call(bf16[512,352]{1,0:T(8,128)(2,1)S(1)} %bitcast.39, bf16[512,352]{1,0:T(8,128)(2,1)S(1)} %bitcast.40, bf16[512,352]{1,0:T(8,128)(2,1)S(1)} %bitcast.41, bf16[512,352]{1,0:T(8,128)(2,1)S(1)} %bitcast.31), custom_call_target="tpu_custom_call" | custom-call | tf_op jit(solution)/shard_map/pallas_call | solution.py:46
  44.6 0.1 collective-permute-start.2
  44.7 1.6 %collective-permute-start = (bf16[3,352,512]{2,1,0:T(8,128)(2,1)S(1)}, bf16[3,352,512]{2,1,0:T(8,128)(2,1)}, u32[]{:S(2)}, u32[]{:S(2)}) collective-permute-start(bf16[3,352,512]{2,1,0:T(8,128)(2,1)S(1)} %shard_map.106.own_ref), channel_id=1, source_target_pairs={{0,4},{4,0},{8,12},{12,8},{16,20},{20,16},{24,28},{28,24},{1,5},{5... | collective-permute-start | bytes 3244040 | tf_op jit(solution)/shard_map/ppermute | solution.py:347
  46.3 1.1 collective-permute-done.2.core_ref.own_core_ref
  47.4 6.9 %shard_map.107 = (bf16[8,16,1408]{2,1,0:T(8,128)(2,1)}, f32[8,16,1408]{2,1,0:T(8,128)S(1)}) custom-call(s32[1]{0:T(128)} %bitcast.9.where_ref, bf16[3,352,512]{2,1,0:T(8,128)(2,1)S(1)} %shard_map.106.own_ref, bf16[3,352,512]{2,1,0:T(8,128)(2,1)S(1)} %collective-permute-done.2.core_ref.own_core_ref, bf16[3,1408,704]{2,1,0:T(8,128)(2,1)} %shard_map.105.w_ref), custom_call_target="tpu_custom_call" | custom-call | tf_op jit(solution)/shard_map/pallas_call | solution.py:198
  54.2 1.5 %collective-permute-start.3 = (bf16[8,16,1408]{2,1,0:T(8,128)(2,1)}, bf16[8,16,1408]{2,1,0:T(8,128)(2,1)}, u32[]{:S(2)}, u32[]{:S(2)}) collective-permute-start(bf16[8,16,1408]{2,1,0:T(8,128)(2,1)} %get-tuple-element.22), channel_id=1, source_target_pairs={{0,2},{1,3},{2,0},{3,1},{4,6},{5,7},{6,4},{7,5},{8,10},{9,11},{10,... | collective-permute-start | bytes 1081352 | tf_op jit(solution)/shard_map/ppermute | solution.py:347
  55.7 0.6 collective-permute-start.1
  56.3 9.6 %collective-permute-done.3.come_ref = bf16[8,16,1408]{2,1,0:T(8,128)(2,1)} collective-permute-done((bf16[8,16,1408]{2,1,0:T(8,128)(2,1)}, bf16[8,16,1408]{2,1,0:T(8,128)(2,1)}, u32[]{:S(2)}, u32[]{:S(2)}) %collective-permute-start.3) | collective-permute-done | bytes 360480 | tf_op jit(solution)/shard_map/ppermute | solution.py:347
  65.8 1.1 shard_map.108
  66.9 1.4 %collective-permute-start.4 = (bf16[2,16,1408]{2,1,0:T(8,128)(2,1)S(1)}, bf16[2,16,1408]{2,1,0:T(8,128)(2,1)S(1)}, u32[]{:S(2)}, u32[]{:S(2)}) collective-permute-start(bf16[2,16,1408]{2,1,0:T(8,128)(2,1)S(1)} %get-tuple-element.40), channel_id=1, source_target_pairs={{0,8},{4,12},{8,0},{12,4},{16,24},{20,28},{24,16},{28,20},{1,9},{5... | collective-permute-start | bytes 270344 | tf_op jit(solution)/shard_map/ppermute | solution.py:347
  68.4 0.4 collective-permute-start.5
  68.8 2.6 %collective-permute-start.6 = (bf16[2,16,1408]{2,1,0:T(8,128)(2,1)S(1)}, bf16[2,16,1408]{2,1,0:T(8,128)(2,1)S(1)}, u32[]{:S(2)}, u32[]{:S(2)}) collective-permute-start(bf16[2,16,1408]{2,1,0:T(8,128)(2,1)S(1)} %get-tuple-element.38), channel_id=1, source_target_pairs={{0,24},{4,28},{8,16},{12,20},{16,8},{20,12},{24,0},{28,4},{1,25},{... | collective-permute-start | bytes 270344 | tf_op jit(solution)/shard_map/ppermute | solution.py:347
  71.4 2.0 %collective-permute-done.1.theirs_ref = bf16[512,352]{1,0:T(8,128)(2,1)} collective-permute-done((bf16[512,352]{1,0:T(8,128)(2,1)S(1)}, bf16[512,352]{1,0:T(8,128)(2,1)}, u32[]{:S(2)}, u32[]{:S(2)}) %collective-permute-start.1) | collective-permute-done | bytes 360480 | tf_op jit(solution)/shard_map/ppermute | solution.py:347
  73.4 0.0 collective-permute-done.other_ref
  73.4 0.0 collective-permute-done.4
  73.4 3.4 %collective-permute-done.5 = bf16[2,16,1408]{2,1,0:T(8,128)(2,1)S(1)} collective-permute-done((bf16[2,16,1408]{2,1,0:T(8,128)(2,1)S(1)}, bf16[2,16,1408]{2,1,0:T(8,128)(2,1)S(1)}, u32[]{:S(2)}, u32[]{:S(2)}) %collective-permute-start.5) | collective-permute-done | bytes 90144 | tf_op jit(solution)/shard_map/ppermute | solution.py:347
  76.9 0.0 collective-permute-done.6
  76.9 0.0 collective-permute-start.7
  76.9 2.9 %collective-permute-done.7.other_core_ref = bf16[3,352,512]{2,1,0:T(8,128)(2,1)S(1)} collective-permute-done((bf16[3,352,512]{2,1,0:T(8,128)(2,1)}, bf16[3,352,512]{2,1,0:T(8,128)(2,1)S(1)}, u32[]{:S(2)}, u32[]{:S(2)}) %collective-permute-start.7) | collective-permute-done | bytes 1081376 | tf_op jit(solution)/shard_map/ppermute | solution.py:347
  79.8 5.2 %shard_map.109 = bf16[8,44,2112]{2,1,0:T(8,128)(2,1)} custom-call(s32[1]{0:T(128)} %bitcast.1.chip_ref, bf16[512,352]{1,0:T(8,128)(2,1)S(1)} %bitcast.33, bf16[512,352]{1,0:T(8,128)(2,1)} %collective-permute-done.1.theirs_ref, bf16[3,352,512]{2,1,0:T(8,128)(2,1)S(1)} %shard_map.106.own_ref, bf16[3,352,512]{2,1,0:T(8,128)(2,1)} %collective-permute-done.other_ref, ...), custom_call_target="tpu_custom_call" | custom-call | tf_op jit(solution)/shard_map/pallas_call | solution.py:250
  85.0 3.7 %all-to-all-start.1 = ((bf16[8,44,2112]{2,1,0:T(8,128)(2,1)}), bf16[8,44,2112]{2,1,0:T(8,128)(2,1)S(1)}, u32[]{:S(2)}, u32[]{:S(2)}) async-start(bf16[8,44,2112]{2,1,0:T(8,128)(2,1)} %shard_map.109), calls=%async_computation.1 | async-start | bytes 3342336 | tf_op jit(solution)/shard_map/all_to_all | solution.py:386
  88.8 0.1 pad_maximum_fusion
  88.9 1.0 collective-permute-start.8
  89.9 5.6 %collective-permute-done.8.come_ref = bf16[4,16,1408]{2,1,0:T(8,128)(2,1)S(1)} collective-permute-done((bf16[4,16,1408]{2,1,0:T(8,128)(2,1)S(1)}, bf16[4,16,1408]{2,1,0:T(8,128)(2,1)S(1)}, u32[]{:S(2)}, u32[]{:S(2)}) %collective-permute-start.8) | collective-permute-done | bytes 180256 | tf_op jit(solution)/shard_map/ppermute | solution.py:347
  95.5 0.0 copy-done.2
  95.6 0.0 copy-done.4
  95.6 1.3 %shard_map.110 = bf16[128,1408]{1,0:T(8,128)(2,1)} custom-call(s32[1]{0:T(128)} %bitcast.tm_ref, bf16[4,16,1408]{2,1,0:T(8,128)(2,1)S(1)} %get-tuple-element.37.stay_ref, bf16[4,16,1408]{2,1,0:T(8,128)(2,1)S(1)} %collective-permute-done.8.come_ref, bf16[128,1408]{1,0:T(8,128)(2,1)S(1)} %bitcast.36, bf16[128,1408]{1,0:T(8,128)(2,1)S(1)} %bitcast.38, ...), custom_call_target="tpu_custom_call" | custom-call | tf_op jit(solution)/shard_map/pallas_call | solution.py:294
  96.9 31.5 %all-to-all-done.1 = bf16[8,44,2112]{2,1,0:T(8,128)(2,1)S(1)} async-done(((bf16[8,44,2112]{2,1,0:T(8,128)(2,1)}), bf16[8,44,2112]{2,1,0:T(8,128)(2,1)S(1)}, u32[]{:S(2)}, u32[]{:S(2)}) %all-to-all-start.1) | async-done | bytes 1486880 | tf_op jit(solution)/shard_map/all_to_all | solution.py:386
  128.4 1.1 shard_map.111
  (4 shorter events, 0.1 us)
Async XLA Ops:
  2.0 2.1 %copy-start = (bf16[1408,1408]{1,0:T(8,128)(2,1)S(1)}, bf16[1408,1408]{1,0:T(8,128)(2,1)}, u32[]{:S(2)}) copy-start(bf16[1408,1408]{1,0:T(8,128)(2,1)} %w_ref.1) | copy-start | bytes 11894788
  4.2 1.0 copy-start.1
  5.1 1.0 copy-start.3
  11.3 27.9 %all-to-all-start = ((bf16[32,2,16,352]{3,2,1,0:T(8,128)(2,1)}), bf16[32,2,16,352]{3,2,1,0:T(8,128)(2,1)S(1)}, u32[]{:S(2)}, u32[]{:S(2)}) async-start(bf16[32,2,16,352]{3,2,1,0:T(8,128)(2,1)} %shard_map.104), calls=%async_computation | async-start | bytes 1572864 | tf_op jit(solution)/shard_map/all_to_all | solution.py:353
  24.8 14.6 %copy-start.5 = (bf16[64,8,352]{2,1,0:T(8,128)(2,1)S(1)}, bf16[64,8,352]{2,1,0:T(8,128)(2,1)}, u32[]{:S(2)}) copy-start(bf16[64,8,352]{2,1,0:T(8,128)(2,1)} %param.14) | copy-start | bytes 1081348
  24.8 14.6 %copy-start.6 = (bf16[64,8,352]{2,1,0:T(8,128)(2,1)S(1)}, bf16[64,8,352]{2,1,0:T(8,128)(2,1)}, u32[]{:S(2)}) copy-start(bf16[64,8,352]{2,1,0:T(8,128)(2,1)} %param.15) | copy-start | bytes 1081348
  24.8 14.6 %copy-start.7 = (bf16[64,8,352]{2,1,0:T(8,128)(2,1)S(1)}, bf16[64,8,352]{2,1,0:T(8,128)(2,1)}, u32[]{:S(2)}) copy-start(bf16[64,8,352]{2,1,0:T(8,128)(2,1)} %param.16) | copy-start | bytes 1081348
  44.6 2.8 %collective-permute-start.2 = (bf16[3,352,512]{2,1,0:T(8,128)(2,1)S(1)}, bf16[3,352,512]{2,1,0:T(8,128)(2,1)S(1)}, u32[]{:S(2)}, u32[]{:S(2)}) collective-permute-start(bf16[3,352,512]{2,1,0:T(8,128)(2,1)S(1)} %shard_map.106.own_ref), channel_id=1, source_target_pairs={{0,1},{1,0},{2,3},{3,2},{4,5},{5,4},{6,7},{7,6},{8,9},{9,8},{10,11... | collective-permute-start | bytes 3244040 | tf_op jit(solution)/shard_map/ppermute | solution.py:347
  44.7 28.8 %collective-permute-start = (bf16[3,352,512]{2,1,0:T(8,128)(2,1)S(1)}, bf16[3,352,512]{2,1,0:T(8,128)(2,1)}, u32[]{:S(2)}, u32[]{:S(2)}) collective-permute-start(bf16[3,352,512]{2,1,0:T(8,128)(2,1)S(1)} %shard_map.106.own_ref), channel_id=1, source_target_pairs={{0,4},{4,0},{8,12},{12,8},{16,20},{20,16},{24,28},{28,24},{1,5},{5... | collective-permute-start | bytes 3244040 | tf_op jit(solution)/shard_map/ppermute | solution.py:347
  54.2 11.6 %collective-permute-start.3 = (bf16[8,16,1408]{2,1,0:T(8,128)(2,1)}, bf16[8,16,1408]{2,1,0:T(8,128)(2,1)}, u32[]{:S(2)}, u32[]{:S(2)}) collective-permute-start(bf16[8,16,1408]{2,1,0:T(8,128)(2,1)} %get-tuple-element.22), channel_id=1, source_target_pairs={{0,2},{1,3},{2,0},{3,1},{4,6},{5,7},{6,4},{7,5},{8,10},{9,11},{10,... | collective-permute-start | bytes 1081352 | tf_op jit(solution)/shard_map/ppermute | solution.py:347
  55.7 17.7 %collective-permute-start.1 = (bf16[512,352]{1,0:T(8,128)(2,1)S(1)}, bf16[512,352]{1,0:T(8,128)(2,1)}, u32[]{:S(2)}, u32[]{:S(2)}) collective-permute-start(bf16[512,352]{1,0:T(8,128)(2,1)S(1)} %bitcast.32), channel_id=1, source_target_pairs={{0,2},{1,3},{2,0},{3,1},{4,6},{5,7},{6,4},{7,5},{8,10},{9,11},{10,... | collective-permute-start | bytes 1081352 | tf_op jit(solution)/shard_map/ppermute | solution.py:347
  66.9 6.5 %collective-permute-start.4 = (bf16[2,16,1408]{2,1,0:T(8,128)(2,1)S(1)}, bf16[2,16,1408]{2,1,0:T(8,128)(2,1)S(1)}, u32[]{:S(2)}, u32[]{:S(2)}) collective-permute-start(bf16[2,16,1408]{2,1,0:T(8,128)(2,1)S(1)} %get-tuple-element.40), channel_id=1, source_target_pairs={{0,8},{4,12},{8,0},{12,4},{16,24},{20,28},{24,16},{28,20},{1,9},{5... | collective-permute-start | bytes 270344 | tf_op jit(solution)/shard_map/ppermute | solution.py:347
  68.4 8.5 %collective-permute-start.5 = (bf16[2,16,1408]{2,1,0:T(8,128)(2,1)S(1)}, bf16[2,16,1408]{2,1,0:T(8,128)(2,1)S(1)}, u32[]{:S(2)}, u32[]{:S(2)}) collective-permute-start(bf16[2,16,1408]{2,1,0:T(8,128)(2,1)S(1)} %get-tuple-element.39), channel_id=1, source_target_pairs={{0,16},{4,20},{8,24},{12,28},{16,0},{20,4},{24,8},{28,12},{1,17},{... | collective-permute-start | bytes 270344 | tf_op jit(solution)/shard_map/ppermute | solution.py:347
  68.8 8.1 %collective-permute-start.6 = (bf16[2,16,1408]{2,1,0:T(8,128)(2,1)S(1)}, bf16[2,16,1408]{2,1,0:T(8,128)(2,1)S(1)}, u32[]{:S(2)}, u32[]{:S(2)}) collective-permute-start(bf16[2,16,1408]{2,1,0:T(8,128)(2,1)S(1)} %get-tuple-element.38), channel_id=1, source_target_pairs={{0,24},{4,28},{8,16},{12,20},{16,8},{20,12},{24,0},{28,4},{1,25},{... | collective-permute-start | bytes 270344 | tf_op jit(solution)/shard_map/ppermute | solution.py:347
  76.9 2.9 %collective-permute-start.7 = (bf16[3,352,512]{2,1,0:T(8,128)(2,1)}, bf16[3,352,512]{2,1,0:T(8,128)(2,1)S(1)}, u32[]{:S(2)}, u32[]{:S(2)}) collective-permute-start(bf16[3,352,512]{2,1,0:T(8,128)(2,1)} %collective-permute-done.other_ref), channel_id=1, source_target_pairs={{0,1},{1,0},{2,3},{3,2},{4,5},{5,4},{6,7},{7,6},{8,9},{9,8},{10,11... | collective-permute-start | bytes 3244040 | tf_op jit(solution)/shard_map/ppermute | solution.py:347
  85.0 10.5 %copy-start.2 = (bf16[2,64,1408]{2,1,0:T(8,128)(2,1)S(1)}, bf16[2,64,1408]{2,1,0:T(8,128)(2,1)}, u32[]{:S(2)}) copy-start(bf16[2,64,1408]{2,1,0:T(8,128)(2,1)} %param.9) | copy-start | bytes 1081348
  85.0 10.5 %copy-start.4 = (bf16[2,64,1408]{2,1,0:T(8,128)(2,1)S(1)}, bf16[2,64,1408]{2,1,0:T(8,128)(2,1)}, u32[]{:S(2)}) copy-start(bf16[2,64,1408]{2,1,0:T(8,128)(2,1)} %param.17) | copy-start | bytes 1081348
  85.0 43.3 %all-to-all-start.1 = ((bf16[8,44,2112]{2,1,0:T(8,128)(2,1)}), bf16[8,44,2112]{2,1,0:T(8,128)(2,1)S(1)}, u32[]{:S(2)}, u32[]{:S(2)}) async-start(bf16[8,44,2112]{2,1,0:T(8,128)(2,1)} %shard_map.109), calls=%async_computation.1 | async-start | bytes 3342336 | tf_op jit(solution)/shard_map/all_to_all | solution.py:386
  88.9 6.7 %collective-permute-start.8 = (bf16[4,16,1408]{2,1,0:T(8,128)(2,1)S(1)}, bf16[4,16,1408]{2,1,0:T(8,128)(2,1)S(1)}, u32[]{:S(2)}, u32[]{:S(2)}) collective-permute-start(bf16[4,16,1408]{2,1,0:T(8,128)(2,1)S(1)} %get-tuple-element.36), channel_id=1, source_target_pairs={{0,4},{4,0},{8,12},{12,8},{16,20},{20,16},{24,28},{28,24},{1,5},{5... | collective-permute-start | bytes 540680 | tf_op jit(solution)/shard_map/ppermute | solution.py:347

commit v7 on v6

--- a/solution.py
+++ b/solution.py
@@ -50,73 +50,26 @@
     )(query, key, value, grad)
 
 
-def first_kernel(
-    gain_ref, bias_ref, x_ref, grad_ref, w_ref, out_ref, x_buf, grad_buf, w_buf, sem, *, n_pair, columns, own_rows, t_dev
-):
-    n_rows, width = x_buf.shape
-    heads, part, _ = w_buf.shape
-    patches = n_rows // t_dev
-    copies = [
-        pltpu.make_async_copy(x_ref, x_buf, sem.at[0]),
-        pltpu.make_async_copy(grad_ref, grad_buf, sem.at[1]),
-    ] + [
-        pltpu.make_async_copy(w_ref.at[pl.ds(j * part, part), :], w_buf.at[j], sem.at[2 + j])
-        for j in range(heads)
-    ]
-    for copy in copies:
-        copy.start()
-
-    def pick(values, at):
-        pieces = [values[t * patches + at : t * patches + at + columns] for t in range(t_dev)]
-        return jnp.concatenate(pieces, axis=0).astype(BF)
-
-    copies[0].wait()
-    rows = x_buf[...].astype(F32)
+def norm_kernel(x_ref, gain_ref, bias_ref, out_ref, *, n_pair, n_chip, columns, own_rows, t_dev):
+    width = x_ref.shape[1]
+    rows = x_ref[...].astype(F32)
     centered = rows - jnp.mean(rows, axis=-1, keepdims=True)
     variance = jnp.mean(centered * centered, axis=-1, keepdims=True)
     norm = centered * lax.rsqrt(variance + 1e-06) * gain_ref[...] + bias_ref[...]
+    patches = x_ref.shape[0] // t_dev
     for y in range(2):
         for c in range(2):
-            starts = [
-                (((2 * z + y) * 2 + x) * 2 + c) * own_rows for z in range(n_pair) for x in range(2)
-            ]
-            quarter = jnp.concatenate([norm[:, at : at + own_rows] for at in starts], axis=1)
+            starts = [((2 * z + y) * n_chip + x) * 2 * own_rows + c * own_rows for z in range(n_pair) for x in range(n_chip)]
+            part = jnp.concatenate([norm[:, s : s + own_rows] for s in starts], axis=1)
             for z in range(n_pair):
-                for x in range(2):
-                    out_ref[((2 * z + y) * 2 + x) * 2 + c, 1] = pick(
-                        quarter, (2 * z + (y ^ x)) * columns
-                    )
-    copies[1].wait()
-    for j in range(heads):
-        copies[2 + j].wait()
-        d_attn = lax.dot_general(grad_buf[...], w_buf[j], COLS, preferred_element_type=F32)
-        for tm in range(2 * n_pair):
-            out_ref[tm * heads + j, 0] = pick(d_attn, tm * columns)
-
-
-def first_product(tokens, gain, bias, grads, w_out, n_pair, columns, own_rows, t_dev):
-    n_rows, width = tokens.shape
-    heads = 4
-    part = width // heads
-    line = pl.BlockSpec((1, width), lambda i: (0, 0))
-    shape = (2 * heads * n_pair, 2, t_dev * columns, part)
-    return pl.pallas_call(
-        functools.partial(
-            first_kernel, n_pair=n_pair, columns=columns, own_rows=own_rows, t_dev=t_dev
-        ),
-        grid=(1,),
-        in_specs=[line, line] + [pl.BlockSpec(memory_space=pl.ANY)] * 3,
-        out_specs=pl.BlockSpec(shape, lambda i: (0, 0, 0, 0)),
-        out_shape=jax.ShapeDtypeStruct(shape, BF),
-        scratch_shapes=[
-            pltpu.VMEM((n_rows, width), BF),
-            pltpu.VMEM((n_rows, width), BF),
-            pltpu.VMEM((heads, part, width), BF),
-            pltpu.SemaphoreType.DMA((2 + heads,)),
-        ],
-        compiler_params=ROOM,
-    )(gain[None], bias[None], tokens, grads, w_out)
-
+                for slot in range(2):
+                    at = (2 * z + (y ^ slot)) * columns
+                    piece = jnp.concatenate([part[t * patches + at : t * patches + at + columns] for t in range(t_dev)], axis=0).astype(BF)
+                    out_ref[((2 * z + y) * 2 + slot) * 2 + c] = piece
+def norm_send(tokens, gain, bias, n_pair, n_chip, columns, own_rows, t_dev):
+    devices = 4 * n_pair * n_chip
+    return pl.pallas_call(functools.partial(norm_kernel,n_pair=n_pair,n_chip=n_chip,columns=columns,own_rows=own_rows,t_dev=t_dev),
+        out_shape=jax.ShapeDtypeStruct((devices,t_dev*columns,tokens.shape[1]//4),BF),compiler_params=ROOM)(tokens,gain[None],bias[None])
 
 def weights_kernel(chip_ref, w_ref, out_ref, win_ref, sem, *, n_chip):
     kinds, width, part = out_ref.shape
@@ -217,47 +170,45 @@
 
 
 def product_kernel(
-    chip_ref, mine_ref, theirs_ref, own_ref, other_ref, own_core_ref, other_core_ref, out_ref, *, factor
+    chip_ref, mine_ref, theirs_ref, own_ref, core_ref, a_ref, b_ref, a_core_ref, b_core_ref, out_ref, *, factor
 ):
-    kinds, part, n_tok = own_ref.shape
+    kinds, part, _ = own_ref.shape
     own_rows = out_ref.shape[1]
-
-    def write(norm_own, norm_other):
-        for r, (own, other) in enumerate(((own_ref, other_ref), (own_core_ref, other_core_ref))):
-            for c in range(kinds):
-                total = jnp.dot(own[c], norm_own[...], preferred_element_type=F32)
-                total += jnp.dot(other[c], norm_other[...], preferred_element_type=F32)
-                total = (total * factor).T
-                at = (r * kinds + c) * part
-                for k in range(out_ref.shape[0]):
-                    rows = total[k * own_rows : (k + 1) * own_rows]
-                    out_ref[k, :, at : at + part] = rows.astype(BF)
-
-    @pl.when(chip_ref[0] == 0)
-    def _():
-        write(mine_ref, theirs_ref)
-
-    @pl.when(chip_ref[0] == 1)
-    def _():
-        write(theirs_ref, mine_ref)
-
-
-def product(chip, mine, theirs, grads, other, core, other_core, own_rows, factor):
+    first = chip_ref[0] == 0
+    mine, theirs = mine_ref[...], theirs_ref[...]
+    norm_own = jnp.where(first, mine, theirs)
+    norm_other = jnp.where(first, theirs, mine)
+    for r, (own, other) in enumerate(
+        ((own_ref, (a_ref, b_ref)), (core_ref, (a_core_ref, b_core_ref)))
+    ):
+        for c in range(kinds):
+            second = other[0][c] if c < other[0].shape[0] else other[1][c - other[0].shape[0]]
+            total = jnp.dot(own[c], norm_own, preferred_element_type=F32)
+            total += jnp.dot(second, norm_other, preferred_element_type=F32)
+            total = (total * factor).T
+            at = (r * kinds + c) * part
+            for k in range(out_ref.shape[0]):
+                rows = total[k * own_rows : (k + 1) * own_rows]
+                out_ref[k, :, at : at + part] = rows.astype(BF)
+
+
+def product(chip, mine, theirs, grads, core, others, own_rows, factor):
     kinds, part, n_tok = grads.shape
-    norm = pl.BlockSpec(mine.shape, lambda i, s: (0, 0))
-    whole = pl.BlockSpec(grads.shape, lambda i, s: (0, 0, 0))
+    arrays = [mine, theirs, grads, core, *others]
     shape = (part // own_rows, own_rows, 2 * kinds * part)
     return pl.pallas_call(
         functools.partial(product_kernel, factor=factor),
         grid_spec=pltpu.PrefetchScalarGridSpec(
             num_scalar_prefetch=1,
             grid=(1,),
-            in_specs=[norm, norm, whole, whole, whole, whole],
+            in_specs=[
+                pl.BlockSpec(array.shape, lambda i, s, n=array.ndim: (0,) * n) for array in arrays
+            ],
             out_specs=pl.BlockSpec(shape, lambda i, s: (0, 0, 0)),
         ),
         out_shape=jax.ShapeDtypeStruct(shape, BF),
         compiler_params=ROOM,
-    )(chip[None], mine, theirs, grads, other, core, other_core)
+    )(chip[None], *arrays)
 
 
 def last_kernel(tm_ref, stay_ref, come_ref, x_ref, grad_ref, gain_ref, out_ref, *, columns, t_dev):
@@ -347,21 +298,26 @@
         return lax.ppermute(values, axis, [(i, i ^ bit) for i in range(size)])
 
     grad_rows = grad_out.reshape(-1, width)
-    sent = first_product(
-        tokens.reshape(-1, width), ln_gain, ln_bias, grad_rows, w_out, n_pair, columns, own_rows, t_dev
-    )
-    got = lax.all_to_all(sent, both, 0, 0, tiled=True)
-    sent, w_late = lax.optimization_barrier((sent, w_qkv))
+    d_attn = jnp.einsum(
+        "to,jfo->jtf", grad_rows, w_out.reshape(n_patch, part, width), preferred_element_type=F32
+    ).astype(BF)
+    d_attn = d_attn.reshape(n_patch, t_dev, n_tm, columns, part).transpose(2, 0, 1, 3, 4)
+    d_attn, token_rows, w_late = lax.optimization_barrier((d_attn, tokens.reshape(-1, width), w_qkv))
+    d_time = lax.all_to_all(
+        d_attn.reshape(devices, t_dev, columns, part), both, 0, 0, tiled=True
+    ).reshape(n_tok, part)
+
+    sent = norm_send(token_rows, ln_gain, ln_bias, n_pair, n_chip, columns, own_rows, t_dev)
     weights = own_weights(w_late, patch // 2, n_chip)
-    got, weights = lax.optimization_barrier((got, weights))
-    d_time = got[:, 0].reshape(n_tok, part)
-    mine = got[:, 1].reshape(n_tok, part)
+    d_time, sent, weights = lax.optimization_barrier((d_time, sent, weights))
+    mine = lax.all_to_all(sent, both, 0, 0, tiled=True).reshape(n_tok, width // 4)
     theirs = swap(mine, "patch", n_patch, 2)
 
     saved = [values.reshape(n_tok, part) for values in (q_time, k_time, v_time)]
     grads = attend(*saved, d_time, columns)
-    grads_other = swap(grads, "tm", n_tm, 1)
     grads_core = swap(grads, "patch", n_patch, 1)
+    grads, grads_core = lax.optimization_barrier((grads, grads_core))
+    grads_other = [swap(piece, "tm", n_tm, 1) for piece in (grads[:1], grads[1:])]
 
     leave, stay = share_send(grads, grads_core, weights, patch, t_dev * columns)
     share = pl.pallas_call(
@@ -371,7 +327,7 @@
     spread = [lax.dynamic_index_in_dim(share, (tm // 2) ^ n, 0, keepdims=False) for n in range(n_pair)]
     spread = spread[:1] + [swap(spread[n], "tm", n_tm, 2 * n) for n in range(1, n_pair)]
     grads_other, theirs, spread = lax.optimization_barrier((grads_other, theirs, spread))
-    grads_other_core = swap(grads_other, "patch", n_patch, 1)
+    grads_other += [swap(piece, "patch", n_patch, 1) for piece in grads_other]
 
     factor = 1.0 / math.sqrt(frames * patches)
     groups = [
@@ -380,7 +336,7 @@
         for c in range(2)
     ]
     partial = product(
-        patch // 2, mine, theirs, grads, grads_other, grads_core, grads_other_core, own_rows, factor
+        patch // 2, mine, theirs, grads, grads_core, grads_other, own_rows, factor
     )
     partial, spread = lax.optimization_barrier((partial, spread))
     pieces = lax.all_to_all(partial, both, 0, 0, axis_index_groups=groups, tiled=True)

time: 130 us -> 124 us (0.954)
  waiting for transfers between devices: 70.6 us -> 55.8 us
  starting transfers between devices: 20.2 us -> 29.4 us
  Pallas kernels: 32.1 us -> 28.3 us
  matrix products: 0 us -> 3.38 us
    all_to_all x1 -> x2, waiting for transfers between devices: 14.5 us -> 6.69 us  [the longest x1 5.41 us: per_device(): lax.all_to_all(d_attn.reshape(devices, t_dev, columns, part), both, 0, 0,...]
    ppermute x9 -> x11, waiting for transfers between devices: 24.7 us -> 18.4 us  [swap(): return lax.ppermute(values, axis, [(i, i ^ bit) for i in range(size)])]
    ppermute x9 -> x11, starting transfers between devices: 9.18 us -> 13.7 us  [swap(): return lax.ppermute(values, axis, [(i, i ^ bit) for i in range(size)])]
    pallas_call x1, Pallas kernels: 5.21 us -> 1.43 us  [norm_send(): pl.pallas_call(functools.partial(norm_kernel, n_pair=n_pair, n_chip=n_chi...]
    dot_general x0 -> x1, matrix products: none -> 3.38 us  [per_device(): jnp.einsum('to,jfo->jtf', grad_rows, w_out.reshape(n_patch, part, width),...]
    all_to_all x1 -> x2, starting transfers between devices: 7.3 us -> 10 us  [the longest x1 7.29 us: per_device(): lax.all_to_all(d_attn.reshape(devices, t_dev, columns, part), both, 0, 0,...]
    unnamed x16 -> x22, local copies, waits for them, and re-layouts: 4.12 us -> 2.01 us
    all_to_all x1, starting transfers between devices: 3.72 us -> 5.63 us  [per_device(): lax.all_to_all(partial, both, 0, 0, axis_index_groups=groups, tiled=True)]
  transfers between devices with their start and end apart: 11 -> 14, of which waited for: 8 -> 8; matrix products, arithmetic and copies ran while one was open for 0% -> 2% of each run, Pallas kernels for 12% -> 14%
where the time goes in v7:
time: 124 us; the launch traced here: 123 us
  waiting for transfers between devices  55.8 us (45%)
  starting transfers between devices  29.4 us (24%)
  Pallas kernels  28.3 us (23%)
  local copies, waits for them, and re-layouts  4.8 us (4%)
  matrix products  3.38 us (3%)
    all_to_all x1, waiting for transfers between devices, per_device(): lax.all_to_all(partial, both, 0, 0, axis_index_groups=groups, tiled=True)  30.7 us
    ppermute x11, waiting for transfers between devices, swap(): return lax.ppermute(values, axis, [(i, i ^ bit) for i in range(size)])  18.4 us
    ppermute x11, starting transfers between devices, swap(): return lax.ppermute(values, axis, [(i, i ^ bit) for i in range(size)])  13.7 us
    all_to_all x1, starting transfers between devices, per_device(): lax.all_to_all(d_attn.reshape(devices, t_dev, columns, part), both, 0, 0,...  7.29 us
    pallas_call x1, Pallas kernels, share_send(): pl.pallas_call(share_kernel, grid_spec=pltpu.PrefetchScalarGridSpec(num_s...  6.86 us
    pallas_call x1, Pallas kernels, own_weights(): pl.pallas_call(functools.partial(weights_kernel, n_chip=n_chip), grid_spe...  6.2 us
    all_to_all x1, starting transfers between devices, per_device(): lax.all_to_all(partial, both, 0, 0, axis_index_groups=groups, tiled=True)  5.63 us
    all_to_all x1, waiting for transfers between devices, per_device(): lax.all_to_all(d_attn.reshape(devices, t_dev, columns, part), both, 0, 0,...  5.41 us
  transfers between devices with their start and end apart: 14, of which 8 were waited for; matrix products, arithmetic and copies ran while one was open for 2% of the time, Pallas kernels for 14%

profile of v7, /device:TPU:0, one launch (start us, length us, event | category | flops | bytes accessed | tf_op | source)
XLA Modules:
  0.0 123.5 jit_solution(5242118370188779531)
XLA Ops:
  0.7 3.4 %fusion = bf16[4,128,352]{1,2,0:T(8,128)(2,1)S(1)} fusion(bf16[4,352,1408]{2,1,0:T(8,128)(2,1)} %bitcast.59, bf16[128,1408,1]{1,0,2:T(8,128)(2,1)} %bitcast.51), kind=kOutput, calls=%fused_computation.1 | convolution fusion | flops 507691008 | bytes 4685824 | tf_op jit(solution)/shard_map/to,jfo->jtf/dot_general | solution.py:301
  4.0 0.2 copy.13
  4.3 0.8 copy.14
  5.1 7.3 %all-to-all-start = ((bf16[32,2,8,352]{3,2,1,0:T(8,128)(2,1)}), bf16[32,2,8,352]{3,2,1,0:T(8,128)(2,1)S(1)}, u32[]{:S(2)}, u32[]{:S(2)}) async-start(bf16[32,2,8,352]{3,2,1,0:T(8,128)(2,1)} %bitcast.9), calls=%async_computation | async-start | bytes 786432 | tf_op jit(solution)/shard_map/all_to_all | solution.py:306
  12.4 0.0 copy-start
  12.4 0.0 copy-start.3
  12.4 0.0 copy-start.4
  12.5 0.0 copy-start.5
  12.5 6.2 %shard_map.105.w_ref = bf16[3,1408,704]{2,1,0:T(8,128)(2,1)} custom-call(s32[1]{0:T(128)} %bitcast.1.chip_ref, bf16[1408,4224]{1,0:T(8,128)(2,1)} %w_ref), custom_call_target="tpu_custom_call" | custom-call | tf_op jit(solution)/shard_map/pallas_call | solution.py:103
  18.7 1.4 %shard_map.104 = bf16[32,16,352]{2,1,0:T(8,128)(2,1)} custom-call(bf16[128,1408]{1,0:T(8,128)(2,1)S(1)} %bitcast.45, f32[1,1408]{1,0:T(1,128)S(1)} %broadcast_in_dim.22.gain_ref, f32[1,1408]{1,0:T(1,128)S(1)} %broadcast_in_dim.23.bias_ref), custom_call_target="tpu_custom_call" | custom-call | tf_op jit(solution)/shard_map/pallas_call | solution.py:71
  20.1 5.4 %all-to-all-done = bf16[32,2,8,352]{3,2,1,0:T(8,128)(2,1)S(1)} async-done(((bf16[32,2,8,352]{3,2,1,0:T(8,128)(2,1)}), bf16[32,2,8,352]{3,2,1,0:T(8,128)(2,1)S(1)}, u32[]{:S(2)}, u32[]{:S(2)}) %all-to-all-start) | async-done | bytes 360480 | tf_op jit(solution)/shard_map/all_to_all | solution.py:306
  25.5 5.2 %shard_map.106.own_ref = bf16[3,352,512]{2,1,0:T(8,128)(2,1)S(1)} custom-call(bf16[512,352]{1,0:T(8,128)(2,1)S(1)} %bitcast.48, bf16[512,352]{1,0:T(8,128)(2,1)S(1)} %bitcast.49, bf16[512,352]{1,0:T(8,128)(2,1)S(1)} %bitcast.50, bf16[512,352]{1,0:T(8,128)(2,1)S(1)} %bitcast.42), custom_call_target="tpu_custom_call" | custom-call | tf_op jit(solution)/shard_map/pallas_call | solution.py:46
  30.8 0.1 collective-permute-start
  30.8 2.7 %all-to-all-start.1 = ((bf16[32,16,352]{2,1,0:T(8,128)(2,1)}), bf16[32,16,352]{2,1,0:T(8,128)(2,1)S(1)}, u32[]{:S(2)}, u32[]{:S(2)}) async-start(bf16[32,16,352]{2,1,0:T(8,128)(2,1)} %shard_map.104), calls=%async_computation.1 | async-start | bytes 786432 | tf_op jit(solution)/shard_map/all_to_all | solution.py:313
  33.6 0.0 collective-permute-done.core_ref
  33.6 0.9 slice.7
  34.5 1.8 %collective-permute-start.2 = (bf16[2,352,512]{2,1,0:T(8,128)(2,1)}, bf16[2,352,512]{2,1,0:T(8,128)(2,1)}, u32[]{:S(2)}, u32[]{:S(2)}) collective-permute-start(bf16[2,352,512]{2,1,0:T(8,128)(2,1)} %slice.7), channel_id=1, source_target_pairs={{0,4},{4,0},{8,12},{12,8},{16,20},{20,16},{24,28},{28,24},{1,5},{5... | collective-permute-start | bytes 2162696 | tf_op jit(solution)/shard_map/ppermute | solution.py:298
  36.3 6.9 %shard_map.107 = (bf16[8,16,1408]{2,1,0:T(8,128)(2,1)}, f32[8,16,1408]{2,1,0:T(8,128)S(1)}) custom-call(s32[1]{0:T(128)} %bitcast.15.where_ref, bf16[3,352,512]{2,1,0:T(8,128)(2,1)S(1)} %shard_map.106.own_ref, bf16[3,352,512]{2,1,0:T(8,128)(2,1)S(1)} %collective-permute-done.core_ref, bf16[3,1408,704]{2,1,0:T(8,128)(2,1)} %shard_map.105.w_ref), custom_call_target="tpu_custom_call" | custom-call | tf_op jit(solution)/shard_map/pallas_call | solution.py:151
  43.2 0.9 copy-done.1
  44.0 1.5 %collective-permute-start.4 = (bf16[8,16,1408]{2,1,0:T(8,128)(2,1)}, bf16[8,16,1408]{2,1,0:T(8,128)(2,1)}, u32[]{:S(2)}, u32[]{:S(2)}) collective-permute-start(bf16[8,16,1408]{2,1,0:T(8,128)(2,1)} %get-tuple-element.33), channel_id=1, source_target_pairs={{0,2},{1,3},{2,0},{3,1},{4,6},{5,7},{6,4},{7,5},{8,10},{9,11},{10,... | collective-permute-start | bytes 1081352 | tf_op jit(solution)/shard_map/ppermute | solution.py:298
  45.5 1.3 %all-to-all-done.1 = bf16[32,16,352]{2,1,0:T(8,128)(2,1)S(1)} async-done(((bf16[32,16,352]{2,1,0:T(8,128)(2,1)}), bf16[32,16,352]{2,1,0:T(8,128)(2,1)S(1)}, u32[]{:S(2)}, u32[]{:S(2)}) %all-to-all-start.1) | async-done | bytes 360480 | tf_op jit(solution)/shard_map/all_to_all | solution.py:313
  46.8 0.5 collective-permute-start.3
  47.2 0.7 slice.6
  48.0 1.5 %collective-permute-start.1 = (bf16[1,352,512]{2,1,0:T(8,128)(2,1)}, bf16[1,352,512]{2,1,0:T(8,128)(2,1)}, u32[]{:S(2)}, u32[]{:S(2)}) collective-permute-start(bf16[1,352,512]{2,1,0:T(8,128)(2,1)} %slice.6), channel_id=1, source_target_pairs={{0,4},{4,0},{8,12},{12,8},{16,20},{20,16},{24,28},{28,24},{1,5},{5... | collective-permute-start | bytes 1081352 | tf_op jit(solution)/shard_map/ppermute | solution.py:298
  49.5 6.2 %collective-permute-done.4.come_ref = bf16[8,16,1408]{2,1,0:T(8,128)(2,1)} collective-permute-done((bf16[8,16,1408]{2,1,0:T(8,128)(2,1)}, bf16[8,16,1408]{2,1,0:T(8,128)(2,1)}, u32[]{:S(2)}, u32[]{:S(2)}) %collective-permute-start.4) | collective-permute-done | bytes 360480 | tf_op jit(solution)/shard_map/ppermute | solution.py:298
  55.6 1.1 copy-done.2
  56.7 1.1 shard_map.108
  57.9 1.5 %collective-permute-start.5 = (bf16[2,16,1408]{2,1,0:T(8,128)(2,1)S(1)}, bf16[2,16,1408]{2,1,0:T(8,128)(2,1)S(1)}, u32[]{:S(2)}, u32[]{:S(2)}) collective-permute-start(bf16[2,16,1408]{2,1,0:T(8,128)(2,1)S(1)} %get-tuple-element.50), channel_id=1, source_target_pairs={{0,8},{4,12},{8,0},{12,4},{16,24},{20,28},{24,16},{28,20},{1,9},{5... | collective-permute-start | bytes 270344 | tf_op jit(solution)/shard_map/ppermute | solution.py:298
  59.4 2.4 %collective-permute-start.6 = (bf16[2,16,1408]{2,1,0:T(8,128)(2,1)S(1)}, bf16[2,16,1408]{2,1,0:T(8,128)(2,1)S(1)}, u32[]{:S(2)}, u32[]{:S(2)}) collective-permute-start(bf16[2,16,1408]{2,1,0:T(8,128)(2,1)S(1)} %get-tuple-element.49), channel_id=1, source_target_pairs={{0,16},{4,20},{8,24},{12,28},{16,0},{20,4},{24,8},{28,12},{1,17},{... | collective-permute-start | bytes 270344 | tf_op jit(solution)/shard_map/ppermute | solution.py:298
  61.8 1.0 collective-permute-done.3.theirs_ref
  62.8 3.3 %collective-permute-start.7 = (bf16[2,16,1408]{2,1,0:T(8,128)(2,1)S(1)}, bf16[2,16,1408]{2,1,0:T(8,128)(2,1)S(1)}, u32[]{:S(2)}, u32[]{:S(2)}) collective-permute-start(bf16[2,16,1408]{2,1,0:T(8,128)(2,1)S(1)} %get-tuple-element.48), channel_id=1, source_target_pairs={{0,24},{4,28},{8,16},{12,20},{16,8},{20,12},{24,0},{28,4},{1,25},{... | collective-permute-start | bytes 270344 | tf_op jit(solution)/shard_map/ppermute | solution.py:298
  66.2 0.0 collective-permute-done.1.a_ref
  66.2 0.0 collective-permute-done.5
  66.2 0.0 collective-permute-done.6
  66.2 0.0 copy-start.7
  66.2 3.1 %collective-permute-done.7 = bf16[2,16,1408]{2,1,0:T(8,128)(2,1)S(1)} collective-permute-done((bf16[2,16,1408]{2,1,0:T(8,128)(2,1)S(1)}, bf16[2,16,1408]{2,1,0:T(8,128)(2,1)S(1)}, u32[]{:S(2)}, u32[]{:S(2)}) %collective-permute-start.7) | collective-permute-done | bytes 90144 | tf_op jit(solution)/shard_map/ppermute | solution.py:298
  69.3 0.0 collective-permute-done.2.b_ref
  69.3 0.5 collective-permute-start.8
  69.8 2.4 %collective-permute-done.8.a_core_ref = bf16[1,352,512]{2,1,0:T(8,128)(2,1)S(1)} collective-permute-done((bf16[1,352,512]{2,1,0:T(8,128)(2,1)}, bf16[1,352,512]{2,1,0:T(8,128)(2,1)S(1)}, u32[]{:S(2)}, u32[]{:S(2)}) %collective-permute-start.8) | collective-permute-done | bytes 360480 | tf_op jit(solution)/shard_map/ppermute | solution.py:298
  72.2 0.0 collective-permute-done.9.b_core_ref
  72.2 5.1 %shard_map.109 = bf16[8,44,2112]{2,1,0:T(8,128)(2,1)} custom-call(s32[1]{0:T(128)} %bitcast.1.chip_ref, bf16[512,352]{1,0:T(8,128)(2,1)S(1)} %bitcast.44, bf16[512,352]{1,0:T(8,128)(2,1)S(1)} %collective-permute-done.3.theirs_ref, bf16[3,352,512]{2,1,0:T(8,128)(2,1)S(1)} %shard_map.106.own_ref, bf16[3,352,512]{2,1,0:T(8,128)(2,1)S(1)} %collective-permute-done.core_ref, ...), custom_call_target="tpu_custom_call" | custom-call | tf_op jit(solution)/shard_map/pallas_call | solution.py:199
  77.3 5.6 %all-to-all-start.2 = ((bf16[8,44,2112]{2,1,0:T(8,128)(2,1)}), bf16[8,44,2112]{2,1,0:T(8,128)(2,1)S(1)}, u32[]{:S(2)}, u32[]{:S(2)}) async-start(bf16[8,44,2112]{2,1,0:T(8,128)(2,1)} %shard_map.109), calls=%async_computation.2 | async-start | bytes 3342336 | tf_op jit(solution)/shard_map/all_to_all | solution.py:342
  82.9 1.0 pad_maximum_fusion
  83.9 0.6 collective-permute-start.10
  84.5 5.8 %collective-permute-done.10.come_ref = bf16[4,16,1408]{2,1,0:T(8,128)(2,1)S(1)} collective-permute-done((bf16[4,16,1408]{2,1,0:T(8,128)(2,1)S(1)}, bf16[4,16,1408]{2,1,0:T(8,128)(2,1)S(1)}, u32[]{:S(2)}, u32[]{:S(2)}) %collective-permute-start.10) | collective-permute-done | bytes 180256 | tf_op jit(solution)/shard_map/ppermute | solution.py:298
  90.3 1.3 %shard_map.110 = bf16[128,1408]{1,0:T(8,128)(2,1)} custom-call(s32[1]{0:T(128)} %bitcast.tm_ref, bf16[4,16,1408]{2,1,0:T(8,128)(2,1)S(1)} %get-tuple-element.47.stay_ref, bf16[4,16,1408]{2,1,0:T(8,128)(2,1)S(1)} %collective-permute-done.10.come_ref, bf16[128,1408]{1,0:T(8,128)(2,1)S(1)} %bitcast.46, bf16[128,1408]{1,0:T(8,128)(2,1)S(1)} %bitcast.52, ...), custom_call_target="tpu_custom_call" | custom-call | tf_op jit(solution)/shard_map/pallas_call | solution.py:245
  91.7 30.7 %all-to-all-done.2 = bf16[8,44,2112]{2,1,0:T(8,128)(2,1)S(1)} async-done(((bf16[8,44,2112]{2,1,0:T(8,128)(2,1)}), bf16[8,44,2112]{2,1,0:T(8,128)(2,1)S(1)}, u32[]{:S(2)}, u32[]{:S(2)}) %all-to-all-start.2) | async-done | bytes 1486880 | tf_op jit(solution)/shard_map/all_to_all | solution.py:342
  122.3 1.1 shard_map.111
  (20 shorter events, 0.1 us)
Async XLA Ops:
  0.6 11.7 %copy-start.9 = (f32[1408]{0:T(1024)S(1)}, f32[1408]{0:T(1024)}, u32[]{:S(2)}) copy-start(f32[1408]{0:T(1024)} %param.10) | copy-start | bytes 16900
  0.6 11.8 %copy-start.10 = (f32[1408]{0:T(1024)S(1)}, f32[1408]{0:T(1024)}, u32[]{:S(2)}) copy-start(f32[1408]{0:T(1024)} %param.11) | copy-start | bytes 16900
  5.1 20.5 %all-to-all-start = ((bf16[32,2,8,352]{3,2,1,0:T(8,128)(2,1)}), bf16[32,2,8,352]{3,2,1,0:T(8,128)(2,1)S(1)}, u32[]{:S(2)}, u32[]{:S(2)}) async-start(bf16[32,2,8,352]{3,2,1,0:T(8,128)(2,1)} %bitcast.9), calls=%async_computation | async-start | bytes 786432 | tf_op jit(solution)/shard_map/all_to_all | solution.py:306
  12.4 6.3 %copy-start = (bf16[2,64,1408]{2,1,0:T(8,128)(2,1)S(1)}, bf16[2,64,1408]{2,1,0:T(8,128)(2,1)}, u32[]{:S(2)}) copy-start(bf16[2,64,1408]{2,1,0:T(8,128)(2,1)} %param.9) | copy-start | bytes 1081348
  12.4 13.1 %copy-start.3 = (bf16[64,8,352]{2,1,0:T(8,128)(2,1)S(1)}, bf16[64,8,352]{2,1,0:T(8,128)(2,1)}, u32[]{:S(2)}) copy-start(bf16[64,8,352]{2,1,0:T(8,128)(2,1)} %param.14) | copy-start | bytes 1081348
  12.4 13.1 %copy-start.4 = (bf16[64,8,352]{2,1,0:T(8,128)(2,1)S(1)}, bf16[64,8,352]{2,1,0:T(8,128)(2,1)}, u32[]{:S(2)}) copy-start(bf16[64,8,352]{2,1,0:T(8,128)(2,1)} %param.15) | copy-start | bytes 1081348
  12.5 13.1 %copy-start.5 = (bf16[64,8,352]{2,1,0:T(8,128)(2,1)S(1)}, bf16[64,8,352]{2,1,0:T(8,128)(2,1)}, u32[]{:S(2)}) copy-start(bf16[64,8,352]{2,1,0:T(8,128)(2,1)} %param.16) | copy-start | bytes 1081348
  30.8 2.8 %collective-permute-start = (bf16[3,352,512]{2,1,0:T(8,128)(2,1)S(1)}, bf16[3,352,512]{2,1,0:T(8,128)(2,1)S(1)}, u32[]{:S(2)}, u32[]{:S(2)}) collective-permute-start(bf16[3,352,512]{2,1,0:T(8,128)(2,1)S(1)} %shard_map.106.own_ref), channel_id=1, source_target_pairs={{0,1},{1,0},{2,3},{3,2},{4,5},{5,4},{6,7},{7,6},{8,9},{9,8},{10,11... | collective-permute-start | bytes 3244040 | tf_op jit(solution)/shard_map/ppermute | solution.py:298
  30.8 15.9 %all-to-all-start.1 = ((bf16[32,16,352]{2,1,0:T(8,128)(2,1)}), bf16[32,16,352]{2,1,0:T(8,128)(2,1)S(1)}, u32[]{:S(2)}, u32[]{:S(2)}) async-start(bf16[32,16,352]{2,1,0:T(8,128)(2,1)} %shard_map.104), calls=%async_computation.1 | async-start | bytes 786432 | tf_op jit(solution)/shard_map/all_to_all | solution.py:313
  34.5 34.8 %collective-permute-start.2 = (bf16[2,352,512]{2,1,0:T(8,128)(2,1)}, bf16[2,352,512]{2,1,0:T(8,128)(2,1)}, u32[]{:S(2)}, u32[]{:S(2)}) collective-permute-start(bf16[2,352,512]{2,1,0:T(8,128)(2,1)} %slice.7), channel_id=1, source_target_pairs={{0,4},{4,0},{8,12},{12,8},{16,20},{20,16},{24,28},{28,24},{1,5},{5... | collective-permute-start | bytes 2162696 | tf_op jit(solution)/shard_map/ppermute | solution.py:298
  43.2 0.9 copy-start.1
  44.0 11.6 %collective-permute-start.4 = (bf16[8,16,1408]{2,1,0:T(8,128)(2,1)}, bf16[8,16,1408]{2,1,0:T(8,128)(2,1)}, u32[]{:S(2)}, u32[]{:S(2)}) collective-permute-start(bf16[8,16,1408]{2,1,0:T(8,128)(2,1)} %get-tuple-element.33), channel_id=1, source_target_pairs={{0,2},{1,3},{2,0},{3,1},{4,6},{5,7},{6,4},{7,5},{8,10},{9,11},{10,... | collective-permute-start | bytes 1081352 | tf_op jit(solution)/shard_map/ppermute | solution.py:298
  46.8 16.1 %collective-permute-start.3 = (bf16[512,352]{1,0:T(8,128)(2,1)S(1)}, bf16[512,352]{1,0:T(8,128)(2,1)S(1)}, u32[]{:S(2)}, u32[]{:S(2)}) collective-permute-start(bf16[512,352]{1,0:T(8,128)(2,1)S(1)} %bitcast.43), channel_id=1, source_target_pairs={{0,2},{1,3},{2,0},{3,1},{4,6},{5,7},{6,4},{7,5},{8,10},{9,11},{10,... | collective-permute-start | bytes 1081352 | tf_op jit(solution)/shard_map/ppermute | solution.py:298
  48.0 18.2 %collective-permute-start.1 = (bf16[1,352,512]{2,1,0:T(8,128)(2,1)}, bf16[1,352,512]{2,1,0:T(8,128)(2,1)}, u32[]{:S(2)}, u32[]{:S(2)}) collective-permute-start(bf16[1,352,512]{2,1,0:T(8,128)(2,1)} %slice.6), channel_id=1, source_target_pairs={{0,4},{4,0},{8,12},{12,8},{16,20},{20,16},{24,28},{28,24},{1,5},{5... | collective-permute-start | bytes 1081352 | tf_op jit(solution)/shard_map/ppermute | solution.py:298
  55.6 1.1 copy-start.2
  57.9 8.3 %collective-permute-start.5 = (bf16[2,16,1408]{2,1,0:T(8,128)(2,1)S(1)}, bf16[2,16,1408]{2,1,0:T(8,128)(2,1)S(1)}, u32[]{:S(2)}, u32[]{:S(2)}) collective-permute-start(bf16[2,16,1408]{2,1,0:T(8,128)(2,1)S(1)} %get-tuple-element.50), channel_id=1, source_target_pairs={{0,8},{4,12},{8,0},{12,4},{16,24},{20,28},{24,16},{28,20},{1,9},{5... | collective-permute-start | bytes 270344 | tf_op jit(solution)/shard_map/ppermute | solution.py:298
  59.4 6.8 %collective-permute-start.6 = (bf16[2,16,1408]{2,1,0:T(8,128)(2,1)S(1)}, bf16[2,16,1408]{2,1,0:T(8,128)(2,1)S(1)}, u32[]{:S(2)}, u32[]{:S(2)}) collective-permute-start(bf16[2,16,1408]{2,1,0:T(8,128)(2,1)S(1)} %get-tuple-element.49), channel_id=1, source_target_pairs={{0,16},{4,20},{8,24},{12,28},{16,0},{20,4},{24,8},{28,12},{1,17},{... | collective-permute-start | bytes 270344 | tf_op jit(solution)/shard_map/ppermute | solution.py:298
  62.8 6.4 %collective-permute-start.7 = (bf16[2,16,1408]{2,1,0:T(8,128)(2,1)S(1)}, bf16[2,16,1408]{2,1,0:T(8,128)(2,1)S(1)}, u32[]{:S(2)}, u32[]{:S(2)}) collective-permute-start(bf16[2,16,1408]{2,1,0:T(8,128)(2,1)S(1)} %get-tuple-element.48), channel_id=1, source_target_pairs={{0,24},{4,28},{8,16},{12,20},{16,8},{20,12},{24,0},{28,4},{1,25},{... | collective-permute-start | bytes 270344 | tf_op jit(solution)/shard_map/ppermute | solution.py:298
  66.2 6.0 %copy-start.7 = (bf16[2,16,1408]{2,1,0:T(8,128)(2,1)}, bf16[2,16,1408]{2,1,0:T(8,128)(2,1)S(1)}, u32[]{:S(2)}) copy-start(bf16[2,16,1408]{2,1,0:T(8,128)(2,1)S(1)} %collective-permute-done.6) | copy-start | bytes 270340
  69.3 2.9 %copy-start.8 = (bf16[2,16,1408]{2,1,0:T(8,128)(2,1)}, bf16[2,16,1408]{2,1,0:T(8,128)(2,1)S(1)}, u32[]{:S(2)}) copy-start(bf16[2,16,1408]{2,1,0:T(8,128)(2,1)S(1)} %collective-permute-done.7) | copy-start | bytes 270340
  69.3 2.9 %collective-permute-start.9 = (bf16[2,352,512]{2,1,0:T(8,128)(2,1)}, bf16[2,352,512]{2,1,0:T(8,128)(2,1)S(1)}, u32[]{:S(2)}, u32[]{:S(2)}) collective-permute-start(bf16[2,352,512]{2,1,0:T(8,128)(2,1)} %collective-permute-done.2.b_ref), channel_id=1, source_target_pairs={{0,1},{1,0},{2,3},{3,2},{4,5},{5,4},{6,7},{7,6},{8,9},{9,8},{10,11... | collective-permute-start | bytes 2162696 | tf_op jit(solution)/shard_map/ppermute | solution.py:298
  69.3 2.9 %collective-permute-start.8 = (bf16[1,352,512]{2,1,0:T(8,128)(2,1)}, bf16[1,352,512]{2,1,0:T(8,128)(2,1)S(1)}, u32[]{:S(2)}, u32[]{:S(2)}) collective-permute-start(bf16[1,352,512]{2,1,0:T(8,128)(2,1)} %collective-permute-done.1.a_ref), channel_id=1, source_target_pairs={{0,1},{1,0},{2,3},{3,2},{4,5},{5,4},{6,7},{7,6},{8,9},{9,8},{10,11... | collective-permute-start | bytes 1081352 | tf_op jit(solution)/shard_map/ppermute | solution.py:298
  77.3 13.0 %copy-start.6 = (bf16[2,64,1408]{2,1,0:T(8,128)(2,1)S(1)}, bf16[2,64,1408]{2,1,0:T(8,128)(2,1)}, u32[]{:S(2)}) copy-start(bf16[2,64,1408]{2,1,0:T(8,128)(2,1)} %param.17) | copy-start | bytes 1081348
  77.3 45.0 %all-to-all-start.2 = ((bf16[8,44,2112]{2,1,0:T(8,128)(2,1)}), bf16[8,44,2112]{2,1,0:T(8,128)(2,1)S(1)}, u32[]{:S(2)}, u32[]{:S(2)}) async-start(bf16[8,44,2112]{2,1,0:T(8,128)(2,1)} %shard_map.109), calls=%async_computation.2 | async-start | bytes 3342336 | tf_op jit(solution)/shard_map/all_to_all | solution.py:342
  83.9 6.4 %collective-permute-start.10 = (bf16[4,16,1408]{2,1,0:T(8,128)(2,1)S(1)}, bf16[4,16,1408]{2,1,0:T(8,128)(2,1)S(1)}, u32[]{:S(2)}, u32[]{:S(2)}) collective-permute-start(bf16[4,16,1408]{2,1,0:T(8,128)(2,1)S(1)} %get-tuple-element.46), channel_id=1, source_target_pairs={{0,4},{4,0},{8,12},{12,8},{16,20},{20,16},{24,28},{28,24},{1,5},{5... | collective-permute-start | bytes 540680 | tf_op jit(solution)/shard_map/ppermute | solution.py:298

commit v8 on v7

--- a/solution.py
+++ b/solution.py
@@ -14,10 +14,10 @@
 ROWS = (((0,), (0,)), ((), ()))
 COLS = (((1,), (1,)), ((), ()))
 CROSS = (((0,), (1,)), ((), ()))
-ROOM = pltpu.CompilerParams(vmem_limit_bytes=48 * 1024 * 1024)
-
-
-def attend_kernel(q_ref, k_ref, v_ref, d_ref, out_ref, *, columns):
+ROOM = pltpu.CompilerParams(vmem_limit_bytes=28 * 1024 * 1024)
+
+
+def attend_kernel(q_ref, k_ref, v_ref, d_ref, all_ref, query_ref, rest_ref, *, columns):
     n_tok, width = q_ref.shape
     factor = 1.0 / math.sqrt(DH)
     source = lax.broadcasted_iota(jnp.int32, (n_tok, n_tok), 0)
@@ -34,18 +34,23 @@
         row_dot = jnp.sum(probability * prob_grad, axis=0, keepdims=True)
         score_grad = (probability * (prob_grad - row_dot) * factor).astype(BF)
         prob_low = probability.astype(BF)
-        for kind, (left, right, dims) in enumerate(
-            ((key, score_grad, ROWS), (query, score_grad, CROSS), (grad, prob_low, CROSS))
+        for kind, (left, right, dims, out_ref) in enumerate(
+            (
+                (key, score_grad, ROWS, query_ref.at[0]),
+                (query, score_grad, CROSS, rest_ref.at[0]),
+                (grad, prob_low, CROSS, rest_ref.at[1]),
+            )
         ):
-            total = lax.dot_general(left, right, dims, preferred_element_type=F32)
-            out_ref[kind, lanes, :] = total.astype(BF)
+            total = lax.dot_general(left, right, dims, preferred_element_type=F32).astype(BF)
+            out_ref[lanes, :] = total
+            all_ref[kind, lanes, :] = total
 
 
 def attend(query, key, value, grad, columns):
     n_tok, width = query.shape
     return pl.pallas_call(
         functools.partial(attend_kernel, columns=columns),
-        out_shape=jax.ShapeDtypeStruct((3, width, n_tok), BF),
+        out_shape=[jax.ShapeDtypeStruct((kinds, width, n_tok), BF) for kinds in (3, 1, 2)],
         compiler_params=ROOM,
     )(query, key, value, grad)
 
@@ -117,18 +122,20 @@
     )(chip[None], w_qkv)
 
 
-def share_kernel(where_ref, own_ref, core_ref, w_ref, leave_ref, stay_ref, turn_ref):
+def share_kernel(where_ref, *refs):
+    grads_refs, (w_ref, leave_ref, stay_ref, turn_ref) = refs[:2], refs[2:]
     patch = where_ref[0]
     chip, core = patch // 2, patch % 2
-    kinds, part, _ = own_ref.shape
+    kinds = w_ref.shape[0]
+    part = w_ref.shape[2] // 2
     n, group, _ = leave_ref.shape
     for side in range(2):
 
         @pl.when(core == side)
         def _(side=side):
-            for c in range(kinds):
-                for grads_ref, at in ((own_ref, side * part), (core_ref, (1 - side) * part)):
-                    rows = grads_ref[c].astype(F32).T.astype(BF)
+            for pieces, at in ((grads_refs[:1], side * part), (grads_refs[1:], (1 - side) * part)):
+                for c, grads in enumerate(kinds_of(pieces)):
+                    rows = grads.astype(F32).T.astype(BF)
                     turn_ref[c, :, :, :, :, at : at + part] = rows.reshape(n, 2, 2, group, part)
 
     total = None
@@ -143,68 +150,103 @@
     stay_ref[...] = total[n * group :].reshape(stay_ref.shape)
 
 
-def share_send(grads, grads_core, weights, patch, group):
-    kinds, part, n_tok = grads.shape
-    width = weights.shape[1]
-    n = n_tok // (4 * group)
-    whole = pl.BlockSpec((kinds, part, n_tok), lambda i, s: (0, 0, 0))
+def kinds_of(refs):
+    return [ref[i] for ref in refs for i in range(ref.shape[0])]
+
+
+def whole_spec(array):
+    return pl.BlockSpec(array.shape, lambda i, s: (0,) * array.ndim)
+
+
+def share_send(pieces, weights, patch, group):
+    kinds, width, double = weights.shape
+    n = pieces[0].shape[-1] // (4 * group)
     return pl.pallas_call(
         share_kernel,
         grid_spec=pltpu.PrefetchScalarGridSpec(
             num_scalar_prefetch=1,
             grid=(1,),
-            in_specs=[whole, whole, pl.BlockSpec((kinds, width, 2 * part), lambda i, s: (0, 0, 0))],
+            in_specs=[whole_spec(array) for array in (*pieces, weights)],
             out_specs=[pl.BlockSpec((n, group, width), lambda i, s: (0, 0, 0))] * 2,
-            scratch_shapes=[pltpu.VMEM((kinds, n, 2, 2, group, 2 * part), BF)],
+            scratch_shapes=[pltpu.VMEM((kinds, n, 2, 2, group, double), BF)],
         ),
         out_shape=[
             jax.ShapeDtypeStruct((n, group, width), BF),
             jax.ShapeDtypeStruct((n, group, width), F32),
         ],
         compiler_params=ROOM,
-    )(patch[None], grads, grads_core, weights)
+    )(patch[None], *pieces, weights)
 
 
 def add_kernel(stay_ref, come_ref, out_ref):
     out_ref[...] = (stay_ref[...] + come_ref[...].astype(F32)).astype(BF)
 
 
-def product_kernel(
-    chip_ref, mine_ref, theirs_ref, own_ref, core_ref, a_ref, b_ref, a_core_ref, b_core_ref, out_ref, *, factor
-):
-    kinds, part, _ = own_ref.shape
-    own_rows = out_ref.shape[1]
-    first = chip_ref[0] == 0
-    mine, theirs = mine_ref[...], theirs_ref[...]
-    norm_own = jnp.where(first, mine, theirs)
-    norm_other = jnp.where(first, theirs, mine)
-    for r, (own, other) in enumerate(
-        ((own_ref, (a_ref, b_ref)), (core_ref, (a_core_ref, b_core_ref)))
-    ):
-        for c in range(kinds):
-            second = other[0][c] if c < other[0].shape[0] else other[1][c - other[0].shape[0]]
-            total = jnp.dot(own[c], norm_own, preferred_element_type=F32)
-            total += jnp.dot(second, norm_other, preferred_element_type=F32)
-            total = (total * factor).T
-            at = (r * kinds + c) * part
-            for k in range(out_ref.shape[0]):
-                rows = total[k * own_rows : (k + 1) * own_rows]
-                out_ref[k, :, at : at + part] = rows.astype(BF)
-
-
-def product(chip, mine, theirs, grads, core, others, own_rows, factor):
-    kinds, part, n_tok = grads.shape
-    arrays = [mine, theirs, grads, core, *others]
-    shape = (part // own_rows, own_rows, 2 * kinds * part)
-    return pl.pallas_call(
-        functools.partial(product_kernel, factor=factor),
-        grid_spec=pltpu.PrefetchScalarGridSpec(
-            num_scalar_prefetch=1,
-            grid=(1,),
-            in_specs=[
-                pl.BlockSpec(array.shape, lambda i, s, n=array.ndim: (0,) * n) for array in arrays
-            ],
+def own_kernel(chip_ref, mine_ref, theirs_ref, *refs):
+    norm = jnp.where(chip_ref[0] == 0, mine_ref[...], theirs_ref[...])
+    part = refs[0].shape[1]
+    for i, grads in enumerate(kinds_of(refs[:-1])):
+        refs[-1][i * part : (i + 1) * part, :] = jnp.dot(grads, norm, preferred_element_type=F32)
+
+
+def own_product(chip, mine, theirs, pieces):
+    part = mine.shape[1]
+    rows = part * sum(piece.shape[0] for piece in pieces)
+    arrays = (mine, theirs, *pieces)
+    return pl.pallas_call(
+        own_kernel,
+        grid_spec=pltpu.PrefetchScalarGridSpec(
+            num_scalar_prefetch=1,
+            grid=(1,),
+            in_specs=[whole_spec(array) for array in arrays],
+            out_specs=pl.BlockSpec((rows, part), lambda i, s: (0, 0)),
+        ),
+        out_shape=jax.ShapeDtypeStruct((rows, part), F32),
+        compiler_params=ROOM,
+    )(chip[None], *arrays)
+
+
+def other_kernel(chip_ref, mine_ref, theirs_ref, acc_ref, *refs, factor, own_rows):
+    pieces, (out_ref, sum_ref) = refs[:-2], refs[-2:]
+    norm = jnp.where(chip_ref[0] == 0, theirs_ref[...], mine_ref[...])
+    part = pieces[0].shape[1]
+    for i, grads in enumerate(kinds_of(pieces)):
+        rows = slice(i * part, (i + 1) * part)
+        total = acc_ref[rows, :] + jnp.dot(grads, norm, preferred_element_type=F32)
+        sum_ref[rows, :] = total * factor
+    full, left = divmod(sum_ref.shape[0], 128)
+    packed = len(out_ref.shape) == 3 and out_ref.shape[2] == 128
+    for n in range(full + (left > 0)):
+        block = sum_ref[n * 128 : (n + 1) * 128, :].T if n < full else sum_ref[n * 128 :, :].T
+        for k in range(out_ref.shape[0]):
+            rows = block[k * own_rows : (k + 1) * own_rows].astype(BF)
+            if not packed:
+                out_ref[k, :, n * 128 : n * 128 + rows.shape[1]] = rows
+            elif n < full:
+                out_ref[k, n * own_rows : (n + 1) * own_rows, :] = rows
+            else:
+                rows = block[k * own_rows : (k + 1) * own_rows]
+                both = jnp.concatenate([rows[: own_rows // 2], rows[own_rows // 2 :]], axis=1)
+                out_ref[k, n * own_rows :, :] = both.astype(BF)
+
+
+def packable(own_rows, lanes):
+    return own_rows % 4 == 0 and lanes % 128 == 64
+
+
+def other_product(chip, mine, theirs, acc, pieces, own_rows, factor):
+    lanes, part = acc.shape
+    chunk = (own_rows * lanes // 128, 128) if packable(own_rows, lanes) else (own_rows, lanes)
+    shape = (part // own_rows,) + chunk
+    arrays = (mine, theirs, acc, *pieces)
+    return pl.pallas_call(
+        functools.partial(other_kernel, factor=factor, own_rows=own_rows),
+        grid_spec=pltpu.PrefetchScalarGridSpec(
+            num_scalar_prefetch=1,
+            grid=(1,),
+            in_specs=[whole_spec(array) for array in arrays],
             out_specs=pl.BlockSpec(shape, lambda i, s: (0, 0, 0)),
+            scratch_shapes=[pltpu.VMEM((lanes, part), F32)],
         ),
         out_shape=jax.ShapeDtypeStruct(shape, BF),
         compiler_params=ROOM,
@@ -256,26 +298,44 @@
 
 
 def final_kernel(core_ref, in_ref, out_ref, *, part, kinds):
-    n_pair, n_chip, own_rows, _ = in_ref.shape
-    for core in range(2):
-        @pl.when(core_ref[0] == core)
-        def _(core=core):
-            for x in range(n_chip):
-                total = in_ref[0, x].astype(F32)
-                for z in range(1, n_pair):
-                    total = total + in_ref[z, x].astype(F32)
+    n_pair, n_chip = in_ref.shape[:2]
+    own_rows = out_ref.shape[0]
+    lanes = 2 * kinds * part
+    for x in range(n_chip):
+        total = in_ref[0, x].astype(F32)
+        for z in range(1, n_pair):
+            total = total + in_ref[z, x].astype(F32)
+        if packable(own_rows, lanes):
+            full = lanes // 128
+            blocks = [total[n * own_rows : (n + 1) * own_rows] for n in range(full)]
+            both, half = total[full * own_rows :], own_rows // 2
+            blocks.append(jnp.concatenate([both[:half, :64], both[:half, 64:]], axis=0))
+            total = jnp.concatenate(blocks, axis=1)
+        for core in range(2):
+
+            @pl.when(core_ref[0] == core)
+            def _(core=core, total=total, x=x):
                 for r in range(2):
                     for c in range(kinds):
                         at = (c * n_chip * 2 + 2 * x + (r ^ core)) * part
                         src = (r * kinds + c) * part
                         out_ref[:, at : at + part] = total[:, src : src + part]
-def final_sum(pieces, core, part, kinds):
-    n_pair,n_chip,own_rows,_=pieces.shape
-    return pl.pallas_call(functools.partial(final_kernel,part=part,kinds=kinds),
-        grid_spec=pltpu.PrefetchScalarGridSpec(num_scalar_prefetch=1,grid=(1,),
-            in_specs=[pl.BlockSpec(pieces.shape,lambda i,s:(0,0,0,0))],
-            out_specs=pl.BlockSpec((own_rows,2*n_chip*kinds*part),lambda i,s:(0,0))),
-        out_shape=jax.ShapeDtypeStruct((own_rows,2*n_chip*kinds*part),F32),compiler_params=ROOM)(core[None],pieces)
+
+
+def final_sum(pieces, core, own_rows, part, kinds):
+    n_chip = pieces.shape[1]
+    shape = (own_rows, 2 * n_chip * kinds * part)
+    return pl.pallas_call(
+        functools.partial(final_kernel, part=part, kinds=kinds),
+        grid_spec=pltpu.PrefetchScalarGridSpec(
+            num_scalar_prefetch=1,
+            grid=(1,),
+            in_specs=[whole_spec(pieces)],
+            out_specs=pl.BlockSpec(shape, lambda i, s: (0, 0)),
+        ),
+        out_shape=jax.ShapeDtypeStruct(shape, F32),
+        compiler_params=ROOM,
+    )(core[None], pieces)
 
 
 def per_device(tokens, ln_gain, ln_bias, w_qkv, w_out, q_time, k_time, v_time, grad_out):
@@ -314,20 +374,24 @@
     theirs = swap(mine, "patch", n_patch, 2)
 
     saved = [values.reshape(n_tok, part) for values in (q_time, k_time, v_time)]
-    grads = attend(*saved, d_time, columns)
-    grads_core = swap(grads, "patch", n_patch, 1)
-    grads, grads_core = lax.optimization_barrier((grads, grads_core))
-    grads_other = [swap(piece, "tm", n_tm, 1) for piece in (grads[:1], grads[1:])]
-
-    leave, stay = share_send(grads, grads_core, weights, patch, t_dev * columns)
+    grads, *others = attend(*saved, d_time, columns)
+    grads_core, others = lax.optimization_barrier((swap(grads, "patch", n_patch, 1), others))
+    pieces = [grads, grads_core]
+    others = [swap(piece, "tm", n_tm, 1) for piece in others]
+
+    leave, stay = share_send(pieces, weights, patch, t_dev * columns)
+    come = swap(leave, "patch", n_patch, 2)
     share = pl.pallas_call(
         add_kernel, out_shape=jax.ShapeDtypeStruct(leave.shape, BF), compiler_params=ROOM
-    )(stay, swap(leave, "patch", n_patch, 2))
+    )(stay, come)
     share = share.reshape((n_pair, 2) + share.shape[1:])
     spread = [lax.dynamic_index_in_dim(share, (tm // 2) ^ n, 0, keepdims=False) for n in range(n_pair)]
     spread = spread[:1] + [swap(spread[n], "tm", n_tm, 2 * n) for n in range(1, n_pair)]
-    grads_other, theirs, spread = lax.optimization_barrier((grads_other, theirs, spread))
-    grads_other += [swap(piece, "patch", n_patch, 1) for piece in grads_other]
+    own = own_product(patch // 2, mine, theirs, pieces)
+    others, theirs, own, early = lax.optimization_barrier((others, theirs, own, spread[:-1]))
+    others = list(others)
+    spread = early + spread[-1:]
+    others += [swap(piece, "patch", n_patch, 1) for piece in others]
 
     factor = 1.0 / math.sqrt(frames * patches)
     groups = [
@@ -335,12 +399,11 @@
         for y in range(2)
         for c in range(2)
     ]
-    partial = product(
-        patch // 2, mine, theirs, grads, grads_core, grads_other, own_rows, factor
-    )
+    partial = other_product(patch // 2, mine, theirs, own, others, own_rows, factor)
     partial, spread = lax.optimization_barrier((partial, spread))
-    pieces = lax.all_to_all(partial, both, 0, 0, axis_index_groups=groups, tiled=True)
-    grad_w_qkv = final_sum(pieces.reshape(n_pair, n_chip, own_rows, 6 * part), core, part, 3)
+    summands = lax.all_to_all(partial, both, 0, 0, axis_index_groups=groups, tiled=True)
+    summands = summands.reshape((n_pair, n_chip) + summands.shape[1:])
+    grad_w_qkv = final_sum(summands, core, own_rows, part, 3)
 
     spread = jnp.stack(spread)
     stay = lax.dynamic_index_in_dim(spread, side, 1, keepdims=False)

time: 124 us -> 117 us (0.944)
  local copies, waits for them, and re-layouts: 4.8 us -> 14.7 us
  waiting for transfers between devices: 55.8 us -> 47.3 us
  Pallas kernels: 28.3 us -> 20.7 us
  starting transfers between devices: 29.4 us -> 28.1 us
    unnamed x22 -> x30, local copies, waits for them, and re-layouts: 2.01 us -> 13.6 us
    pallas_call x1, Pallas kernels: 6.2 us -> 0.89 us  [own_weights(): pl.pallas_call(functools.partial(weights_kernel, n_chip=n_chip), grid_spe...]
    all_to_all x1, waiting for transfers between devices: 30.7 us -> 26.8 us  [per_device(): lax.all_to_all(partial, both, 0, 0, axis_index_groups=groups, tiled=True)]
    ppermute x11, waiting for transfers between devices: 18.4 us -> 14.7 us  [swap(): return lax.ppermute(values, axis, [(i, i ^ bit) for i in range(size)])]
    pallas_call x1, Pallas kernels: 6.86 us -> 4.04 us  [share_send(): pl.pallas_call(share_kernel, grid_spec=pltpu.PrefetchScalarGridSpec(num_s...]
    all_to_all x1, waiting for transfers between devices: 5.41 us -> 3.68 us  [per_device(): lax.all_to_all(d_attn.reshape(devices, t_dev, columns, part), both, 0, 0,...]
    slice x2 -> x0, local copies, waits for them, and re-layouts: 1.69 us -> none  [the longest x1 0.94 us: per_device(): grads[1:]]
    pallas_call x1 -> x2, Pallas kernels: 5.07 us -> 5.3 us  [the longest x1 4.02 us: other_product(): pl.pallas_call(functools.partial(other_kernel, factor=factor, own_rows=ow...]
  transfers between devices with their start and end apart: 14 -> 14, of which waited for: 8 -> 9; matrix products, arithmetic and copies ran while one was open for 2% -> 1% of each run, Pallas kernels for 14% -> 12%
where the time goes in v8:
time: 117 us; the launch traced here: 116 us
  waiting for transfers between devices  47.3 us (40%)
  starting transfers between devices  28.1 us (24%)
  Pallas kernels  20.7 us (18%)
  local copies, waits for them, and re-layouts  14.7 us (13%)
  matrix products  3.38 us (3%)
    all_to_all x1, waiting for transfers between devices, per_device(): lax.all_to_all(partial, both, 0, 0, axis_index_groups=groups, tiled=True)  26.8 us
    ppermute x11, waiting for transfers between devices, swap(): return lax.ppermute(values, axis, [(i, i ^ bit) for i in range(size)])  14.7 us
    unnamed x30, local copies, waits for them, and re-layouts  13.6 us
    ppermute x11, starting transfers between devices, swap(): return lax.ppermute(values, axis, [(i, i ^ bit) for i in range(size)])  12.7 us
    all_to_all x1, starting transfers between devices, per_device(): lax.all_to_all(d_attn.reshape(devices, t_dev, columns, part), both, 0, 0,...  7.29 us
    pallas_call x1, Pallas kernels, attend(): pl.pallas_call(functools.partial(attend_kernel, columns=columns), out_sha...  5.21 us
    all_to_all x1, starting transfers between devices, per_device(): lax.all_to_all(partial, both, 0, 0, axis_index_groups=groups, tiled=True)  4.54 us
    pallas_call x1, Pallas kernels, share_send(): pl.pallas_call(share_kernel, grid_spec=pltpu.PrefetchScalarGridSpec(num_s...  4.04 us
  transfers between devices with their start and end apart: 14, of which 9 were waited for; matrix products, arithmetic and copies ran while one was open for 1% of the time, Pallas kernels for 12%

profile of v8, /device:TPU:0, one launch (start us, length us, event | category | flops | bytes accessed | tf_op | source)
XLA Modules:
  0.0 116.1 jit_solution(16577706390388343639)
XLA Ops:
  0.7 3.4 %fusion = bf16[4,128,352]{1,2,0:T(8,128)(2,1)S(1)} fusion(bf16[4,352,1408]{2,1,0:T(8,128)(2,1)} %bitcast.59, bf16[128,1408,1]{1,0,2:T(8,128)(2,1)} %bitcast.52), kind=kOutput, calls=%fused_computation.1 | convolution fusion | flops 507691008 | bytes 4685824 | tf_op jit(solution)/shard_map/to,jfo->jtf/dot_general | solution.py:361
  4.0 0.2 copy.13
  4.3 0.8 copy.14
  5.1 7.3 %all-to-all-start = ((bf16[32,2,8,352]{3,2,1,0:T(8,128)(2,1)}), bf16[32,2,8,352]{3,2,1,0:T(8,128)(2,1)S(1)}, u32[]{:S(2)}, u32[]{:S(2)}) async-start(bf16[32,2,8,352]{3,2,1,0:T(8,128)(2,1)} %bitcast.9), calls=%async_computation | async-start | bytes 786432 | tf_op jit(solution)/shard_map/all_to_all | solution.py:366
  12.4 0.0 copy-start.2
  12.4 4.4 %copy-done.2 = bf16[1408,4224]{1,0:T(8,128)(2,1)S(1)} copy-done((bf16[1408,4224]{1,0:T(8,128)(2,1)S(1)}, bf16[1408,4224]{1,0:T(8,128)(2,1)}, u32[]{:S(2)}) %copy-start.2) | copy-done | bytes 11894808
  16.8 0.9 shard_map.105.refs_2_
  17.7 2.7 %copy-done = bf16[3,1408,704]{2,1,0:T(8,128)(2,1)} copy-done((bf16[3,1408,704]{2,1,0:T(8,128)(2,1)}, bf16[3,1408,704]{2,1,0:T(8,128)(2,1)S(1)}, u32[]{:S(2)}) %copy-start) | copy-done | bytes 5947416
  20.5 1.4 %shard_map.104 = bf16[32,16,352]{2,1,0:T(8,128)(2,1)} custom-call(bf16[128,1408]{1,0:T(8,128)(2,1)S(1)} %bitcast.46, f32[1,1408]{1,0:T(1,128)S(1)} %broadcast_in_dim.23.gain_ref, f32[1,1408]{1,0:T(1,128)S(1)} %broadcast_in_dim.24.bias_ref), custom_call_target="tpu_custom_call" | custom-call | tf_op jit(solution)/shard_map/pallas_call | solution.py:76
  21.9 3.7 %all-to-all-done = bf16[32,2,8,352]{3,2,1,0:T(8,128)(2,1)S(1)} async-done(((bf16[32,2,8,352]{3,2,1,0:T(8,128)(2,1)}), bf16[32,2,8,352]{3,2,1,0:T(8,128)(2,1)S(1)}, u32[]{:S(2)}, u32[]{:S(2)}) %all-to-all-start) | async-done | bytes 360480 | tf_op jit(solution)/shard_map/all_to_all | solution.py:366
  25.5 5.2 %shard_map.106 = (bf16[3,352,512]{2,1,0:T(8,128)(2,1)S(1)}, bf16[1,352,512]{2,1,0:T(8,128)(2,1)S(1)}, bf16[2,352,512]{2,1,0:T(8,128)(2,1)S(1)}) custom-call(bf16[512,352]{1,0:T(8,128)(2,1)S(1)} %bitcast.49, bf16[512,352]{1,0:T(8,128)(2,1)S(1)} %bitcast.50, bf16[512,352]{1,0:T(8,128)(2,1)S(1)} %bitcast.51, bf16[512,352]{1,0:T(8,128)(2,1)S(1)} %bitcast.45), custom_call_target="tpu_custom_call" | custom-call | tf_op jit(solution)/shard_map/pallas_call | solution.py:51
  30.8 0.9 copy-done.10
  31.7 0.8 copy-done.11
  32.4 0.0 collective-permute-start
  32.4 3.6 %all-to-all-start.1 = ((bf16[32,16,352]{2,1,0:T(8,128)(2,1)}), bf16[32,16,352]{2,1,0:T(8,128)(2,1)S(1)}, u32[]{:S(2)}, u32[]{:S(2)}) async-start(bf16[32,16,352]{2,1,0:T(8,128)(2,1)} %shard_map.104), calls=%async_computation.1 | async-start | bytes 786432 | tf_op jit(solution)/shard_map/all_to_all | solution.py:373
  36.1 0.0 collective-permute-done.refs_1_
  36.1 1.8 %collective-permute-start.2 = (bf16[2,352,512]{2,1,0:T(8,128)(2,1)}, bf16[2,352,512]{2,1,0:T(8,128)(2,1)}, u32[]{:S(2)}, u32[]{:S(2)}) collective-permute-start(bf16[2,352,512]{2,1,0:T(8,128)(2,1)} %copy-done.10), channel_id=1, source_target_pairs={{0,4},{4,0},{8,12},{12,8},{16,20},{20,16},{24,28},{28,24},{1,5},{5... | collective-permute-start | bytes 2162696 | tf_op jit(solution)/shard_map/ppermute | solution.py:358
  37.9 2.8 %copy-done.1 = bf16[3,1408,704]{2,1,0:T(8,128)(2,1)S(1)} copy-done((bf16[3,1408,704]{2,1,0:T(8,128)(2,1)S(1)}, bf16[3,1408,704]{2,1,0:T(8,128)(2,1)}, u32[]{:S(2)}) %copy-start.1) | copy-done | bytes 5947416
  40.8 4.0 %shard_map.108 = (bf16[8,16,1408]{2,1,0:T(8,128)(2,1)}, f32[8,16,1408]{2,1,0:T(8,128)S(1)}) custom-call(s32[1]{0:T(128)} %bitcast.15.where_ref, bf16[3,352,512]{2,1,0:T(8,128)(2,1)S(1)} %get-tuple-element.33.refs_0_, bf16[3,352,512]{2,1,0:T(8,128)(2,1)S(1)} %collective-permute-done.refs_1_, bf16[3,1408,704]{2,1,0:T(8,128)(2,1)S(1)} %copy-done.1), custom_call_target="tpu_custom_call" | custom-call | tf_op jit(solution)/shard_map/pallas_call | solution.py:164
  44.8 0.9 copy-done.4
  45.7 1.5 %collective-permute-start.4 = (bf16[8,16,1408]{2,1,0:T(8,128)(2,1)}, bf16[8,16,1408]{2,1,0:T(8,128)(2,1)}, u32[]{:S(2)}, u32[]{:S(2)}) collective-permute-start(bf16[8,16,1408]{2,1,0:T(8,128)(2,1)} %get-tuple-element.41), channel_id=1, source_target_pairs={{0,2},{1,3},{2,0},{3,1},{4,6},{5,7},{6,4},{7,5},{8,10},{9,11},{10,... | collective-permute-start | bytes 1081352 | tf_op jit(solution)/shard_map/ppermute | solution.py:358
  47.1 2.1 %all-to-all-done.1 = bf16[32,16,352]{2,1,0:T(8,128)(2,1)S(1)} async-done(((bf16[32,16,352]{2,1,0:T(8,128)(2,1)}), bf16[32,16,352]{2,1,0:T(8,128)(2,1)S(1)}, u32[]{:S(2)}, u32[]{:S(2)}) %all-to-all-start.1) | async-done | bytes 360480 | tf_op jit(solution)/shard_map/all_to_all | solution.py:373
  49.3 0.5 collective-permute-start.3
  49.7 1.5 %collective-permute-start.1 = (bf16[1,352,512]{2,1,0:T(8,128)(2,1)}, bf16[1,352,512]{2,1,0:T(8,128)(2,1)}, u32[]{:S(2)}, u32[]{:S(2)}) collective-permute-start(bf16[1,352,512]{2,1,0:T(8,128)(2,1)} %copy-done.11), channel_id=1, source_target_pairs={{0,4},{4,0},{8,12},{12,8},{16,20},{20,16},{24,28},{28,24},{1,5},{5... | collective-permute-start | bytes 1081352 | tf_op jit(solution)/shard_map/ppermute | solution.py:358
  51.2 6.1 %collective-permute-done.4.come_ref = bf16[8,16,1408]{2,1,0:T(8,128)(2,1)} collective-permute-done((bf16[8,16,1408]{2,1,0:T(8,128)(2,1)}, bf16[8,16,1408]{2,1,0:T(8,128)(2,1)}, u32[]{:S(2)}, u32[]{:S(2)}) %collective-permute-start.4) | collective-permute-done | bytes 360480 | tf_op jit(solution)/shard_map/ppermute | solution.py:358
  57.3 1.1 copy-done.5
  58.4 1.1 shard_map.109
  59.5 1.5 %collective-permute-start.5 = (bf16[2,16,1408]{2,1,0:T(8,128)(2,1)S(1)}, bf16[2,16,1408]{2,1,0:T(8,128)(2,1)S(1)}, u32[]{:S(2)}, u32[]{:S(2)}) collective-permute-start(bf16[2,16,1408]{2,1,0:T(8,128)(2,1)S(1)} %get-tuple-element.58), channel_id=1, source_target_pairs={{0,8},{4,12},{8,0},{12,4},{16,24},{20,28},{24,16},{28,20},{1,9},{5... | collective-permute-start | bytes 270344 | tf_op jit(solution)/shard_map/ppermute | solution.py:358
  61.1 2.4 %collective-permute-start.6 = (bf16[2,16,1408]{2,1,0:T(8,128)(2,1)S(1)}, bf16[2,16,1408]{2,1,0:T(8,128)(2,1)S(1)}, u32[]{:S(2)}, u32[]{:S(2)}) collective-permute-start(bf16[2,16,1408]{2,1,0:T(8,128)(2,1)S(1)} %get-tuple-element.57), channel_id=1, source_target_pairs={{0,16},{4,20},{8,24},{12,28},{16,0},{20,4},{24,8},{28,12},{1,17},{... | collective-permute-start | bytes 270344 | tf_op jit(solution)/shard_map/ppermute | solution.py:358
  63.5 1.1 collective-permute-done.3.theirs_ref
  64.6 1.3 %shard_map.107.acc_ref = f32[2112,352]{1,0:T(8,128)S(1)} custom-call(s32[1]{0:T(128)} %bitcast.1.chip_ref, bf16[512,352]{1,0:T(8,128)(2,1)S(1)} %bitcast.43, bf16[512,352]{1,0:T(8,128)(2,1)S(1)} %collective-permute-done.3.theirs_ref, bf16[3,352,512]{2,1,0:T(8,128)(2,1)S(1)} %get-tuple-element.33.refs_0_, bf16[3,352,512]{2,1,0:T(8,128)(2,1)S(1)} %collective-permute-done.refs_1_), custom_call_target="tpu_custom_call" | custom-call | tf_op jit(solution)/shard_map/pallas_call | solution.py:196
  65.9 0.5 collective-permute-done.1.refs_0_
  66.4 0.0 collective-permute-done.5
  66.5 1.0 collective-permute-done.6
  67.5 0.0 collective-permute-done.2.refs_1_
  67.5 0.0 collective-permute-start.8
  67.5 0.5 collective-permute-start.7
  68.0 2.4 %collective-permute-start.9 = (bf16[2,16,1408]{2,1,0:T(8,128)(2,1)S(1)}, bf16[2,16,1408]{2,1,0:T(8,128)(2,1)}, u32[]{:S(2)}, u32[]{:S(2)}) collective-permute-start(bf16[2,16,1408]{2,1,0:T(8,128)(2,1)S(1)} %get-tuple-element.56), channel_id=1, source_target_pairs={{0,24},{4,28},{8,16},{12,20},{16,8},{20,12},{24,0},{28,4},{1,25},{... | collective-permute-start | bytes 270344 | tf_op jit(solution)/shard_map/ppermute | solution.py:358
  70.4 0.0 collective-permute-done.8.refs_3_
  70.4 4.0 %shard_map.110 = bf16[8,726,128]{2,1,0:T(8,128)(2,1)} custom-call(s32[1]{0:T(128)} %bitcast.1.chip_ref, bf16[512,352]{1,0:T(8,128)(2,1)S(1)} %bitcast.44, bf16[512,352]{1,0:T(8,128)(2,1)S(1)} %collective-permute-done.3.theirs_ref, f32[2112,352]{1,0:T(8,128)S(1)} %shard_map.107.acc_ref, bf16[1,352,512]{2,1,0:T(8,128)(2,1)} %collective-permute-done.1.refs_0_, ...), custom_call_target="tpu_custom_call" | custom-call | tf_op jit(solution)/shard_map/pallas_call | solution.py:242
  74.4 0.1 collective-permute-done.9
  74.6 4.5 %all-to-all-start.2 = ((bf16[8,726,128]{2,1,0:T(8,128)(2,1)}), bf16[8,726,128]{2,1,0:T(8,128)(2,1)S(1)}, u32[]{:S(2)}, u32[]{:S(2)}) async-start(bf16[8,726,128]{2,1,0:T(8,128)(2,1)} %shard_map.110), calls=%async_computation.2 | async-start | bytes 2981888 | tf_op jit(solution)/shard_map/all_to_all | solution.py:404
  79.1 1.0 pad_maximum_fusion
  80.1 0.5 collective-permute-start.10
  80.6 5.8 %collective-permute-done.10.come_ref = bf16[4,16,1408]{2,1,0:T(8,128)(2,1)S(1)} collective-permute-done((bf16[4,16,1408]{2,1,0:T(8,128)(2,1)S(1)}, bf16[4,16,1408]{2,1,0:T(8,128)(2,1)S(1)}, u32[]{:S(2)}, u32[]{:S(2)}) %collective-permute-start.10) | collective-permute-done | bytes 180256 | tf_op jit(solution)/shard_map/ppermute | solution.py:358
  86.5 1.3 %shard_map.111 = bf16[128,1408]{1,0:T(8,128)(2,1)} custom-call(s32[1]{0:T(128)} %bitcast.tm_ref, bf16[4,16,1408]{2,1,0:T(8,128)(2,1)S(1)} %get-tuple-element.55.stay_ref, bf16[4,16,1408]{2,1,0:T(8,128)(2,1)S(1)} %collective-permute-done.10.come_ref, bf16[128,1408]{1,0:T(8,128)(2,1)S(1)} %bitcast.47, bf16[128,1408]{1,0:T(8,128)(2,1)S(1)} %bitcast.53, ...), custom_call_target="tpu_custom_call" | custom-call | tf_op jit(solution)/shard_map/pallas_call | solution.py:287
  87.8 26.8 %all-to-all-done.2 = bf16[8,726,128]{2,1,0:T(8,128)(2,1)S(1)} async-done(((bf16[8,726,128]{2,1,0:T(8,128)(2,1)}), bf16[8,726,128]{2,1,0:T(8,128)(2,1)S(1)}, u32[]{:S(2)}, u32[]{:S(2)}) %all-to-all-start.2) | async-done | bytes 1486880 | tf_op jit(solution)/shard_map/all_to_all | solution.py:404
  114.6 1.5 %shard_map.112 = f32[44,4224]{1,0:T(8,128)} custom-call(s32[1]{0:T(128)} %bitcast.28.core_ref, bf16[4,2,726,128]{3,2,1,0:T(8,128)(2,1)S(1)} %bitcast.41), custom_call_target="tpu_custom_call" | custom-call | tf_op jit(solution)/shard_map/pallas_call | solution.py:328
  (27 shorter events, 0.1 us)
Async XLA Ops:
  0.6 11.7 %copy-start.13 = (f32[1408]{0:T(1024)S(1)}, f32[1408]{0:T(1024)}, u32[]{:S(2)}) copy-start(f32[1408]{0:T(1024)} %param.10) | copy-start | bytes 16900
  0.6 11.8 %copy-start.14 = (f32[1408]{0:T(1024)S(1)}, f32[1408]{0:T(1024)}, u32[]{:S(2)}) copy-start(f32[1408]{0:T(1024)} %param.11) | copy-start | bytes 16900
  5.1 20.5 %all-to-all-start = ((bf16[32,2,8,352]{3,2,1,0:T(8,128)(2,1)}), bf16[32,2,8,352]{3,2,1,0:T(8,128)(2,1)S(1)}, u32[]{:S(2)}, u32[]{:S(2)}) async-start(bf16[32,2,8,352]{3,2,1,0:T(8,128)(2,1)} %bitcast.9), calls=%async_computation | async-start | bytes 786432 | tf_op jit(solution)/shard_map/all_to_all | solution.py:366
  12.4 4.4 %copy-start.2 = (bf16[1408,4224]{1,0:T(8,128)(2,1)S(1)}, bf16[1408,4224]{1,0:T(8,128)(2,1)}, u32[]{:S(2)}) copy-start(bf16[1408,4224]{1,0:T(8,128)(2,1)} %w_ref) | copy-start | bytes 35684356
  16.8 3.6 %copy-start.3 = (bf16[2,64,1408]{2,1,0:T(8,128)(2,1)S(1)}, bf16[2,64,1408]{2,1,0:T(8,128)(2,1)}, u32[]{:S(2)}) copy-start(bf16[2,64,1408]{2,1,0:T(8,128)(2,1)} %param.9) | copy-start | bytes 1081348
  16.8 8.7 %copy-start.6 = (bf16[64,8,352]{2,1,0:T(8,128)(2,1)S(1)}, bf16[64,8,352]{2,1,0:T(8,128)(2,1)}, u32[]{:S(2)}) copy-start(bf16[64,8,352]{2,1,0:T(8,128)(2,1)} %param.14) | copy-start | bytes 1081348
  16.8 8.7 %copy-start.7 = (bf16[64,8,352]{2,1,0:T(8,128)(2,1)S(1)}, bf16[64,8,352]{2,1,0:T(8,128)(2,1)}, u32[]{:S(2)}) copy-start(bf16[64,8,352]{2,1,0:T(8,128)(2,1)} %param.15) | copy-start | bytes 1081348
  16.8 8.7 %copy-start.8 = (bf16[64,8,352]{2,1,0:T(8,128)(2,1)S(1)}, bf16[64,8,352]{2,1,0:T(8,128)(2,1)}, u32[]{:S(2)}) copy-start(bf16[64,8,352]{2,1,0:T(8,128)(2,1)} %param.16) | copy-start | bytes 1081348
  17.7 2.7 %copy-start = (bf16[3,1408,704]{2,1,0:T(8,128)(2,1)}, bf16[3,1408,704]{2,1,0:T(8,128)(2,1)S(1)}, u32[]{:S(2)}) copy-start(bf16[3,1408,704]{2,1,0:T(8,128)(2,1)S(1)} %shard_map.105.refs_2_) | copy-start | bytes 17842180
  30.8 0.9 copy-start.10
  31.7 0.8 copy-start.11
  32.4 3.6 %collective-permute-start = (bf16[3,352,512]{2,1,0:T(8,128)(2,1)S(1)}, bf16[3,352,512]{2,1,0:T(8,128)(2,1)S(1)}, u32[]{:S(2)}, u32[]{:S(2)}) collective-permute-start(bf16[3,352,512]{2,1,0:T(8,128)(2,1)S(1)} %get-tuple-element.33.refs_0_), channel_id=1, source_target_pairs={{0,1},{1,0},{2,3},{3,2},{4,5},{5,4},{6,7},{7,6},{8,9},{9,8},{10,11... | collective-permute-start | bytes 3244040 | tf_op jit(solution)/shard_map/ppermute | solution.py:358
  32.4 16.8 %all-to-all-start.1 = ((bf16[32,16,352]{2,1,0:T(8,128)(2,1)}), bf16[32,16,352]{2,1,0:T(8,128)(2,1)S(1)}, u32[]{:S(2)}, u32[]{:S(2)}) async-start(bf16[32,16,352]{2,1,0:T(8,128)(2,1)} %shard_map.104), calls=%async_computation.1 | async-start | bytes 786432 | tf_op jit(solution)/shard_map/all_to_all | solution.py:373
  36.1 31.4 %collective-permute-start.2 = (bf16[2,352,512]{2,1,0:T(8,128)(2,1)}, bf16[2,352,512]{2,1,0:T(8,128)(2,1)}, u32[]{:S(2)}, u32[]{:S(2)}) collective-permute-start(bf16[2,352,512]{2,1,0:T(8,128)(2,1)} %copy-done.10), channel_id=1, source_target_pairs={{0,4},{4,0},{8,12},{12,8},{16,20},{20,16},{24,28},{28,24},{1,5},{5... | collective-permute-start | bytes 2162696 | tf_op jit(solution)/shard_map/ppermute | solution.py:358
  37.9 2.8 %copy-start.1 = (bf16[3,1408,704]{2,1,0:T(8,128)(2,1)S(1)}, bf16[3,1408,704]{2,1,0:T(8,128)(2,1)}, u32[]{:S(2)}) copy-start(bf16[3,1408,704]{2,1,0:T(8,128)(2,1)} %copy-done) | copy-start | bytes 17842180
  44.8 0.9 copy-start.4
  45.7 11.6 %collective-permute-start.4 = (bf16[8,16,1408]{2,1,0:T(8,128)(2,1)}, bf16[8,16,1408]{2,1,0:T(8,128)(2,1)}, u32[]{:S(2)}, u32[]{:S(2)}) collective-permute-start(bf16[8,16,1408]{2,1,0:T(8,128)(2,1)} %get-tuple-element.41), channel_id=1, source_target_pairs={{0,2},{1,3},{2,0},{3,1},{4,6},{5,7},{6,4},{7,5},{8,10},{9,11},{10,... | collective-permute-start | bytes 1081352 | tf_op jit(solution)/shard_map/ppermute | solution.py:358
  49.3 15.3 %collective-permute-start.3 = (bf16[512,352]{1,0:T(8,128)(2,1)S(1)}, bf16[512,352]{1,0:T(8,128)(2,1)S(1)}, u32[]{:S(2)}, u32[]{:S(2)}) collective-permute-start(bf16[512,352]{1,0:T(8,128)(2,1)S(1)} %bitcast.42), channel_id=1, source_target_pairs={{0,2},{1,3},{2,0},{3,1},{4,6},{5,7},{6,4},{7,5},{8,10},{9,11},{10,... | collective-permute-start | bytes 1081352 | tf_op jit(solution)/shard_map/ppermute | solution.py:358
  49.7 16.7 %collective-permute-start.1 = (bf16[1,352,512]{2,1,0:T(8,128)(2,1)}, bf16[1,352,512]{2,1,0:T(8,128)(2,1)}, u32[]{:S(2)}, u32[]{:S(2)}) collective-permute-start(bf16[1,352,512]{2,1,0:T(8,128)(2,1)} %copy-done.11), channel_id=1, source_target_pairs={{0,4},{4,0},{8,12},{12,8},{16,20},{20,16},{24,28},{28,24},{1,5},{5... | collective-permute-start | bytes 1081352 | tf_op jit(solution)/shard_map/ppermute | solution.py:358
  57.3 1.1 copy-start.5
  59.5 6.9 %collective-permute-start.5 = (bf16[2,16,1408]{2,1,0:T(8,128)(2,1)S(1)}, bf16[2,16,1408]{2,1,0:T(8,128)(2,1)S(1)}, u32[]{:S(2)}, u32[]{:S(2)}) collective-permute-start(bf16[2,16,1408]{2,1,0:T(8,128)(2,1)S(1)} %get-tuple-element.58), channel_id=1, source_target_pairs={{0,8},{4,12},{8,0},{12,4},{16,24},{20,28},{24,16},{28,20},{1,9},{5... | collective-permute-start | bytes 270344 | tf_op jit(solution)/shard_map/ppermute | solution.py:358
  61.1 6.4 %collective-permute-start.6 = (bf16[2,16,1408]{2,1,0:T(8,128)(2,1)S(1)}, bf16[2,16,1408]{2,1,0:T(8,128)(2,1)S(1)}, u32[]{:S(2)}, u32[]{:S(2)}) collective-permute-start(bf16[2,16,1408]{2,1,0:T(8,128)(2,1)S(1)} %get-tuple-element.57), channel_id=1, source_target_pairs={{0,16},{4,20},{8,24},{12,28},{16,0},{20,4},{24,8},{28,12},{1,17},{... | collective-permute-start | bytes 270344 | tf_op jit(solution)/shard_map/ppermute | solution.py:358
  67.5 3.0 %copy-start.12 = (bf16[2,16,1408]{2,1,0:T(8,128)(2,1)}, bf16[2,16,1408]{2,1,0:T(8,128)(2,1)S(1)}, u32[]{:S(2)}) copy-start(bf16[2,16,1408]{2,1,0:T(8,128)(2,1)S(1)} %collective-permute-done.6) | copy-start | bytes 270340
  67.5 3.0 %collective-permute-start.8 = (bf16[2,352,512]{2,1,0:T(8,128)(2,1)}, bf16[2,352,512]{2,1,0:T(8,128)(2,1)S(1)}, u32[]{:S(2)}, u32[]{:S(2)}) collective-permute-start(bf16[2,352,512]{2,1,0:T(8,128)(2,1)} %collective-permute-done.2.refs_1_), channel_id=1, source_target_pairs={{0,1},{1,0},{2,3},{3,2},{4,5},{5,4},{6,7},{7,6},{8,9},{9,8},{10,11... | collective-permute-start | bytes 2162696 | tf_op jit(solution)/shard_map/ppermute | solution.py:358
  67.5 2.9 %collective-permute-start.7 = (bf16[1,352,512]{2,1,0:T(8,128)(2,1)}, bf16[1,352,512]{2,1,0:T(8,128)(2,1)S(1)}, u32[]{:S(2)}, u32[]{:S(2)}) collective-permute-start(bf16[1,352,512]{2,1,0:T(8,128)(2,1)} %collective-permute-done.1.refs_0_), channel_id=1, source_target_pairs={{0,1},{1,0},{2,3},{3,2},{4,5},{5,4},{6,7},{7,6},{8,9},{9,8},{10,11... | collective-permute-start | bytes 1081352 | tf_op jit(solution)/shard_map/ppermute | solution.py:358
  68.0 6.6 %collective-permute-start.9 = (bf16[2,16,1408]{2,1,0:T(8,128)(2,1)S(1)}, bf16[2,16,1408]{2,1,0:T(8,128)(2,1)}, u32[]{:S(2)}, u32[]{:S(2)}) collective-permute-start(bf16[2,16,1408]{2,1,0:T(8,128)(2,1)S(1)} %get-tuple-element.56), channel_id=1, source_target_pairs={{0,24},{4,28},{8,16},{12,20},{16,8},{20,12},{24,0},{28,4},{1,25},{... | collective-permute-start | bytes 270344 | tf_op jit(solution)/shard_map/ppermute | solution.py:358
  74.4 12.0 %copy-start.9 = (bf16[2,64,1408]{2,1,0:T(8,128)(2,1)S(1)}, bf16[2,64,1408]{2,1,0:T(8,128)(2,1)}, u32[]{:S(2)}) copy-start(bf16[2,64,1408]{2,1,0:T(8,128)(2,1)} %param.17) | copy-start | bytes 1081348
  74.6 40.0 %all-to-all-start.2 = ((bf16[8,726,128]{2,1,0:T(8,128)(2,1)}), bf16[8,726,128]{2,1,0:T(8,128)(2,1)S(1)}, u32[]{:S(2)}, u32[]{:S(2)}) async-start(bf16[8,726,128]{2,1,0:T(8,128)(2,1)} %shard_map.110), calls=%async_computation.2 | async-start | bytes 2981888 | tf_op jit(solution)/shard_map/all_to_all | solution.py:404
  80.1 6.3 %collective-permute-start.10 = (bf16[4,16,1408]{2,1,0:T(8,128)(2,1)S(1)}, bf16[4,16,1408]{2,1,0:T(8,128)(2,1)S(1)}, u32[]{:S(2)}, u32[]{:S(2)}) collective-permute-start(bf16[4,16,1408]{2,1,0:T(8,128)(2,1)S(1)} %get-tuple-element.54), channel_id=1, source_target_pairs={{0,4},{4,0},{8,12},{12,8},{16,20},{20,16},{24,28},{28,24},{1,5},{5... | collective-permute-start | bytes 540680 | tf_op jit(solution)/shard_map/ppermute | solution.py:358

commit v9 on v8

--- a/solution.py
+++ b/solution.py
@@ -17,7 +17,7 @@
 ROOM = pltpu.CompilerParams(vmem_limit_bytes=28 * 1024 * 1024)
 
 
-def attend_kernel(q_ref, k_ref, v_ref, d_ref, all_ref, query_ref, rest_ref, *, columns):
+def attend_kernel(q_ref, k_ref, v_ref, d_ref, all_ref, query_ref, rest_ref, sem, *, columns):
     n_tok, width = q_ref.shape
     factor = 1.0 / math.sqrt(DH)
     source = lax.broadcasted_iota(jnp.int32, (n_tok, n_tok), 0)
@@ -34,23 +34,29 @@
         row_dot = jnp.sum(probability * prob_grad, axis=0, keepdims=True)
         score_grad = (probability * (prob_grad - row_dot) * factor).astype(BF)
         prob_low = probability.astype(BF)
-        for kind, (left, right, dims, out_ref) in enumerate(
-            (
-                (key, score_grad, ROWS, query_ref.at[0]),
-                (query, score_grad, CROSS, rest_ref.at[0]),
-                (grad, prob_low, CROSS, rest_ref.at[1]),
-            )
+        for kind, (left, right, dims) in enumerate(
+            ((key, score_grad, ROWS), (query, score_grad, CROSS), (grad, prob_low, CROSS))
         ):
-            total = lax.dot_general(left, right, dims, preferred_element_type=F32).astype(BF)
-            out_ref[lanes, :] = total
-            all_ref[kind, lanes, :] = total
+            total = lax.dot_general(left, right, dims, preferred_element_type=F32)
+            all_ref[kind, lanes, :] = total.astype(BF)
+    copies = [
+        pltpu.make_async_copy(all_ref.at[pl.ds(at, ref.shape[0])], ref, sem.at[at])
+        for at, ref in ((0, query_ref), (1, rest_ref))
+    ]
+    for copy in copies:
+        copy.start()
+    for copy in copies:
+        copy.wait()
 
 
 def attend(query, key, value, grad, columns):
     n_tok, width = query.shape
     return pl.pallas_call(
         functools.partial(attend_kernel, columns=columns),
-        out_shape=[jax.ShapeDtypeStruct((kinds, width, n_tok), BF) for kinds in (3, 1, 2)],
+        out_specs=[pl.BlockSpec(memory_space=pltpu.VMEM)] + [pl.BlockSpec(memory_space=pltpu.HBM)] * 2,
+        scratch_shapes=[pltpu.SemaphoreType.DMA((2,))],
+        out_shape=[jax.ShapeDtypeStruct((3, width, n_tok), BF)]
+        + [pltpu.HBM((kinds, width, n_tok), BF) for kinds in (1, 2)],
         compiler_params=ROOM,
     )(query, key, value, grad)
 
@@ -117,13 +123,18 @@
                 pltpu.SemaphoreType.DMA((kinds,)),
             ],
         ),
-        out_shape=jax.ShapeDtypeStruct((kinds, width, part), BF),
-        compiler_params=ROOM,
-    )(chip[None], w_qkv)
+        out_shape=pltpu.HBM((kinds, width, part), BF),
+        compiler_params=ROOM,
+    )(chip[None], pltpu.with_memory_space_constraint(w_qkv, pltpu.HBM))
 
 
 def share_kernel(where_ref, *refs):
-    grads_refs, (w_ref, leave_ref, stay_ref, turn_ref) = refs[:2], refs[2:]
+    grads_refs, (w_hbm, leave_ref, stay_hbm, turn_ref, w_ref, stay_ref, sem) = refs[:2], refs[2:]
+    copies = [
+        pltpu.make_async_copy(w_hbm.at[c], w_ref.at[c], sem.at[c]) for c in range(w_ref.shape[0])
+    ]
+    for copy in copies:
+        copy.start()
     patch = where_ref[0]
     chip, core = patch // 2, patch % 2
     kinds = w_ref.shape[0]
@@ -140,14 +151,18 @@
 
     total = None
     for c in range(kinds):
+        copies[c].wait()
         rows = jnp.concatenate(
             [turn_ref[c, :, which, core].reshape(n * group, 2 * part) for which in (1 - chip, chip)],
             axis=0,
         )
         one = lax.dot_general(rows, w_ref[c], COLS, preferred_element_type=F32)
         total = one if total is None else total + one
+    stay_ref[...] = total[n * group :].reshape(stay_ref.shape)
+    copy = pltpu.make_async_copy(stay_ref, stay_hbm, sem.at[kinds])
+    copy.start()
     leave_ref[...] = total[: n * group].reshape(leave_ref.shape).astype(BF)
-    stay_ref[...] = total[n * group :].reshape(stay_ref.shape)
+    copy.wait()
 
 
 def kinds_of(refs):
@@ -166,19 +181,30 @@
         grid_spec=pltpu.PrefetchScalarGridSpec(
             num_scalar_prefetch=1,
             grid=(1,),
-            in_specs=[whole_spec(array) for array in (*pieces, weights)],
-            out_specs=[pl.BlockSpec((n, group, width), lambda i, s: (0, 0, 0))] * 2,
-            scratch_shapes=[pltpu.VMEM((kinds, n, 2, 2, group, double), BF)],
+            in_specs=[whole_spec(array) for array in pieces] + [pl.BlockSpec(memory_space=pltpu.HBM)],
+            out_specs=[
+                pl.BlockSpec((n, group, width), lambda i, s: (0, 0, 0)),
+                pl.BlockSpec(memory_space=pltpu.HBM),
+            ],
+            scratch_shapes=[
+                pltpu.VMEM((kinds, n, 2, 2, group, double), BF),
+                pltpu.VMEM((kinds, width, double), BF),
+                pltpu.VMEM((n, group, width), F32),
+                pltpu.SemaphoreType.DMA((kinds + 1,)),
+            ],
         ),
         out_shape=[
             jax.ShapeDtypeStruct((n, group, width), BF),
-            jax.ShapeDtypeStruct((n, group, width), F32),
+            pltpu.HBM((n, group, width), F32),
         ],
         compiler_params=ROOM,
-    )(patch[None], *pieces, weights)
-
-
-def add_kernel(stay_ref, come_ref, out_ref):
+    )(patch[None], *pieces, pltpu.with_memory_space_constraint(weights, pltpu.HBM))
+
+
+def add_kernel(stay_hbm, come_ref, out_ref, stay_ref, sem):
+    copy = pltpu.make_async_copy(stay_hbm, stay_ref, sem)
+    copy.start()
+    copy.wait()
     out_ref[...] = (stay_ref[...] + come_ref[...].astype(F32)).astype(BF)
 
 
@@ -382,8 +408,12 @@
     leave, stay = share_send(pieces, weights, patch, t_dev * columns)
     come = swap(leave, "patch", n_patch, 2)
     share = pl.pallas_call(
-        add_kernel, out_shape=jax.ShapeDtypeStruct(leave.shape, BF), compiler_params=ROOM
-    )(stay, come)
+        add_kernel,
+        in_specs=[pl.BlockSpec(memory_space=space) for space in (pltpu.HBM, pltpu.VMEM)],
+        out_shape=jax.ShapeDtypeStruct(leave.shape, BF),
+        scratch_shapes=[pltpu.VMEM(stay.shape, F32), pltpu.SemaphoreType.DMA(())],
+        compiler_params=ROOM,
+    )(pltpu.with_memory_space_constraint(stay, pltpu.HBM), come)
     share = share.reshape((n_pair, 2) + share.shape[1:])
     spread = [lax.dynamic_index_in_dim(share, (tm // 2) ^ n, 0, keepdims=False) for n in range(n_pair)]
     spread = spread[:1] + [swap(spread[n], "tm", n_tm, 2 * n) for n in range(1, n_pair)]

time: 117 us -> 115 us (0.983)
  local copies, waits for them, and re-layouts: 14.7 us -> 1.77 us
  Pallas kernels: 20.7 us -> 30 us
  waiting for transfers between devices: 47.3 us -> 50.6 us
    unnamed x30 -> x18, local copies, waits for them, and re-layouts: 13.6 us -> 0.67 us
    pallas_call x1, Pallas kernels: 0.89 us -> 6.19 us  [own_weights(): pl.pallas_call(functools.partial(weights_kernel, n_chip=n_chip), grid_spe...]
    pallas_call x2, Pallas kernels: 6.28 us -> 8.36 us  [the longest x1 6.19 us: attend(): pl.pallas_call(functools.partial(attend_kernel, columns=columns), out_spe...]
    pallas_call x1, Pallas kernels: 4.04 us -> 6.05 us  [share_send(): pl.pallas_call(share_kernel, grid_spec=pltpu.PrefetchScalarGridSpec(num_s...]
    all_to_all x1, waiting for transfers between devices: 3.68 us -> 5.44 us  [per_device(): lax.all_to_all(d_attn.reshape(devices, t_dev, columns, part), both, 0, 0,...]
    all_to_all x1, waiting for transfers between devices: 2.13 us -> 3.75 us  [per_device(): lax.all_to_all(sent, both, 0, 0, tiled=True).reshape(n_tok, width // 4)]
  transfers between devices with their start and end apart: 14 -> 14, of which waited for: 9 -> 7; matrix products, arithmetic and copies ran while one was open for 1% -> 0% of each run, Pallas kernels for 12% -> 19%
where the time goes in v9:
time: 115 us
  waiting for transfers between devices  50.6 us (44%)
  Pallas kernels  30 us (26%)
  starting transfers between devices  28.3 us (25%)
  matrix products  3.38 us (3%)
  local copies, waits for them, and re-layouts  1.77 us (2%)
    all_to_all x1, waiting for transfers between devices, per_device(): lax.all_to_all(partial, both, 0, 0, axis_index_groups=groups, tiled=True)  27.7 us
    ppermute x11, waiting for transfers between devices, swap(): return lax.ppermute(values, axis, [(i, i ^ bit) for i in range(size)])  13.7 us
    ppermute x11, starting transfers between devices, swap(): return lax.ppermute(values, axis, [(i, i ^ bit) for i in range(size)])  13.6 us
    all_to_all x1, starting transfers between devices, per_device(): lax.all_to_all(d_attn.reshape(devices, t_dev, columns, part), both, 0, 0,...  7.29 us
    pallas_call x1, Pallas kernels, attend(): pl.pallas_call(functools.partial(attend_kernel, columns=columns), out_spe...  6.19 us
    pallas_call x1, Pallas kernels, own_weights(): pl.pallas_call(functools.partial(weights_kernel, n_chip=n_chip), grid_spe...  6.19 us
    pallas_call x1, Pallas kernels, share_send(): pl.pallas_call(share_kernel, grid_spec=pltpu.PrefetchScalarGridSpec(num_s...  6.05 us
    all_to_all x1, waiting for transfers between devices, per_device(): lax.all_to_all(d_attn.reshape(devices, t_dev, columns, part), both, 0, 0,...  5.44 us
  transfers between devices with their start and end apart: 14, of which 7 were waited for; matrix products, arithmetic and copies ran while one was open for 0% of the time, Pallas kernels for 19%

profile of v9, /device:TPU:0, one launch (start us, length us, event | category | flops | bytes accessed | tf_op | source)
XLA Modules:
  0.0 115.1 jit_solution(13893787018127348315)
XLA Ops:
  0.6 0.0 copy-start.7
  0.6 0.0 copy-start.8
  0.7 3.4 %fusion = bf16[4,128,352]{1,2,0:T(8,128)(2,1)S(1)} fusion(bf16[4,352,1408]{2,1,0:T(8,128)(2,1)} %bitcast.60, bf16[128,1408,1]{1,0,2:T(8,128)(2,1)} %bitcast.52), kind=kOutput, calls=%fused_computation.1 | convolution fusion | flops 507691008 | bytes 4685824 | tf_op jit(solution)/shard_map/to,jfo->jtf/dot_general | solution.py:387
  4.0 0.2 copy.13
  4.3 0.8 copy.14
  5.1 7.3 %all-to-all-start = ((bf16[32,2,8,352]{3,2,1,0:T(8,128)(2,1)}), bf16[32,2,8,352]{3,2,1,0:T(8,128)(2,1)S(1)}, u32[]{:S(2)}, u32[]{:S(2)}) async-start(bf16[32,2,8,352]{3,2,1,0:T(8,128)(2,1)} %bitcast.9), calls=%async_computation | async-start | bytes 786432 | tf_op jit(solution)/shard_map/all_to_all | solution.py:392
  12.4 0.0 copy-start
  12.4 0.0 copy-start.1
  12.5 0.0 copy-start.2
  12.5 0.0 copy-start.3
  12.5 6.2 %shard_map.105.refs_2_ = bf16[3,1408,704]{2,1,0:T(8,128)(2,1)} custom-call(s32[1]{0:T(128)} %bitcast.1.chip_ref, bf16[1408,4224]{1,0:T(8,128)(2,1)} %w_ref), custom_call_target="tpu_custom_call" | custom-call | tf_op jit(solution)/shard_map/pallas_call | solution.py:114
  18.7 1.4 %shard_map.104 = bf16[32,16,352]{2,1,0:T(8,128)(2,1)} custom-call(bf16[128,1408]{1,0:T(8,128)(2,1)S(1)} %bitcast.46, f32[1,1408]{1,0:T(1,128)S(1)} %broadcast_in_dim.23.gain_ref, f32[1,1408]{1,0:T(1,128)S(1)} %broadcast_in_dim.24.bias_ref), custom_call_target="tpu_custom_call" | custom-call | tf_op jit(solution)/shard_map/pallas_call | solution.py:82
  20.1 5.4 %all-to-all-done = bf16[32,2,8,352]{3,2,1,0:T(8,128)(2,1)S(1)} async-done(((bf16[32,2,8,352]{3,2,1,0:T(8,128)(2,1)}), bf16[32,2,8,352]{3,2,1,0:T(8,128)(2,1)S(1)}, u32[]{:S(2)}, u32[]{:S(2)}) %all-to-all-start) | async-done | bytes 360480 | tf_op jit(solution)/shard_map/all_to_all | solution.py:392
  25.5 6.2 %shard_map.106 = (bf16[3,352,512]{2,1,0:T(8,128)(2,1)S(1)}, bf16[1,352,512]{2,1,0:T(8,128)(2,1)}, bf16[2,352,512]{2,1,0:T(8,128)(2,1)}) custom-call(bf16[512,352]{1,0:T(8,128)(2,1)S(1)} %bitcast.49, bf16[512,352]{1,0:T(8,128)(2,1)S(1)} %bitcast.50, bf16[512,352]{1,0:T(8,128)(2,1)S(1)} %bitcast.51, bf16[512,352]{1,0:T(8,128)(2,1)S(1)} %bitcast.45), custom_call_target="tpu_custom_call" | custom-call | tf_op jit(solution)/shard_map/pallas_call | solution.py:54
  31.7 0.1 collective-permute-start
  31.8 2.7 %all-to-all-start.1 = ((bf16[32,16,352]{2,1,0:T(8,128)(2,1)}), bf16[32,16,352]{2,1,0:T(8,128)(2,1)S(1)}, u32[]{:S(2)}, u32[]{:S(2)}) async-start(bf16[32,16,352]{2,1,0:T(8,128)(2,1)} %shard_map.104), calls=%async_computation.1 | async-start | bytes 786432 | tf_op jit(solution)/shard_map/all_to_all | solution.py:399
  34.6 0.0 collective-permute-done.refs_1_
  34.6 1.8 %collective-permute-start.2 = (bf16[2,352,512]{2,1,0:T(8,128)(2,1)}, bf16[2,352,512]{2,1,0:T(8,128)(2,1)}, u32[]{:S(2)}, u32[]{:S(2)}) collective-permute-start(bf16[2,352,512]{2,1,0:T(8,128)(2,1)} %get-tuple-element.37), channel_id=1, source_target_pairs={{0,4},{4,0},{8,12},{12,8},{16,20},{20,16},{24,28},{28,24},{1,5},{5... | collective-permute-start | bytes 2162696 | tf_op jit(solution)/shard_map/ppermute | solution.py:384
  36.4 6.0 %shard_map.108 = (bf16[8,16,1408]{2,1,0:T(8,128)(2,1)}, f32[8,16,1408]{2,1,0:T(8,128)}) custom-call(s32[1]{0:T(128)} %bitcast.15.where_ref, bf16[3,352,512]{2,1,0:T(8,128)(2,1)S(1)} %get-tuple-element.33.refs_0_, bf16[3,352,512]{2,1,0:T(8,128)(2,1)S(1)} %collective-permute-done.refs_1_, bf16[3,1408,704]{2,1,0:T(8,128)(2,1)} %shard_map.105.refs_2_), custom_call_target="tpu_custom_call" | custom-call | tf_op jit(solution)/shard_map/pallas_call | solution.py:179
  42.5 1.5 %collective-permute-start.4 = (bf16[8,16,1408]{2,1,0:T(8,128)(2,1)}, bf16[8,16,1408]{2,1,0:T(8,128)(2,1)}, u32[]{:S(2)}, u32[]{:S(2)}) collective-permute-start(bf16[8,16,1408]{2,1,0:T(8,128)(2,1)} %get-tuple-element.41), channel_id=1, source_target_pairs={{0,2},{1,3},{2,0},{3,1},{4,6},{5,7},{6,4},{7,5},{8,10},{9,11},{10,... | collective-permute-start | bytes 1081352 | tf_op jit(solution)/shard_map/ppermute | solution.py:384
  44.0 3.8 %all-to-all-done.1 = bf16[32,16,352]{2,1,0:T(8,128)(2,1)S(1)} async-done(((bf16[32,16,352]{2,1,0:T(8,128)(2,1)}), bf16[32,16,352]{2,1,0:T(8,128)(2,1)S(1)}, u32[]{:S(2)}, u32[]{:S(2)}) %all-to-all-start.1) | async-done | bytes 360480 | tf_op jit(solution)/shard_map/all_to_all | solution.py:399
  47.8 0.5 collective-permute-start.3
  48.2 1.5 %collective-permute-start.1 = (bf16[1,352,512]{2,1,0:T(8,128)(2,1)}, bf16[1,352,512]{2,1,0:T(8,128)(2,1)}, u32[]{:S(2)}, u32[]{:S(2)}) collective-permute-start(bf16[1,352,512]{2,1,0:T(8,128)(2,1)} %get-tuple-element.36), channel_id=1, source_target_pairs={{0,4},{4,0},{8,12},{12,8},{16,20},{20,16},{24,28},{28,24},{1,5},{5... | collective-permute-start | bytes 1081352 | tf_op jit(solution)/shard_map/ppermute | solution.py:384
  49.7 4.6 %collective-permute-done.4.come_ref = bf16[8,16,1408]{2,1,0:T(8,128)(2,1)} collective-permute-done((bf16[8,16,1408]{2,1,0:T(8,128)(2,1)}, bf16[8,16,1408]{2,1,0:T(8,128)(2,1)}, u32[]{:S(2)}, u32[]{:S(2)}) %collective-permute-start.4) | collective-permute-done | bytes 360480 | tf_op jit(solution)/shard_map/ppermute | solution.py:384
  54.3 2.2 %shard_map.109 = bf16[8,16,1408]{2,1,0:T(8,128)(2,1)S(1)} custom-call(f32[8,16,1408]{2,1,0:T(8,128)} %get-tuple-element.40.stay_hbm, bf16[8,16,1408]{2,1,0:T(8,128)(2,1)} %collective-permute-done.4.come_ref), custom_call_target="tpu_custom_call" | custom-call | tf_op jit(solution)/shard_map/pallas_call | solution.py:410
  56.5 1.5 %collective-permute-start.5 = (bf16[2,16,1408]{2,1,0:T(8,128)(2,1)S(1)}, bf16[2,16,1408]{2,1,0:T(8,128)(2,1)S(1)}, u32[]{:S(2)}, u32[]{:S(2)}) collective-permute-start(bf16[2,16,1408]{2,1,0:T(8,128)(2,1)S(1)} %get-tuple-element.58), channel_id=1, source_target_pairs={{0,8},{4,12},{8,0},{12,4},{16,24},{20,28},{24,16},{28,20},{1,9},{5... | collective-permute-start | bytes 270344 | tf_op jit(solution)/shard_map/ppermute | solution.py:384
  58.0 2.3 %collective-permute-start.6 = (bf16[2,16,1408]{2,1,0:T(8,128)(2,1)S(1)}, bf16[2,16,1408]{2,1,0:T(8,128)(2,1)S(1)}, u32[]{:S(2)}, u32[]{:S(2)}) collective-permute-start(bf16[2,16,1408]{2,1,0:T(8,128)(2,1)S(1)} %get-tuple-element.57), channel_id=1, source_target_pairs={{0,16},{4,20},{8,24},{12,28},{16,0},{20,4},{24,8},{28,12},{1,17},{... | collective-permute-start | bytes 270344 | tf_op jit(solution)/shard_map/ppermute | solution.py:384
  60.4 1.4 %collective-permute-done.3.theirs_ref = bf16[512,352]{1,0:T(8,128)(2,1)S(1)} collective-permute-done((bf16[512,352]{1,0:T(8,128)(2,1)S(1)}, bf16[512,352]{1,0:T(8,128)(2,1)S(1)}, u32[]{:S(2)}, u32[]{:S(2)}) %collective-permute-start.3) | collective-permute-done | bytes 360480 | tf_op jit(solution)/shard_map/ppermute | solution.py:384
  61.8 1.3 %shard_map.107.acc_ref = f32[2112,352]{1,0:T(8,128)S(1)} custom-call(s32[1]{0:T(128)} %bitcast.1.chip_ref, bf16[512,352]{1,0:T(8,128)(2,1)S(1)} %bitcast.43, bf16[512,352]{1,0:T(8,128)(2,1)S(1)} %collective-permute-done.3.theirs_ref, bf16[3,352,512]{2,1,0:T(8,128)(2,1)S(1)} %get-tuple-element.33.refs_0_, bf16[3,352,512]{2,1,0:T(8,128)(2,1)S(1)} %collective-permute-done.refs_1_), custom_call_target="tpu_custom_call" | custom-call | tf_op jit(solution)/shard_map/pallas_call | solution.py:222
  63.1 1.9 %collective-permute-done.1.refs_0_ = bf16[1,352,512]{2,1,0:T(8,128)(2,1)} collective-permute-done((bf16[1,352,512]{2,1,0:T(8,128)(2,1)}, bf16[1,352,512]{2,1,0:T(8,128)(2,1)}, u32[]{:S(2)}, u32[]{:S(2)}) %collective-permute-start.1) | collective-permute-done | bytes 360480 | tf_op jit(solution)/shard_map/ppermute | solution.py:384
  64.9 0.0 collective-permute-done.5
  64.9 0.0 collective-permute-done.6
  64.9 0.0 collective-permute-done.2.refs_1_
  65.0 0.6 copy-done.5
  65.6 0.0 collective-permute-start.8
  65.6 0.5 collective-permute-start.7
  66.1 3.4 %collective-permute-start.9 = (bf16[2,16,1408]{2,1,0:T(8,128)(2,1)S(1)}, bf16[2,16,1408]{2,1,0:T(8,128)(2,1)S(1)}, u32[]{:S(2)}, u32[]{:S(2)}) collective-permute-start(bf16[2,16,1408]{2,1,0:T(8,128)(2,1)S(1)} %get-tuple-element.56), channel_id=1, source_target_pairs={{0,24},{4,28},{8,16},{12,20},{16,8},{20,12},{24,0},{28,4},{1,25},{... | collective-permute-start | bytes 270344 | tf_op jit(solution)/shard_map/ppermute | solution.py:384
  69.5 0.0 collective-permute-done.7.refs_2_
  69.5 0.0 collective-permute-done.8.refs_3_
  69.5 3.9 %shard_map.110 = bf16[8,726,128]{2,1,0:T(8,128)(2,1)} custom-call(s32[1]{0:T(128)} %bitcast.1.chip_ref, bf16[512,352]{1,0:T(8,128)(2,1)S(1)} %bitcast.44, bf16[512,352]{1,0:T(8,128)(2,1)S(1)} %collective-permute-done.3.theirs_ref, f32[2112,352]{1,0:T(8,128)S(1)} %shard_map.107.acc_ref, bf16[1,352,512]{2,1,0:T(8,128)(2,1)} %collective-permute-done.1.refs_0_, ...), custom_call_target="tpu_custom_call" | custom-call | tf_op jit(solution)/shard_map/pallas_call | solution.py:268
  73.4 0.0 collective-permute-done.9
  73.4 4.7 %all-to-all-start.2 = ((bf16[8,726,128]{2,1,0:T(8,128)(2,1)}), bf16[8,726,128]{2,1,0:T(8,128)(2,1)S(1)}, u32[]{:S(2)}, u32[]{:S(2)}) async-start(bf16[8,726,128]{2,1,0:T(8,128)(2,1)} %shard_map.110), calls=%async_computation.2 | async-start | bytes 2981888 | tf_op jit(solution)/shard_map/all_to_all | solution.py:434
  78.1 0.1 pad_maximum_fusion
  78.2 0.5 collective-permute-start.10
  78.7 5.8 %collective-permute-done.10.come_ref = bf16[4,16,1408]{2,1,0:T(8,128)(2,1)S(1)} collective-permute-done((bf16[4,16,1408]{2,1,0:T(8,128)(2,1)S(1)}, bf16[4,16,1408]{2,1,0:T(8,128)(2,1)S(1)}, u32[]{:S(2)}, u32[]{:S(2)}) %collective-permute-start.10) | collective-permute-done | bytes 180256 | tf_op jit(solution)/shard_map/ppermute | solution.py:384
  84.5 1.3 %shard_map.111 = bf16[128,1408]{1,0:T(8,128)(2,1)} custom-call(s32[1]{0:T(128)} %bitcast.tm_ref, bf16[4,16,1408]{2,1,0:T(8,128)(2,1)S(1)} %get-tuple-element.55.stay_ref, bf16[4,16,1408]{2,1,0:T(8,128)(2,1)S(1)} %collective-permute-done.10.come_ref, bf16[128,1408]{1,0:T(8,128)(2,1)S(1)} %bitcast.47, bf16[128,1408]{1,0:T(8,128)(2,1)S(1)} %bitcast.53, ...), custom_call_target="tpu_custom_call" | custom-call | tf_op jit(solution)/shard_map/pallas_call | solution.py:313
  85.9 27.7 %all-to-all-done.2 = bf16[8,726,128]{2,1,0:T(8,128)(2,1)S(1)} async-done(((bf16[8,726,128]{2,1,0:T(8,128)(2,1)}), bf16[8,726,128]{2,1,0:T(8,128)(2,1)S(1)}, u32[]{:S(2)}, u32[]{:S(2)}) %all-to-all-start.2) | async-done | bytes 1486880 | tf_op jit(solution)/shard_map/all_to_all | solution.py:434
  113.6 1.5 %shard_map.112 = f32[44,4224]{1,0:T(8,128)} custom-call(s32[1]{0:T(128)} %bitcast.28.core_ref, bf16[4,2,726,128]{3,2,1,0:T(8,128)(2,1)S(1)} %bitcast.41), custom_call_target="tpu_custom_call" | custom-call | tf_op jit(solution)/shard_map/pallas_call | solution.py:354
  (15 shorter events, 0.1 us)
Async XLA Ops:
  0.6 11.7 %copy-start.7 = (f32[1408]{0:T(1024)S(1)}, f32[1408]{0:T(1024)}, u32[]{:S(2)}) copy-start(f32[1408]{0:T(1024)} %param.10) | copy-start | bytes 16900
  0.6 11.8 %copy-start.8 = (f32[1408]{0:T(1024)S(1)}, f32[1408]{0:T(1024)}, u32[]{:S(2)}) copy-start(f32[1408]{0:T(1024)} %param.11) | copy-start | bytes 16900
  5.1 20.5 %all-to-all-start = ((bf16[32,2,8,352]{3,2,1,0:T(8,128)(2,1)}), bf16[32,2,8,352]{3,2,1,0:T(8,128)(2,1)S(1)}, u32[]{:S(2)}, u32[]{:S(2)}) async-start(bf16[32,2,8,352]{3,2,1,0:T(8,128)(2,1)} %bitcast.9), calls=%async_computation | async-start | bytes 786432 | tf_op jit(solution)/shard_map/all_to_all | solution.py:392
  12.4 6.2 %copy-start = (bf16[2,64,1408]{2,1,0:T(8,128)(2,1)S(1)}, bf16[2,64,1408]{2,1,0:T(8,128)(2,1)}, u32[]{:S(2)}) copy-start(bf16[2,64,1408]{2,1,0:T(8,128)(2,1)} %param.9) | copy-start | bytes 1081348
  12.4 13.1 %copy-start.1 = (bf16[64,8,352]{2,1,0:T(8,128)(2,1)S(1)}, bf16[64,8,352]{2,1,0:T(8,128)(2,1)}, u32[]{:S(2)}) copy-start(bf16[64,8,352]{2,1,0:T(8,128)(2,1)} %param.14) | copy-start | bytes 1081348
  12.5 13.1 %copy-start.2 = (bf16[64,8,352]{2,1,0:T(8,128)(2,1)S(1)}, bf16[64,8,352]{2,1,0:T(8,128)(2,1)}, u32[]{:S(2)}) copy-start(bf16[64,8,352]{2,1,0:T(8,128)(2,1)} %param.15) | copy-start | bytes 1081348
  12.5 13.1 %copy-start.3 = (bf16[64,8,352]{2,1,0:T(8,128)(2,1)S(1)}, bf16[64,8,352]{2,1,0:T(8,128)(2,1)}, u32[]{:S(2)}) copy-start(bf16[64,8,352]{2,1,0:T(8,128)(2,1)} %param.16) | copy-start | bytes 1081348
  31.7 2.8 %collective-permute-start = (bf16[3,352,512]{2,1,0:T(8,128)(2,1)S(1)}, bf16[3,352,512]{2,1,0:T(8,128)(2,1)S(1)}, u32[]{:S(2)}, u32[]{:S(2)}) collective-permute-start(bf16[3,352,512]{2,1,0:T(8,128)(2,1)S(1)} %get-tuple-element.33.refs_0_), channel_id=1, source_target_pairs={{0,1},{1,0},{2,3},{3,2},{4,5},{5,4},{6,7},{7,6},{8,9},{9,8},{10,11... | collective-permute-start | bytes 3244040 | tf_op jit(solution)/shard_map/ppermute | solution.py:384
  31.8 15.9 %all-to-all-start.1 = ((bf16[32,16,352]{2,1,0:T(8,128)(2,1)}), bf16[32,16,352]{2,1,0:T(8,128)(2,1)S(1)}, u32[]{:S(2)}, u32[]{:S(2)}) async-start(bf16[32,16,352]{2,1,0:T(8,128)(2,1)} %shard_map.104), calls=%async_computation.1 | async-start | bytes 786432 | tf_op jit(solution)/shard_map/all_to_all | solution.py:399
  34.6 30.4 %collective-permute-start.2 = (bf16[2,352,512]{2,1,0:T(8,128)(2,1)}, bf16[2,352,512]{2,1,0:T(8,128)(2,1)}, u32[]{:S(2)}, u32[]{:S(2)}) collective-permute-start(bf16[2,352,512]{2,1,0:T(8,128)(2,1)} %get-tuple-element.37), channel_id=1, source_target_pairs={{0,4},{4,0},{8,12},{12,8},{16,20},{20,16},{24,28},{28,24},{1,5},{5... | collective-permute-start | bytes 2162696 | tf_op jit(solution)/shard_map/ppermute | solution.py:384
  42.5 11.8 %collective-permute-start.4 = (bf16[8,16,1408]{2,1,0:T(8,128)(2,1)}, bf16[8,16,1408]{2,1,0:T(8,128)(2,1)}, u32[]{:S(2)}, u32[]{:S(2)}) collective-permute-start(bf16[8,16,1408]{2,1,0:T(8,128)(2,1)} %get-tuple-element.41), channel_id=1, source_target_pairs={{0,2},{1,3},{2,0},{3,1},{4,6},{5,7},{6,4},{7,5},{8,10},{9,11},{10,... | collective-permute-start | bytes 1081352 | tf_op jit(solution)/shard_map/ppermute | solution.py:384
  47.8 14.0 %collective-permute-start.3 = (bf16[512,352]{1,0:T(8,128)(2,1)S(1)}, bf16[512,352]{1,0:T(8,128)(2,1)S(1)}, u32[]{:S(2)}, u32[]{:S(2)}) collective-permute-start(bf16[512,352]{1,0:T(8,128)(2,1)S(1)} %bitcast.42), channel_id=1, source_target_pairs={{0,2},{1,3},{2,0},{3,1},{4,6},{5,7},{6,4},{7,5},{8,10},{9,11},{10,... | collective-permute-start | bytes 1081352 | tf_op jit(solution)/shard_map/ppermute | solution.py:384
  48.2 16.7 %collective-permute-start.1 = (bf16[1,352,512]{2,1,0:T(8,128)(2,1)}, bf16[1,352,512]{2,1,0:T(8,128)(2,1)}, u32[]{:S(2)}, u32[]{:S(2)}) collective-permute-start(bf16[1,352,512]{2,1,0:T(8,128)(2,1)} %get-tuple-element.36), channel_id=1, source_target_pairs={{0,4},{4,0},{8,12},{12,8},{16,20},{20,16},{24,28},{28,24},{1,5},{5... | collective-permute-start | bytes 1081352 | tf_op jit(solution)/shard_map/ppermute | solution.py:384
  56.5 8.4 %collective-permute-start.5 = (bf16[2,16,1408]{2,1,0:T(8,128)(2,1)S(1)}, bf16[2,16,1408]{2,1,0:T(8,128)(2,1)S(1)}, u32[]{:S(2)}, u32[]{:S(2)}) collective-permute-start(bf16[2,16,1408]{2,1,0:T(8,128)(2,1)S(1)} %get-tuple-element.58), channel_id=1, source_target_pairs={{0,8},{4,12},{8,0},{12,4},{16,24},{20,28},{24,16},{28,20},{1,9},{5... | collective-permute-start | bytes 270344 | tf_op jit(solution)/shard_map/ppermute | solution.py:384
  58.0 6.9 %collective-permute-start.6 = (bf16[2,16,1408]{2,1,0:T(8,128)(2,1)S(1)}, bf16[2,16,1408]{2,1,0:T(8,128)(2,1)S(1)}, u32[]{:S(2)}, u32[]{:S(2)}) collective-permute-start(bf16[2,16,1408]{2,1,0:T(8,128)(2,1)S(1)} %get-tuple-element.57), channel_id=1, source_target_pairs={{0,16},{4,20},{8,24},{12,28},{16,0},{20,4},{24,8},{28,12},{1,17},{... | collective-permute-start | bytes 270344 | tf_op jit(solution)/shard_map/ppermute | solution.py:384
  64.9 0.6 copy-start.5
  65.6 3.9 %collective-permute-start.8 = (bf16[2,352,512]{2,1,0:T(8,128)(2,1)}, bf16[2,352,512]{2,1,0:T(8,128)(2,1)S(1)}, u32[]{:S(2)}, u32[]{:S(2)}) collective-permute-start(bf16[2,352,512]{2,1,0:T(8,128)(2,1)} %collective-permute-done.2.refs_1_), channel_id=1, source_target_pairs={{0,1},{1,0},{2,3},{3,2},{4,5},{5,4},{6,7},{7,6},{8,9},{9,8},{10,11... | collective-permute-start | bytes 2162696 | tf_op jit(solution)/shard_map/ppermute | solution.py:384
  65.6 3.9 %collective-permute-start.7 = (bf16[1,352,512]{2,1,0:T(8,128)(2,1)}, bf16[1,352,512]{2,1,0:T(8,128)(2,1)S(1)}, u32[]{:S(2)}, u32[]{:S(2)}) collective-permute-start(bf16[1,352,512]{2,1,0:T(8,128)(2,1)} %collective-permute-done.1.refs_0_), channel_id=1, source_target_pairs={{0,1},{1,0},{2,3},{3,2},{4,5},{5,4},{6,7},{7,6},{8,9},{9,8},{10,11... | collective-permute-start | bytes 1081352 | tf_op jit(solution)/shard_map/ppermute | solution.py:384
  66.1 12.0 %copy-start.6 = (bf16[2,16,1408]{2,1,0:T(8,128)(2,1)S(1)}, bf16[2,16,1408]{2,1,0:T(8,128)(2,1)}, u32[]{:S(2)}) copy-start(bf16[2,16,1408]{2,1,0:T(8,128)(2,1)} %copy-done.5) | copy-start | bytes 270340
  66.1 7.3 %collective-permute-start.9 = (bf16[2,16,1408]{2,1,0:T(8,128)(2,1)S(1)}, bf16[2,16,1408]{2,1,0:T(8,128)(2,1)S(1)}, u32[]{:S(2)}, u32[]{:S(2)}) collective-permute-start(bf16[2,16,1408]{2,1,0:T(8,128)(2,1)S(1)} %get-tuple-element.56), channel_id=1, source_target_pairs={{0,24},{4,28},{8,16},{12,20},{16,8},{20,12},{24,0},{28,4},{1,25},{... | collective-permute-start | bytes 270344 | tf_op jit(solution)/shard_map/ppermute | solution.py:384
  73.4 11.1 %copy-start.4 = (bf16[2,64,1408]{2,1,0:T(8,128)(2,1)S(1)}, bf16[2,64,1408]{2,1,0:T(8,128)(2,1)}, u32[]{:S(2)}) copy-start(bf16[2,64,1408]{2,1,0:T(8,128)(2,1)} %param.17) | copy-start | bytes 1081348
  73.4 40.2 %all-to-all-start.2 = ((bf16[8,726,128]{2,1,0:T(8,128)(2,1)}), bf16[8,726,128]{2,1,0:T(8,128)(2,1)S(1)}, u32[]{:S(2)}, u32[]{:S(2)}) async-start(bf16[8,726,128]{2,1,0:T(8,128)(2,1)} %shard_map.110), calls=%async_computation.2 | async-start | bytes 2981888 | tf_op jit(solution)/shard_map/all_to_all | solution.py:434
  78.2 6.3 %collective-permute-start.10 = (bf16[4,16,1408]{2,1,0:T(8,128)(2,1)S(1)}, bf16[4,16,1408]{2,1,0:T(8,128)(2,1)S(1)}, u32[]{:S(2)}, u32[]{:S(2)}) collective-permute-start(bf16[4,16,1408]{2,1,0:T(8,128)(2,1)S(1)} %get-tuple-element.54), channel_id=1, source_target_pairs={{0,4},{4,0},{8,12},{12,8},{16,20},{20,16},{24,28},{28,24},{1,5},{5... | collective-permute-start | bytes 540680 | tf_op jit(solution)/shard_map/ppermute | solution.py:384

commit v10 on v9

--- a/solution.py
+++ b/solution.py
@@ -20,10 +20,11 @@
 def attend_kernel(q_ref, k_ref, v_ref, d_ref, all_ref, query_ref, rest_ref, sem, *, columns):
     n_tok, width = q_ref.shape
     factor = 1.0 / math.sqrt(DH)
-    source = lax.broadcasted_iota(jnp.int32, (n_tok, n_tok), 0)
-    target = lax.broadcasted_iota(jnp.int32, (n_tok, n_tok), 1)
-    same = ((source ^ target) & (columns - 1)) == 0
-    for start in range(0, width, DH):
+    key_row = lax.broadcasted_iota(jnp.int32, (n_tok, n_tok), 0)
+    query_row = lax.broadcasted_iota(jnp.int32, (n_tok, n_tok), 1)
+    same = ((key_row ^ query_row) & (columns - 1)) == 0
+    copies = []
+    for head, start in enumerate(range(0, width, DH)):
         lanes = slice(start, start + DH)
         query, key, value, grad = [ref[:, lanes] for ref in (q_ref, k_ref, v_ref, d_ref)]
         scores = lax.dot_general(key, query, COLS, preferred_element_type=F32) * factor
@@ -39,12 +40,11 @@
         ):
             total = lax.dot_general(left, right, dims, preferred_element_type=F32)
             all_ref[kind, lanes, :] = total.astype(BF)
-    copies = [
-        pltpu.make_async_copy(all_ref.at[pl.ds(at, ref.shape[0])], ref, sem.at[at])
-        for at, ref in ((0, query_ref), (1, rest_ref))
-    ]
-    for copy in copies:
-        copy.start()
+        for at, ref in ((0, query_ref), (1, rest_ref)):
+            source = all_ref.at[pl.ds(at, ref.shape[0]), pl.ds(start, DH)]
+            copy = pltpu.make_async_copy(source, ref.at[:, pl.ds(start, DH)], sem.at[head, at])
+            copy.start()
+            copies.append(copy)
     for copy in copies:
         copy.wait()
 
@@ -54,7 +54,7 @@
     return pl.pallas_call(
         functools.partial(attend_kernel, columns=columns),
         out_specs=[pl.BlockSpec(memory_space=pltpu.VMEM)] + [pl.BlockSpec(memory_space=pltpu.HBM)] * 2,
-        scratch_shapes=[pltpu.SemaphoreType.DMA((2,))],
+        scratch_shapes=[pltpu.SemaphoreType.DMA((width // DH, 2))],
         out_shape=[jax.ShapeDtypeStruct((3, width, n_tok), BF)]
         + [pltpu.HBM((kinds, width, n_tok), BF) for kinds in (1, 2)],
         compiler_params=ROOM,
@@ -401,7 +401,7 @@
 
     saved = [values.reshape(n_tok, part) for values in (q_time, k_time, v_time)]
     grads, *others = attend(*saved, d_time, columns)
-    grads_core, others = lax.optimization_barrier((swap(grads, "patch", n_patch, 1), others))
+    grads_core = swap(grads, "patch", n_patch, 1)
     pieces = [grads, grads_core]
     others = [swap(piece, "tm", n_tm, 1) for piece in others]
 
@@ -418,9 +418,9 @@
     spread = [lax.dynamic_index_in_dim(share, (tm // 2) ^ n, 0, keepdims=False) for n in range(n_pair)]
     spread = spread[:1] + [swap(spread[n], "tm", n_tm, 2 * n) for n in range(1, n_pair)]
     own = own_product(patch // 2, mine, theirs, pieces)
-    others, theirs, own, early = lax.optimization_barrier((others, theirs, own, spread[:-1]))
+    others, theirs, own, early = lax.optimization_barrier((others, theirs, own, spread[2:]))
     others = list(others)
-    spread = early + spread[-1:]
+    spread = spread[:2] + early
     others += [swap(piece, "patch", n_patch, 1) for piece in others]
 
     factor = 1.0 / math.sqrt(frames * patches)

time: 115 us -> 115 us (level)
    ppermute x11, starting transfers between devices: 13.6 us -> 11.9 us  [swap(): return lax.ppermute(values, axis, [(i, i ^ bit) for i in range(size)])]
    ppermute x11, waiting for transfers between devices: 13.7 us -> 14.9 us  [swap(): return lax.ppermute(values, axis, [(i, i ^ bit) for i in range(size)])]
  transfers between devices with their start and end apart: 14 -> 14, of which waited for: 7 -> 9; matrix products, arithmetic and copies ran while one was open for 0% -> 1% of each run, Pallas kernels for 19% -> 20%
where the time goes in v10:
time: 115 us; the launch traced here: 114 us
  waiting for transfers between devices  50.9 us (44%)
  Pallas kernels  29.8 us (26%)
  starting transfers between devices  27.2 us (24%)
  matrix products  3.38 us (3%)
    all_to_all x1, waiting for transfers between devices, per_device(): lax.all_to_all(partial, both, 0, 0, axis_index_groups=groups, tiled=True)  26.8 us
    ppermute x11, waiting for transfers between devices, swap(): return lax.ppermute(values, axis, [(i, i ^ bit) for i in range(size)])  14.9 us
    ppermute x11, starting transfers between devices, swap(): return lax.ppermute(values, axis, [(i, i ^ bit) for i in range(size)])  11.9 us
    all_to_all x1, starting transfers between devices, per_device(): lax.all_to_all(d_attn.reshape(devices, t_dev, columns, part), both, 0, 0,...  7.29 us
    pallas_call x1, Pallas kernels, own_weights(): pl.pallas_call(functools.partial(weights_kernel, n_chip=n_chip), grid_spe...  6.19 us
    pallas_call x1, Pallas kernels, share_send(): pl.pallas_call(share_kernel, grid_spec=pltpu.PrefetchScalarGridSpec(num_s...  6.03 us
    pallas_call x1, Pallas kernels, attend(): pl.pallas_call(functools.partial(attend_kernel, columns=columns), out_spe...  5.97 us
    all_to_all x1, waiting for transfers between devices, per_device(): lax.all_to_all(d_attn.reshape(devices, t_dev, columns, part), both, 0, 0,...  5.44 us
  transfers between devices with their start and end apart: 14, of which 9 were waited for; matrix products, arithmetic and copies ran while one was open for 1% of the time, Pallas kernels for 20%

profile of v10, /device:TPU:0, one launch (start us, length us, event | category | flops | bytes accessed | tf_op | source)
XLA Modules:
  0.0 114.3 jit_solution(14670071942816691958)
XLA Ops:
  0.7 3.4 %fusion = bf16[4,128,352]{1,2,0:T(8,128)(2,1)S(1)} fusion(bf16[4,352,1408]{2,1,0:T(8,128)(2,1)} %bitcast.59, bf16[128,1408,1]{1,0,2:T(8,128)(2,1)} %bitcast.52), kind=kOutput, calls=%fused_computation.1 | convolution fusion | flops 507691008 | bytes 4685824 | tf_op jit(solution)/shard_map/to,jfo->jtf/dot_general | solution.py:387
  4.0 0.2 copy.13
  4.3 0.8 copy.14
  5.1 7.3 %all-to-all-start = ((bf16[32,2,8,352]{3,2,1,0:T(8,128)(2,1)}), bf16[32,2,8,352]{3,2,1,0:T(8,128)(2,1)S(1)}, u32[]{:S(2)}, u32[]{:S(2)}) async-start(bf16[32,2,8,352]{3,2,1,0:T(8,128)(2,1)} %bitcast.9), calls=%async_computation | async-start | bytes 786432 | tf_op jit(solution)/shard_map/all_to_all | solution.py:392
  12.4 0.0 copy-start
  12.4 0.0 copy-start.1
  12.5 0.0 copy-start.2
  12.5 0.0 copy-start.3
  12.5 6.2 %shard_map.105.refs_2_ = bf16[3,1408,704]{2,1,0:T(8,128)(2,1)} custom-call(s32[1]{0:T(128)} %bitcast.1.chip_ref, bf16[1408,4224]{1,0:T(8,128)(2,1)} %w_ref), custom_call_target="tpu_custom_call" | custom-call | tf_op jit(solution)/shard_map/pallas_call | solution.py:114
  18.7 0.0 copy-done
  18.7 1.4 %shard_map.104 = bf16[32,16,352]{2,1,0:T(8,128)(2,1)} custom-call(bf16[128,1408]{1,0:T(8,128)(2,1)S(1)} %bitcast.46, f32[1,1408]{1,0:T(1,128)S(1)} %broadcast_in_dim.23.gain_ref, f32[1,1408]{1,0:T(1,128)S(1)} %broadcast_in_dim.24.bias_ref), custom_call_target="tpu_custom_call" | custom-call | tf_op jit(solution)/shard_map/pallas_call | solution.py:82
  20.1 5.4 %all-to-all-done = bf16[32,2,8,352]{3,2,1,0:T(8,128)(2,1)S(1)} async-done(((bf16[32,2,8,352]{3,2,1,0:T(8,128)(2,1)}), bf16[32,2,8,352]{3,2,1,0:T(8,128)(2,1)S(1)}, u32[]{:S(2)}, u32[]{:S(2)}) %all-to-all-start) | async-done | bytes 360480 | tf_op jit(solution)/shard_map/all_to_all | solution.py:392
  25.5 0.0 copy-done.1
  25.5 0.0 copy-done.3
  25.5 6.0 %shard_map.106 = (bf16[3,352,512]{2,1,0:T(8,128)(2,1)S(1)}, bf16[1,352,512]{2,1,0:T(8,128)(2,1)}, bf16[2,352,512]{2,1,0:T(8,128)(2,1)}) custom-call(bf16[512,352]{1,0:T(8,128)(2,1)S(1)} %bitcast.49, bf16[512,352]{1,0:T(8,128)(2,1)S(1)} %bitcast.50, bf16[512,352]{1,0:T(8,128)(2,1)S(1)} %bitcast.51, bf16[512,352]{1,0:T(8,128)(2,1)S(1)} %bitcast.45), custom_call_target="tpu_custom_call" | custom-call | tf_op jit(solution)/shard_map/pallas_call | solution.py:54
  31.5 0.1 collective-permute-start.3
  31.6 2.7 %all-to-all-start.1 = ((bf16[32,16,352]{2,1,0:T(8,128)(2,1)}), bf16[32,16,352]{2,1,0:T(8,128)(2,1)S(1)}, u32[]{:S(2)}, u32[]{:S(2)}) async-start(bf16[32,16,352]{2,1,0:T(8,128)(2,1)} %shard_map.104), calls=%async_computation.1 | async-start | bytes 786432 | tf_op jit(solution)/shard_map/all_to_all | solution.py:399
  34.4 1.8 %collective-permute-start.1 = (bf16[2,352,512]{2,1,0:T(8,128)(2,1)}, bf16[2,352,512]{2,1,0:T(8,128)(2,1)}, u32[]{:S(2)}, u32[]{:S(2)}) collective-permute-start(bf16[2,352,512]{2,1,0:T(8,128)(2,1)} %get-tuple-element.30), channel_id=1, source_target_pairs={{0,4},{4,0},{8,12},{12,8},{16,20},{20,16},{24,28},{28,24},{1,5},{5... | collective-permute-start | bytes 2162696 | tf_op jit(solution)/shard_map/ppermute | solution.py:384
  36.2 0.0 collective-permute-done.3.refs_1_
  36.2 6.0 %shard_map.108 = (bf16[8,16,1408]{2,1,0:T(8,128)(2,1)}, f32[8,16,1408]{2,1,0:T(8,128)}) custom-call(s32[1]{0:T(128)} %bitcast.15.where_ref, bf16[3,352,512]{2,1,0:T(8,128)(2,1)S(1)} %get-tuple-element.31.refs_0_, bf16[3,352,512]{2,1,0:T(8,128)(2,1)S(1)} %collective-permute-done.3.refs_1_, bf16[3,1408,704]{2,1,0:T(8,128)(2,1)} %shard_map.105.refs_2_), custom_call_target="tpu_custom_call" | custom-call | tf_op jit(solution)/shard_map/pallas_call | solution.py:179
  42.2 1.5 %collective-permute-start.4 = (bf16[8,16,1408]{2,1,0:T(8,128)(2,1)}, bf16[8,16,1408]{2,1,0:T(8,128)(2,1)}, u32[]{:S(2)}, u32[]{:S(2)}) collective-permute-start(bf16[8,16,1408]{2,1,0:T(8,128)(2,1)} %get-tuple-element.34), channel_id=1, source_target_pairs={{0,2},{1,3},{2,0},{3,1},{4,6},{5,7},{6,4},{7,5},{8,10},{9,11},{10,... | collective-permute-start | bytes 1081352 | tf_op jit(solution)/shard_map/ppermute | solution.py:384
  43.8 3.8 %all-to-all-done.1 = bf16[32,16,352]{2,1,0:T(8,128)(2,1)S(1)} async-done(((bf16[32,16,352]{2,1,0:T(8,128)(2,1)}), bf16[32,16,352]{2,1,0:T(8,128)(2,1)S(1)}, u32[]{:S(2)}, u32[]{:S(2)}) %all-to-all-start.1) | async-done | bytes 360480 | tf_op jit(solution)/shard_map/all_to_all | solution.py:399
  47.5 0.5 collective-permute-start.2
  48.0 1.5 %collective-permute-start = (bf16[1,352,512]{2,1,0:T(8,128)(2,1)}, bf16[1,352,512]{2,1,0:T(8,128)(2,1)}, u32[]{:S(2)}, u32[]{:S(2)}) collective-permute-start(bf16[1,352,512]{2,1,0:T(8,128)(2,1)} %get-tuple-element.29), channel_id=1, source_target_pairs={{0,4},{4,0},{8,12},{12,8},{16,20},{20,16},{24,28},{28,24},{1,5},{5... | collective-permute-start | bytes 1081352 | tf_op jit(solution)/shard_map/ppermute | solution.py:384
  49.5 4.6 %collective-permute-done.4.come_ref = bf16[8,16,1408]{2,1,0:T(8,128)(2,1)} collective-permute-done((bf16[8,16,1408]{2,1,0:T(8,128)(2,1)}, bf16[8,16,1408]{2,1,0:T(8,128)(2,1)}, u32[]{:S(2)}, u32[]{:S(2)}) %collective-permute-start.4) | collective-permute-done | bytes 360480 | tf_op jit(solution)/shard_map/ppermute | solution.py:384
  54.1 2.2 %shard_map.109 = bf16[8,16,1408]{2,1,0:T(8,128)(2,1)S(1)} custom-call(f32[8,16,1408]{2,1,0:T(8,128)} %get-tuple-element.33.stay_hbm, bf16[8,16,1408]{2,1,0:T(8,128)(2,1)} %collective-permute-done.4.come_ref), custom_call_target="tpu_custom_call" | custom-call | tf_op jit(solution)/shard_map/pallas_call | solution.py:410
  56.3 2.3 %collective-permute-start.5 = (bf16[2,16,1408]{2,1,0:T(8,128)(2,1)S(1)}, bf16[2,16,1408]{2,1,0:T(8,128)(2,1)S(1)}, u32[]{:S(2)}, u32[]{:S(2)}) collective-permute-start(bf16[2,16,1408]{2,1,0:T(8,128)(2,1)S(1)} %get-tuple-element.51), channel_id=1, source_target_pairs={{0,16},{4,20},{8,24},{12,28},{16,0},{20,4},{24,8},{28,12},{1,17},{... | collective-permute-start | bytes 270344 | tf_op jit(solution)/shard_map/ppermute | solution.py:384
  58.6 1.6 %collective-permute-start.6 = (bf16[2,16,1408]{2,1,0:T(8,128)(2,1)S(1)}, bf16[2,16,1408]{2,1,0:T(8,128)(2,1)}, u32[]{:S(2)}, u32[]{:S(2)}) collective-permute-start(bf16[2,16,1408]{2,1,0:T(8,128)(2,1)S(1)} %get-tuple-element.50), channel_id=1, source_target_pairs={{0,24},{4,28},{8,16},{12,20},{16,8},{20,12},{24,0},{28,4},{1,25},{... | collective-permute-start | bytes 270344 | tf_op jit(solution)/shard_map/ppermute | solution.py:384
  60.2 1.4 %collective-permute-done.2.theirs_ref = bf16[512,352]{1,0:T(8,128)(2,1)S(1)} collective-permute-done((bf16[512,352]{1,0:T(8,128)(2,1)S(1)}, bf16[512,352]{1,0:T(8,128)(2,1)S(1)}, u32[]{:S(2)}, u32[]{:S(2)}) %collective-permute-start.2) | collective-permute-done | bytes 360480 | tf_op jit(solution)/shard_map/ppermute | solution.py:384
  61.5 1.3 %shard_map.107.acc_ref = f32[2112,352]{1,0:T(8,128)S(1)} custom-call(s32[1]{0:T(128)} %bitcast.1.chip_ref, bf16[512,352]{1,0:T(8,128)(2,1)S(1)} %bitcast.43, bf16[512,352]{1,0:T(8,128)(2,1)S(1)} %collective-permute-done.2.theirs_ref, bf16[3,352,512]{2,1,0:T(8,128)(2,1)S(1)} %get-tuple-element.31.refs_0_, bf16[3,352,512]{2,1,0:T(8,128)(2,1)S(1)} %collective-permute-done.3.refs_1_), custom_call_target="tpu_custom_call" | custom-call | tf_op jit(solution)/shard_map/pallas_call | solution.py:222
  62.8 1.9 %collective-permute-done.refs_0_ = bf16[1,352,512]{2,1,0:T(8,128)(2,1)} collective-permute-done((bf16[1,352,512]{2,1,0:T(8,128)(2,1)}, bf16[1,352,512]{2,1,0:T(8,128)(2,1)}, u32[]{:S(2)}, u32[]{:S(2)}) %collective-permute-start) | collective-permute-done | bytes 360480 | tf_op jit(solution)/shard_map/ppermute | solution.py:384
  64.7 0.0 collective-permute-done.1.refs_1_
  64.7 0.4 collective-permute-done.5
  65.1 0.0 collective-permute-done.6
  65.1 0.0 collective-permute-start.8
  65.1 0.5 collective-permute-start.7
  65.6 1.6 %collective-permute-start.9 = (bf16[2,16,1408]{2,1,0:T(8,128)(2,1)S(1)}, bf16[2,16,1408]{2,1,0:T(8,128)(2,1)S(1)}, u32[]{:S(2)}, u32[]{:S(2)}) collective-permute-start(bf16[2,16,1408]{2,1,0:T(8,128)(2,1)S(1)} %get-tuple-element.48), channel_id=1, source_target_pairs={{0,8},{4,12},{8,0},{12,4},{16,24},{20,28},{24,16},{28,20},{1,9},{5... | collective-permute-start | bytes 270344 | tf_op jit(solution)/shard_map/ppermute | solution.py:384
  67.3 0.8 collective-permute-done.7.refs_2_
  68.0 0.0 collective-permute-done.8.refs_3_
  68.0 3.9 %shard_map.110 = bf16[8,726,128]{2,1,0:T(8,128)(2,1)} custom-call(s32[1]{0:T(128)} %bitcast.1.chip_ref, bf16[512,352]{1,0:T(8,128)(2,1)S(1)} %bitcast.44, bf16[512,352]{1,0:T(8,128)(2,1)S(1)} %collective-permute-done.2.theirs_ref, f32[2112,352]{1,0:T(8,128)S(1)} %shard_map.107.acc_ref, bf16[1,352,512]{2,1,0:T(8,128)(2,1)} %collective-permute-done.refs_0_, ...), custom_call_target="tpu_custom_call" | custom-call | tf_op jit(solution)/shard_map/pallas_call | solution.py:268
  72.0 0.0 collective-permute-done.9
  72.0 5.3 %all-to-all-start.2 = ((bf16[8,726,128]{2,1,0:T(8,128)(2,1)}), bf16[8,726,128]{2,1,0:T(8,128)(2,1)S(1)}, u32[]{:S(2)}, u32[]{:S(2)}) async-start(bf16[8,726,128]{2,1,0:T(8,128)(2,1)} %shard_map.110), calls=%async_computation.2 | async-start | bytes 2981888 | tf_op jit(solution)/shard_map/all_to_all | solution.py:434
  77.2 0.9 pad_maximum_fusion
  78.2 0.5 collective-permute-start.10
  78.7 5.9 %collective-permute-done.10.come_ref = bf16[4,16,1408]{2,1,0:T(8,128)(2,1)S(1)} collective-permute-done((bf16[4,16,1408]{2,1,0:T(8,128)(2,1)S(1)}, bf16[4,16,1408]{2,1,0:T(8,128)(2,1)S(1)}, u32[]{:S(2)}, u32[]{:S(2)}) %collective-permute-start.10) | collective-permute-done | bytes 180256 | tf_op jit(solution)/shard_map/ppermute | solution.py:384
  84.6 1.3 %shard_map.111 = bf16[128,1408]{1,0:T(8,128)(2,1)} custom-call(s32[1]{0:T(128)} %bitcast.tm_ref, bf16[4,16,1408]{2,1,0:T(8,128)(2,1)S(1)} %get-tuple-element.47.stay_ref, bf16[4,16,1408]{2,1,0:T(8,128)(2,1)S(1)} %collective-permute-done.10.come_ref, bf16[128,1408]{1,0:T(8,128)(2,1)S(1)} %bitcast.47, bf16[128,1408]{1,0:T(8,128)(2,1)S(1)} %bitcast.53, ...), custom_call_target="tpu_custom_call" | custom-call | tf_op jit(solution)/shard_map/pallas_call | solution.py:313
  86.0 26.8 %all-to-all-done.2 = bf16[8,726,128]{2,1,0:T(8,128)(2,1)S(1)} async-done(((bf16[8,726,128]{2,1,0:T(8,128)(2,1)}), bf16[8,726,128]{2,1,0:T(8,128)(2,1)S(1)}, u32[]{:S(2)}, u32[]{:S(2)}) %all-to-all-start.2) | async-done | bytes 1486880 | tf_op jit(solution)/shard_map/all_to_all | solution.py:434
  112.8 1.5 %shard_map.112 = f32[44,4224]{1,0:T(8,128)} custom-call(s32[1]{0:T(128)} %bitcast.28.core_ref, bf16[4,2,726,128]{3,2,1,0:T(8,128)(2,1)S(1)} %bitcast.41), custom_call_target="tpu_custom_call" | custom-call | tf_op jit(solution)/shard_map/pallas_call | solution.py:354
  (11 shorter events, 0.1 us)
Async XLA Ops:
  0.6 11.7 %copy-start.5 = (f32[1408]{0:T(1024)S(1)}, f32[1408]{0:T(1024)}, u32[]{:S(2)}) copy-start(f32[1408]{0:T(1024)} %param.10) | copy-start | bytes 16900
  0.6 11.8 %copy-start.6 = (f32[1408]{0:T(1024)S(1)}, f32[1408]{0:T(1024)}, u32[]{:S(2)}) copy-start(f32[1408]{0:T(1024)} %param.11) | copy-start | bytes 16900
  5.1 20.5 %all-to-all-start = ((bf16[32,2,8,352]{3,2,1,0:T(8,128)(2,1)}), bf16[32,2,8,352]{3,2,1,0:T(8,128)(2,1)S(1)}, u32[]{:S(2)}, u32[]{:S(2)}) async-start(bf16[32,2,8,352]{3,2,1,0:T(8,128)(2,1)} %bitcast.9), calls=%async_computation | async-start | bytes 786432 | tf_op jit(solution)/shard_map/all_to_all | solution.py:392
  12.4 6.2 %copy-start = (bf16[2,64,1408]{2,1,0:T(8,128)(2,1)S(1)}, bf16[2,64,1408]{2,1,0:T(8,128)(2,1)}, u32[]{:S(2)}) copy-start(bf16[2,64,1408]{2,1,0:T(8,128)(2,1)} %param.9) | copy-start | bytes 1081348
  12.4 13.1 %copy-start.1 = (bf16[64,8,352]{2,1,0:T(8,128)(2,1)S(1)}, bf16[64,8,352]{2,1,0:T(8,128)(2,1)}, u32[]{:S(2)}) copy-start(bf16[64,8,352]{2,1,0:T(8,128)(2,1)} %param.14) | copy-start | bytes 1081348
  12.5 13.1 %copy-start.2 = (bf16[64,8,352]{2,1,0:T(8,128)(2,1)S(1)}, bf16[64,8,352]{2,1,0:T(8,128)(2,1)}, u32[]{:S(2)}) copy-start(bf16[64,8,352]{2,1,0:T(8,128)(2,1)} %param.15) | copy-start | bytes 1081348
  12.5 13.1 %copy-start.3 = (bf16[64,8,352]{2,1,0:T(8,128)(2,1)S(1)}, bf16[64,8,352]{2,1,0:T(8,128)(2,1)}, u32[]{:S(2)}) copy-start(bf16[64,8,352]{2,1,0:T(8,128)(2,1)} %param.16) | copy-start | bytes 1081348
  31.5 4.7 %collective-permute-start.3 = (bf16[3,352,512]{2,1,0:T(8,128)(2,1)S(1)}, bf16[3,352,512]{2,1,0:T(8,128)(2,1)S(1)}, u32[]{:S(2)}, u32[]{:S(2)}) collective-permute-start(bf16[3,352,512]{2,1,0:T(8,128)(2,1)S(1)} %get-tuple-element.31.refs_0_), channel_id=1, source_target_pairs={{0,1},{1,0},{2,3},{3,2},{4,5},{5,4},{6,7},{7,6},{8,9},{9,8},{10,11... | collective-permute-start | bytes 3244040 | tf_op jit(solution)/shard_map/ppermute | solution.py:384
  31.6 15.9 %all-to-all-start.1 = ((bf16[32,16,352]{2,1,0:T(8,128)(2,1)}), bf16[32,16,352]{2,1,0:T(8,128)(2,1)S(1)}, u32[]{:S(2)}, u32[]{:S(2)}) async-start(bf16[32,16,352]{2,1,0:T(8,128)(2,1)} %shard_map.104), calls=%async_computation.1 | async-start | bytes 786432 | tf_op jit(solution)/shard_map/all_to_all | solution.py:399
  34.4 30.4 %collective-permute-start.1 = (bf16[2,352,512]{2,1,0:T(8,128)(2,1)}, bf16[2,352,512]{2,1,0:T(8,128)(2,1)}, u32[]{:S(2)}, u32[]{:S(2)}) collective-permute-start(bf16[2,352,512]{2,1,0:T(8,128)(2,1)} %get-tuple-element.30), channel_id=1, source_target_pairs={{0,4},{4,0},{8,12},{12,8},{16,20},{20,16},{24,28},{28,24},{1,5},{5... | collective-permute-start | bytes 2162696 | tf_op jit(solution)/shard_map/ppermute | solution.py:384
  42.2 11.8 %collective-permute-start.4 = (bf16[8,16,1408]{2,1,0:T(8,128)(2,1)}, bf16[8,16,1408]{2,1,0:T(8,128)(2,1)}, u32[]{:S(2)}, u32[]{:S(2)}) collective-permute-start(bf16[8,16,1408]{2,1,0:T(8,128)(2,1)} %get-tuple-element.34), channel_id=1, source_target_pairs={{0,2},{1,3},{2,0},{3,1},{4,6},{5,7},{6,4},{7,5},{8,10},{9,11},{10,... | collective-permute-start | bytes 1081352 | tf_op jit(solution)/shard_map/ppermute | solution.py:384
  47.5 14.0 %collective-permute-start.2 = (bf16[512,352]{1,0:T(8,128)(2,1)S(1)}, bf16[512,352]{1,0:T(8,128)(2,1)S(1)}, u32[]{:S(2)}, u32[]{:S(2)}) collective-permute-start(bf16[512,352]{1,0:T(8,128)(2,1)S(1)} %bitcast.42), channel_id=1, source_target_pairs={{0,2},{1,3},{2,0},{3,1},{4,6},{5,7},{6,4},{7,5},{8,10},{9,11},{10,... | collective-permute-start | bytes 1081352 | tf_op jit(solution)/shard_map/ppermute | solution.py:384
  48.0 16.7 %collective-permute-start = (bf16[1,352,512]{2,1,0:T(8,128)(2,1)}, bf16[1,352,512]{2,1,0:T(8,128)(2,1)}, u32[]{:S(2)}, u32[]{:S(2)}) collective-permute-start(bf16[1,352,512]{2,1,0:T(8,128)(2,1)} %get-tuple-element.29), channel_id=1, source_target_pairs={{0,4},{4,0},{8,12},{12,8},{16,20},{20,16},{24,28},{28,24},{1,5},{5... | collective-permute-start | bytes 1081352 | tf_op jit(solution)/shard_map/ppermute | solution.py:384
  56.3 8.8 %collective-permute-start.5 = (bf16[2,16,1408]{2,1,0:T(8,128)(2,1)S(1)}, bf16[2,16,1408]{2,1,0:T(8,128)(2,1)S(1)}, u32[]{:S(2)}, u32[]{:S(2)}) collective-permute-start(bf16[2,16,1408]{2,1,0:T(8,128)(2,1)S(1)} %get-tuple-element.51), channel_id=1, source_target_pairs={{0,16},{4,20},{8,24},{12,28},{16,0},{20,4},{24,8},{28,12},{1,17},{... | collective-permute-start | bytes 270344 | tf_op jit(solution)/shard_map/ppermute | solution.py:384
  58.6 6.5 %collective-permute-start.6 = (bf16[2,16,1408]{2,1,0:T(8,128)(2,1)S(1)}, bf16[2,16,1408]{2,1,0:T(8,128)(2,1)}, u32[]{:S(2)}, u32[]{:S(2)}) collective-permute-start(bf16[2,16,1408]{2,1,0:T(8,128)(2,1)S(1)} %get-tuple-element.50), channel_id=1, source_target_pairs={{0,24},{4,28},{8,16},{12,20},{16,8},{20,12},{24,0},{28,4},{1,25},{... | collective-permute-start | bytes 270344 | tf_op jit(solution)/shard_map/ppermute | solution.py:384
  65.1 2.9 %collective-permute-start.8 = (bf16[2,352,512]{2,1,0:T(8,128)(2,1)}, bf16[2,352,512]{2,1,0:T(8,128)(2,1)S(1)}, u32[]{:S(2)}, u32[]{:S(2)}) collective-permute-start(bf16[2,352,512]{2,1,0:T(8,128)(2,1)} %collective-permute-done.1.refs_1_), channel_id=1, source_target_pairs={{0,1},{1,0},{2,3},{3,2},{4,5},{5,4},{6,7},{7,6},{8,9},{9,8},{10,11... | collective-permute-start | bytes 2162696 | tf_op jit(solution)/shard_map/ppermute | solution.py:384
  65.1 2.9 %collective-permute-start.7 = (bf16[1,352,512]{2,1,0:T(8,128)(2,1)}, bf16[1,352,512]{2,1,0:T(8,128)(2,1)S(1)}, u32[]{:S(2)}, u32[]{:S(2)}) collective-permute-start(bf16[1,352,512]{2,1,0:T(8,128)(2,1)} %collective-permute-done.refs_0_), channel_id=1, source_target_pairs={{0,1},{1,0},{2,3},{3,2},{4,5},{5,4},{6,7},{7,6},{8,9},{9,8},{10,11... | collective-permute-start | bytes 1081352 | tf_op jit(solution)/shard_map/ppermute | solution.py:384
  65.6 6.4 %collective-permute-start.9 = (bf16[2,16,1408]{2,1,0:T(8,128)(2,1)S(1)}, bf16[2,16,1408]{2,1,0:T(8,128)(2,1)S(1)}, u32[]{:S(2)}, u32[]{:S(2)}) collective-permute-start(bf16[2,16,1408]{2,1,0:T(8,128)(2,1)S(1)} %get-tuple-element.48), channel_id=1, source_target_pairs={{0,8},{4,12},{8,0},{12,4},{16,24},{20,28},{24,16},{28,20},{1,9},{5... | collective-permute-start | bytes 270344 | tf_op jit(solution)/shard_map/ppermute | solution.py:384
  72.0 12.6 %copy-start.4 = (bf16[2,64,1408]{2,1,0:T(8,128)(2,1)S(1)}, bf16[2,64,1408]{2,1,0:T(8,128)(2,1)}, u32[]{:S(2)}) copy-start(bf16[2,64,1408]{2,1,0:T(8,128)(2,1)} %param.17) | copy-start | bytes 1081348
  72.0 40.8 %all-to-all-start.2 = ((bf16[8,726,128]{2,1,0:T(8,128)(2,1)}), bf16[8,726,128]{2,1,0:T(8,128)(2,1)S(1)}, u32[]{:S(2)}, u32[]{:S(2)}) async-start(bf16[8,726,128]{2,1,0:T(8,128)(2,1)} %shard_map.110), calls=%async_computation.2 | async-start | bytes 2981888 | tf_op jit(solution)/shard_map/all_to_all | solution.py:434
  78.2 6.4 %collective-permute-start.10 = (bf16[4,16,1408]{2,1,0:T(8,128)(2,1)S(1)}, bf16[4,16,1408]{2,1,0:T(8,128)(2,1)S(1)}, u32[]{:S(2)}, u32[]{:S(2)}) collective-permute-start(bf16[4,16,1408]{2,1,0:T(8,128)(2,1)S(1)} %get-tuple-element.46), channel_id=1, source_target_pairs={{0,4},{4,0},{8,12},{12,8},{16,20},{20,16},{24,28},{28,24},{1,5},{5... | collective-permute-start | bytes 540680 | tf_op jit(solution)/shard_map/ppermute | solution.py:384

commit v11 on v10

--- a/solution.py
+++ b/solution.py
@@ -232,7 +232,7 @@
     )(chip[None], *arrays)
 
 
-def other_kernel(chip_ref, mine_ref, theirs_ref, acc_ref, *refs, factor, own_rows):
+def other_kernel(chip_ref, mine_ref, theirs_ref, acc_ref, *refs, factor, own_rows, relative):
     pieces, (out_ref, sum_ref) = refs[:-2], refs[-2:]
     norm = jnp.where(chip_ref[0] == 0, theirs_ref[...], mine_ref[...])
     part = pieces[0].shape[1]
@@ -246,27 +246,28 @@
         block = sum_ref[n * 128 : (n + 1) * 128, :].T if n < full else sum_ref[n * 128 :, :].T
         for k in range(out_ref.shape[0]):
             rows = block[k * own_rows : (k + 1) * own_rows].astype(BF)
+            to = ((k // 2) ^ chip_ref[1]) * 2 + ((k % 2) ^ chip_ref[0]) if relative else k
             if not packed:
-                out_ref[k, :, n * 128 : n * 128 + rows.shape[1]] = rows
+                out_ref[to, :, n * 128 : n * 128 + rows.shape[1]] = rows
             elif n < full:
-                out_ref[k, n * own_rows : (n + 1) * own_rows, :] = rows
+                out_ref[to, n * own_rows : (n + 1) * own_rows, :] = rows
             else:
                 rows = block[k * own_rows : (k + 1) * own_rows]
                 both = jnp.concatenate([rows[: own_rows // 2], rows[own_rows // 2 :]], axis=1)
-                out_ref[k, n * own_rows :, :] = both.astype(BF)
+                out_ref[to, n * own_rows :, :] = both.astype(BF)
 
 
 def packable(own_rows, lanes):
     return own_rows % 4 == 0 and lanes % 128 == 64
 
 
-def other_product(chip, mine, theirs, acc, pieces, own_rows, factor):
+def other_product(place, mine, theirs, acc, pieces, own_rows, factor, relative):
     lanes, part = acc.shape
     chunk = (own_rows * lanes // 128, 128) if packable(own_rows, lanes) else (own_rows, lanes)
     shape = (part // own_rows,) + chunk
     arrays = (mine, theirs, acc, *pieces)
     return pl.pallas_call(
-        functools.partial(other_kernel, factor=factor, own_rows=own_rows),
+        functools.partial(other_kernel, factor=factor, own_rows=own_rows, relative=relative),
         grid_spec=pltpu.PrefetchScalarGridSpec(
             num_scalar_prefetch=1,
             grid=(1,),
@@ -276,7 +277,7 @@
         ),
         out_shape=jax.ShapeDtypeStruct(shape, BF),
         compiler_params=ROOM,
-    )(chip[None], *arrays)
+    )(place, *arrays)
 
 
 def last_kernel(tm_ref, stay_ref, come_ref, x_ref, grad_ref, gain_ref, out_ref, *, columns, t_dev):
@@ -323,14 +324,16 @@
     )(tm[None], stay, come, tokens, grads, gain[None])
 
 
-def final_kernel(core_ref, in_ref, out_ref, *, part, kinds):
-    n_pair, n_chip = in_ref.shape[:2]
+def final_kernel(place_ref, *refs, part, kinds, n_chip):
+    out_ref = refs[-1]
     own_rows = out_ref.shape[0]
     lanes = 2 * kinds * part
+    count = (len(refs) - 1) // n_chip
     for x in range(n_chip):
-        total = in_ref[0, x].astype(F32)
-        for z in range(1, n_pair):
-            total = total + in_ref[z, x].astype(F32)
+        total = None
+        for ref in refs[x * count : (x + 1) * count]:
+            values = ref[...].astype(F32)
+            total = values if total is None else total + values
         if packable(own_rows, lanes):
             full = lanes // 128
             blocks = [total[n * own_rows : (n + 1) * own_rows] for n in range(full)]
@@ -338,30 +341,30 @@
             blocks.append(jnp.concatenate([both[:half, :64], both[:half, 64:]], axis=0))
             total = jnp.concatenate(blocks, axis=1)
         for core in range(2):
-
-            @pl.when(core_ref[0] == core)
-            def _(core=core, total=total, x=x):
-                for r in range(2):
-                    for c in range(kinds):
-                        at = (c * n_chip * 2 + 2 * x + (r ^ core)) * part
-                        src = (r * kinds + c) * part
-                        out_ref[:, at : at + part] = total[:, src : src + part]
-
-
-def final_sum(pieces, core, own_rows, part, kinds):
-    n_chip = pieces.shape[1]
+            for first in range(2):
+
+                @pl.when((place_ref[0] == core) & (place_ref[1] == first))
+                def _(core=core, first=first, total=total, x=x):
+                    for r in range(2):
+                        for c in range(kinds):
+                            at = (c * n_chip * 2 + 2 * (x ^ first) + (r ^ core)) * part
+                            src = (r * kinds + c) * part
+                            out_ref[:, at : at + part] = total[:, src : src + part]
+
+
+def final_sum(arrays, core, first, own_rows, part, kinds, n_chip):
     shape = (own_rows, 2 * n_chip * kinds * part)
     return pl.pallas_call(
-        functools.partial(final_kernel, part=part, kinds=kinds),
-        grid_spec=pltpu.PrefetchScalarGridSpec(
-            num_scalar_prefetch=1,
-            grid=(1,),
-            in_specs=[whole_spec(pieces)],
+        functools.partial(final_kernel, part=part, kinds=kinds, n_chip=n_chip),
+        grid_spec=pltpu.PrefetchScalarGridSpec(
+            num_scalar_prefetch=1,
+            grid=(1,),
+            in_specs=[whole_spec(array) for array in arrays],
             out_specs=pl.BlockSpec(shape, lambda i, s: (0, 0)),
         ),
         out_shape=jax.ShapeDtypeStruct(shape, F32),
         compiler_params=ROOM,
-    )(core[None], pieces)
+    )(jnp.stack([core, first]), *arrays)
 
 
 def per_device(tokens, ln_gain, ln_bias, w_qkv, w_out, q_time, k_time, v_time, grad_out):
@@ -424,16 +427,30 @@
     others += [swap(piece, "patch", n_patch, 1) for piece in others]
 
     factor = 1.0 / math.sqrt(frames * patches)
-    groups = [
-        [(2 * z + y) * n_patch + 2 * x + c for z in range(n_pair) for x in range(n_chip)]
-        for y in range(2)
-        for c in range(2)
-    ]
-    partial = other_product(patch // 2, mine, theirs, own, others, own_rows, factor)
+    across = n_pair == 4 and n_chip == 2
+    place = jnp.stack([patch // 2, tm // 2])
+    partial = other_product(place, mine, theirs, own, others, own_rows, factor, across)
     partial, spread = lax.optimization_barrier((partial, spread))
-    summands = lax.all_to_all(partial, both, 0, 0, axis_index_groups=groups, tiled=True)
-    summands = summands.reshape((n_pair, n_chip) + summands.shape[1:])
-    grad_w_qkv = final_sum(summands, core, own_rows, part, 3)
+    if across:
+        def send(values, dz, dx):
+            flip = 2 * dz * n_patch + 2 * dx
+            return lax.ppermute(values, both, [(i, i ^ flip) for i in range(devices)])
+
+        passed = send(partial[6:8], 1, 0)
+        summed = (partial[4:6].astype(F32) + passed.astype(F32)).astype(BF)
+        own_chip = [partial[0], send(partial[2], 1, 0), send(summed[0], 2, 0)]
+        other_chip = [send(partial[1], 0, 1), send(partial[3], 1, 1), send(summed[1], 2, 1)]
+        summands, first = own_chip + other_chip, patch // 2
+    else:
+        groups = [
+            [(2 * z + y) * n_patch + 2 * x + c for z in range(n_pair) for x in range(n_chip)]
+            for y in range(2)
+            for c in range(2)
+        ]
+        pieces = lax.all_to_all(partial, both, 0, 0, axis_index_groups=groups, tiled=True)
+        summands = [pieces[z * n_chip + x] for x in range(n_chip) for z in range(n_pair)]
+        first = 0 * core
+    grad_w_qkv = final_sum(summands, core, first, own_rows, part, 3, n_chip)
 
     spread = jnp.stack(spread)
     stay = lax.dynamic_index_in_dim(spread, side, 1, keepdims=False)

time: 115 us -> 110 us (0.957)
  waiting for transfers between devices: 50.9 us -> 35.5 us
  local copies, waits for them, and re-layouts: 1.14 us -> 9.14 us
  starting transfers between devices: 27.2 us -> 30.8 us
  Pallas kernels: 29.8 us -> 28.6 us
    all_to_all x1 -> x0, waiting for transfers between devices: 26.8 us -> none  [per_device(): lax.all_to_all(partial, both, 0, 0, axis_index_groups=groups, tiled=True)]
    ppermute x0 -> x6, waiting for transfers between devices: none -> 18.4 us  [send(): return lax.ppermute(values, both, [(i, i ^ flip) for i in range(devices)])]
    ppermute x0 -> x6, starting transfers between devices: none -> 8.56 us  [send(): return lax.ppermute(values, both, [(i, i ^ flip) for i in range(devices)])]
    ppermute x11, waiting for transfers between devices: 14.9 us -> 7.52 us  [swap(): return lax.ppermute(values, axis, [(i, i ^ bit) for i in range(size)])]
    unnamed x14 -> x36, local copies, waits for them, and re-layouts: 0.04 us -> 7.26 us
    all_to_all x1 -> x0, starting transfers between devices: 5.26 us -> none  [per_device(): lax.all_to_all(partial, both, 0, 0, axis_index_groups=groups, tiled=True)]
  transfers between devices with their start and end apart: 14 -> 19, of which waited for: 9 -> 10; matrix products, arithmetic and copies ran while one was open for 1% -> 1% of each run, Pallas kernels for 20% -> 19%
where the time goes in v11:
time: 110 us
  waiting for transfers between devices  35.5 us (32%)
  starting transfers between devices  30.8 us (28%)
  Pallas kernels  28.6 us (26%)
  local copies, waits for them, and re-layouts  9.14 us (8%)
  matrix products  3.38 us (3%)
  other arithmetic  1.24 us (1%)
    ppermute x6, waiting for transfers between devices, send(): return lax.ppermute(values, both, [(i, i ^ flip) for i in range(devices)])  18.4 us
    ppermute x11, starting transfers between devices, swap(): return lax.ppermute(values, axis, [(i, i ^ bit) for i in range(size)])  12.3 us
    ppermute x6, starting transfers between devices, send(): return lax.ppermute(values, both, [(i, i ^ flip) for i in range(devices)])  8.56 us
    ppermute x11, waiting for transfers between devices, swap(): return lax.ppermute(values, axis, [(i, i ^ bit) for i in range(size)])  7.52 us
    all_to_all x1, starting transfers between devices, per_device(): lax.all_to_all(d_attn.reshape(devices, t_dev, columns, part), both, 0, 0,...  7.29 us
    unnamed x36, local copies, waits for them, and re-layouts  7.26 us
    pallas_call x1, Pallas kernels, own_weights(): pl.pallas_call(functools.partial(weights_kernel, n_chip=n_chip), grid_spe...  6.24 us
    pallas_call x1, Pallas kernels, attend(): pl.pallas_call(functools.partial(attend_kernel, columns=columns), out_spe...  5.92 us
  transfers between devices with their start and end apart: 19, of which 10 were waited for; matrix products, arithmetic and copies ran while one was open for 1% of the time, Pallas kernels for 19%

profile of v11, /device:TPU:0, one launch (start us, length us, event | category | flops | bytes accessed | tf_op | source)
XLA Modules:
  0.0 109.7 jit_solution(9358820644741544025)
XLA Ops:
  0.7 3.4 %fusion = bf16[4,128,352]{1,2,0:T(8,128)(2,1)S(1)} fusion(bf16[4,352,1408]{2,1,0:T(8,128)(2,1)} %bitcast.69, bf16[128,1408,1]{1,0,2:T(8,128)(2,1)} %bitcast.63), kind=kOutput, calls=%fused_computation.1 | convolution fusion | flops 507691008 | bytes 4685824 | tf_op jit(solution)/shard_map/to,jfo->jtf/dot_general | solution.py:390
  4.0 0.2 copy.13
  4.3 0.8 copy.14
  5.1 7.3 %all-to-all-start = ((bf16[32,2,8,352]{3,2,1,0:T(8,128)(2,1)}), bf16[32,2,8,352]{3,2,1,0:T(8,128)(2,1)S(1)}, u32[]{:S(2)}, u32[]{:S(2)}) async-start(bf16[32,2,8,352]{3,2,1,0:T(8,128)(2,1)} %bitcast.10), calls=%async_computation | async-start | bytes 786432 | tf_op jit(solution)/shard_map/all_to_all | solution.py:395
  12.5 6.2 %shard_map.105.refs_2_ = bf16[3,1408,704]{2,1,0:T(8,128)(2,1)} custom-call(s32[1]{0:T(128)} %bitcast.1.chip_ref, bf16[1408,4224]{1,0:T(8,128)(2,1)} %w_ref), custom_call_target="tpu_custom_call" | custom-call | tf_op jit(solution)/shard_map/pallas_call | solution.py:114
  18.7 1.4 %shard_map.104 = bf16[32,16,352]{2,1,0:T(8,128)(2,1)} custom-call(bf16[128,1408]{1,0:T(8,128)(2,1)S(1)} %bitcast.57, f32[1,1408]{1,0:T(1,128)S(1)} %broadcast_in_dim.16.gain_ref, f32[1,1408]{1,0:T(1,128)S(1)} %broadcast_in_dim.17.bias_ref), custom_call_target="tpu_custom_call" | custom-call | tf_op jit(solution)/shard_map/pallas_call | solution.py:82
  20.1 5.4 %all-to-all-done = bf16[32,2,8,352]{3,2,1,0:T(8,128)(2,1)S(1)} async-done(((bf16[32,2,8,352]{3,2,1,0:T(8,128)(2,1)}), bf16[32,2,8,352]{3,2,1,0:T(8,128)(2,1)S(1)}, u32[]{:S(2)}, u32[]{:S(2)}) %all-to-all-start) | async-done | bytes 360480 | tf_op jit(solution)/shard_map/all_to_all | solution.py:395
  25.5 5.9 %shard_map.106 = (bf16[3,352,512]{2,1,0:T(8,128)(2,1)S(1)}, bf16[1,352,512]{2,1,0:T(8,128)(2,1)}, bf16[2,352,512]{2,1,0:T(8,128)(2,1)}) custom-call(bf16[512,352]{1,0:T(8,128)(2,1)S(1)} %bitcast.60, bf16[512,352]{1,0:T(8,128)(2,1)S(1)} %bitcast.61, bf16[512,352]{1,0:T(8,128)(2,1)S(1)} %bitcast.62, bf16[512,352]{1,0:T(8,128)(2,1)S(1)} %bitcast.56), custom_call_target="tpu_custom_call" | custom-call | tf_op jit(solution)/shard_map/pallas_call | solution.py:54
  31.6 2.7 %all-to-all-start.1 = ((bf16[32,16,352]{2,1,0:T(8,128)(2,1)}), bf16[32,16,352]{2,1,0:T(8,128)(2,1)S(1)}, u32[]{:S(2)}, u32[]{:S(2)}) async-start(bf16[32,16,352]{2,1,0:T(8,128)(2,1)} %shard_map.104), calls=%async_computation.1 | async-start | bytes 786432 | tf_op jit(solution)/shard_map/all_to_all | solution.py:402
  34.3 1.8 %collective-permute-start.1 = (bf16[2,352,512]{2,1,0:T(8,128)(2,1)}, bf16[2,352,512]{2,1,0:T(8,128)(2,1)}, u32[]{:S(2)}, u32[]{:S(2)}) collective-permute-start(bf16[2,352,512]{2,1,0:T(8,128)(2,1)} %get-tuple-element.30), channel_id=1, source_target_pairs={{0,4},{4,0},{8,12},{12,8},{16,20},{20,16},{24,28},{28,24},{1,5},{5... | collective-permute-start | bytes 2162696 | tf_op jit(solution)/shard_map/ppermute | solution.py:387
  36.1 5.7 %shard_map.108 = (bf16[8,16,1408]{2,1,0:T(8,128)(2,1)S(1)}, f32[8,16,1408]{2,1,0:T(8,128)}) custom-call(s32[1]{0:T(128)} %bitcast.16.where_ref, bf16[3,352,512]{2,1,0:T(8,128)(2,1)S(1)} %get-tuple-element.31.refs_0_, bf16[3,352,512]{2,1,0:T(8,128)(2,1)S(1)} %collective-permute-done.3.refs_1_, bf16[3,1408,704]{2,1,0:T(8,128)(2,1)} %shard_map.105.refs_2_), custom_call_target="tpu_custom_call" | custom-call | tf_op jit(solution)/shard_map/pallas_call | solution.py:179
  41.8 1.5 %collective-permute-start.4 = (bf16[8,16,1408]{2,1,0:T(8,128)(2,1)S(1)}, bf16[8,16,1408]{2,1,0:T(8,128)(2,1)S(1)}, u32[]{:S(2)}, u32[]{:S(2)}) collective-permute-start(bf16[8,16,1408]{2,1,0:T(8,128)(2,1)S(1)} %get-tuple-element.34), channel_id=1, source_target_pairs={{0,2},{1,3},{2,0},{3,1},{4,6},{5,7},{6,4},{7,5},{8,10},{9,11},{10,... | collective-permute-start | bytes 1081352 | tf_op jit(solution)/shard_map/ppermute | solution.py:387
  43.4 4.1 %all-to-all-done.1 = bf16[32,16,352]{2,1,0:T(8,128)(2,1)S(1)} async-done(((bf16[32,16,352]{2,1,0:T(8,128)(2,1)}), bf16[32,16,352]{2,1,0:T(8,128)(2,1)S(1)}, u32[]{:S(2)}, u32[]{:S(2)}) %all-to-all-start.1) | async-done | bytes 360480 | tf_op jit(solution)/shard_map/all_to_all | solution.py:402
  47.5 0.5 collective-permute-start.2
  48.0 1.5 %collective-permute-start = (bf16[1,352,512]{2,1,0:T(8,128)(2,1)}, bf16[1,352,512]{2,1,0:T(8,128)(2,1)}, u32[]{:S(2)}, u32[]{:S(2)}) collective-permute-start(bf16[1,352,512]{2,1,0:T(8,128)(2,1)} %get-tuple-element.29), channel_id=1, source_target_pairs={{0,4},{4,0},{8,12},{12,8},{16,20},{20,16},{24,28},{28,24},{1,5},{5... | collective-permute-start | bytes 1081352 | tf_op jit(solution)/shard_map/ppermute | solution.py:387
  49.5 4.0 %collective-permute-done.4.come_ref = bf16[8,16,1408]{2,1,0:T(8,128)(2,1)S(1)} collective-permute-done((bf16[8,16,1408]{2,1,0:T(8,128)(2,1)S(1)}, bf16[8,16,1408]{2,1,0:T(8,128)(2,1)S(1)}, u32[]{:S(2)}, u32[]{:S(2)}) %collective-permute-start.4) | collective-permute-done | bytes 360480 | tf_op jit(solution)/shard_map/ppermute | solution.py:387
  53.5 1.2 %shard_map.109 = bf16[8,16,1408]{2,1,0:T(8,128)(2,1)S(1)} custom-call(f32[8,16,1408]{2,1,0:T(8,128)} %get-tuple-element.33.stay_hbm, bf16[8,16,1408]{2,1,0:T(8,128)(2,1)S(1)} %collective-permute-done.4.come_ref), custom_call_target="tpu_custom_call" | custom-call | tf_op jit(solution)/shard_map/pallas_call | solution.py:413
  54.7 2.2 %collective-permute-start.5 = (bf16[2,16,1408]{2,1,0:T(8,128)(2,1)S(1)}, bf16[2,16,1408]{2,1,0:T(8,128)(2,1)}, u32[]{:S(2)}, u32[]{:S(2)}) collective-permute-start(bf16[2,16,1408]{2,1,0:T(8,128)(2,1)S(1)} %get-tuple-element.57), channel_id=1, source_target_pairs={{0,16},{4,20},{8,24},{12,28},{16,0},{20,4},{24,8},{28,12},{1,17},{... | collective-permute-start | bytes 270344 | tf_op jit(solution)/shard_map/ppermute | solution.py:387
  56.9 1.9 %collective-permute-start.6 = (bf16[2,16,1408]{2,1,0:T(8,128)(2,1)S(1)}, bf16[2,16,1408]{2,1,0:T(8,128)(2,1)}, u32[]{:S(2)}, u32[]{:S(2)}) collective-permute-start(bf16[2,16,1408]{2,1,0:T(8,128)(2,1)S(1)} %get-tuple-element.56), channel_id=1, source_target_pairs={{0,24},{4,28},{8,16},{12,20},{16,8},{20,12},{24,0},{28,4},{1,25},{... | collective-permute-start | bytes 270344 | tf_op jit(solution)/shard_map/ppermute | solution.py:387
  58.7 2.4 %collective-permute-done.2.theirs_ref = bf16[512,352]{1,0:T(8,128)(2,1)S(1)} collective-permute-done((bf16[512,352]{1,0:T(8,128)(2,1)S(1)}, bf16[512,352]{1,0:T(8,128)(2,1)S(1)}, u32[]{:S(2)}, u32[]{:S(2)}) %collective-permute-start.2) | collective-permute-done | bytes 360480 | tf_op jit(solution)/shard_map/ppermute | solution.py:387
  61.2 0.8 copy-done.7
  61.9 1.2 %copy-done.1 = bf16[3,352,512]{2,1,0:T(8,128)(2,1)S(1)} copy-done((bf16[3,352,512]{2,1,0:T(8,128)(2,1)S(1)}, bf16[3,352,512]{2,1,0:T(8,128)(2,1)}, u32[]{:S(2)}) %copy-start.1) | copy-done | bytes 1081368
  63.2 1.2 %copy-done.3 = bf16[3,352,512]{2,1,0:T(8,128)(2,1)S(1)} copy-done((bf16[3,352,512]{2,1,0:T(8,128)(2,1)S(1)}, bf16[3,352,512]{2,1,0:T(8,128)(2,1)}, u32[]{:S(2)}) %copy-start.3) | copy-done | bytes 1081368
  64.4 1.0 copy-done.5
  65.4 1.0 copy-done.8
  66.4 1.3 %shard_map.107.acc_ref = f32[2112,352]{1,0:T(8,128)S(1)} custom-call(s32[1]{0:T(128)} %bitcast.1.chip_ref, bf16[512,352]{1,0:T(8,128)(2,1)S(1)} %bitcast.54, bf16[512,352]{1,0:T(8,128)(2,1)S(1)} %copy-done.8, bf16[3,352,512]{2,1,0:T(8,128)(2,1)S(1)} %copy-done.1, bf16[3,352,512]{2,1,0:T(8,128)(2,1)S(1)} %copy-done.3), custom_call_target="tpu_custom_call" | custom-call | tf_op jit(solution)/shard_map/pallas_call | solution.py:222
  67.8 0.5 collective-permute-start.7
  68.3 1.4 %collective-permute-start.9 = (bf16[2,16,1408]{2,1,0:T(8,128)(2,1)S(1)}, bf16[2,16,1408]{2,1,0:T(8,128)(2,1)S(1)}, u32[]{:S(2)}, u32[]{:S(2)}) collective-permute-start(bf16[2,16,1408]{2,1,0:T(8,128)(2,1)S(1)} %get-tuple-element.54), channel_id=1, source_target_pairs={{0,8},{4,12},{8,0},{12,4},{16,24},{20,28},{24,16},{28,20},{1,9},{5... | collective-permute-start | bytes 270344 | tf_op jit(solution)/shard_map/ppermute | solution.py:387
  69.8 1.1 collective-permute-done.7.refs_2_
  70.9 1.0 copy-done.6
  71.9 1.0 copy-done.9
  72.9 3.7 %shard_map.110 = bf16[8,726,128]{2,1,0:T(8,128)(2,1)S(1)} custom-call(s32[2]{0:T(128)S(1)} %pad_add_fusion.chip_ref, bf16[512,352]{1,0:T(8,128)(2,1)S(1)} %bitcast.55, bf16[512,352]{1,0:T(8,128)(2,1)S(1)} %copy-done.9, f32[2112,352]{1,0:T(8,128)S(1)} %shard_map.107.acc_ref, bf16[1,352,512]{2,1,0:T(8,128)(2,1)} %collective-permute-done.refs_0_, ...), custom_call_target="tpu_custom_call" | custom-call | tf_op jit(solution)/shard_map/pallas_call | solution.py:269
  76.6 0.7 slice_bitcast_fusion.2
  77.3 1.4 %collective-permute-start.12 = (bf16[2,726,128]{2,1,0:T(8,128)(2,1)S(1)}, bf16[2,726,128]{2,1,0:T(8,128)(2,1)S(1)}, u32[]{:S(2)}, u32[]{:S(2)}) collective-permute-start(bf16[2,726,128]{2,1,0:T(8,128)(2,1)S(1)} %slice.27), channel_id=1, source_target_pairs={{0,8},{1,9},{2,10},{3,11},{4,12},{5,13},{6,14},{7,15},{8,0},{9,1},... | collective-permute-start | bytes 1115144 | tf_op jit(solution)/shard_map/ppermute | solution.py:437
  78.7 0.6 collective-permute-start.11
  79.4 1.2 %collective-permute-start.14 = (bf16[726,128]{1,0:T(8,128)(2,1)S(1)}, bf16[726,128]{1,0:T(8,128)(2,1)S(1)}, u32[]{:S(2)}, u32[]{:S(2)}) collective-permute-start(bf16[726,128]{1,0:T(8,128)(2,1)S(1)} %get-tuple-element.47), channel_id=1, source_target_pairs={{0,2},{1,3},{2,0},{3,1},{4,6},{5,7},{6,4},{7,5},{8,10},{9,11},{10,... | collective-permute-start | bytes 557576 | tf_op jit(solution)/shard_map/ppermute | solution.py:437
  80.6 1.6 %collective-permute-start.15 = (bf16[726,128]{1,0:T(8,128)(2,1)S(1)}, bf16[726,128]{1,0:T(8,128)(2,1)S(1)}, u32[]{:S(2)}, u32[]{:S(2)}) collective-permute-start(bf16[726,128]{1,0:T(8,128)(2,1)S(1)} %get-tuple-element.46), channel_id=1, source_target_pairs={{0,10},{1,11},{2,8},{3,9},{4,14},{5,15},{6,12},{7,13},{8,2},{9,3},... | collective-permute-start | bytes 557576 | tf_op jit(solution)/shard_map/ppermute | solution.py:437
  82.2 1.0 pad_maximum_fusion
  83.3 0.8 collective-permute-start.10
  84.1 4.8 %collective-permute-done.12 = bf16[2,726,128]{2,1,0:T(8,128)(2,1)S(1)} collective-permute-done((bf16[2,726,128]{2,1,0:T(8,128)(2,1)S(1)}, bf16[2,726,128]{2,1,0:T(8,128)(2,1)S(1)}, u32[]{:S(2)}, u32[]{:S(2)}) %collective-permute-start.12) | collective-permute-done | bytes 371744 | tf_op jit(solution)/shard_map/ppermute | solution.py:437
  89.0 1.9 %collective-permute-start.13 = (bf16[726,128]{1,0:T(8,128)(2,1)S(1)}, bf16[726,128]{1,0:T(8,128)(2,1)S(1)}, u32[]{:S(2)}, u32[]{:S(2)}) collective-permute-start(bf16[726,128]{1,0:T(8,128)(2,1)S(1)} %get-tuple-element.51), channel_id=1, source_target_pairs={{0,16},{1,17},{2,18},{3,19},{4,20},{5,21},{6,22},{7,23},{8,24},{9,... | collective-permute-start | bytes 557576 | tf_op jit(solution)/shard_map/ppermute | solution.py:437
  90.9 1.8 %collective-permute-start.16 = (bf16[726,128]{1,0:T(8,128)(2,1)S(1)}, bf16[726,128]{1,0:T(8,128)(2,1)S(1)}, u32[]{:S(2)}, u32[]{:S(2)}) collective-permute-start(bf16[726,128]{1,0:T(8,128)(2,1)S(1)} %get-tuple-element.50), channel_id=1, source_target_pairs={{0,18},{1,19},{2,16},{3,17},{4,22},{5,23},{6,20},{7,21},{8,26},{9,... | collective-permute-start | bytes 557576 | tf_op jit(solution)/shard_map/ppermute | solution.py:437
  92.8 1.3 %shard_map.111 = bf16[128,1408]{1,0:T(8,128)(2,1)} custom-call(s32[1]{0:T(128)} %bitcast.tm_ref, bf16[4,16,1408]{2,1,0:T(8,128)(2,1)S(1)} %get-tuple-element.53.stay_ref, bf16[4,16,1408]{2,1,0:T(8,128)(2,1)S(1)} %collective-permute-done.10.come_ref, bf16[128,1408]{1,0:T(8,128)(2,1)S(1)} %bitcast.58, bf16[128,1408]{1,0:T(8,128)(2,1)S(1)} %bitcast.64, ...), custom_call_target="tpu_custom_call" | custom-call | tf_op jit(solution)/shard_map/pallas_call | solution.py:314
  94.1 4.7 %collective-permute-done.11.refs_1_ = bf16[726,128]{1,0:T(8,128)(2,1)S(1)} collective-permute-done((bf16[726,128]{1,0:T(8,128)(2,1)}, bf16[726,128]{1,0:T(8,128)(2,1)S(1)}, u32[]{:S(2)}, u32[]{:S(2)}) %collective-permute-start.11) | collective-permute-done | bytes 185888 | tf_op jit(solution)/shard_map/ppermute | solution.py:437
  98.8 4.3 %collective-permute-done.15.refs_4_ = bf16[726,128]{1,0:T(8,128)(2,1)S(1)} collective-permute-done((bf16[726,128]{1,0:T(8,128)(2,1)S(1)}, bf16[726,128]{1,0:T(8,128)(2,1)S(1)}, u32[]{:S(2)}, u32[]{:S(2)}) %collective-permute-start.15) | collective-permute-done | bytes 185888 | tf_op jit(solution)/shard_map/ppermute | solution.py:437
  103.2 2.3 %collective-permute-done.13.refs_2_ = bf16[726,128]{1,0:T(8,128)(2,1)S(1)} collective-permute-done((bf16[726,128]{1,0:T(8,128)(2,1)S(1)}, bf16[726,128]{1,0:T(8,128)(2,1)S(1)}, u32[]{:S(2)}, u32[]{:S(2)}) %collective-permute-start.13) | collective-permute-done | bytes 185888 | tf_op jit(solution)/shard_map/ppermute | solution.py:437
  105.4 2.4 %collective-permute-done.16.refs_5_ = bf16[726,128]{1,0:T(8,128)(2,1)S(1)} collective-permute-done((bf16[726,128]{1,0:T(8,128)(2,1)S(1)}, bf16[726,128]{1,0:T(8,128)(2,1)S(1)}, u32[]{:S(2)}, u32[]{:S(2)}) %collective-permute-start.16) | collective-permute-done | bytes 185888 | tf_op jit(solution)/shard_map/ppermute | solution.py:437
  107.8 2.0 %shard_map.112 = f32[44,4224]{1,0:T(8,128)} custom-call(s32[2]{0:T(128)S(1)} %pad_add_fusion.1.place_ref, bf16[726,128]{1,0:T(8,128)(2,1)S(1)} %get-tuple-element.49.refs_0_, bf16[726,128]{1,0:T(8,128)(2,1)S(1)} %collective-permute-done.11.refs_1_, bf16[726,128]{1,0:T(8,128)(2,1)S(1)} %collective-permute-done.13.refs_2_, ...), custom_call_target="tpu_custom_call" | custom-call | tf_op jit(solution)/shard_map/pallas_call | solution.py:357
  (49 shorter events, 0.6 us)
Async XLA Ops:
  0.6 11.7 %copy-start.16 = (f32[1408]{0:T(1024)S(1)}, f32[1408]{0:T(1024)}, u32[]{:S(2)}) copy-start(f32[1408]{0:T(1024)} %param.10) | copy-start | bytes 16900
  0.6 11.8 %copy-start.17 = (f32[1408]{0:T(1024)S(1)}, f32[1408]{0:T(1024)}, u32[]{:S(2)}) copy-start(f32[1408]{0:T(1024)} %param.11) | copy-start | bytes 16900
  5.1 20.5 %all-to-all-start = ((bf16[32,2,8,352]{3,2,1,0:T(8,128)(2,1)}), bf16[32,2,8,352]{3,2,1,0:T(8,128)(2,1)S(1)}, u32[]{:S(2)}, u32[]{:S(2)}) async-start(bf16[32,2,8,352]{3,2,1,0:T(8,128)(2,1)} %bitcast.10), calls=%async_computation | async-start | bytes 786432 | tf_op jit(solution)/shard_map/all_to_all | solution.py:395
  12.4 6.3 %copy-start.10 = (bf16[2,64,1408]{2,1,0:T(8,128)(2,1)S(1)}, bf16[2,64,1408]{2,1,0:T(8,128)(2,1)}, u32[]{:S(2)}) copy-start(bf16[2,64,1408]{2,1,0:T(8,128)(2,1)} %param.9) | copy-start | bytes 1081348
  12.4 13.1 %copy-start.12 = (bf16[64,8,352]{2,1,0:T(8,128)(2,1)S(1)}, bf16[64,8,352]{2,1,0:T(8,128)(2,1)}, u32[]{:S(2)}) copy-start(bf16[64,8,352]{2,1,0:T(8,128)(2,1)} %param.14) | copy-start | bytes 1081348
  12.5 13.1 %copy-start.13 = (bf16[64,8,352]{2,1,0:T(8,128)(2,1)S(1)}, bf16[64,8,352]{2,1,0:T(8,128)(2,1)}, u32[]{:S(2)}) copy-start(bf16[64,8,352]{2,1,0:T(8,128)(2,1)} %param.15) | copy-start | bytes 1081348
  12.5 13.1 %copy-start.14 = (bf16[64,8,352]{2,1,0:T(8,128)(2,1)S(1)}, bf16[64,8,352]{2,1,0:T(8,128)(2,1)}, u32[]{:S(2)}) copy-start(bf16[64,8,352]{2,1,0:T(8,128)(2,1)} %param.16) | copy-start | bytes 1081348
  31.5 10.4 %copy-start = (bf16[3,352,512]{2,1,0:T(8,128)(2,1)}, bf16[3,352,512]{2,1,0:T(8,128)(2,1)S(1)}, u32[]{:S(2)}) copy-start(bf16[3,352,512]{2,1,0:T(8,128)(2,1)S(1)} %get-tuple-element.31.refs_0_) | copy-start | bytes 3244036
  31.5 4.7 %collective-permute-start.3 = (bf16[3,352,512]{2,1,0:T(8,128)(2,1)S(1)}, bf16[3,352,512]{2,1,0:T(8,128)(2,1)S(1)}, u32[]{:S(2)}, u32[]{:S(2)}) collective-permute-start(bf16[3,352,512]{2,1,0:T(8,128)(2,1)S(1)} %get-tuple-element.31.refs_0_), channel_id=1, source_target_pairs={{0,1},{1,0},{2,3},{3,2},{4,5},{5,4},{6,7},{7,6},{8,9},{9,8},{10,11... | collective-permute-start | bytes 3244040 | tf_op jit(solution)/shard_map/ppermute | solution.py:387
  31.6 15.9 %all-to-all-start.1 = ((bf16[32,16,352]{2,1,0:T(8,128)(2,1)}), bf16[32,16,352]{2,1,0:T(8,128)(2,1)S(1)}, u32[]{:S(2)}, u32[]{:S(2)}) async-start(bf16[32,16,352]{2,1,0:T(8,128)(2,1)} %shard_map.104), calls=%async_computation.1 | async-start | bytes 786432 | tf_op jit(solution)/shard_map/all_to_all | solution.py:402
  34.3 33.4 %collective-permute-start.1 = (bf16[2,352,512]{2,1,0:T(8,128)(2,1)}, bf16[2,352,512]{2,1,0:T(8,128)(2,1)}, u32[]{:S(2)}, u32[]{:S(2)}) collective-permute-start(bf16[2,352,512]{2,1,0:T(8,128)(2,1)} %get-tuple-element.30), channel_id=1, source_target_pairs={{0,4},{4,0},{8,12},{12,8},{16,20},{20,16},{24,28},{28,24},{1,5},{5... | collective-permute-start | bytes 2162696 | tf_op jit(solution)/shard_map/ppermute | solution.py:387
  36.1 5.7 %copy-start.2 = (bf16[3,352,512]{2,1,0:T(8,128)(2,1)}, bf16[3,352,512]{2,1,0:T(8,128)(2,1)S(1)}, u32[]{:S(2)}) copy-start(bf16[3,352,512]{2,1,0:T(8,128)(2,1)S(1)} %collective-permute-done.3.refs_1_) | copy-start | bytes 3244036
  41.8 11.6 %collective-permute-start.4 = (bf16[8,16,1408]{2,1,0:T(8,128)(2,1)S(1)}, bf16[8,16,1408]{2,1,0:T(8,128)(2,1)S(1)}, u32[]{:S(2)}, u32[]{:S(2)}) collective-permute-start(bf16[8,16,1408]{2,1,0:T(8,128)(2,1)S(1)} %get-tuple-element.34), channel_id=1, source_target_pairs={{0,2},{1,3},{2,0},{3,1},{4,6},{5,7},{6,4},{7,5},{8,10},{9,11},{10,... | collective-permute-start | bytes 1081352 | tf_op jit(solution)/shard_map/ppermute | solution.py:387
  47.5 11.3 %copy-start.4 = (bf16[32,16,352]{2,1,0:T(8,128)(2,1)}, bf16[32,16,352]{2,1,0:T(8,128)(2,1)S(1)}, u32[]{:S(2)}) copy-start(bf16[32,16,352]{2,1,0:T(8,128)(2,1)S(1)} %all-to-all-done.1) | copy-start | bytes 1081348
  47.5 13.7 %collective-permute-start.2 = (bf16[512,352]{1,0:T(8,128)(2,1)S(1)}, bf16[512,352]{1,0:T(8,128)(2,1)S(1)}, u32[]{:S(2)}, u32[]{:S(2)}) collective-permute-start(bf16[512,352]{1,0:T(8,128)(2,1)S(1)} %bitcast.53), channel_id=1, source_target_pairs={{0,2},{1,3},{2,0},{3,1},{4,6},{5,7},{6,4},{7,5},{8,10},{9,11},{10,... | collective-permute-start | bytes 1081352 | tf_op jit(solution)/shard_map/ppermute | solution.py:387
  48.0 19.7 %collective-permute-start = (bf16[1,352,512]{2,1,0:T(8,128)(2,1)}, bf16[1,352,512]{2,1,0:T(8,128)(2,1)}, u32[]{:S(2)}, u32[]{:S(2)}) collective-permute-start(bf16[1,352,512]{2,1,0:T(8,128)(2,1)} %get-tuple-element.29), channel_id=1, source_target_pairs={{0,4},{4,0},{8,12},{12,8},{16,20},{20,16},{24,28},{28,24},{1,5},{5... | collective-permute-start | bytes 1081352 | tf_op jit(solution)/shard_map/ppermute | solution.py:387
  54.7 13.0 %collective-permute-start.5 = (bf16[2,16,1408]{2,1,0:T(8,128)(2,1)S(1)}, bf16[2,16,1408]{2,1,0:T(8,128)(2,1)}, u32[]{:S(2)}, u32[]{:S(2)}) collective-permute-start(bf16[2,16,1408]{2,1,0:T(8,128)(2,1)S(1)} %get-tuple-element.57), channel_id=1, source_target_pairs={{0,16},{4,20},{8,24},{12,28},{16,0},{20,4},{24,8},{28,12},{1,17},{... | collective-permute-start | bytes 270344 | tf_op jit(solution)/shard_map/ppermute | solution.py:387
  56.9 10.8 %collective-permute-start.6 = (bf16[2,16,1408]{2,1,0:T(8,128)(2,1)S(1)}, bf16[2,16,1408]{2,1,0:T(8,128)(2,1)}, u32[]{:S(2)}, u32[]{:S(2)}) collective-permute-start(bf16[2,16,1408]{2,1,0:T(8,128)(2,1)S(1)} %get-tuple-element.56), channel_id=1, source_target_pairs={{0,24},{4,28},{8,16},{12,20},{16,8},{20,12},{24,0},{28,4},{1,25},{... | collective-permute-start | bytes 270344 | tf_op jit(solution)/shard_map/ppermute | solution.py:387
  61.2 0.8 copy-start.7
  61.9 1.2 %copy-start.1 = (bf16[3,352,512]{2,1,0:T(8,128)(2,1)S(1)}, bf16[3,352,512]{2,1,0:T(8,128)(2,1)}, u32[]{:S(2)}) copy-start(bf16[3,352,512]{2,1,0:T(8,128)(2,1)} %copy-done) | copy-start | bytes 3244036
  63.2 1.2 %copy-start.3 = (bf16[3,352,512]{2,1,0:T(8,128)(2,1)S(1)}, bf16[3,352,512]{2,1,0:T(8,128)(2,1)}, u32[]{:S(2)}) copy-start(bf16[3,352,512]{2,1,0:T(8,128)(2,1)} %copy-done.2) | copy-start | bytes 3244036
  64.4 1.0 copy-start.5
  65.4 1.0 copy-start.8
  67.7 3.1 %collective-permute-start.8 = (bf16[2,352,512]{2,1,0:T(8,128)(2,1)}, bf16[2,352,512]{2,1,0:T(8,128)(2,1)}, u32[]{:S(2)}, u32[]{:S(2)}) collective-permute-start(bf16[2,352,512]{2,1,0:T(8,128)(2,1)} %collective-permute-done.1.refs_1_), channel_id=1, source_target_pairs={{0,1},{1,0},{2,3},{3,2},{4,5},{5,4},{6,7},{7,6},{8,9},{9,8},{10,11... | collective-permute-start | bytes 2162696 | tf_op jit(solution)/shard_map/ppermute | solution.py:387
  67.8 3.0 %collective-permute-start.7 = (bf16[1,352,512]{2,1,0:T(8,128)(2,1)}, bf16[1,352,512]{2,1,0:T(8,128)(2,1)}, u32[]{:S(2)}, u32[]{:S(2)}) collective-permute-start(bf16[1,352,512]{2,1,0:T(8,128)(2,1)} %collective-permute-done.refs_0_), channel_id=1, source_target_pairs={{0,1},{1,0},{2,3},{3,2},{4,5},{5,4},{6,7},{7,6},{8,9},{9,8},{10,11... | collective-permute-start | bytes 1081352 | tf_op jit(solution)/shard_map/ppermute | solution.py:387
  68.3 8.3 %collective-permute-start.9 = (bf16[2,16,1408]{2,1,0:T(8,128)(2,1)S(1)}, bf16[2,16,1408]{2,1,0:T(8,128)(2,1)S(1)}, u32[]{:S(2)}, u32[]{:S(2)}) collective-permute-start(bf16[2,16,1408]{2,1,0:T(8,128)(2,1)S(1)} %get-tuple-element.54), channel_id=1, source_target_pairs={{0,8},{4,12},{8,0},{12,4},{16,24},{20,28},{24,16},{28,20},{1,9},{5... | collective-permute-start | bytes 270344 | tf_op jit(solution)/shard_map/ppermute | solution.py:387
  70.9 1.0 copy-start.6
  71.9 1.0 copy-start.9
  76.5 16.2 %copy-start.11 = (bf16[2,64,1408]{2,1,0:T(8,128)(2,1)S(1)}, bf16[2,64,1408]{2,1,0:T(8,128)(2,1)}, u32[]{:S(2)}) copy-start(bf16[2,64,1408]{2,1,0:T(8,128)(2,1)} %param.9) | copy-start | bytes 1081348
  76.6 16.2 %copy-start.15 = (bf16[2,64,1408]{2,1,0:T(8,128)(2,1)S(1)}, bf16[2,64,1408]{2,1,0:T(8,128)(2,1)}, u32[]{:S(2)}) copy-start(bf16[2,64,1408]{2,1,0:T(8,128)(2,1)} %param.17) | copy-start | bytes 1081348
  77.3 11.5 %collective-permute-start.12 = (bf16[2,726,128]{2,1,0:T(8,128)(2,1)S(1)}, bf16[2,726,128]{2,1,0:T(8,128)(2,1)S(1)}, u32[]{:S(2)}, u32[]{:S(2)}) collective-permute-start(bf16[2,726,128]{2,1,0:T(8,128)(2,1)S(1)} %slice.27), channel_id=1, source_target_pairs={{0,8},{1,9},{2,10},{3,11},{4,12},{5,13},{6,14},{7,15},{8,0},{9,1},... | collective-permute-start | bytes 1115144 | tf_op jit(solution)/shard_map/ppermute | solution.py:437
  78.7 20.1 %collective-permute-start.11 = (bf16[726,128]{1,0:T(8,128)(2,1)}, bf16[726,128]{1,0:T(8,128)(2,1)S(1)}, u32[]{:S(2)}, u32[]{:S(2)}) collective-permute-start(bf16[726,128]{1,0:T(8,128)(2,1)} %get-tuple-element.48), channel_id=1, source_target_pairs={{0,8},{1,9},{2,10},{3,11},{4,12},{5,13},{6,14},{7,15},{8,0},{9,1},... | collective-permute-start | bytes 557576 | tf_op jit(solution)/shard_map/ppermute | solution.py:437
  79.4 19.5 %collective-permute-start.14 = (bf16[726,128]{1,0:T(8,128)(2,1)S(1)}, bf16[726,128]{1,0:T(8,128)(2,1)S(1)}, u32[]{:S(2)}, u32[]{:S(2)}) collective-permute-start(bf16[726,128]{1,0:T(8,128)(2,1)S(1)} %get-tuple-element.47), channel_id=1, source_target_pairs={{0,2},{1,3},{2,0},{3,1},{4,6},{5,7},{6,4},{7,5},{8,10},{9,11},{10,... | collective-permute-start | bytes 557576 | tf_op jit(solution)/shard_map/ppermute | solution.py:437
  80.6 22.5 %collective-permute-start.15 = (bf16[726,128]{1,0:T(8,128)(2,1)S(1)}, bf16[726,128]{1,0:T(8,128)(2,1)S(1)}, u32[]{:S(2)}, u32[]{:S(2)}) collective-permute-start(bf16[726,128]{1,0:T(8,128)(2,1)S(1)} %get-tuple-element.46), channel_id=1, source_target_pairs={{0,10},{1,11},{2,8},{3,9},{4,14},{5,15},{6,12},{7,13},{8,2},{9,3},... | collective-permute-start | bytes 557576 | tf_op jit(solution)/shard_map/ppermute | solution.py:437
  83.3 7.6 %collective-permute-start.10 = (bf16[4,16,1408]{2,1,0:T(8,128)(2,1)S(1)}, bf16[4,16,1408]{2,1,0:T(8,128)(2,1)S(1)}, u32[]{:S(2)}, u32[]{:S(2)}) collective-permute-start(bf16[4,16,1408]{2,1,0:T(8,128)(2,1)S(1)} %get-tuple-element.52), channel_id=1, source_target_pairs={{0,4},{4,0},{8,12},{12,8},{16,20},{20,16},{24,28},{28,24},{1,5},{5... | collective-permute-start | bytes 540680 | tf_op jit(solution)/shard_map/ppermute | solution.py:387
  89.0 16.4 %collective-permute-start.13 = (bf16[726,128]{1,0:T(8,128)(2,1)S(1)}, bf16[726,128]{1,0:T(8,128)(2,1)S(1)}, u32[]{:S(2)}, u32[]{:S(2)}) collective-permute-start(bf16[726,128]{1,0:T(8,128)(2,1)S(1)} %get-tuple-element.51), channel_id=1, source_target_pairs={{0,16},{1,17},{2,18},{3,19},{4,20},{5,21},{6,22},{7,23},{8,24},{9,... | collective-permute-start | bytes 557576 | tf_op jit(solution)/shard_map/ppermute | solution.py:437
  90.9 16.9 %collective-permute-start.16 = (bf16[726,128]{1,0:T(8,128)(2,1)S(1)}, bf16[726,128]{1,0:T(8,128)(2,1)S(1)}, u32[]{:S(2)}, u32[]{:S(2)}) collective-permute-start(bf16[726,128]{1,0:T(8,128)(2,1)S(1)} %get-tuple-element.50), channel_id=1, source_target_pairs={{0,18},{1,19},{2,16},{3,17},{4,22},{5,23},{6,20},{7,21},{8,26},{9,... | collective-permute-start | bytes 557576 | tf_op jit(solution)/shard_map/ppermute | solution.py:437

commit v12 on v11

--- a/solution.py
+++ b/solution.py
@@ -218,7 +218,7 @@
 def own_product(chip, mine, theirs, pieces):
     part = mine.shape[1]
     rows = part * sum(piece.shape[0] for piece in pieces)
-    arrays = (mine, theirs, *pieces)
+    arrays = [pltpu.with_memory_space_constraint(x, pltpu.HBM) for x in (mine, theirs, *pieces)]
     return pl.pallas_call(
         own_kernel,
         grid_spec=pltpu.PrefetchScalarGridSpec(
@@ -265,6 +265,7 @@
     lanes, part = acc.shape
     chunk = (own_rows * lanes // 128, 128) if packable(own_rows, lanes) else (own_rows, lanes)
     shape = (part // own_rows,) + chunk
+    mine, theirs = [pltpu.with_memory_space_constraint(x, pltpu.HBM) for x in (mine, theirs)]
     arrays = (mine, theirs, acc, *pieces)
     return pl.pallas_call(
         functools.partial(other_kernel, factor=factor, own_rows=own_rows, relative=relative),

time: 110 us -> 106 us (0.964)
  local copies, waits for them, and re-layouts: 9.14 us -> 1.94 us
  Pallas kernels: 28.6 us -> 30.7 us
    unnamed x36 -> x22, local copies, waits for them, and re-layouts: 7.26 us -> 0.06 us
    pallas_call x1, Pallas kernels: 1.29 us -> 3.09 us  [own_product(): pl.pallas_call(own_kernel, grid_spec=pltpu.PrefetchScalarGridSpec(num_sca...]
  transfers between devices with their start and end apart: 19 -> 19, of which waited for: 10 -> 10; matrix products, arithmetic and copies ran while one was open for 1% -> 1% of each run, Pallas kernels for 19% -> 22%
where the time goes in v12:
time: 106 us; the launch traced here: 105 us
  waiting for transfers between devices  35.4 us (33%)
  starting transfers between devices  31.7 us (30%)
  Pallas kernels  30.7 us (29%)
  matrix products  3.38 us (3%)
  local copies, waits for them, and re-layouts  1.94 us (2%)
  other arithmetic  1.24 us (1%)
    ppermute x6, waiting for transfers between devices, send(): return lax.ppermute(values, both, [(i, i ^ flip) for i in range(devices)])  18.2 us
    ppermute x11, starting transfers between devices, swap(): return lax.ppermute(values, axis, [(i, i ^ bit) for i in range(size)])  12.6 us
    ppermute x6, starting transfers between devices, send(): return lax.ppermute(values, both, [(i, i ^ flip) for i in range(devices)])  9.04 us
    ppermute x11, waiting for transfers between devices, swap(): return lax.ppermute(values, axis, [(i, i ^ bit) for i in range(size)])  7.63 us
    all_to_all x1, starting transfers between devices, per_device(): lax.all_to_all(d_attn.reshape(devices, t_dev, columns, part), both, 0, 0,...  7.29 us
    pallas_call x1, Pallas kernels, own_weights(): pl.pallas_call(functools.partial(weights_kernel, n_chip=n_chip), grid_spe...  6.24 us
    pallas_call x1, Pallas kernels, attend(): pl.pallas_call(functools.partial(attend_kernel, columns=columns), out_spe...  5.92 us
    pallas_call x1, Pallas kernels, share_send(): pl.pallas_call(share_kernel, grid_spec=pltpu.PrefetchScalarGridSpec(num_s...  5.65 us
  transfers between devices with their start and end apart: 19, of which 10 were waited for; matrix products, arithmetic and copies ran while one was open for 1% of the time, Pallas kernels for 22%

profile of v12, /device:TPU:0, one launch (start us, length us, event | category | flops | bytes accessed | tf_op | source)
XLA Modules:
  0.0 105.2 jit_solution(10295733869892513043)
XLA Ops:
  0.7 3.4 %fusion = bf16[4,128,352]{1,2,0:T(8,128)(2,1)S(1)} fusion(bf16[4,352,1408]{2,1,0:T(8,128)(2,1)} %bitcast.69, bf16[128,1408,1]{1,0,2:T(8,128)(2,1)} %bitcast.60), kind=kOutput, calls=%fused_computation.1 | convolution fusion | flops 507691008 | bytes 4685824 | tf_op jit(solution)/shard_map/to,jfo->jtf/dot_general | solution.py:391
  4.0 0.2 copy.13
  4.3 0.8 copy.14
  5.1 7.3 %all-to-all-start = ((bf16[32,2,8,352]{3,2,1,0:T(8,128)(2,1)}), bf16[32,2,8,352]{3,2,1,0:T(8,128)(2,1)S(1)}, u32[]{:S(2)}, u32[]{:S(2)}) async-start(bf16[32,2,8,352]{3,2,1,0:T(8,128)(2,1)} %bitcast.10), calls=%async_computation | async-start | bytes 786432 | tf_op jit(solution)/shard_map/all_to_all | solution.py:396
  12.4 0.0 copy-start.4
  12.5 0.0 copy-start.5
  12.5 6.2 %shard_map.105.refs_2_ = bf16[3,1408,704]{2,1,0:T(8,128)(2,1)} custom-call(s32[1]{0:T(128)} %bitcast.1.chip_ref, bf16[1408,4224]{1,0:T(8,128)(2,1)} %w_ref), custom_call_target="tpu_custom_call" | custom-call | tf_op jit(solution)/shard_map/pallas_call | solution.py:114
  18.7 1.4 %shard_map.104 = bf16[32,16,352]{2,1,0:T(8,128)(2,1)} custom-call(bf16[128,1408]{1,0:T(8,128)(2,1)S(1)} %bitcast.54, f32[1,1408]{1,0:T(1,128)S(1)} %broadcast_in_dim.16.gain_ref, f32[1,1408]{1,0:T(1,128)S(1)} %broadcast_in_dim.17.bias_ref), custom_call_target="tpu_custom_call" | custom-call | tf_op jit(solution)/shard_map/pallas_call | solution.py:82
  20.1 5.4 %all-to-all-done = bf16[32,2,8,352]{3,2,1,0:T(8,128)(2,1)S(1)} async-done(((bf16[32,2,8,352]{3,2,1,0:T(8,128)(2,1)}), bf16[32,2,8,352]{3,2,1,0:T(8,128)(2,1)S(1)}, u32[]{:S(2)}, u32[]{:S(2)}) %all-to-all-start) | async-done | bytes 360480 | tf_op jit(solution)/shard_map/all_to_all | solution.py:396
  25.5 5.9 %shard_map.106 = (bf16[3,352,512]{2,1,0:T(8,128)(2,1)S(1)}, bf16[1,352,512]{2,1,0:T(8,128)(2,1)}, bf16[2,352,512]{2,1,0:T(8,128)(2,1)}) custom-call(bf16[512,352]{1,0:T(8,128)(2,1)S(1)} %bitcast.57, bf16[512,352]{1,0:T(8,128)(2,1)S(1)} %bitcast.58, bf16[512,352]{1,0:T(8,128)(2,1)S(1)} %bitcast.59, bf16[512,352]{1,0:T(8,128)(2,1)S(1)} %bitcast.53), custom_call_target="tpu_custom_call" | custom-call | tf_op jit(solution)/shard_map/pallas_call | solution.py:54
  31.5 0.1 collective-permute-start.3
  31.6 2.7 %all-to-all-start.1 = ((bf16[32,16,352]{2,1,0:T(8,128)(2,1)}), bf16[32,16,352]{2,1,0:T(8,128)(2,1)S(1)}, u32[]{:S(2)}, u32[]{:S(2)}) async-start(bf16[32,16,352]{2,1,0:T(8,128)(2,1)} %shard_map.104), calls=%async_computation.1 | async-start | bytes 786432 | tf_op jit(solution)/shard_map/all_to_all | solution.py:403
  34.3 1.8 %collective-permute-start.1 = (bf16[2,352,512]{2,1,0:T(8,128)(2,1)}, bf16[2,352,512]{2,1,0:T(8,128)(2,1)}, u32[]{:S(2)}, u32[]{:S(2)}) collective-permute-start(bf16[2,352,512]{2,1,0:T(8,128)(2,1)} %get-tuple-element.30), channel_id=1, source_target_pairs={{0,4},{4,0},{8,12},{12,8},{16,20},{20,16},{24,28},{28,24},{1,5},{5... | collective-permute-start | bytes 2162696 | tf_op jit(solution)/shard_map/ppermute | solution.py:388
  36.1 5.7 %shard_map.108 = (bf16[8,16,1408]{2,1,0:T(8,128)(2,1)S(1)}, f32[8,16,1408]{2,1,0:T(8,128)}) custom-call(s32[1]{0:T(128)} %bitcast.16.where_ref, bf16[3,352,512]{2,1,0:T(8,128)(2,1)S(1)} %get-tuple-element.31.refs_0_, bf16[3,352,512]{2,1,0:T(8,128)(2,1)S(1)} %collective-permute-done.3.refs_1_, bf16[3,1408,704]{2,1,0:T(8,128)(2,1)} %shard_map.105.refs_2_), custom_call_target="tpu_custom_call" | custom-call | tf_op jit(solution)/shard_map/pallas_call | solution.py:179
  41.8 1.5 %collective-permute-start.4 = (bf16[8,16,1408]{2,1,0:T(8,128)(2,1)S(1)}, bf16[8,16,1408]{2,1,0:T(8,128)(2,1)S(1)}, u32[]{:S(2)}, u32[]{:S(2)}) collective-permute-start(bf16[8,16,1408]{2,1,0:T(8,128)(2,1)S(1)} %get-tuple-element.34), channel_id=1, source_target_pairs={{0,2},{1,3},{2,0},{3,1},{4,6},{5,7},{6,4},{7,5},{8,10},{9,11},{10,... | collective-permute-start | bytes 1081352 | tf_op jit(solution)/shard_map/ppermute | solution.py:388
  43.4 4.1 %all-to-all-done.1 = bf16[32,16,352]{2,1,0:T(8,128)(2,1)S(1)} async-done(((bf16[32,16,352]{2,1,0:T(8,128)(2,1)}), bf16[32,16,352]{2,1,0:T(8,128)(2,1)S(1)}, u32[]{:S(2)}, u32[]{:S(2)}) %all-to-all-start.1) | async-done | bytes 360480 | tf_op jit(solution)/shard_map/all_to_all | solution.py:403
  47.5 0.5 collective-permute-start.2
  48.0 1.5 %collective-permute-start = (bf16[1,352,512]{2,1,0:T(8,128)(2,1)}, bf16[1,352,512]{2,1,0:T(8,128)(2,1)}, u32[]{:S(2)}, u32[]{:S(2)}) collective-permute-start(bf16[1,352,512]{2,1,0:T(8,128)(2,1)} %get-tuple-element.29), channel_id=1, source_target_pairs={{0,4},{4,0},{8,12},{12,8},{16,20},{20,16},{24,28},{28,24},{1,5},{5... | collective-permute-start | bytes 1081352 | tf_op jit(solution)/shard_map/ppermute | solution.py:388
  49.5 4.0 %collective-permute-done.4.come_ref = bf16[8,16,1408]{2,1,0:T(8,128)(2,1)S(1)} collective-permute-done((bf16[8,16,1408]{2,1,0:T(8,128)(2,1)S(1)}, bf16[8,16,1408]{2,1,0:T(8,128)(2,1)S(1)}, u32[]{:S(2)}, u32[]{:S(2)}) %collective-permute-start.4) | collective-permute-done | bytes 360480 | tf_op jit(solution)/shard_map/ppermute | solution.py:388
  53.4 1.2 %shard_map.109 = bf16[8,16,1408]{2,1,0:T(8,128)(2,1)S(1)} custom-call(f32[8,16,1408]{2,1,0:T(8,128)} %get-tuple-element.33.stay_hbm, bf16[8,16,1408]{2,1,0:T(8,128)(2,1)S(1)} %collective-permute-done.4.come_ref), custom_call_target="tpu_custom_call" | custom-call | tf_op jit(solution)/shard_map/pallas_call | solution.py:414
  54.7 2.2 %collective-permute-start.5 = (bf16[2,16,1408]{2,1,0:T(8,128)(2,1)S(1)}, bf16[2,16,1408]{2,1,0:T(8,128)(2,1)}, u32[]{:S(2)}, u32[]{:S(2)}) collective-permute-start(bf16[2,16,1408]{2,1,0:T(8,128)(2,1)S(1)} %get-tuple-element.57), channel_id=1, source_target_pairs={{0,16},{4,20},{8,24},{12,28},{16,0},{20,4},{24,8},{28,12},{1,17},{... | collective-permute-start | bytes 270344 | tf_op jit(solution)/shard_map/ppermute | solution.py:388
  56.9 1.9 %collective-permute-start.6 = (bf16[2,16,1408]{2,1,0:T(8,128)(2,1)S(1)}, bf16[2,16,1408]{2,1,0:T(8,128)(2,1)}, u32[]{:S(2)}, u32[]{:S(2)}) collective-permute-start(bf16[2,16,1408]{2,1,0:T(8,128)(2,1)S(1)} %get-tuple-element.56), channel_id=1, source_target_pairs={{0,24},{4,28},{8,16},{12,20},{16,8},{20,12},{24,0},{28,4},{1,25},{... | collective-permute-start | bytes 270344 | tf_op jit(solution)/shard_map/ppermute | solution.py:388
  58.7 2.5 %collective-permute-done.2.theirs_ref = bf16[512,352]{1,0:T(8,128)(2,1)} collective-permute-done((bf16[512,352]{1,0:T(8,128)(2,1)S(1)}, bf16[512,352]{1,0:T(8,128)(2,1)}, u32[]{:S(2)}, u32[]{:S(2)}) %collective-permute-start.2) | collective-permute-done | bytes 360480 | tf_op jit(solution)/shard_map/ppermute | solution.py:388
  61.3 3.1 %shard_map.107.acc_ref = f32[2112,352]{1,0:T(8,128)S(1)} custom-call(s32[1]{0:T(128)} %bitcast.1.chip_ref, bf16[512,352]{1,0:T(8,128)(2,1)} %bitcast.63, bf16[512,352]{1,0:T(8,128)(2,1)} %collective-permute-done.2.theirs_ref, bf16[3,352,512]{2,1,0:T(8,128)(2,1)} %copy-done, bf16[3,352,512]{2,1,0:T(8,128)(2,1)} %copy-done.1), custom_call_target="tpu_custom_call" | custom-call | tf_op jit(solution)/shard_map/pallas_call | solution.py:222
  64.4 0.3 collective-permute-done.refs_0_
  64.7 0.1 collective-permute-start.8
  64.8 0.5 collective-permute-start.7
  65.3 1.7 %collective-permute-start.9 = (bf16[2,16,1408]{2,1,0:T(8,128)(2,1)S(1)}, bf16[2,16,1408]{2,1,0:T(8,128)(2,1)S(1)}, u32[]{:S(2)}, u32[]{:S(2)}) collective-permute-start(bf16[2,16,1408]{2,1,0:T(8,128)(2,1)S(1)} %get-tuple-element.54), channel_id=1, source_target_pairs={{0,8},{4,12},{8,0},{12,4},{16,24},{20,28},{24,16},{28,20},{1,9},{5... | collective-permute-start | bytes 270344 | tf_op jit(solution)/shard_map/ppermute | solution.py:388
  66.9 0.1 pad_add_fusion.chip_ref
  67.0 0.8 collective-permute-done.7.refs_2_
  67.8 3.9 %shard_map.110 = bf16[8,726,128]{2,1,0:T(8,128)(2,1)S(1)} custom-call(s32[2]{0:T(128)S(1)} %pad_add_fusion.chip_ref, bf16[512,352]{1,0:T(8,128)(2,1)} %bitcast.64, bf16[512,352]{1,0:T(8,128)(2,1)} %collective-permute-done.2.theirs_ref, f32[2112,352]{1,0:T(8,128)S(1)} %shard_map.107.acc_ref, bf16[1,352,512]{2,1,0:T(8,128)(2,1)} %collective-permute-done.refs_0_, ...), custom_call_target="tpu_custom_call" | custom-call | tf_op jit(solution)/shard_map/pallas_call | solution.py:270
  71.8 0.7 slice_bitcast_fusion.2
  72.5 1.7 %collective-permute-start.12 = (bf16[2,726,128]{2,1,0:T(8,128)(2,1)S(1)}, bf16[2,726,128]{2,1,0:T(8,128)(2,1)S(1)}, u32[]{:S(2)}, u32[]{:S(2)}) collective-permute-start(bf16[2,726,128]{2,1,0:T(8,128)(2,1)S(1)} %slice.27), channel_id=1, source_target_pairs={{0,8},{1,9},{2,10},{3,11},{4,12},{5,13},{6,14},{7,15},{8,0},{9,1},... | collective-permute-start | bytes 1115144 | tf_op jit(solution)/shard_map/ppermute | solution.py:438
  74.2 0.4 collective-permute-start.11
  74.5 1.5 %collective-permute-start.14 = (bf16[726,128]{1,0:T(8,128)(2,1)S(1)}, bf16[726,128]{1,0:T(8,128)(2,1)S(1)}, u32[]{:S(2)}, u32[]{:S(2)}) collective-permute-start(bf16[726,128]{1,0:T(8,128)(2,1)S(1)} %get-tuple-element.47), channel_id=1, source_target_pairs={{0,2},{1,3},{2,0},{3,1},{4,6},{5,7},{6,4},{7,5},{8,10},{9,11},{10,... | collective-permute-start | bytes 557576 | tf_op jit(solution)/shard_map/ppermute | solution.py:438
  76.0 1.7 %collective-permute-start.15 = (bf16[726,128]{1,0:T(8,128)(2,1)S(1)}, bf16[726,128]{1,0:T(8,128)(2,1)S(1)}, u32[]{:S(2)}, u32[]{:S(2)}) collective-permute-start(bf16[726,128]{1,0:T(8,128)(2,1)S(1)} %get-tuple-element.46), channel_id=1, source_target_pairs={{0,10},{1,11},{2,8},{3,9},{4,14},{5,15},{6,12},{7,13},{8,2},{9,3},... | collective-permute-start | bytes 557576 | tf_op jit(solution)/shard_map/ppermute | solution.py:438
  77.7 1.0 pad_maximum_fusion
  78.7 0.9 collective-permute-start.10
  79.6 4.4 %collective-permute-done.12 = bf16[2,726,128]{2,1,0:T(8,128)(2,1)S(1)} collective-permute-done((bf16[2,726,128]{2,1,0:T(8,128)(2,1)S(1)}, bf16[2,726,128]{2,1,0:T(8,128)(2,1)S(1)}, u32[]{:S(2)}, u32[]{:S(2)}) %collective-permute-start.12) | collective-permute-done | bytes 371744 | tf_op jit(solution)/shard_map/ppermute | solution.py:438
  84.0 0.1 add_convert_fusion
  84.2 2.5 %collective-permute-start.13 = (bf16[726,128]{1,0:T(8,128)(2,1)S(1)}, bf16[726,128]{1,0:T(8,128)(2,1)S(1)}, u32[]{:S(2)}, u32[]{:S(2)}) collective-permute-start(bf16[726,128]{1,0:T(8,128)(2,1)S(1)} %get-tuple-element.51), channel_id=1, source_target_pairs={{0,16},{1,17},{2,18},{3,19},{4,20},{5,21},{6,22},{7,23},{8,24},{9,... | collective-permute-start | bytes 557576 | tf_op jit(solution)/shard_map/ppermute | solution.py:438
  86.7 1.4 %collective-permute-start.16 = (bf16[726,128]{1,0:T(8,128)(2,1)S(1)}, bf16[726,128]{1,0:T(8,128)(2,1)S(1)}, u32[]{:S(2)}, u32[]{:S(2)}) collective-permute-start(bf16[726,128]{1,0:T(8,128)(2,1)S(1)} %get-tuple-element.50), channel_id=1, source_target_pairs={{0,18},{1,19},{2,16},{3,17},{4,22},{5,23},{6,20},{7,21},{8,26},{9,... | collective-permute-start | bytes 557576 | tf_op jit(solution)/shard_map/ppermute | solution.py:438
  88.1 0.1 pad_add_fusion.1.place_ref
  88.2 1.3 %shard_map.111 = bf16[128,1408]{1,0:T(8,128)(2,1)} custom-call(s32[1]{0:T(128)} %bitcast.tm_ref, bf16[4,16,1408]{2,1,0:T(8,128)(2,1)S(1)} %get-tuple-element.53.stay_ref, bf16[4,16,1408]{2,1,0:T(8,128)(2,1)S(1)} %collective-permute-done.10.come_ref, bf16[128,1408]{1,0:T(8,128)(2,1)S(1)} %bitcast.55, bf16[128,1408]{1,0:T(8,128)(2,1)S(1)} %bitcast.61, ...), custom_call_target="tpu_custom_call" | custom-call | tf_op jit(solution)/shard_map/pallas_call | solution.py:315
  89.5 5.0 %collective-permute-done.11.refs_1_ = bf16[726,128]{1,0:T(8,128)(2,1)S(1)} collective-permute-done((bf16[726,128]{1,0:T(8,128)(2,1)}, bf16[726,128]{1,0:T(8,128)(2,1)S(1)}, u32[]{:S(2)}, u32[]{:S(2)}) %collective-permute-start.11) | collective-permute-done | bytes 185888 | tf_op jit(solution)/shard_map/ppermute | solution.py:438
  94.5 4.3 %collective-permute-done.15.refs_4_ = bf16[726,128]{1,0:T(8,128)(2,1)S(1)} collective-permute-done((bf16[726,128]{1,0:T(8,128)(2,1)S(1)}, bf16[726,128]{1,0:T(8,128)(2,1)S(1)}, u32[]{:S(2)}, u32[]{:S(2)}) %collective-permute-start.15) | collective-permute-done | bytes 185888 | tf_op jit(solution)/shard_map/ppermute | solution.py:438
  98.8 4.4 %collective-permute-done.16.refs_5_ = bf16[726,128]{1,0:T(8,128)(2,1)S(1)} collective-permute-done((bf16[726,128]{1,0:T(8,128)(2,1)S(1)}, bf16[726,128]{1,0:T(8,128)(2,1)S(1)}, u32[]{:S(2)}, u32[]{:S(2)}) %collective-permute-start.16) | collective-permute-done | bytes 185888 | tf_op jit(solution)/shard_map/ppermute | solution.py:438
  103.3 2.0 %shard_map.112 = f32[44,4224]{1,0:T(8,128)} custom-call(s32[2]{0:T(128)S(1)} %pad_add_fusion.1.place_ref, bf16[726,128]{1,0:T(8,128)(2,1)S(1)} %get-tuple-element.49.refs_0_, bf16[726,128]{1,0:T(8,128)(2,1)S(1)} %collective-permute-done.11.refs_1_, bf16[726,128]{1,0:T(8,128)(2,1)S(1)} %collective-permute-done.13.refs_2_, ...), custom_call_target="tpu_custom_call" | custom-call | tf_op jit(solution)/shard_map/pallas_call | solution.py:358
  (35 shorter events, 0.2 us)
Async XLA Ops:
  0.6 11.7 %copy-start.9 = (f32[1408]{0:T(1024)S(1)}, f32[1408]{0:T(1024)}, u32[]{:S(2)}) copy-start(f32[1408]{0:T(1024)} %param.10) | copy-start | bytes 16900
  0.6 11.8 %copy-start.10 = (f32[1408]{0:T(1024)S(1)}, f32[1408]{0:T(1024)}, u32[]{:S(2)}) copy-start(f32[1408]{0:T(1024)} %param.11) | copy-start | bytes 16900
  5.1 20.5 %all-to-all-start = ((bf16[32,2,8,352]{3,2,1,0:T(8,128)(2,1)}), bf16[32,2,8,352]{3,2,1,0:T(8,128)(2,1)S(1)}, u32[]{:S(2)}, u32[]{:S(2)}) async-start(bf16[32,2,8,352]{3,2,1,0:T(8,128)(2,1)} %bitcast.10), calls=%async_computation | async-start | bytes 786432 | tf_op jit(solution)/shard_map/all_to_all | solution.py:396
  12.4 6.3 %copy-start.2 = (bf16[2,64,1408]{2,1,0:T(8,128)(2,1)S(1)}, bf16[2,64,1408]{2,1,0:T(8,128)(2,1)}, u32[]{:S(2)}) copy-start(bf16[2,64,1408]{2,1,0:T(8,128)(2,1)} %param.9) | copy-start | bytes 1081348
  12.4 13.1 %copy-start.4 = (bf16[64,8,352]{2,1,0:T(8,128)(2,1)S(1)}, bf16[64,8,352]{2,1,0:T(8,128)(2,1)}, u32[]{:S(2)}) copy-start(bf16[64,8,352]{2,1,0:T(8,128)(2,1)} %param.14) | copy-start | bytes 1081348
  12.5 13.1 %copy-start.5 = (bf16[64,8,352]{2,1,0:T(8,128)(2,1)S(1)}, bf16[64,8,352]{2,1,0:T(8,128)(2,1)}, u32[]{:S(2)}) copy-start(bf16[64,8,352]{2,1,0:T(8,128)(2,1)} %param.15) | copy-start | bytes 1081348
  12.5 13.1 %copy-start.6 = (bf16[64,8,352]{2,1,0:T(8,128)(2,1)S(1)}, bf16[64,8,352]{2,1,0:T(8,128)(2,1)}, u32[]{:S(2)}) copy-start(bf16[64,8,352]{2,1,0:T(8,128)(2,1)} %param.16) | copy-start | bytes 1081348
  31.5 10.3 %copy-start = (bf16[3,352,512]{2,1,0:T(8,128)(2,1)}, bf16[3,352,512]{2,1,0:T(8,128)(2,1)S(1)}, u32[]{:S(2)}) copy-start(bf16[3,352,512]{2,1,0:T(8,128)(2,1)S(1)} %get-tuple-element.31.refs_0_) | copy-start | bytes 3244036
  31.5 4.7 %collective-permute-start.3 = (bf16[3,352,512]{2,1,0:T(8,128)(2,1)S(1)}, bf16[3,352,512]{2,1,0:T(8,128)(2,1)S(1)}, u32[]{:S(2)}, u32[]{:S(2)}) collective-permute-start(bf16[3,352,512]{2,1,0:T(8,128)(2,1)S(1)} %get-tuple-element.31.refs_0_), channel_id=1, source_target_pairs={{0,1},{1,0},{2,3},{3,2},{4,5},{5,4},{6,7},{7,6},{8,9},{9,8},{10,11... | collective-permute-start | bytes 3244040 | tf_op jit(solution)/shard_map/ppermute | solution.py:388
  31.6 15.9 %all-to-all-start.1 = ((bf16[32,16,352]{2,1,0:T(8,128)(2,1)}), bf16[32,16,352]{2,1,0:T(8,128)(2,1)S(1)}, u32[]{:S(2)}, u32[]{:S(2)}) async-start(bf16[32,16,352]{2,1,0:T(8,128)(2,1)} %shard_map.104), calls=%async_computation.1 | async-start | bytes 786432 | tf_op jit(solution)/shard_map/all_to_all | solution.py:403
  34.3 30.4 %collective-permute-start.1 = (bf16[2,352,512]{2,1,0:T(8,128)(2,1)}, bf16[2,352,512]{2,1,0:T(8,128)(2,1)}, u32[]{:S(2)}, u32[]{:S(2)}) collective-permute-start(bf16[2,352,512]{2,1,0:T(8,128)(2,1)} %get-tuple-element.30), channel_id=1, source_target_pairs={{0,4},{4,0},{8,12},{12,8},{16,20},{20,16},{24,28},{28,24},{1,5},{5... | collective-permute-start | bytes 2162696 | tf_op jit(solution)/shard_map/ppermute | solution.py:388
  36.1 5.7 %copy-start.1 = (bf16[3,352,512]{2,1,0:T(8,128)(2,1)}, bf16[3,352,512]{2,1,0:T(8,128)(2,1)S(1)}, u32[]{:S(2)}) copy-start(bf16[3,352,512]{2,1,0:T(8,128)(2,1)S(1)} %collective-permute-done.3.refs_1_) | copy-start | bytes 3244036
  41.8 11.6 %collective-permute-start.4 = (bf16[8,16,1408]{2,1,0:T(8,128)(2,1)S(1)}, bf16[8,16,1408]{2,1,0:T(8,128)(2,1)S(1)}, u32[]{:S(2)}, u32[]{:S(2)}) collective-permute-start(bf16[8,16,1408]{2,1,0:T(8,128)(2,1)S(1)} %get-tuple-element.34), channel_id=1, source_target_pairs={{0,2},{1,3},{2,0},{3,1},{4,6},{5,7},{6,4},{7,5},{8,10},{9,11},{10,... | collective-permute-start | bytes 1081352 | tf_op jit(solution)/shard_map/ppermute | solution.py:388
  47.5 11.2 %copy-start.8 = (bf16[32,16,352]{2,1,0:T(8,128)(2,1)}, bf16[32,16,352]{2,1,0:T(8,128)(2,1)S(1)}, u32[]{:S(2)}) copy-start(bf16[32,16,352]{2,1,0:T(8,128)(2,1)S(1)} %all-to-all-done.1) | copy-start | bytes 1081348
  47.5 13.8 %collective-permute-start.2 = (bf16[512,352]{1,0:T(8,128)(2,1)S(1)}, bf16[512,352]{1,0:T(8,128)(2,1)}, u32[]{:S(2)}, u32[]{:S(2)}) collective-permute-start(bf16[512,352]{1,0:T(8,128)(2,1)S(1)} %bitcast.62), channel_id=1, source_target_pairs={{0,2},{1,3},{2,0},{3,1},{4,6},{5,7},{6,4},{7,5},{8,10},{9,11},{10,... | collective-permute-start | bytes 1081352 | tf_op jit(solution)/shard_map/ppermute | solution.py:388
  48.0 16.7 %collective-permute-start = (bf16[1,352,512]{2,1,0:T(8,128)(2,1)}, bf16[1,352,512]{2,1,0:T(8,128)(2,1)}, u32[]{:S(2)}, u32[]{:S(2)}) collective-permute-start(bf16[1,352,512]{2,1,0:T(8,128)(2,1)} %get-tuple-element.29), channel_id=1, source_target_pairs={{0,4},{4,0},{8,12},{12,8},{16,20},{20,16},{24,28},{28,24},{1,5},{5... | collective-permute-start | bytes 1081352 | tf_op jit(solution)/shard_map/ppermute | solution.py:388
  54.7 10.0 %collective-permute-start.5 = (bf16[2,16,1408]{2,1,0:T(8,128)(2,1)S(1)}, bf16[2,16,1408]{2,1,0:T(8,128)(2,1)}, u32[]{:S(2)}, u32[]{:S(2)}) collective-permute-start(bf16[2,16,1408]{2,1,0:T(8,128)(2,1)S(1)} %get-tuple-element.57), channel_id=1, source_target_pairs={{0,16},{4,20},{8,24},{12,28},{16,0},{20,4},{24,8},{28,12},{1,17},{... | collective-permute-start | bytes 270344 | tf_op jit(solution)/shard_map/ppermute | solution.py:388
  56.9 7.8 %collective-permute-start.6 = (bf16[2,16,1408]{2,1,0:T(8,128)(2,1)S(1)}, bf16[2,16,1408]{2,1,0:T(8,128)(2,1)}, u32[]{:S(2)}, u32[]{:S(2)}) collective-permute-start(bf16[2,16,1408]{2,1,0:T(8,128)(2,1)S(1)} %get-tuple-element.56), channel_id=1, source_target_pairs={{0,24},{4,28},{8,16},{12,20},{16,8},{20,12},{24,0},{28,4},{1,25},{... | collective-permute-start | bytes 270344 | tf_op jit(solution)/shard_map/ppermute | solution.py:388
  64.7 3.1 %collective-permute-start.8 = (bf16[2,352,512]{2,1,0:T(8,128)(2,1)}, bf16[2,352,512]{2,1,0:T(8,128)(2,1)}, u32[]{:S(2)}, u32[]{:S(2)}) collective-permute-start(bf16[2,352,512]{2,1,0:T(8,128)(2,1)} %collective-permute-done.1.refs_1_), channel_id=1, source_target_pairs={{0,1},{1,0},{2,3},{3,2},{4,5},{5,4},{6,7},{7,6},{8,9},{9,8},{10,11... | collective-permute-start | bytes 2162696 | tf_op jit(solution)/shard_map/ppermute | solution.py:388
  64.8 3.0 %collective-permute-start.7 = (bf16[1,352,512]{2,1,0:T(8,128)(2,1)}, bf16[1,352,512]{2,1,0:T(8,128)(2,1)}, u32[]{:S(2)}, u32[]{:S(2)}) collective-permute-start(bf16[1,352,512]{2,1,0:T(8,128)(2,1)} %collective-permute-done.refs_0_), channel_id=1, source_target_pairs={{0,1},{1,0},{2,3},{3,2},{4,5},{5,4},{6,7},{7,6},{8,9},{9,8},{10,11... | collective-permute-start | bytes 1081352 | tf_op jit(solution)/shard_map/ppermute | solution.py:388
  65.3 6.5 %collective-permute-start.9 = (bf16[2,16,1408]{2,1,0:T(8,128)(2,1)S(1)}, bf16[2,16,1408]{2,1,0:T(8,128)(2,1)S(1)}, u32[]{:S(2)}, u32[]{:S(2)}) collective-permute-start(bf16[2,16,1408]{2,1,0:T(8,128)(2,1)S(1)} %get-tuple-element.54), channel_id=1, source_target_pairs={{0,8},{4,12},{8,0},{12,4},{16,24},{20,28},{24,16},{28,20},{1,9},{5... | collective-permute-start | bytes 270344 | tf_op jit(solution)/shard_map/ppermute | solution.py:388
  71.7 16.4 %copy-start.3 = (bf16[2,64,1408]{2,1,0:T(8,128)(2,1)S(1)}, bf16[2,64,1408]{2,1,0:T(8,128)(2,1)}, u32[]{:S(2)}) copy-start(bf16[2,64,1408]{2,1,0:T(8,128)(2,1)} %param.9) | copy-start | bytes 1081348
  71.7 16.4 %copy-start.7 = (bf16[2,64,1408]{2,1,0:T(8,128)(2,1)S(1)}, bf16[2,64,1408]{2,1,0:T(8,128)(2,1)}, u32[]{:S(2)}) copy-start(bf16[2,64,1408]{2,1,0:T(8,128)(2,1)} %param.17) | copy-start | bytes 1081348
  72.5 11.5 %collective-permute-start.12 = (bf16[2,726,128]{2,1,0:T(8,128)(2,1)S(1)}, bf16[2,726,128]{2,1,0:T(8,128)(2,1)S(1)}, u32[]{:S(2)}, u32[]{:S(2)}) collective-permute-start(bf16[2,726,128]{2,1,0:T(8,128)(2,1)S(1)} %slice.27), channel_id=1, source_target_pairs={{0,8},{1,9},{2,10},{3,11},{4,12},{5,13},{6,14},{7,15},{8,0},{9,1},... | collective-permute-start | bytes 1115144 | tf_op jit(solution)/shard_map/ppermute | solution.py:438
  74.2 20.3 %collective-permute-start.11 = (bf16[726,128]{1,0:T(8,128)(2,1)}, bf16[726,128]{1,0:T(8,128)(2,1)S(1)}, u32[]{:S(2)}, u32[]{:S(2)}) collective-permute-start(bf16[726,128]{1,0:T(8,128)(2,1)} %get-tuple-element.48), channel_id=1, source_target_pairs={{0,8},{1,9},{2,10},{3,11},{4,12},{5,13},{6,14},{7,15},{8,0},{9,1},... | collective-permute-start | bytes 557576 | tf_op jit(solution)/shard_map/ppermute | solution.py:438
  74.5 20.0 %collective-permute-start.14 = (bf16[726,128]{1,0:T(8,128)(2,1)S(1)}, bf16[726,128]{1,0:T(8,128)(2,1)S(1)}, u32[]{:S(2)}, u32[]{:S(2)}) collective-permute-start(bf16[726,128]{1,0:T(8,128)(2,1)S(1)} %get-tuple-element.47), channel_id=1, source_target_pairs={{0,2},{1,3},{2,0},{3,1},{4,6},{5,7},{6,4},{7,5},{8,10},{9,11},{10,... | collective-permute-start | bytes 557576 | tf_op jit(solution)/shard_map/ppermute | solution.py:438
  76.0 22.8 %collective-permute-start.15 = (bf16[726,128]{1,0:T(8,128)(2,1)S(1)}, bf16[726,128]{1,0:T(8,128)(2,1)S(1)}, u32[]{:S(2)}, u32[]{:S(2)}) collective-permute-start(bf16[726,128]{1,0:T(8,128)(2,1)S(1)} %get-tuple-element.46), channel_id=1, source_target_pairs={{0,10},{1,11},{2,8},{3,9},{4,14},{5,15},{6,12},{7,13},{8,2},{9,3},... | collective-permute-start | bytes 557576 | tf_op jit(solution)/shard_map/ppermute | solution.py:438
  78.7 8.0 %collective-permute-start.10 = (bf16[4,16,1408]{2,1,0:T(8,128)(2,1)S(1)}, bf16[4,16,1408]{2,1,0:T(8,128)(2,1)S(1)}, u32[]{:S(2)}, u32[]{:S(2)}) collective-permute-start(bf16[4,16,1408]{2,1,0:T(8,128)(2,1)S(1)} %get-tuple-element.52), channel_id=1, source_target_pairs={{0,4},{4,0},{8,12},{12,8},{16,20},{20,16},{24,28},{28,24},{1,5},{5... | collective-permute-start | bytes 540680 | tf_op jit(solution)/shard_map/ppermute | solution.py:388
  84.2 14.7 %collective-permute-start.13 = (bf16[726,128]{1,0:T(8,128)(2,1)S(1)}, bf16[726,128]{1,0:T(8,128)(2,1)S(1)}, u32[]{:S(2)}, u32[]{:S(2)}) collective-permute-start(bf16[726,128]{1,0:T(8,128)(2,1)S(1)} %get-tuple-element.51), channel_id=1, source_target_pairs={{0,16},{1,17},{2,18},{3,19},{4,20},{5,21},{6,22},{7,23},{8,24},{9,... | collective-permute-start | bytes 557576 | tf_op jit(solution)/shard_map/ppermute | solution.py:438
  86.7 16.6 %collective-permute-start.16 = (bf16[726,128]{1,0:T(8,128)(2,1)S(1)}, bf16[726,128]{1,0:T(8,128)(2,1)S(1)}, u32[]{:S(2)}, u32[]{:S(2)}) collective-permute-start(bf16[726,128]{1,0:T(8,128)(2,1)S(1)} %get-tuple-element.50), channel_id=1, source_target_pairs={{0,18},{1,19},{2,16},{3,17},{4,22},{5,23},{6,20},{7,21},{8,26},{9,... | collective-permute-start | bytes 557576 | tf_op jit(solution)/shard_map/ppermute | solution.py:438

commit v13 on v12

--- a/solution.py
+++ b/solution.py
@@ -439,8 +439,9 @@
 
         passed = send(partial[6:8], 1, 0)
         summed = (partial[4:6].astype(F32) + passed.astype(F32)).astype(BF)
-        own_chip = [partial[0], send(partial[2], 1, 0), send(summed[0], 2, 0)]
-        other_chip = [send(partial[1], 0, 1), send(partial[3], 1, 1), send(summed[1], 2, 1)]
+        near, summed = lax.optimization_barrier((partial[2:4], summed))
+        own_chip = [partial[0], send(near[0], 1, 0), send(summed[0], 2, 0)]
+        other_chip = [send(partial[1], 0, 1), send(near[1], 1, 1), send(summed[1], 2, 1)]
         summands, first = own_chip + other_chip, patch // 2
     else:
         groups = [

time: 106 us -> 106 us (level)
  waiting for transfers between devices: 35.4 us -> 37.3 us
    ppermute x6, waiting for transfers between devices: 18.2 us -> 20.7 us  [send(): return lax.ppermute(values, both, [(i, i ^ flip) for i in range(devices)])]
  transfers between devices with their start and end apart: 19 -> 19, of which waited for: 10 -> 11; matrix products, arithmetic and copies ran while one was open for 1% -> 1% of each run, Pallas kernels for 22% -> 22%
where the time goes in v13:
time: 106 us
  waiting for transfers between devices  37.3 us (35%)
  starting transfers between devices  31.2 us (29%)
  Pallas kernels  30.7 us (29%)
  matrix products  3.38 us (3%)
  local copies, waits for them, and re-layouts  1.91 us (2%)
    ppermute x6, waiting for transfers between devices, send(): return lax.ppermute(values, both, [(i, i ^ flip) for i in range(devices)])  20.7 us
    ppermute x11, starting transfers between devices, swap(): return lax.ppermute(values, axis, [(i, i ^ bit) for i in range(size)])  12.2 us
    ppermute x6, starting transfers between devices, send(): return lax.ppermute(values, both, [(i, i ^ flip) for i in range(devices)])  8.97 us
    all_to_all x1, starting transfers between devices, per_device(): lax.all_to_all(d_attn.reshape(devices, t_dev, columns, part), both, 0, 0,...  7.29 us
    ppermute x11, waiting for transfers between devices, swap(): return lax.ppermute(values, axis, [(i, i ^ bit) for i in range(size)])  7.08 us
    pallas_call x1, Pallas kernels, own_weights(): pl.pallas_call(functools.partial(weights_kernel, n_chip=n_chip), grid_spe...  6.23 us
    pallas_call x1, Pallas kernels, attend(): pl.pallas_call(functools.partial(attend_kernel, columns=columns), out_spe...  5.92 us
    pallas_call x1, Pallas kernels, share_send(): pl.pallas_call(share_kernel, grid_spec=pltpu.PrefetchScalarGridSpec(num_s...  5.66 us
  transfers between devices with their start and end apart: 19, of which 11 were waited for; matrix products, arithmetic and copies ran while one was open for 1% of the time, Pallas kernels for 22%

profile of v13, /device:TPU:0, one launch (start us, length us, event | category | flops | bytes accessed | tf_op | source)
XLA Modules:
  0.0 105.8 jit_solution(10315869542342682244)
XLA Ops:
  0.7 3.4 %fusion = bf16[4,128,352]{1,2,0:T(8,128)(2,1)S(1)} fusion(bf16[4,352,1408]{2,1,0:T(8,128)(2,1)} %bitcast.71, bf16[128,1408,1]{1,0,2:T(8,128)(2,1)} %bitcast.60), kind=kOutput, calls=%fused_computation.1 | convolution fusion | flops 507691008 | bytes 4685824 | tf_op jit(solution)/shard_map/to,jfo->jtf/dot_general | solution.py:391
  4.0 0.2 copy.13
  4.3 0.8 copy.14
  5.1 7.3 %all-to-all-start = ((bf16[32,2,8,352]{3,2,1,0:T(8,128)(2,1)}), bf16[32,2,8,352]{3,2,1,0:T(8,128)(2,1)S(1)}, u32[]{:S(2)}, u32[]{:S(2)}) async-start(bf16[32,2,8,352]{3,2,1,0:T(8,128)(2,1)} %bitcast.10), calls=%async_computation | async-start | bytes 786432 | tf_op jit(solution)/shard_map/all_to_all | solution.py:396
  12.5 6.2 %shard_map.105.refs_2_ = bf16[3,1408,704]{2,1,0:T(8,128)(2,1)} custom-call(s32[1]{0:T(128)} %bitcast.1.chip_ref, bf16[1408,4224]{1,0:T(8,128)(2,1)} %w_ref), custom_call_target="tpu_custom_call" | custom-call | tf_op jit(solution)/shard_map/pallas_call | solution.py:114
  18.7 1.4 %shard_map.104 = bf16[32,16,352]{2,1,0:T(8,128)(2,1)} custom-call(bf16[128,1408]{1,0:T(8,128)(2,1)S(1)} %bitcast.54, f32[1,1408]{1,0:T(1,128)S(1)} %broadcast_in_dim.16.gain_ref, f32[1,1408]{1,0:T(1,128)S(1)} %broadcast_in_dim.17.bias_ref), custom_call_target="tpu_custom_call" | custom-call | tf_op jit(solution)/shard_map/pallas_call | solution.py:82
  20.1 5.4 %all-to-all-done = bf16[32,2,8,352]{3,2,1,0:T(8,128)(2,1)S(1)} async-done(((bf16[32,2,8,352]{3,2,1,0:T(8,128)(2,1)}), bf16[32,2,8,352]{3,2,1,0:T(8,128)(2,1)S(1)}, u32[]{:S(2)}, u32[]{:S(2)}) %all-to-all-start) | async-done | bytes 360480 | tf_op jit(solution)/shard_map/all_to_all | solution.py:396
  25.5 5.9 %shard_map.106 = (bf16[3,352,512]{2,1,0:T(8,128)(2,1)S(1)}, bf16[1,352,512]{2,1,0:T(8,128)(2,1)}, bf16[2,352,512]{2,1,0:T(8,128)(2,1)}) custom-call(bf16[512,352]{1,0:T(8,128)(2,1)S(1)} %bitcast.57, bf16[512,352]{1,0:T(8,128)(2,1)S(1)} %bitcast.58, bf16[512,352]{1,0:T(8,128)(2,1)S(1)} %bitcast.59, bf16[512,352]{1,0:T(8,128)(2,1)S(1)} %bitcast.53), custom_call_target="tpu_custom_call" | custom-call | tf_op jit(solution)/shard_map/pallas_call | solution.py:54
  31.5 0.1 collective-permute-start.3
  31.6 2.7 %all-to-all-start.1 = ((bf16[32,16,352]{2,1,0:T(8,128)(2,1)}), bf16[32,16,352]{2,1,0:T(8,128)(2,1)S(1)}, u32[]{:S(2)}, u32[]{:S(2)}) async-start(bf16[32,16,352]{2,1,0:T(8,128)(2,1)} %shard_map.104), calls=%async_computation.1 | async-start | bytes 786432 | tf_op jit(solution)/shard_map/all_to_all | solution.py:403
  34.3 1.8 %collective-permute-start.1 = (bf16[2,352,512]{2,1,0:T(8,128)(2,1)}, bf16[2,352,512]{2,1,0:T(8,128)(2,1)}, u32[]{:S(2)}, u32[]{:S(2)}) collective-permute-start(bf16[2,352,512]{2,1,0:T(8,128)(2,1)} %get-tuple-element.32), channel_id=1, source_target_pairs={{0,4},{4,0},{8,12},{12,8},{16,20},{20,16},{24,28},{28,24},{1,5},{5... | collective-permute-start | bytes 2162696 | tf_op jit(solution)/shard_map/ppermute | solution.py:388
  36.1 5.7 %shard_map.108 = (bf16[8,16,1408]{2,1,0:T(8,128)(2,1)S(1)}, f32[8,16,1408]{2,1,0:T(8,128)}) custom-call(s32[1]{0:T(128)} %bitcast.16.where_ref, bf16[3,352,512]{2,1,0:T(8,128)(2,1)S(1)} %get-tuple-element.33.refs_0_, bf16[3,352,512]{2,1,0:T(8,128)(2,1)S(1)} %collective-permute-done.3.refs_1_, bf16[3,1408,704]{2,1,0:T(8,128)(2,1)} %shard_map.105.refs_2_), custom_call_target="tpu_custom_call" | custom-call | tf_op jit(solution)/shard_map/pallas_call | solution.py:179
  41.8 1.5 %collective-permute-start.4 = (bf16[8,16,1408]{2,1,0:T(8,128)(2,1)S(1)}, bf16[8,16,1408]{2,1,0:T(8,128)(2,1)S(1)}, u32[]{:S(2)}, u32[]{:S(2)}) collective-permute-start(bf16[8,16,1408]{2,1,0:T(8,128)(2,1)S(1)} %get-tuple-element.36), channel_id=1, source_target_pairs={{0,2},{1,3},{2,0},{3,1},{4,6},{5,7},{6,4},{7,5},{8,10},{9,11},{10,... | collective-permute-start | bytes 1081352 | tf_op jit(solution)/shard_map/ppermute | solution.py:388
  43.4 4.1 %all-to-all-done.1 = bf16[32,16,352]{2,1,0:T(8,128)(2,1)S(1)} async-done(((bf16[32,16,352]{2,1,0:T(8,128)(2,1)}), bf16[32,16,352]{2,1,0:T(8,128)(2,1)S(1)}, u32[]{:S(2)}, u32[]{:S(2)}) %all-to-all-start.1) | async-done | bytes 360480 | tf_op jit(solution)/shard_map/all_to_all | solution.py:403
  47.5 0.5 collective-permute-start.2
  48.0 1.5 %collective-permute-start = (bf16[1,352,512]{2,1,0:T(8,128)(2,1)}, bf16[1,352,512]{2,1,0:T(8,128)(2,1)}, u32[]{:S(2)}, u32[]{:S(2)}) collective-permute-start(bf16[1,352,512]{2,1,0:T(8,128)(2,1)} %get-tuple-element.31), channel_id=1, source_target_pairs={{0,4},{4,0},{8,12},{12,8},{16,20},{20,16},{24,28},{28,24},{1,5},{5... | collective-permute-start | bytes 1081352 | tf_op jit(solution)/shard_map/ppermute | solution.py:388
  49.5 4.0 %collective-permute-done.4.come_ref = bf16[8,16,1408]{2,1,0:T(8,128)(2,1)S(1)} collective-permute-done((bf16[8,16,1408]{2,1,0:T(8,128)(2,1)S(1)}, bf16[8,16,1408]{2,1,0:T(8,128)(2,1)S(1)}, u32[]{:S(2)}, u32[]{:S(2)}) %collective-permute-start.4) | collective-permute-done | bytes 360480 | tf_op jit(solution)/shard_map/ppermute | solution.py:388
  53.4 1.2 %shard_map.109 = bf16[8,16,1408]{2,1,0:T(8,128)(2,1)S(1)} custom-call(f32[8,16,1408]{2,1,0:T(8,128)} %get-tuple-element.35.stay_hbm, bf16[8,16,1408]{2,1,0:T(8,128)(2,1)S(1)} %collective-permute-done.4.come_ref), custom_call_target="tpu_custom_call" | custom-call | tf_op jit(solution)/shard_map/pallas_call | solution.py:414
  54.6 0.7 dynamic-slice_bitcast_fusion.2
  55.3 2.1 %collective-permute-start.5 = (bf16[2,16,1408]{2,1,0:T(8,128)(2,1)S(1)}, bf16[2,16,1408]{2,1,0:T(8,128)(2,1)S(1)}, u32[]{:S(2)}, u32[]{:S(2)}) collective-permute-start(bf16[2,16,1408]{2,1,0:T(8,128)(2,1)S(1)} %get-tuple-element.63), channel_id=1, source_target_pairs={{0,16},{4,20},{8,24},{12,28},{16,0},{20,4},{24,8},{28,12},{1,17},{... | collective-permute-start | bytes 270344 | tf_op jit(solution)/shard_map/ppermute | solution.py:388
  57.4 1.9 %collective-permute-start.6 = (bf16[2,16,1408]{2,1,0:T(8,128)(2,1)S(1)}, bf16[2,16,1408]{2,1,0:T(8,128)(2,1)S(1)}, u32[]{:S(2)}, u32[]{:S(2)}) collective-permute-start(bf16[2,16,1408]{2,1,0:T(8,128)(2,1)S(1)} %get-tuple-element.62), channel_id=1, source_target_pairs={{0,24},{4,28},{8,16},{12,20},{16,8},{20,12},{24,0},{28,4},{1,25},{... | collective-permute-start | bytes 270344 | tf_op jit(solution)/shard_map/ppermute | solution.py:388
  59.3 2.0 %collective-permute-done.2.theirs_ref = bf16[512,352]{1,0:T(8,128)(2,1)} collective-permute-done((bf16[512,352]{1,0:T(8,128)(2,1)S(1)}, bf16[512,352]{1,0:T(8,128)(2,1)}, u32[]{:S(2)}, u32[]{:S(2)}) %collective-permute-start.2) | collective-permute-done | bytes 360480 | tf_op jit(solution)/shard_map/ppermute | solution.py:388
  61.3 3.1 %shard_map.107.acc_ref = f32[2112,352]{1,0:T(8,128)S(1)} custom-call(s32[1]{0:T(128)} %bitcast.1.chip_ref, bf16[512,352]{1,0:T(8,128)(2,1)} %bitcast.63, bf16[512,352]{1,0:T(8,128)(2,1)} %collective-permute-done.2.theirs_ref, bf16[3,352,512]{2,1,0:T(8,128)(2,1)} %copy-done, bf16[3,352,512]{2,1,0:T(8,128)(2,1)} %copy-done.1), custom_call_target="tpu_custom_call" | custom-call | tf_op jit(solution)/shard_map/pallas_call | solution.py:222
  64.4 0.3 collective-permute-done.refs_0_
  64.7 0.1 collective-permute-start.8
  64.8 0.5 collective-permute-start.7
  65.3 1.7 %collective-permute-start.9 = (bf16[2,16,1408]{2,1,0:T(8,128)(2,1)}, bf16[2,16,1408]{2,1,0:T(8,128)(2,1)S(1)}, u32[]{:S(2)}, u32[]{:S(2)}) collective-permute-start(bf16[2,16,1408]{2,1,0:T(8,128)(2,1)} %get-tuple-element.60), channel_id=1, source_target_pairs={{0,8},{4,12},{8,0},{12,4},{16,24},{20,28},{24,16},{28,20},{1,9},{5... | collective-permute-start | bytes 270344 | tf_op jit(solution)/shard_map/ppermute | solution.py:388
  66.9 0.1 pad_add_fusion.chip_ref
  67.0 0.8 collective-permute-done.7.refs_2_
  67.8 3.9 %shard_map.110 = bf16[8,726,128]{2,1,0:T(8,128)(2,1)S(1)} custom-call(s32[2]{0:T(128)S(1)} %pad_add_fusion.chip_ref, bf16[512,352]{1,0:T(8,128)(2,1)} %bitcast.64, bf16[512,352]{1,0:T(8,128)(2,1)} %collective-permute-done.2.theirs_ref, f32[2112,352]{1,0:T(8,128)S(1)} %shard_map.107.acc_ref, bf16[1,352,512]{2,1,0:T(8,128)(2,1)} %collective-permute-done.refs_0_, ...), custom_call_target="tpu_custom_call" | custom-call | tf_op jit(solution)/shard_map/pallas_call | solution.py:270
  71.8 0.1 fusion.1
  71.9 1.7 %collective-permute-start.11 = (bf16[2,726,128]{2,1,0:T(8,128)(2,1)S(1)}, bf16[2,726,128]{2,1,0:T(8,128)(2,1)S(1)}, u32[]{:S(2)}, u32[]{:S(2)}) collective-permute-start(bf16[2,726,128]{2,1,0:T(8,128)(2,1)S(1)} %get-tuple-element.52), channel_id=1, source_target_pairs={{0,8},{1,9},{2,10},{3,11},{4,12},{5,13},{6,14},{7,15},{8,0},{9,1},... | collective-permute-start | bytes 1115144 | tf_op jit(solution)/shard_map/ppermute | solution.py:438
  73.6 1.3 %collective-permute-start.14 = (bf16[726,128]{1,0:T(8,128)(2,1)S(1)}, bf16[726,128]{1,0:T(8,128)(2,1)S(1)}, u32[]{:S(2)}, u32[]{:S(2)}) collective-permute-start(bf16[726,128]{1,0:T(8,128)(2,1)S(1)} %get-tuple-element.50), channel_id=1, source_target_pairs={{0,2},{1,3},{2,0},{3,1},{4,6},{5,7},{6,4},{7,5},{8,10},{9,11},{10,... | collective-permute-start | bytes 557576 | tf_op jit(solution)/shard_map/ppermute | solution.py:438
  74.8 0.1 pad_maximum_fusion
  75.0 0.6 collective-permute-start.10
  75.6 7.1 %collective-permute-done.11 = bf16[2,726,128]{2,1,0:T(8,128)(2,1)S(1)} collective-permute-done((bf16[2,726,128]{2,1,0:T(8,128)(2,1)S(1)}, bf16[2,726,128]{2,1,0:T(8,128)(2,1)S(1)}, u32[]{:S(2)}, u32[]{:S(2)}) %collective-permute-start.11) | collective-permute-done | bytes 371744 | tf_op jit(solution)/shard_map/ppermute | solution.py:438
  82.6 0.1 add_convert_fusion
  82.8 1.7 %collective-permute-start.12 = (bf16[726,128]{1,0:T(8,128)(2,1)S(1)}, bf16[726,128]{1,0:T(8,128)(2,1)S(1)}, u32[]{:S(2)}, u32[]{:S(2)}) collective-permute-start(bf16[726,128]{1,0:T(8,128)(2,1)S(1)} %get-tuple-element.57), channel_id=1, source_target_pairs={{0,8},{1,9},{2,10},{3,11},{4,12},{5,13},{6,14},{7,15},{8,0},{9,1},... | collective-permute-start | bytes 557576 | tf_op jit(solution)/shard_map/ppermute | solution.py:438
  84.5 2.3 %collective-permute-start.13 = (bf16[726,128]{1,0:T(8,128)(2,1)S(1)}, bf16[726,128]{1,0:T(8,128)(2,1)S(1)}, u32[]{:S(2)}, u32[]{:S(2)}) collective-permute-start(bf16[726,128]{1,0:T(8,128)(2,1)S(1)} %get-tuple-element.55), channel_id=1, source_target_pairs={{0,16},{1,17},{2,18},{3,19},{4,20},{5,21},{6,22},{7,23},{8,24},{9,... | collective-permute-start | bytes 557576 | tf_op jit(solution)/shard_map/ppermute | solution.py:438
  86.9 1.4 %collective-permute-start.15 = (bf16[726,128]{1,0:T(8,128)(2,1)S(1)}, bf16[726,128]{1,0:T(8,128)(2,1)S(1)}, u32[]{:S(2)}, u32[]{:S(2)}) collective-permute-start(bf16[726,128]{1,0:T(8,128)(2,1)S(1)} %get-tuple-element.56), channel_id=1, source_target_pairs={{0,10},{1,11},{2,8},{3,9},{4,14},{5,15},{6,12},{7,13},{8,2},{9,3},... | collective-permute-start | bytes 557576 | tf_op jit(solution)/shard_map/ppermute | solution.py:438
  88.2 0.6 collective-permute-start.16
  88.8 0.1 pad_add_fusion.1.place_ref
  88.9 1.3 %shard_map.111 = bf16[128,1408]{1,0:T(8,128)(2,1)} custom-call(s32[1]{0:T(128)} %bitcast.tm_ref, bf16[4,16,1408]{2,1,0:T(8,128)(2,1)S(1)} %get-tuple-element.59.stay_ref, bf16[4,16,1408]{2,1,0:T(8,128)(2,1)S(1)} %collective-permute-done.10.come_ref, bf16[128,1408]{1,0:T(8,128)(2,1)S(1)} %bitcast.55, bf16[128,1408]{1,0:T(8,128)(2,1)S(1)} %bitcast.61, ...), custom_call_target="tpu_custom_call" | custom-call | tf_op jit(solution)/shard_map/pallas_call | solution.py:315
  90.2 4.2 %collective-permute-done.12.refs_1_ = bf16[726,128]{1,0:T(8,128)(2,1)S(1)} collective-permute-done((bf16[726,128]{1,0:T(8,128)(2,1)S(1)}, bf16[726,128]{1,0:T(8,128)(2,1)S(1)}, u32[]{:S(2)}, u32[]{:S(2)}) %collective-permute-start.12) | collective-permute-done | bytes 185888 | tf_op jit(solution)/shard_map/ppermute | solution.py:438
  94.4 2.4 %collective-permute-done.13.refs_2_ = bf16[726,128]{1,0:T(8,128)(2,1)S(1)} collective-permute-done((bf16[726,128]{1,0:T(8,128)(2,1)S(1)}, bf16[726,128]{1,0:T(8,128)(2,1)S(1)}, u32[]{:S(2)}, u32[]{:S(2)}) %collective-permute-start.13) | collective-permute-done | bytes 185888 | tf_op jit(solution)/shard_map/ppermute | solution.py:438
  96.8 4.5 %collective-permute-done.15.refs_4_ = bf16[726,128]{1,0:T(8,128)(2,1)S(1)} collective-permute-done((bf16[726,128]{1,0:T(8,128)(2,1)S(1)}, bf16[726,128]{1,0:T(8,128)(2,1)S(1)}, u32[]{:S(2)}, u32[]{:S(2)}) %collective-permute-start.15) | collective-permute-done | bytes 185888 | tf_op jit(solution)/shard_map/ppermute | solution.py:438
  101.3 2.5 %collective-permute-done.16.refs_5_ = bf16[726,128]{1,0:T(8,128)(2,1)S(1)} collective-permute-done((bf16[726,128]{1,0:T(8,128)(2,1)S(1)}, bf16[726,128]{1,0:T(8,128)(2,1)S(1)}, u32[]{:S(2)}, u32[]{:S(2)}) %collective-permute-start.16) | collective-permute-done | bytes 185888 | tf_op jit(solution)/shard_map/ppermute | solution.py:438
  103.8 2.0 %shard_map.112 = f32[44,4224]{1,0:T(8,128)} custom-call(s32[2]{0:T(128)S(1)} %pad_add_fusion.1.place_ref, bf16[726,128]{1,0:T(8,128)(2,1)S(1)} %get-tuple-element.51.refs_0_, bf16[726,128]{1,0:T(8,128)(2,1)S(1)} %collective-permute-done.12.refs_1_, bf16[726,128]{1,0:T(8,128)(2,1)S(1)} %collective-permute-done.13.refs_2_, ...), custom_call_target="tpu_custom_call" | custom-call | tf_op jit(solution)/shard_map/pallas_call | solution.py:358
  (36 shorter events, 0.2 us)
Async XLA Ops:
  0.6 11.7 %copy-start.9 = (f32[1408]{0:T(1024)S(1)}, f32[1408]{0:T(1024)}, u32[]{:S(2)}) copy-start(f32[1408]{0:T(1024)} %param.10) | copy-start | bytes 16900
  0.6 11.8 %copy-start.10 = (f32[1408]{0:T(1024)S(1)}, f32[1408]{0:T(1024)}, u32[]{:S(2)}) copy-start(f32[1408]{0:T(1024)} %param.11) | copy-start | bytes 16900
  5.1 20.5 %all-to-all-start = ((bf16[32,2,8,352]{3,2,1,0:T(8,128)(2,1)}), bf16[32,2,8,352]{3,2,1,0:T(8,128)(2,1)S(1)}, u32[]{:S(2)}, u32[]{:S(2)}) async-start(bf16[32,2,8,352]{3,2,1,0:T(8,128)(2,1)} %bitcast.10), calls=%async_computation | async-start | bytes 786432 | tf_op jit(solution)/shard_map/all_to_all | solution.py:396
  12.4 6.3 %copy-start.2 = (bf16[2,64,1408]{2,1,0:T(8,128)(2,1)S(1)}, bf16[2,64,1408]{2,1,0:T(8,128)(2,1)}, u32[]{:S(2)}) copy-start(bf16[2,64,1408]{2,1,0:T(8,128)(2,1)} %param.9) | copy-start | bytes 1081348
  12.4 13.1 %copy-start.4 = (bf16[64,8,352]{2,1,0:T(8,128)(2,1)S(1)}, bf16[64,8,352]{2,1,0:T(8,128)(2,1)}, u32[]{:S(2)}) copy-start(bf16[64,8,352]{2,1,0:T(8,128)(2,1)} %param.14) | copy-start | bytes 1081348
  12.5 13.1 %copy-start.5 = (bf16[64,8,352]{2,1,0:T(8,128)(2,1)S(1)}, bf16[64,8,352]{2,1,0:T(8,128)(2,1)}, u32[]{:S(2)}) copy-start(bf16[64,8,352]{2,1,0:T(8,128)(2,1)} %param.15) | copy-start | bytes 1081348
  12.5 13.1 %copy-start.6 = (bf16[64,8,352]{2,1,0:T(8,128)(2,1)S(1)}, bf16[64,8,352]{2,1,0:T(8,128)(2,1)}, u32[]{:S(2)}) copy-start(bf16[64,8,352]{2,1,0:T(8,128)(2,1)} %param.16) | copy-start | bytes 1081348
  31.5 10.3 %copy-start = (bf16[3,352,512]{2,1,0:T(8,128)(2,1)}, bf16[3,352,512]{2,1,0:T(8,128)(2,1)S(1)}, u32[]{:S(2)}) copy-start(bf16[3,352,512]{2,1,0:T(8,128)(2,1)S(1)} %get-tuple-element.33.refs_0_) | copy-start | bytes 3244036
  31.5 4.7 %collective-permute-start.3 = (bf16[3,352,512]{2,1,0:T(8,128)(2,1)S(1)}, bf16[3,352,512]{2,1,0:T(8,128)(2,1)S(1)}, u32[]{:S(2)}, u32[]{:S(2)}) collective-permute-start(bf16[3,352,512]{2,1,0:T(8,128)(2,1)S(1)} %get-tuple-element.33.refs_0_), channel_id=1, source_target_pairs={{0,1},{1,0},{2,3},{3,2},{4,5},{5,4},{6,7},{7,6},{8,9},{9,8},{10,11... | collective-permute-start | bytes 3244040 | tf_op jit(solution)/shard_map/ppermute | solution.py:388
  31.6 15.9 %all-to-all-start.1 = ((bf16[32,16,352]{2,1,0:T(8,128)(2,1)}), bf16[32,16,352]{2,1,0:T(8,128)(2,1)S(1)}, u32[]{:S(2)}, u32[]{:S(2)}) async-start(bf16[32,16,352]{2,1,0:T(8,128)(2,1)} %shard_map.104), calls=%async_computation.1 | async-start | bytes 786432 | tf_op jit(solution)/shard_map/all_to_all | solution.py:403
  34.3 30.4 %collective-permute-start.1 = (bf16[2,352,512]{2,1,0:T(8,128)(2,1)}, bf16[2,352,512]{2,1,0:T(8,128)(2,1)}, u32[]{:S(2)}, u32[]{:S(2)}) collective-permute-start(bf16[2,352,512]{2,1,0:T(8,128)(2,1)} %get-tuple-element.32), channel_id=1, source_target_pairs={{0,4},{4,0},{8,12},{12,8},{16,20},{20,16},{24,28},{28,24},{1,5},{5... | collective-permute-start | bytes 2162696 | tf_op jit(solution)/shard_map/ppermute | solution.py:388
  36.1 5.7 %copy-start.1 = (bf16[3,352,512]{2,1,0:T(8,128)(2,1)}, bf16[3,352,512]{2,1,0:T(8,128)(2,1)S(1)}, u32[]{:S(2)}) copy-start(bf16[3,352,512]{2,1,0:T(8,128)(2,1)S(1)} %collective-permute-done.3.refs_1_) | copy-start | bytes 3244036
  41.8 11.6 %collective-permute-start.4 = (bf16[8,16,1408]{2,1,0:T(8,128)(2,1)S(1)}, bf16[8,16,1408]{2,1,0:T(8,128)(2,1)S(1)}, u32[]{:S(2)}, u32[]{:S(2)}) collective-permute-start(bf16[8,16,1408]{2,1,0:T(8,128)(2,1)S(1)} %get-tuple-element.36), channel_id=1, source_target_pairs={{0,2},{1,3},{2,0},{3,1},{4,6},{5,7},{6,4},{7,5},{8,10},{9,11},{10,... | collective-permute-start | bytes 1081352 | tf_op jit(solution)/shard_map/ppermute | solution.py:388
  47.5 11.8 %copy-start.8 = (bf16[32,16,352]{2,1,0:T(8,128)(2,1)}, bf16[32,16,352]{2,1,0:T(8,128)(2,1)S(1)}, u32[]{:S(2)}) copy-start(bf16[32,16,352]{2,1,0:T(8,128)(2,1)S(1)} %all-to-all-done.1) | copy-start | bytes 1081348
  47.5 13.8 %collective-permute-start.2 = (bf16[512,352]{1,0:T(8,128)(2,1)S(1)}, bf16[512,352]{1,0:T(8,128)(2,1)}, u32[]{:S(2)}, u32[]{:S(2)}) collective-permute-start(bf16[512,352]{1,0:T(8,128)(2,1)S(1)} %bitcast.62), channel_id=1, source_target_pairs={{0,2},{1,3},{2,0},{3,1},{4,6},{5,7},{6,4},{7,5},{8,10},{9,11},{10,... | collective-permute-start | bytes 1081352 | tf_op jit(solution)/shard_map/ppermute | solution.py:388
  48.0 16.7 %collective-permute-start = (bf16[1,352,512]{2,1,0:T(8,128)(2,1)}, bf16[1,352,512]{2,1,0:T(8,128)(2,1)}, u32[]{:S(2)}, u32[]{:S(2)}) collective-permute-start(bf16[1,352,512]{2,1,0:T(8,128)(2,1)} %get-tuple-element.31), channel_id=1, source_target_pairs={{0,4},{4,0},{8,12},{12,8},{16,20},{20,16},{24,28},{28,24},{1,5},{5... | collective-permute-start | bytes 1081352 | tf_op jit(solution)/shard_map/ppermute | solution.py:388
  55.3 9.4 %collective-permute-start.5 = (bf16[2,16,1408]{2,1,0:T(8,128)(2,1)S(1)}, bf16[2,16,1408]{2,1,0:T(8,128)(2,1)S(1)}, u32[]{:S(2)}, u32[]{:S(2)}) collective-permute-start(bf16[2,16,1408]{2,1,0:T(8,128)(2,1)S(1)} %get-tuple-element.63), channel_id=1, source_target_pairs={{0,16},{4,20},{8,24},{12,28},{16,0},{20,4},{24,8},{28,12},{1,17},{... | collective-permute-start | bytes 270344 | tf_op jit(solution)/shard_map/ppermute | solution.py:388
  57.4 7.2 %collective-permute-start.6 = (bf16[2,16,1408]{2,1,0:T(8,128)(2,1)S(1)}, bf16[2,16,1408]{2,1,0:T(8,128)(2,1)S(1)}, u32[]{:S(2)}, u32[]{:S(2)}) collective-permute-start(bf16[2,16,1408]{2,1,0:T(8,128)(2,1)S(1)} %get-tuple-element.62), channel_id=1, source_target_pairs={{0,24},{4,28},{8,16},{12,20},{16,8},{20,12},{24,0},{28,4},{1,25},{... | collective-permute-start | bytes 270344 | tf_op jit(solution)/shard_map/ppermute | solution.py:388
  64.7 3.1 %collective-permute-start.8 = (bf16[2,352,512]{2,1,0:T(8,128)(2,1)}, bf16[2,352,512]{2,1,0:T(8,128)(2,1)}, u32[]{:S(2)}, u32[]{:S(2)}) collective-permute-start(bf16[2,352,512]{2,1,0:T(8,128)(2,1)} %collective-permute-done.1.refs_1_), channel_id=1, source_target_pairs={{0,1},{1,0},{2,3},{3,2},{4,5},{5,4},{6,7},{7,6},{8,9},{9,8},{10,11... | collective-permute-start | bytes 2162696 | tf_op jit(solution)/shard_map/ppermute | solution.py:388
  64.8 3.0 %collective-permute-start.7 = (bf16[1,352,512]{2,1,0:T(8,128)(2,1)}, bf16[1,352,512]{2,1,0:T(8,128)(2,1)}, u32[]{:S(2)}, u32[]{:S(2)}) collective-permute-start(bf16[1,352,512]{2,1,0:T(8,128)(2,1)} %collective-permute-done.refs_0_), channel_id=1, source_target_pairs={{0,1},{1,0},{2,3},{3,2},{4,5},{5,4},{6,7},{7,6},{8,9},{9,8},{10,11... | collective-permute-start | bytes 1081352 | tf_op jit(solution)/shard_map/ppermute | solution.py:388
  65.3 6.5 %collective-permute-start.9 = (bf16[2,16,1408]{2,1,0:T(8,128)(2,1)}, bf16[2,16,1408]{2,1,0:T(8,128)(2,1)S(1)}, u32[]{:S(2)}, u32[]{:S(2)}) collective-permute-start(bf16[2,16,1408]{2,1,0:T(8,128)(2,1)} %get-tuple-element.60), channel_id=1, source_target_pairs={{0,8},{4,12},{8,0},{12,4},{16,24},{20,28},{24,16},{28,20},{1,9},{5... | collective-permute-start | bytes 270344 | tf_op jit(solution)/shard_map/ppermute | solution.py:388
  71.7 17.1 %copy-start.3 = (bf16[2,64,1408]{2,1,0:T(8,128)(2,1)S(1)}, bf16[2,64,1408]{2,1,0:T(8,128)(2,1)}, u32[]{:S(2)}) copy-start(bf16[2,64,1408]{2,1,0:T(8,128)(2,1)} %param.9) | copy-start | bytes 1081348
  71.7 17.1 %copy-start.7 = (bf16[2,64,1408]{2,1,0:T(8,128)(2,1)S(1)}, bf16[2,64,1408]{2,1,0:T(8,128)(2,1)}, u32[]{:S(2)}) copy-start(bf16[2,64,1408]{2,1,0:T(8,128)(2,1)} %param.17) | copy-start | bytes 1081348
  71.9 10.8 %collective-permute-start.11 = (bf16[2,726,128]{2,1,0:T(8,128)(2,1)S(1)}, bf16[2,726,128]{2,1,0:T(8,128)(2,1)S(1)}, u32[]{:S(2)}, u32[]{:S(2)}) collective-permute-start(bf16[2,726,128]{2,1,0:T(8,128)(2,1)S(1)} %get-tuple-element.52), channel_id=1, source_target_pairs={{0,8},{1,9},{2,10},{3,11},{4,12},{5,13},{6,14},{7,15},{8,0},{9,1},... | collective-permute-start | bytes 1115144 | tf_op jit(solution)/shard_map/ppermute | solution.py:438
  73.6 16.6 %collective-permute-start.14 = (bf16[726,128]{1,0:T(8,128)(2,1)S(1)}, bf16[726,128]{1,0:T(8,128)(2,1)S(1)}, u32[]{:S(2)}, u32[]{:S(2)}) collective-permute-start(bf16[726,128]{1,0:T(8,128)(2,1)S(1)} %get-tuple-element.50), channel_id=1, source_target_pairs={{0,2},{1,3},{2,0},{3,1},{4,6},{5,7},{6,4},{7,5},{8,10},{9,11},{10,... | collective-permute-start | bytes 557576 | tf_op jit(solution)/shard_map/ppermute | solution.py:438
  75.0 13.3 %collective-permute-start.10 = (bf16[4,16,1408]{2,1,0:T(8,128)(2,1)S(1)}, bf16[4,16,1408]{2,1,0:T(8,128)(2,1)S(1)}, u32[]{:S(2)}, u32[]{:S(2)}) collective-permute-start(bf16[4,16,1408]{2,1,0:T(8,128)(2,1)S(1)} %get-tuple-element.58), channel_id=1, source_target_pairs={{0,4},{4,0},{8,12},{12,8},{16,20},{20,16},{24,28},{28,24},{1,5},{5... | collective-permute-start | bytes 540680 | tf_op jit(solution)/shard_map/ppermute | solution.py:388
  82.8 11.6 %collective-permute-start.12 = (bf16[726,128]{1,0:T(8,128)(2,1)S(1)}, bf16[726,128]{1,0:T(8,128)(2,1)S(1)}, u32[]{:S(2)}, u32[]{:S(2)}) collective-permute-start(bf16[726,128]{1,0:T(8,128)(2,1)S(1)} %get-tuple-element.57), channel_id=1, source_target_pairs={{0,8},{1,9},{2,10},{3,11},{4,12},{5,13},{6,14},{7,15},{8,0},{9,1},... | collective-permute-start | bytes 557576 | tf_op jit(solution)/shard_map/ppermute | solution.py:438
  84.5 12.3 %collective-permute-start.13 = (bf16[726,128]{1,0:T(8,128)(2,1)S(1)}, bf16[726,128]{1,0:T(8,128)(2,1)S(1)}, u32[]{:S(2)}, u32[]{:S(2)}) collective-permute-start(bf16[726,128]{1,0:T(8,128)(2,1)S(1)} %get-tuple-element.55), channel_id=1, source_target_pairs={{0,16},{1,17},{2,18},{3,19},{4,20},{5,21},{6,22},{7,23},{8,24},{9,... | collective-permute-start | bytes 557576 | tf_op jit(solution)/shard_map/ppermute | solution.py:438
  86.9 14.4 %collective-permute-start.15 = (bf16[726,128]{1,0:T(8,128)(2,1)S(1)}, bf16[726,128]{1,0:T(8,128)(2,1)S(1)}, u32[]{:S(2)}, u32[]{:S(2)}) collective-permute-start(bf16[726,128]{1,0:T(8,128)(2,1)S(1)} %get-tuple-element.56), channel_id=1, source_target_pairs={{0,10},{1,11},{2,8},{3,9},{4,14},{5,15},{6,12},{7,13},{8,2},{9,3},... | collective-permute-start | bytes 557576 | tf_op jit(solution)/shard_map/ppermute | solution.py:438
  88.2 15.6 %collective-permute-start.16 = (bf16[726,128]{1,0:T(8,128)(2,1)S(1)}, bf16[726,128]{1,0:T(8,128)(2,1)S(1)}, u32[]{:S(2)}, u32[]{:S(2)}) collective-permute-start(bf16[726,128]{1,0:T(8,128)(2,1)S(1)} %get-tuple-element.54), channel_id=1, source_target_pairs={{0,18},{1,19},{2,16},{3,17},{4,22},{5,23},{6,20},{7,21},{8,26},{9,... | collective-permute-start | bytes 557576 | tf_op jit(solution)/shard_map/ppermute | solution.py:438
